TPU v7x, 32 devices: a whole 2x2x4 slice. The times are simulated.
32 devices in a mesh: seq: 4 (over y, x), dp: 8 (over z, core).
Axes of the slice: x: 2, y: 2, z: 4, core: 2. Of those that a mesh axis runs over, the one named last changes fastest.
Arguments:
- layer_input: bfloat16 [8, 1024, 2048], P('dp', 'seq'), may hold values from -6 to 6
- out_cotangent: bfloat16 [8, 1024, 2048], P('dp', 'seq'), may hold values from -6 to 6
- gain_attention: float32 [2048], replicated, may hold values from 0.5 to 1.5
- gain_query: float32 [128], replicated, may hold values from 1 to 2
- gain_key: float32 [128], replicated, may hold values from 1 to 2
- gain_ffn: float32 [2048], replicated, may hold values from 0.5 to 1.5
- w_qkv: bfloat16 [3, 2048, 2048], P(None, None, ('seq', 'dp')), may hold values from -0.125 to 0.125
- w_output: bfloat16 [2048, 2048], P(('seq', 'dp')), may hold values from -0.5 to 0.5
- a_attention: bfloat16 [4, 2048, 128], P(None, ('seq', 'dp')), may hold values from -0.125 to 0.125
- b_attention: bfloat16 [4, 128, 2048], P(None, None, ('seq', 'dp')), may hold values from -0.75 to 0.75
- expert_w_in: bfloat16 [16, 2, 2048, 1024], P('dp'), may hold values from -0.125 to 0.125
- expert_w_down: bfloat16 [16, 1024, 2048], P('dp'), may hold values from -0.75 to 0.75
- expert_a_in: bfloat16 [16, 2, 2048, 128], P('dp'), may hold values from -0.125 to 0.125
- expert_b_in: bfloat16 [16, 2, 128, 1024], P('dp'), may hold values from -0.75 to 0.75
- expert_a_down: bfloat16 [16, 1024, 128], P('dp'), may hold values from -0.1875 to 0.1875
- expert_b_down: bfloat16 [16, 128, 2048], P('dp'), may hold values from -0.75 to 0.75
- route_experts: int32 [8, 1024, 8], P('dp', 'seq'), may hold values from 0 to 15, all different within a row; in each aligned block of 256 rows (0 to 255, 256 to 511, ..., all dimensions but the last counted through in order) at most 144 rows name the same one
- route_gates: float32 [8, 1024, 8], P('dp', 'seq'), may hold values from 0.0625 to 0.1875
- doc_lengths: int32 [8, 8], P('dp'), may hold values from 1 to 512, 1024 in all within a row
- adapter_ids: int32 [8, 8], P('dp'), may hold values from 0 to 7
Outputs:
- layer_output: bfloat16 [8, 1024, 2048], P('dp', 'seq')
- input_grad: bfloat16 [8, 1024, 2048], P('dp', 'seq')
- grad_a_attention: float32 [4, 2048, 128], P(None, ('seq', 'dp'))
- grad_b_attention: float32 [4, 128, 2048], P(None, None, ('seq', 'dp'))
- grad_expert_a_in: float32 [16, 2, 2048, 128], P('dp', None, 'seq')
- grad_expert_b_in: float32 [16, 2, 128, 1024], P('dp', None, None, 'seq')
- grad_expert_a_down: float32 [16, 1024, 128], P('dp', 'seq')
- grad_expert_b_down: float32 [16, 128, 2048], P('dp', None, 'seq')
Inputs may be any that keep to these rules, and one draw needn't show every extreme that they name: `route_experts`: each row names 8 different experts; within the rows of one device no expert is named more than 144 times, and in some device's rows one expert is named exactly 144 times. `doc_lengths`: each sequence's 8 lengths sum to 1024, and its longest document has 512 tokens.
All inputs are finite; a program needn't handle non-finite values.
Results may differ from a plain program's by a relative error of at most 0.024.
Values may be sent and summed in bfloat16 or wider, within the bound.
A program may use at most 320 MiB of HBM per device.

v0:
```python
import jax
import jax.numpy as jnp
from jax import lax
from jax.sharding import PartitionSpec as P

H = 16
HD = 128
TOP = 8
R = 16


norm_epsilon = 1e-06
rope_base = 10000.0
masked_score = -1000000000.0


def rms_scale(values, gain_vector):
    return (
        values
        * lax.rsqrt(jnp.mean(values * values, axis=-1, keepdims=True) + norm_epsilon)
        * gain_vector
    )


def rotate(values, offset):
    full_width = values.shape[-1]
    half_width = full_width // 2
    frequency = rope_base ** (-(jnp.arange(half_width, dtype=jnp.float32) * 2.0) / full_width)
    angles = offset.astype(jnp.float32)[:, None] * frequency[None, :]
    cosine = jnp.concatenate([jnp.cos(angles), jnp.cos(angles)], axis=-1)[:, None, :]
    sine_table = jnp.concatenate([jnp.sin(angles), jnp.sin(angles)], axis=-1)[:, None, :]
    turned = jnp.concatenate([-values[..., half_width:], values[..., :half_width]], axis=-1)
    return values * cosine + turned * sine_table


def head_prepare(raw_heads, gain_vector, offset):
    return rotate(rms_scale(raw_heads, gain_vector), offset)


def doc_layout(lengths, chosen, length):
    doc_ends = jnp.cumsum(lengths)
    starts = doc_ends - lengths
    position = jnp.arange(length, dtype=jnp.int32)
    segment = jnp.sum((position[:, None] >= doc_ends[None, :]).astype(jnp.int32), axis=1)
    doc_pick = (segment[:, None] == jnp.arange(lengths.shape[0], dtype=jnp.int32)[None, :]).astype(
        jnp.int32
    )
    offset = position - jnp.sum(doc_pick * starts[None, :], axis=1)
    adapter = jnp.sum(doc_pick * chosen[None, :], axis=1)
    return (segment, offset, adapter)


def column_mask(adapter, columns):
    groups = jnp.arange(columns, dtype=jnp.int32) // R
    return (groups[None, :] == adapter[:, None]).astype(jnp.float32)


def project(inputs, weight, down_map, up_map, set_mask):
    reduced = (set_mask * jnp.dot(inputs, down_map, preferred_element_type=jnp.float32)).astype(
        jnp.bfloat16
    )
    result = jnp.dot(inputs, weight, preferred_element_type=jnp.float32) + jnp.dot(
        reduced, up_map, preferred_element_type=jnp.float32
    )
    return (result, reduced)


def project_back(inputs, weight, down_map, up_map, set_mask, reduced, grad_result):
    grad_up = jnp.dot(reduced.T, grad_result, preferred_element_type=jnp.float32)
    grad_reduced = (
        set_mask * jnp.dot(grad_result, up_map.T, preferred_element_type=jnp.float32)
    ).astype(jnp.bfloat16)
    grad_down = jnp.dot(inputs.T, grad_reduced, preferred_element_type=jnp.float32)
    grad_inputs = jnp.dot(grad_result, weight.T, preferred_element_type=jnp.float32) + jnp.dot(
        grad_reduced, down_map.T, preferred_element_type=jnp.float32
    )
    return (grad_inputs, grad_down, grad_up)


def block_scores(query_part, part_segment, key, segment):
    score_scale = query_part.shape[-1] ** (-0.5)
    scores = (
        jnp.einsum("qhd,khd->hqk", query_part, key, preferred_element_type=jnp.float32)
        * score_scale
    )
    same_doc = part_segment[:, None] == segment[None, :]
    return jnp.where(same_doc[None], scores, masked_score)


def attend(query, key, value, segment):
    length = query.shape[0]
    block_rows = min(512, length)
    block_count = length // block_rows

    def one_block(operand):
        query_part, part_segment = operand
        scores = block_scores(query_part, part_segment, key, segment)
        row_max = jnp.max(scores, axis=-1, keepdims=True)
        row_exp = jnp.exp(scores - row_max)
        row_total = jnp.sum(row_exp, axis=-1, keepdims=True)
        soft_low = (row_exp / row_total).astype(jnp.bfloat16)
        mixed_part = jnp.einsum("hqk,khd->qhd", soft_low, value, preferred_element_type=jnp.float32)
        return (mixed_part, (row_max + jnp.log(row_total))[..., 0])

    mixed, logsum = lax.map(
        one_block,
        (
            query.reshape((block_count, block_rows) + query.shape[1:]),
            segment.reshape(block_count, block_rows),
        ),
    )
    return (mixed.reshape(query.shape), logsum)


def attend_back(query, key, value, segment, logsum, grad_mixed):
    length = query.shape[0]
    block_rows = min(512, length)
    block_count = length // block_rows
    score_scale = query.shape[-1] ** (-0.5)

    def one_block(running, operand):
        grad_key, grad_value = running
        query_part, part_segment, part_logsum, part_grad = operand
        scores = block_scores(query_part, part_segment, key, segment)
        soft_full = jnp.exp(scores - part_logsum[..., None])
        soft_low = soft_full.astype(jnp.bfloat16)
        grad_soft = jnp.einsum("qhd,khd->hqk", part_grad, value, preferred_element_type=jnp.float32)
        row_delta = jnp.sum(soft_full * grad_soft, axis=-1, keepdims=True)
        grad_scores = (soft_full * (grad_soft - row_delta)).astype(jnp.bfloat16)
        grad_part = (
            jnp.einsum("hqk,khd->qhd", grad_scores, key, preferred_element_type=jnp.float32)
            * score_scale
        )
        grad_key = (
            grad_key
            + jnp.einsum(
                "hqk,qhd->khd", grad_scores, query_part, preferred_element_type=jnp.float32
            )
            * score_scale
        )
        grad_value = grad_value + jnp.einsum(
            "hqk,qhd->khd", soft_low, part_grad, preferred_element_type=jnp.float32
        )
        return ((grad_key, grad_value), grad_part)

    zeros_heads = jnp.zeros(query.shape, jnp.float32)
    block_shape = (block_count, block_rows) + query.shape[1:]
    (grad_key, grad_value), grad_query = lax.scan(
        one_block,
        (zeros_heads, zeros_heads),
        (
            query.reshape(block_shape),
            segment.reshape(block_count, block_rows),
            logsum,
            grad_mixed.reshape(block_shape),
        ),
    )
    return (grad_query.reshape(query.shape), grad_key, grad_value)


def expert_forward(inputs, set_mask, w_in, w_down, a_in, b_in, a_down, b_down):
    gate_raw, gate_reduced = project(inputs, w_in[0], a_in[0], b_in[0], set_mask)
    up_raw, up_reduced = project(inputs, w_in[1], a_in[1], b_in[1], set_mask)
    activated = (jax.nn.silu(gate_raw) * up_raw).astype(jnp.bfloat16)
    down_raw, down_reduced = project(activated, w_down, a_down, b_down, set_mask)
    return (
        down_raw.astype(jnp.bfloat16),
        (gate_raw, up_raw, gate_reduced, up_reduced, activated, down_reduced),
    )


def expert_backward(inputs, set_mask, w_in, w_down, a_in, b_in, a_down, b_down, kept, grad_rows):
    gate_raw, up_raw, gate_reduced, up_reduced, activated, down_reduced = kept
    grad_act, grad_a_down, grad_b_down = project_back(
        activated, w_down, a_down, b_down, set_mask, down_reduced, grad_rows
    )
    unused, pull_gated = jax.vjp(
        lambda gate_in, up_in: jax.nn.silu(gate_in) * up_in, gate_raw, up_raw
    )
    grad_gate, grad_up = pull_gated(grad_act)
    grad_from_gate, grad_a_gate, grad_b_gate = project_back(
        inputs, w_in[0], a_in[0], b_in[0], set_mask, gate_reduced, grad_gate.astype(jnp.bfloat16)
    )
    grad_from_up, grad_a_up, grad_b_up = project_back(
        inputs, w_in[1], a_in[1], b_in[1], set_mask, up_reduced, grad_up.astype(jnp.bfloat16)
    )
    grad_inputs = (grad_from_gate + grad_from_up).astype(jnp.bfloat16)
    return (
        grad_inputs,
        jnp.stack([grad_a_gate, grad_a_up]),
        jnp.stack([grad_b_gate, grad_b_up]),
        grad_a_down,
        grad_b_down,
    )


def local(
    layer_input,
    out_cotangent,
    gain_attention,
    gain_query,
    gain_key,
    gain_ffn,
    w_qkv,
    w_output,
    a_attention,
    b_attention,
    expert_w_in,
    expert_w_down,
    expert_a_in,
    expert_b_in,
    expert_a_down,
    expert_b_down,
    route_experts,
    route_gates,
    doc_lengths,
    adapter_ids,
):
    own_rows = layer_input.shape[1]
    full_width = layer_input.shape[2]
    seq_count = lax.axis_size("seq")
    dp_count = lax.axis_size("dp")
    seq_rank = lax.axis_index("seq")
    length = own_rows * seq_count
    rank_columns = a_attention.shape[2]
    group_width = full_width // seq_count
    group_heads = H // seq_count
    group_start = seq_rank * group_width
    segment, offset, adapter = doc_layout(doc_lengths[0], adapter_ids[0], length)
    own_adapter = lax.dynamic_slice_in_dim(adapter, seq_rank * own_rows, own_rows)
    own_mask = column_mask(own_adapter, rank_columns)
    tokens = layer_input[0].astype(jnp.float32)
    normed = rms_scale(tokens, gain_attention).astype(jnp.bfloat16)
    qkv_group, output_group, down_piece, up_piece = (
        lax.all_gather(w_qkv, "dp", axis=2, tiled=True),
        lax.all_gather(w_output, "dp", axis=0, tiled=True),
        lax.all_gather(a_attention, "dp", axis=1, tiled=True),
        lax.all_gather(b_attention, "dp", axis=2, tiled=True),
    )
    normed_all, down_full, up_full = (
        lax.all_gather(normed, "seq", axis=0, tiled=True),
        lax.all_gather(down_piece, "seq", axis=1, tiled=True),
        lax.all_gather(up_piece, "seq", axis=2, tiled=True),
    )
    full_mask = column_mask(adapter, rank_columns)
    raw_list = []
    reduced_list = []
    for member in range(3):
        reduced = (
            full_mask * jnp.dot(normed_all, down_full[member], preferred_element_type=jnp.float32)
        ).astype(jnp.bfloat16)
        up_cols = lax.dynamic_slice_in_dim(up_full[member], group_start, group_width, 1)
        raw_value = jnp.dot(
            normed_all, qkv_group[member], preferred_element_type=jnp.float32
        ) + jnp.dot(reduced, up_cols, preferred_element_type=jnp.float32)
        raw_list.append(raw_value)
        reduced_list.append(reduced)
    query_raw = raw_list[0].reshape(length, group_heads, HD)
    key_raw = raw_list[1].reshape(length, group_heads, HD)
    query_heads = head_prepare(query_raw, gain_query, offset).astype(jnp.bfloat16)
    key_heads = head_prepare(key_raw, gain_key, offset).astype(jnp.bfloat16)
    value_heads = raw_list[2].astype(jnp.bfloat16).reshape(length, group_heads, HD)
    mixed, logsum = attend(query_heads, key_heads, value_heads, segment)
    mixed_group = mixed.astype(jnp.bfloat16).reshape(length, group_width)
    down_rows = lax.dynamic_slice_in_dim(down_full[3], group_start, group_width, 0)
    partial_out = jnp.dot(mixed_group, output_group, preferred_element_type=jnp.float32)
    partial_reduced = jnp.dot(mixed_group, down_rows, preferred_element_type=jnp.float32)
    summed_out, summed_reduced = (
        lax.psum_scatter(
            partial_out.astype(jnp.bfloat16), "seq", scatter_dimension=0, tiled=True
        ).astype(jnp.float32),
        lax.psum_scatter(
            partial_reduced.astype(jnp.bfloat16), "seq", scatter_dimension=0, tiled=True
        ).astype(jnp.float32),
    )
    output_reduced = (own_mask * summed_reduced).astype(jnp.bfloat16)
    attended = summed_out + jnp.dot(output_reduced, up_full[3], preferred_element_type=jnp.float32)
    hidden = tokens + attended
    normed_ffn = rms_scale(hidden, gain_ffn).astype(jnp.bfloat16)
    local_count = expert_w_in.shape[0]
    expert_count = local_count * dp_count
    capacity = own_rows * TOP // expert_count * 9 // 8
    slot_total = expert_count * capacity
    pair_expert = route_experts[0].reshape(-1)
    pair_count = own_rows * TOP
    one_hot = (pair_expert[:, None] == jnp.arange(expert_count, dtype=jnp.int32)[None, :]).astype(
        jnp.int32
    )
    pair_rank = jnp.sum(jnp.cumsum(one_hot, axis=0) * one_hot, axis=1) - 1
    slot_index = (
        pair_expert % local_count * dp_count + pair_expert // local_count
    ) * capacity + pair_rank
    slot_source = (
        jnp.full((slot_total,), own_rows, jnp.int32)
        .at[slot_index]
        .set(jnp.arange(pair_count, dtype=jnp.int32) // TOP)
    )
    slot_gate = jnp.zeros((slot_total,), jnp.float32).at[slot_index].set(route_gates[0].reshape(-1))
    padded_rows = jnp.concatenate([normed_ffn, jnp.zeros((1, full_width), jnp.bfloat16)], axis=0)
    padded_sets = jnp.concatenate([own_adapter, jnp.zeros((1,), jnp.int32)])
    send_rows = padded_rows[slot_source].reshape(local_count, dp_count, capacity, full_width)
    send_sets = (
        padded_sets[slot_source].astype(jnp.bfloat16).reshape(local_count, dp_count, capacity)
    )
    grad_out = out_cotangent[0].astype(jnp.float32)
    padded_grad = jnp.concatenate([grad_out, jnp.zeros((1, full_width), jnp.float32)], axis=0)
    send_grad = (
        (slot_gate[:, None] * padded_grad[slot_source])
        .astype(jnp.bfloat16)
        .reshape(local_count, dp_count, capacity, full_width)
    )
    got_rows, got_sets, got_grad = (
        lax.all_to_all(send_rows, "dp", split_axis=1, concat_axis=1, tiled=True),
        lax.all_to_all(send_sets, "dp", split_axis=1, concat_axis=1, tiled=True),
        lax.all_to_all(send_grad, "dp", split_axis=1, concat_axis=1, tiled=True),
    )
    expert_outputs = []
    grad_inputs_list = []
    grad_a_in_list = []
    grad_b_in_list = []
    grad_a_down_list = []
    grad_b_down_list = []
    for member in range(local_count):
        inputs = got_rows[member].reshape(dp_count * capacity, full_width)
        row_mask = column_mask(got_sets[member].reshape(-1).astype(jnp.int32), rank_columns)
        produced, kept = expert_forward(
            inputs,
            row_mask,
            expert_w_in[member],
            expert_w_down[member],
            expert_a_in[member],
            expert_b_in[member],
            expert_a_down[member],
            expert_b_down[member],
        )
        expert_outputs.append(produced)
        grad_rows = got_grad[member].reshape(dp_count * capacity, full_width)
        grad_inputs, grad_a_in, grad_b_in, grad_a_down, grad_b_down = expert_backward(
            inputs,
            row_mask,
            expert_w_in[member],
            expert_w_down[member],
            expert_a_in[member],
            expert_b_in[member],
            expert_a_down[member],
            expert_b_down[member],
            kept,
            grad_rows,
        )
        grad_inputs_list.append(grad_inputs)
        grad_a_in_list.append(grad_a_in)
        grad_b_in_list.append(grad_b_in)
        grad_a_down_list.append(grad_a_down)
        grad_b_down_list.append(grad_b_down)
    produced_all = jnp.stack(expert_outputs).reshape(local_count, dp_count, capacity, full_width)
    grad_inputs_all = jnp.stack(grad_inputs_list).reshape(
        local_count, dp_count, capacity, full_width
    )
    returned, back_rows = (
        lax.all_to_all(produced_all, "dp", split_axis=1, concat_axis=1, tiled=True),
        lax.all_to_all(grad_inputs_all, "dp", split_axis=1, concat_axis=1, tiled=True),
    )
    picked = returned.reshape(slot_total, full_width)[slot_index].reshape(own_rows, TOP, full_width)
    mixture = jnp.einsum("tk,tkd->td", route_gates[0], picked, preferred_element_type=jnp.float32)
    layer_output = (hidden + mixture).astype(jnp.bfloat16)[None]
    grad_normed_ffn = jnp.sum(
        back_rows.reshape(slot_total, full_width)[slot_index]
        .reshape(own_rows, TOP, full_width)
        .astype(jnp.float32),
        axis=1,
    )
    unused, pull_ffn = jax.vjp(lambda values: rms_scale(values, gain_ffn), hidden)
    grad_hidden = grad_out + pull_ffn(grad_normed_ffn)[0]
    grad_hidden_low = grad_hidden.astype(jnp.bfloat16)
    grad_down_list = []
    grad_up_list = []
    grad_up_output = jnp.dot(output_reduced.T, grad_hidden_low, preferred_element_type=jnp.float32)
    grad_reduced_output = (
        own_mask * jnp.dot(grad_hidden_low, up_full[3].T, preferred_element_type=jnp.float32)
    ).astype(jnp.bfloat16)
    grad_all, grad_reduced_all = (
        lax.all_gather(grad_hidden_low, "seq", axis=0, tiled=True),
        lax.all_gather(grad_reduced_output, "seq", axis=0, tiled=True),
    )
    grad_mixed_group = (
        jnp.dot(grad_all, output_group.T, preferred_element_type=jnp.float32)
        + jnp.dot(grad_reduced_all, down_rows.T, preferred_element_type=jnp.float32)
    ).astype(jnp.bfloat16)
    grad_down_rows = jnp.dot(mixed_group.T, grad_reduced_all, preferred_element_type=jnp.float32)
    grad_down_output = lax.dynamic_update_slice_in_dim(
        jnp.zeros((full_width, rank_columns), jnp.float32), grad_down_rows, group_start, 0
    )
    grad_query, grad_key, grad_value = attend_back(
        query_heads,
        key_heads,
        value_heads,
        segment,
        logsum,
        grad_mixed_group.reshape(length, group_heads, HD),
    )
    unused_query, pull_query = jax.vjp(
        lambda values: head_prepare(values, gain_query, offset), query_raw
    )
    unused_key, pull_key = jax.vjp(lambda values: head_prepare(values, gain_key, offset), key_raw)
    grad_raw_list = [
        pull_query(grad_query.astype(jnp.bfloat16).astype(jnp.float32))[0]
        .reshape(length, group_width)
        .astype(jnp.bfloat16),
        pull_key(grad_key.astype(jnp.bfloat16).astype(jnp.float32))[0]
        .reshape(length, group_width)
        .astype(jnp.bfloat16),
        grad_value.astype(jnp.bfloat16).reshape(length, group_width),
    ]
    partial_normed = jnp.zeros((length, full_width), jnp.float32)
    partial_reduced_list = []
    up_blocks = []
    for member in range(3):
        up_cols = lax.dynamic_slice_in_dim(up_full[member], group_start, group_width, 1)
        partial_normed = partial_normed + jnp.dot(
            grad_raw_list[member], qkv_group[member].T, preferred_element_type=jnp.float32
        )
        partial_reduced_list.append(
            jnp.dot(grad_raw_list[member], up_cols.T, preferred_element_type=jnp.float32)
        )
        up_block = jnp.dot(
            reduced_list[member].T, grad_raw_list[member], preferred_element_type=jnp.float32
        )
        up_blocks.append(
            lax.dynamic_update_slice_in_dim(
                jnp.zeros((rank_columns, full_width), jnp.float32), up_block, group_start, 1
            )
        )
    grad_normed_part, reduced_sums = (
        lax.psum_scatter(
            partial_normed.astype(jnp.bfloat16), "seq", scatter_dimension=0, tiled=True
        ).astype(jnp.float32),
        lax.psum_scatter(
            jnp.stack(partial_reduced_list).astype(jnp.bfloat16),
            "seq",
            scatter_dimension=1,
            tiled=True,
        ).astype(jnp.float32),
    )
    grad_normed = grad_normed_part
    for member in range(3):
        grad_reduced = (own_mask * reduced_sums[member]).astype(jnp.bfloat16)
        grad_normed = grad_normed + jnp.dot(
            grad_reduced, down_full[member].T, preferred_element_type=jnp.float32
        )
        grad_down_list.append(jnp.dot(normed.T, grad_reduced, preferred_element_type=jnp.float32))
        grad_up_list.append(up_blocks[member])
    grad_down_list.append(grad_down_output)
    grad_up_list.append(grad_up_output)
    unused_input, pull_input = jax.vjp(lambda values: rms_scale(values, gain_attention), tokens)
    input_grad = (grad_hidden + pull_input(grad_normed)[0]).astype(jnp.bfloat16)[None]
    grad_a_attention, grad_b_attention = (
        lax.psum_scatter(jnp.stack(grad_down_list), ("seq", "dp"), scatter_dimension=1, tiled=True),
        lax.psum_scatter(jnp.stack(grad_up_list), ("seq", "dp"), scatter_dimension=2, tiled=True),
    )
    grad_expert_a_in, grad_expert_b_in, grad_expert_a_down, grad_expert_b_down = (
        lax.psum_scatter(
            jnp.stack(grad_a_in_list).astype(jnp.bfloat16), "seq", scatter_dimension=2, tiled=True
        ).astype(jnp.float32),
        lax.psum_scatter(
            jnp.stack(grad_b_in_list).astype(jnp.bfloat16), "seq", scatter_dimension=3, tiled=True
        ).astype(jnp.float32),
        lax.psum_scatter(
            jnp.stack(grad_a_down_list).astype(jnp.bfloat16), "seq", scatter_dimension=1, tiled=True
        ).astype(jnp.float32),
        lax.psum_scatter(
            jnp.stack(grad_b_down_list).astype(jnp.bfloat16), "seq", scatter_dimension=2, tiled=True
        ).astype(jnp.float32),
    )
    return (
        layer_output,
        input_grad,
        grad_a_attention,
        grad_b_attention,
        grad_expert_a_in,
        grad_expert_b_in,
        grad_expert_a_down,
        grad_expert_b_down,
    )


def solution(mesh):
    return jax.shard_map(
        local,
        mesh=mesh,
        in_specs=(
            P("dp", "seq", None),
            P("dp", "seq", None),
            P(),
            P(),
            P(),
            P(),
            P(None, None, ("seq", "dp")),
            P(("seq", "dp"), None),
            P(None, ("seq", "dp"), None),
            P(None, None, ("seq", "dp")),
            P("dp", None, None, None),
            P("dp", None, None),
            P("dp", None, None, None),
            P("dp", None, None, None),
            P("dp", None, None),
            P("dp", None, None),
            P("dp", "seq", None),
            P("dp", "seq", None),
            P("dp", None),
            P("dp", None),
        ),
        out_specs=(
            P("dp", "seq", None),
            P("dp", "seq", None),
            P(None, ("seq", "dp"), None),
            P(None, None, ("seq", "dp")),
            P("dp", None, "seq", None),
            P("dp", None, None, "seq"),
            P("dp", "seq", None),
            P("dp", None, "seq"),
        ),
        check_vma=False,
    )
```

profile of v0, /device:TPU:0, one launch (start us, length us, event | category | flops | bytes accessed | tf_op | source)
XLA Modules:
  0.0 1808.1 jit_solution(4160155078802362925)
XLA Ops:
  7.2 17.7 all_gather.31
  25.1 16.1 all_gather.29
  61.6 13.9 gather_fusion.1
  87.3 11.4 gather_fusion.3
  111.5 10.2 fusion.32
  126.2 27.4 %all-gather.7.cloned.1.call-done = bf16[1024,2048]{1,0:T(8,128)(2,1)} async-done(((bf16[256,2048]{1,0:T(8,128)(2,1)}), bf16[1024,2048]{1,0:T(8,128)(2,1)}) %all-gather.7.cloned.1.call-update) | async-done | bytes 4194320 | tf_op jit(solution)/shard_map/all_gather | solution.py:241
  160.6 59.2 %all-gather.9.cloned.1.call-done = bf16[3,2048,512]{1,2,0:T(8,128)(2,1)} async-done(((bf16[3,2048,64]{1,2,0:T(8,128)(2,1)}), bf16[3,2048,512]{1,2,0:T(8,128)(2,1)}) %all-gather.9.cloned.1.call-update) | async-done | bytes 6291472 | tf_op jit(solution)/shard_map/all_gather | solution.py:235
  275.7 16.4 while.27
  304.6 19.1 %reduce-scatter.12.cloned.1.call-done = bf16[256,128]{1,0:T(8,128)(2,1)} async-done(((bf16[1024,128]{1,0:T(8,128)(2,1)}), bf16[256,128]{1,0:T(8,128)(2,1)}) %reduce-scatter.12.cloned.1.call-update) | async-done | bytes 65552 | tf_op jit(solution)/shard_map/reduce_scatter | solution.py:272
  323.7 55.6 %reduce-scatter.10.cloned.1.call-done = bf16[256,2048]{1,0:T(8,128)(2,1)} async-done(((bf16[1024,2048]{1,0:T(8,128)(2,1)}), bf16[256,2048]{1,0:T(8,128)(2,1)}) %reduce-scatter.10.cloned.1.call-update) | async-done | bytes 1048592 | tf_op jit(solution)/shard_map/reduce_scatter | solution.py:269
  402.2 79.8 %all-to-all-done.3 = bf16[2,8,144,2048]{3,2,0,1:T(8,128)(2,1)} async-done(((bf16[2,8,144,2048]{3,2,0,1:T(8,128)(2,1)}), bf16[2,8,144,2048]{3,2,0,1:T(8,128)(2,1)}, u32[]{:S(2)}, u32[]{:S(2)}) %all-to-all-start.3) | async-done | bytes 9437216 | tf_op jit(solution)/shard_map/all_to_all | solution.py:315
  516.5 176.9 %all-to-all-done = bf16[2,8,144,2048]{3,2,0,1:T(8,128)(2,1)} async-done(((bf16[2,8,144,2048]{3,2,0,1:T(8,128)(2,1)}), bf16[2,8,144,2048]{3,2,0,1:T(8,128)(2,1)}, u32[]{:S(2)}, u32[]{:S(2)}) %all-to-all-start) | async-done | bytes 9437216 | tf_op jit(solution)/shard_map/all_to_all | solution.py:313
  775.1 10.8 fusion.53
  833.4 206.3 %all-to-all-done.4 = bf16[2,8,144,2048]{3,2,0,1:T(8,128)(2,1)} async-done(((bf16[2,8,144,2048]{3,2,0,1:T(8,128)(2,1)}), bf16[2,8,144,2048]{3,2,0,1:T(8,128)(2,1)}, u32[]{:S(2)}, u32[]{:S(2)}) %all-to-all-start.4) | async-done | bytes 9437216 | tf_op jit(solution)/shard_map/all_to_all | solution.py:361
  1048.9 21.7 %gather_fusion.4 = bf16[2048,2048]{1,0:T(8,128)(2,1)} fusion(bf16[2304,2048]{1,0:T(8,128)(2,1)} %bitcast.535, s32[2048]{0:T(1024)S(1)} %broadcast_clamp_fusion), kind=kCustom, calls=%fused_computation.4 | custom fusion | bytes 16785408 | tf_op jit(solution)/shard_map/gather | solution.py:367
  1070.6 11.5 convert_reduce_fusion
  1098.3 39.6 %all-gather.17.cloned.1.call-done = bf16[1024,2048]{1,0:T(8,128)(2,1)} async-done(((bf16[256,2048]{1,0:T(8,128)(2,1)}), bf16[1024,2048]{1,0:T(8,128)(2,1)}) %all-gather.17.cloned.1.call-update) | async-done | bytes 4194320 | tf_op jit(solution)/shard_map/all_gather | solution.py:382
  1147.9 42.9 %while.28 = (s32[]{:T(128)}, f32[1024,4,128]{0,2,1:T(8,128)S(1)}, f32[1024,4,128]{0,2,1:T(8,128)}, bf16[2,512,4,128]{3,1,0,2:T(8,128)(2,1)}, bf16[2,512,4,128]{3...) while((s32[]{:T(128)}, f32[1024,4,128]{0,2,1:T(8,128)S(1)}, ...), condition=%wide.region_23.24_spmd.clone, body=%wide.region_21.23_spmd.clone.sunk | while | flops 2719217664 | bytes 181473200 | solution.py:148
  1339.9 36.4 %reduce-scatter.20.cloned.1.call-done = bf16[2,2,512,128]{3,2,1,0:T(8,128)(2,1)} async-done(((bf16[2,2,2048,128]{3,2,1,0:T(8,128)(2,1)}), bf16[2,2,512,128]{3,2,1,0:T(8,128)(2,1)}) %reduce-scatter.20.cloned.1.call-update) | async-done | bytes 524304 | tf_op jit(solution)/shard_map/reduce_scatter | solution.py:461
  1378.4 149.2 %all-to-all-done.2 = bf16[2,8,144,2048]{3,2,0,1:T(8,128)(2,1)} async-done(((bf16[2,8,144,2048]{3,2,0,1:T(8,128)(2,1)}), bf16[2,8,144,2048]{3,2,0,1:T(8,128)(2,1)}, u32[]{:S(2)}, u32[]{:S(2)}) %all-to-all-start.2) | async-done | bytes 9437216 | tf_op jit(solution)/shard_map/all_to_all | solution.py:360
  1536.9 21.3 %gather_fusion.2 = bf16[2048,2048]{1,0:T(8,128)(2,1)} fusion(bf16[2304,2048]{1,0:T(8,128)(2,1)} %bitcast.534, s32[2048]{0:T(1024)S(1)} %copy-done.104), kind=kCustom, calls=%fused_computation.2 | custom fusion | bytes 16785408 | tf_op jit(solution)/shard_map/gather | solution.py:363
  1563.9 35.8 %all-reduce.9.cloned.1.call-done = f32[4,128,2048]{1,0,2:T(4,128)} async-done(((f32[4,128,2048]{1,0,2:T(4,128)}), f32[4,128,2048]{1,0,2:T(4,128)}) %all-reduce.9.cloned.1.call-update) | async-done | bytes 4194320
  1601.3 53.1 %reduce-scatter.14.cloned.1.call-done = bf16[256,2048]{1,0:T(8,128)(2,1)} async-done(((bf16[1024,2048]{1,0:T(8,128)(2,1)}), bf16[256,2048]{1,0:T(8,128)(2,1)}) %reduce-scatter.14.cloned.1.call-update) | async-done | bytes 1048592 | tf_op jit(solution)/shard_map/reduce_scatter | solution.py:434
  1662.8 138.3 %reduce-scatter.18.cloned.1.call-done = f32[4,64,128]{2,1,0:T(8,128)} async-done(((f32[4,2048,128]{2,1,0:T(8,128)}), f32[4,64,128]{2,1,0:T(8,128)}) %reduce-scatter.18.cloned.1.call-update) | async-done | bytes 131088 | tf_op jit(solution)/shard_map/reduce_scatter | solution.py:457
  (592 shorter events, 579.5 us)
Async XLA Ops:
  7.2 114.5 %all-gather.13.cloned.1.call-start = ((), (), s32[]{:S(2)}) async-start(), calls=%async_computation.17 | async-start | bytes 2621440 | tf_op jit(solution)/shard_map/all_gather | solution.py:243
  25.0 99.1 %all-gather.11.cloned.1.call-start = ((), (), s32[]{:S(2)}) async-start(), calls=%async_computation.16 | async-start | bytes 2621440 | tf_op jit(solution)/shard_map/all_gather | solution.py:242
  41.2 112.4 %all-gather.7.cloned.1.call-start = ((), (), s32[]{:S(2)}) async-start(), calls=%async_computation.14 | async-start | bytes 5242880 | tf_op jit(solution)/shard_map/all_gather | solution.py:241
  46.5 173.3 %all-gather.9.cloned.1.call-start = ((), (), s32[]{:S(2)}) async-start(), calls=%async_computation.15 | async-start | bytes 7077888 | tf_op jit(solution)/shard_map/all_gather | solution.py:235
  76.3 194.3 %all-to-all-start.1 = ((bf16[2,8,144]{2,0,1:T(2,128)(2,1)}), bf16[2,8,144]{2,0,1:T(2,128)(2,1)S(1)}, u32[]{:S(2)}, u32[]{:S(2)}) async-start(bf16[2,8,144]{2,0,1:T(2,128)(2,1)} %copy.172), calls=%async_computation.3 | async-start | bytes 16384 | tf_op jit(solution)/shard_map/all_to_all | solution.py:314
  81.1 217.2 %all-gather.15.cloned.1.call-start = ((), (), s32[]{:S(2)}) async-start(), calls=%async_computation.18 | async-start | bytes 2359296 | tf_op jit(solution)/shard_map/all_gather | solution.py:236
  81.7 1004.8 %copy-start.111 = (s32[128]{0:T(128)}, s32[128]{0:T(128)S(1)}, u32[]{:S(2)}) copy-start(s32[128]{0:T(128)S(1)} %and_select_fusion.2) | copy-start | bytes 1540
  270.6 211.4 %all-to-all-start.3 = ((bf16[2,8,144,2048]{3,2,0,1:T(8,128)(2,1)}), bf16[2,8,144,2048]{3,2,0,1:T(8,128)(2,1)}, u32[]{:S(2)}, u32[]{:S(2)}) async-start(bf16[2,8,144,2048]{3,2,0,1:T(8,128)(2,1)} %fusion.32), calls=%async_computation.5 | async-start | bytes 18874368 | tf_op jit(solution)/shard_map/all_to_all | solution.py:315
  275.7 48.0 %reduce-scatter.12.cloned.1.call-start = ((), (), s32[]{:S(2)}) async-start(), calls=%async_computation.20 | async-start | bytes 327680 | tf_op jit(solution)/shard_map/reduce_scatter | solution.py:272
  298.0 81.3 %reduce-scatter.10.cloned.1.call-start = ((), (), s32[]{:S(2)}) async-start(), calls=%async_computation.19 | async-start | bytes 5242880 | tf_op jit(solution)/shard_map/reduce_scatter | solution.py:269
  482.0 211.4 %all-to-all-start = ((bf16[2,8,144,2048]{3,2,0,1:T(8,128)(2,1)}), bf16[2,8,144,2048]{3,2,0,1:T(8,128)(2,1)}, u32[]{:S(2)}, u32[]{:S(2)}) async-start(bf16[2,8,144,2048]{3,2,0,1:T(8,128)(2,1)} %copy.171), calls=%async_computation.2 | async-start | bytes 18874368 | tf_op jit(solution)/shard_map/all_to_all | solution.py:313
  487.2 269.0 %copy-start.125 = (s32[1152]{0:T(1024)}, s32[1152]{0:T(1024)S(1)}, u32[]{:S(2)}) copy-start(s32[1152]{0:T(1024)S(1)} %reshape.683) | copy-start | bytes 13828
  487.3 298.6 %copy-start.123 = (s32[1152]{0:T(1024)}, s32[1152]{0:T(1024)S(1)}, u32[]{:S(2)}) copy-start(s32[1152]{0:T(1024)S(1)} %reshape.684) | copy-start | bytes 13828
  828.1 211.5 %all-to-all-start.4 = ((bf16[2,8,144,2048]{3,2,0,1:T(8,128)(2,1)}), bf16[2,8,144,2048]{3,2,0,1:T(8,128)(2,1)}, u32[]{:S(2)}, u32[]{:S(2)}) async-start(bf16[2,8,144,2048]{3,2,0,1:T(8,128)(2,1)} %pad_maximum_fusion.1), calls=%async_computation.6 | async-start | bytes 18874368 | tf_op jit(solution)/shard_map/all_to_all | solution.py:361
  833.3 304.5 %all-gather.17.cloned.1.call-start = ((), (), s32[]{:S(2)}) async-start(), calls=%async_computation.21 | async-start | bytes 5242880 | tf_op jit(solution)/shard_map/all_gather | solution.py:382
  1086.4 237.9 %reduce-scatter.16.cloned.1.call-start = ((), (), s32[]{:S(2)}) async-start(), calls=%async_computation.23 | async-start | bytes 983040 | tf_op jit(solution)/shard_map/reduce_scatter | solution.py:437
  1220.6 110.5 %reduce-scatter.24.cloned.1.call-start = ((), (), s32[]{:S(2)}) async-start(), calls=%async_computation.27 | async-start | bytes 655360 | tf_op jit(solution)/shard_map/reduce_scatter | solution.py:467
  1229.1 103.6 %reduce-scatter.26.cloned.1.call-start = ((), (), s32[]{:S(2)}) async-start(), calls=%async_computation.28 | async-start | bytes 1310720 | tf_op jit(solution)/shard_map/reduce_scatter | solution.py:470
  1239.4 98.7 %reduce-scatter.22.cloned.1.call-start = ((), (), s32[]{:S(2)}) async-start(), calls=%async_computation.26 | async-start | bytes 1310720 | tf_op jit(solution)/shard_map/reduce_scatter | solution.py:464
  1246.6 129.7 %reduce-scatter.20.cloned.1.call-start = ((), (), s32[]{:S(2)}) async-start(), calls=%async_computation.25 | async-start | bytes 2621440 | tf_op jit(solution)/shard_map/reduce_scatter | solution.py:461
  1290.2 237.4 %all-to-all-start.2 = ((bf16[2,8,144,2048]{3,2,0,1:T(8,128)(2,1)}), bf16[2,8,144,2048]{3,2,0,1:T(8,128)(2,1)}, u32[]{:S(2)}, u32[]{:S(2)}) async-start(bf16[2,8,144,2048]{3,2,0,1:T(8,128)(2,1)} %pad_maximum_fusion), calls=%async_computation.4 | async-start | bytes 18874368 | tf_op jit(solution)/shard_map/all_to_all | solution.py:360
  1295.4 304.4 %all-reduce.9.cloned.1.call-start = ((), (), s32[]{:S(2)}) async-start(), calls=%async_computation.29 | async-start | bytes 8388608
  1307.5 347.0 %reduce-scatter.14.cloned.1.call-start = ((), (), s32[]{:S(2)}) async-start(), calls=%async_computation.22 | async-start | bytes 5242880 | tf_op jit(solution)/shard_map/reduce_scatter | solution.py:434
  1322.6 478.5 %reduce-scatter.18.cloned.1.call-start = ((), (), s32[]{:S(2)}) async-start(), calls=%async_computation.24 | async-start | bytes 4325376 | tf_op jit(solution)/shard_map/reduce_scatter | solution.py:457
  (151 other events, 2404.0 us)
Sparse Core Ops, SparseCore 0:
  25.1 36.3 all-gather.12
  63.4 35.1 all-gather.10
  101.0 52.5 all-gather.6
  155.1 64.6 all-gather.8
  221.2 27.7 all-gather.14
  298.1 25.5 reduce-scatter.11
  326.7 52.5 reduce-scatter.9
  1086.5 51.2 all-gather.16
  1220.7 26.1 reduce-scatter.15
  1250.1 25.1 reduce-scatter.23
  1278.7 27.9 reduce-scatter.25
  1310.0 28.0 reduce-scatter.21
  1341.1 35.1 reduce-scatter.19
  1381.7 218.0 all-reduce.8
  1602.6 51.8 reduce-scatter.13
  1657.1 143.9 reduce-scatter.17
where the time goes:
time: 1820 us; the launch traced here: 1810 us
  waiting for transfers between devices  1080 us (59%)
  matrix products  328 us (18%)
  local copies, waits for them, and re-layouts  182 us (10%)
  other arithmetic  128 us (7%)
  blocking collectives  43.9 us (2%)
  starting transfers between devices  27 us (1%)
    all_to_all x1, waiting for transfers between devices, local(): lax.all_to_all(grad_inputs_all, 'dp', split_axis=1, concat_axis=1, tiled=...  206 us
    all_to_all x1, waiting for transfers between devices, local(): lax.all_to_all(send_rows, 'dp', split_axis=1, concat_axis=1, tiled=True)  177 us
    all_to_all x1, waiting for transfers between devices, local(): lax.all_to_all(produced_all, 'dp', split_axis=1, concat_axis=1, tiled=True)  149 us
    reduce_scatter x1, waiting for transfers between devices, local(): lax.psum_scatter(jnp.stack(grad_down_list), ('seq', 'dp'), scatter_dimens...  138 us
    all_to_all x1, waiting for transfers between devices, local(): lax.all_to_all(send_grad, 'dp', split_axis=1, concat_axis=1, tiled=True)  79.8 us
    all_gather x1, waiting for transfers between devices, local(): lax.all_gather(w_qkv, 'dp', axis=2, tiled=True)  59.2 us
    reduce_scatter x1, waiting for transfers between devices, local(): lax.psum_scatter(partial_out.astype(jnp.bfloat16), 'seq', scatter_dimensi...  55.6 us
    reduce_scatter x1, waiting for transfers between devices, local(): lax.psum_scatter(partial_normed.astype(jnp.bfloat16), 'seq', scatter_dime...  53.1 us
  transfers between devices with their start and end apart: 21, of which 14 were waited for; matrix products, arithmetic and copies ran while one was open for 20% of the time, Pallas kernels for 0%

commit v1 on v0

v1 whole, which is shorter than its diff:
```python
import jax
import jax.numpy as jnp
from jax import lax
from jax.sharding import PartitionSpec as P

H = 16
HD = 128
TOP = 8
R = 16


norm_epsilon = 1e-06
rope_base = 10000.0
masked_score = -1000000000.0


def rms_scale(values, gain_vector):
    return (
        values
        * lax.rsqrt(jnp.mean(values * values, axis=-1, keepdims=True) + norm_epsilon)
        * gain_vector
    )


def rotate(values, offset):
    full_width = values.shape[-1]
    half_width = full_width // 2
    frequency = rope_base ** (-(jnp.arange(half_width, dtype=jnp.float32) * 2.0) / full_width)
    angles = offset.astype(jnp.float32)[:, None] * frequency[None, :]
    cosine = jnp.concatenate([jnp.cos(angles), jnp.cos(angles)], axis=-1)[:, None, :]
    sine_table = jnp.concatenate([jnp.sin(angles), jnp.sin(angles)], axis=-1)[:, None, :]
    turned = jnp.concatenate([-values[..., half_width:], values[..., :half_width]], axis=-1)
    return values * cosine + turned * sine_table


def head_prepare(raw_heads, gain_vector, offset):
    return rotate(rms_scale(raw_heads, gain_vector), offset)


def doc_layout(lengths, chosen, position):
    slots = jnp.arange(lengths.shape[0], dtype=jnp.int32)
    doc_ends = jnp.sum(jnp.where(slots[:, None] >= slots[None, :], lengths[None, :], 0), axis=1)
    starts = doc_ends - lengths
    segment = jnp.sum((position[:, None] >= doc_ends[None, :]).astype(jnp.int32), axis=1)
    doc_pick = (segment[:, None] == slots[None, :]).astype(jnp.int32)
    offset = position - jnp.sum(doc_pick * starts[None, :], axis=1)
    adapter = jnp.sum(doc_pick * chosen[None, :], axis=1)
    return (segment, offset, adapter)


def column_mask(adapter, columns):
    groups = jnp.arange(columns, dtype=jnp.int32) // R
    return (groups[None, :] == adapter[:, None]).astype(jnp.float32)


def project(inputs, weight, down_map, up_map, set_mask):
    reduced = (set_mask * jnp.dot(inputs, down_map, preferred_element_type=jnp.float32)).astype(
        jnp.bfloat16
    )
    result = jnp.dot(inputs, weight, preferred_element_type=jnp.float32) + jnp.dot(
        reduced, up_map, preferred_element_type=jnp.float32
    )
    return (result, reduced)


def project_back(inputs, weight, down_map, up_map, set_mask, reduced, grad_result):
    grad_up = jnp.dot(reduced.T, grad_result, preferred_element_type=jnp.float32)
    grad_reduced = (
        set_mask * jnp.dot(grad_result, up_map.T, preferred_element_type=jnp.float32)
    ).astype(jnp.bfloat16)
    grad_down = jnp.dot(inputs.T, grad_reduced, preferred_element_type=jnp.float32)
    grad_inputs = jnp.dot(grad_result, weight.T, preferred_element_type=jnp.float32) + jnp.dot(
        grad_reduced, down_map.T, preferred_element_type=jnp.float32
    )
    return (grad_inputs, grad_down, grad_up)


def block_scores(query_part, part_segment, key, segment):
    score_scale = query_part.shape[-1] ** (-0.5)
    scores = (
        jnp.einsum("qhd,khd->hqk", query_part, key, preferred_element_type=jnp.float32)
        * score_scale
    )
    same_doc = part_segment[:, None] == segment[None, :]
    return jnp.where(same_doc[None], scores, masked_score)


def attend(query, key, value, segment):
    length = query.shape[0]
    block_rows = min(512, length)
    block_count = length // block_rows

    def one_block(operand):
        query_part, part_segment = operand
        scores = block_scores(query_part, part_segment, key, segment)
        row_max = jnp.max(scores, axis=-1, keepdims=True)
        row_exp = jnp.exp(scores - row_max)
        row_total = jnp.sum(row_exp, axis=-1, keepdims=True)
        soft_low = (row_exp / row_total).astype(jnp.bfloat16)
        mixed_part = jnp.einsum("hqk,khd->qhd", soft_low, value, preferred_element_type=jnp.float32)
        return (mixed_part, (row_max + jnp.log(row_total))[..., 0])

    mixed, logsum = lax.map(
        one_block,
        (
            query.reshape((block_count, block_rows) + query.shape[1:]),
            segment.reshape(block_count, block_rows),
        ),
    )
    return (mixed.reshape(query.shape), logsum)


def attend_back(query, key, value, segment, logsum, grad_mixed):
    length = query.shape[0]
    block_rows = min(512, length)
    block_count = length // block_rows
    score_scale = query.shape[-1] ** (-0.5)

    def one_block(running, operand):
        grad_key, grad_value = running
        query_part, part_segment, part_logsum, part_grad = operand
        scores = block_scores(query_part, part_segment, key, segment)
        soft_full = jnp.exp(scores - part_logsum[..., None])
        soft_low = soft_full.astype(jnp.bfloat16)
        grad_soft = jnp.einsum("qhd,khd->hqk", part_grad, value, preferred_element_type=jnp.float32)
        row_delta = jnp.sum(soft_full * grad_soft, axis=-1, keepdims=True)
        grad_scores = (soft_full * (grad_soft - row_delta)).astype(jnp.bfloat16)
        grad_part = (
            jnp.einsum("hqk,khd->qhd", grad_scores, key, preferred_element_type=jnp.float32)
            * score_scale
        )
        grad_key = (
            grad_key
            + jnp.einsum(
                "hqk,qhd->khd", grad_scores, query_part, preferred_element_type=jnp.float32
            )
            * score_scale
        )
        grad_value = grad_value + jnp.einsum(
            "hqk,qhd->khd", soft_low, part_grad, preferred_element_type=jnp.float32
        )
        return ((grad_key, grad_value), grad_part)

    zeros_heads = jnp.zeros(query.shape, jnp.float32)
    block_shape = (block_count, block_rows) + query.shape[1:]
    (grad_key, grad_value), grad_query = lax.scan(
        one_block,
        (zeros_heads, zeros_heads),
        (
            query.reshape(block_shape),
            segment.reshape(block_count, block_rows),
            logsum,
            grad_mixed.reshape(block_shape),
        ),
    )
    return (grad_query.reshape(query.shape), grad_key, grad_value)


def expert_forward(inputs, set_mask, w_in, w_down, a_in, b_in, a_down, b_down):
    gate_raw, gate_reduced = project(inputs, w_in[0], a_in[0], b_in[0], set_mask)
    up_raw, up_reduced = project(inputs, w_in[1], a_in[1], b_in[1], set_mask)
    activated = (jax.nn.silu(gate_raw) * up_raw).astype(jnp.bfloat16)
    down_raw, down_reduced = project(activated, w_down, a_down, b_down, set_mask)
    return (
        down_raw.astype(jnp.bfloat16),
        (gate_raw, up_raw, gate_reduced, up_reduced, activated, down_reduced),
    )


def expert_backward(inputs, set_mask, w_in, w_down, a_in, b_in, a_down, b_down, kept, grad_rows):
    gate_raw, up_raw, gate_reduced, up_reduced, activated, down_reduced = kept
    grad_act, grad_a_down, grad_b_down = project_back(
        activated, w_down, a_down, b_down, set_mask, down_reduced, grad_rows
    )
    unused, pull_gated = jax.vjp(
        lambda gate_in, up_in: jax.nn.silu(gate_in) * up_in, gate_raw, up_raw
    )
    grad_gate, grad_up = pull_gated(grad_act)
    grad_from_gate, grad_a_gate, grad_b_gate = project_back(
        inputs, w_in[0], a_in[0], b_in[0], set_mask, gate_reduced, grad_gate.astype(jnp.bfloat16)
    )
    grad_from_up, grad_a_up, grad_b_up = project_back(
        inputs, w_in[1], a_in[1], b_in[1], set_mask, up_reduced, grad_up.astype(jnp.bfloat16)
    )
    grad_inputs = (grad_from_gate + grad_from_up).astype(jnp.bfloat16)
    return (
        grad_inputs,
        jnp.stack([grad_a_gate, grad_a_up]),
        jnp.stack([grad_b_gate, grad_b_up]),
        grad_a_down,
        grad_b_down,
    )


def swap(values, axis, distance, count):
    return lax.ppermute(values, axis, [(i, i ^ distance) for i in range(count)])


def spread(values, axis, count):
    return [values] + [swap(values, axis, k, count) for k in range(1, count)]


def collect(blocks, axis, count):
    total = blocks[0].astype(jnp.float32)
    for k in range(1, count):
        total = total + swap(blocks[k], axis, k, count).astype(jnp.float32)
    return total


def after(values, *earlier):
    return lax.optimization_barrier((values,) + earlier)[0]


def local(
    layer_input,
    out_cotangent,
    gain_attention,
    gain_query,
    gain_key,
    gain_ffn,
    w_qkv,
    w_output,
    a_attention,
    b_attention,
    expert_w_in,
    expert_w_down,
    expert_a_in,
    expert_b_in,
    expert_a_down,
    expert_b_down,
    route_experts,
    route_gates,
    doc_lengths,
    adapter_ids,
):
    low = jnp.bfloat16
    f32 = jnp.float32
    own_rows = layer_input.shape[1]
    full_width = layer_input.shape[2]
    n = lax.axis_size("seq")
    dp_count = lax.axis_size("dp")
    s = lax.axis_index("seq")
    d = lax.axis_index("dp")
    length = own_rows * n
    rank_columns = a_attention.shape[2]
    group_width = full_width // n
    group_heads = H // n
    piece = group_width // dp_count
    group_start = s * group_width
    order = s ^ jnp.arange(n, dtype=jnp.int32)
    position = (order[:, None] * own_rows + jnp.arange(own_rows, dtype=jnp.int32)[None, :]).reshape(-1)
    segment, offset, adapter = doc_layout(doc_lengths[0], adapter_ids[0], position)
    own_adapter = adapter[:own_rows]
    own_mask = column_mask(own_adapter, rank_columns)
    full_mask = column_mask(adapter, rank_columns)

    ab_piece = jnp.concatenate([a_attention, jnp.swapaxes(b_attention, 1, 2)], axis=0)
    ab_group = lax.all_gather(ab_piece, "dp", axis=0)
    ab_group = jnp.swapaxes(ab_group, 0, 1).reshape(8, group_width, rank_columns)
    wt_piece = jnp.swapaxes(w_qkv, 1, 2)
    w_group = [lax.all_gather(wt_piece[m], "dp", axis=0, tiled=True) for m in range(3)]
    wo_group = lax.all_gather(w_output, "dp", axis=0, tiled=True)
    meta = jnp.concatenate(
        [
            route_experts[0].T.astype(f32),
            route_gates[0].T,
            own_adapter[None, :].astype(f32),
            jnp.zeros((7, own_rows), f32),
        ],
        axis=0,
    )
    meta_all = lax.all_gather(meta, "dp", axis=0)
    grad_all_tokens = lax.all_gather(
        after(out_cotangent[0], wo_group), "dp", axis=0
    )

    tokens = layer_input[0].astype(f32)
    normed = rms_scale(tokens, gain_attention).astype(low)
    normed_blocks = spread(normed, "seq", n)
    normed_all = jnp.concatenate(normed_blocks, axis=0)
    share = jnp.concatenate([ab_group[0:3], ab_group[7:8]], axis=0)
    share_blocks = jnp.stack(spread(share, "seq", n))
    share_full = share_blocks[order]
    share_full = jnp.swapaxes(share_full, 0, 1).reshape(4, full_width, rank_columns)
    down_cat = jnp.swapaxes(share_full[0:3], 0, 1).reshape(full_width, 3 * rank_columns)
    upt_output = share_full[3]
    upt_group = ab_group[4:7]
    down_rows = ab_group[3]

    dot = lambda a, b: jnp.dot(a, b, preferred_element_type=f32)
    dot_t = lambda a, b: lax.dot_general(a, b, (((1,), (1,)), ((), ())), preferred_element_type=f32)
    dot_l = lambda a, b: lax.dot_general(a, b, (((0,), (0,)), ((), ())), preferred_element_type=f32)

    reduced_cat = (jnp.tile(full_mask, (1, 3)) * dot(normed_all, down_cat)).astype(low)
    reduced_list = [reduced_cat[:, m * rank_columns : (m + 1) * rank_columns] for m in range(3)]
    raw_list = [
        dot_t(normed_all, w_group[m]) + dot_t(reduced_list[m], upt_group[m]) for m in range(3)
    ]
    query_raw = raw_list[0].reshape(length, group_heads, HD)
    key_raw = raw_list[1].reshape(length, group_heads, HD)
    query_heads = head_prepare(query_raw, gain_query, offset).astype(low)
    key_heads = head_prepare(key_raw, gain_key, offset).astype(low)
    value_heads = raw_list[2].astype(low).reshape(length, group_heads, HD)
    mixed, logsum = attend(query_heads, key_heads, value_heads, segment)
    mixed_group = mixed.astype(low).reshape(length, group_width)

    out_maps = jnp.concatenate([wo_group, down_rows], axis=1)
    partial_out = dot(mixed_group, out_maps).astype(low).reshape(n, own_rows, full_width + rank_columns)
    summed = collect([partial_out[k] for k in range(n)], "seq", n)
    output_reduced = (own_mask * summed[:, full_width:]).astype(low)
    attended = summed[:, :full_width] + dot_t(output_reduced, upt_output)
    hidden = tokens + attended
    normed_ffn = rms_scale(hidden, gain_ffn).astype(low)
    rows_all = lax.all_gather(normed_ffn, "dp", axis=0)

    local_count = expert_w_in.shape[0]
    expert_count = local_count * dp_count
    capacity = own_rows * TOP // expert_count * 9 // 8
    named = meta_all[:, 0:TOP, :].astype(jnp.int32)
    gates_all = meta_all[:, TOP : 2 * TOP, :]
    sets_all = meta_all[:, 2 * TOP, :]
    mine = d * local_count + jnp.arange(local_count, dtype=jnp.int32)
    hit = (named[None] == mine[:, None, None, None]).astype(f32)
    member = jnp.sum(hit, axis=2)
    token_gate = jnp.sum(hit * gates_all[None], axis=2)
    t_index = jnp.arange(own_rows, dtype=jnp.int32)
    upto = (t_index[:, None] <= t_index[None, :]).astype(low)
    rank = jnp.einsum("ejt,tu->eju", member.astype(low), upto, preferred_element_type=f32) - 1.0
    slots = jnp.arange(capacity, dtype=jnp.int32).astype(f32)
    pick = (slots[None, None, :, None] == rank[:, :, None, :]) & (member[:, :, None, :] > 0.5)
    slot_gate = jnp.sum(jnp.where(pick, token_gate[:, :, None, :], 0.0), axis=-1)
    slot_set = jnp.sum(jnp.where(pick, sets_all[None, :, None, :], 0.0), axis=-1)
    pick = pick.astype(low)

    slot_rows = dp_count * capacity
    outs = []
    backs = []
    adapter_parts = []
    for e in range(local_count):
        inputs = jnp.einsum(
            "jct,jtd->jcd", pick[e], rows_all, preferred_element_type=f32
        ).astype(low).reshape(slot_rows, full_width)
        grad_picked = jnp.einsum("jct,jtd->jcd", pick[e], grad_all_tokens, preferred_element_type=f32)
        grad_rows = (slot_gate[e][:, :, None] * grad_picked).astype(low).reshape(slot_rows, full_width)
        row_mask = column_mask(slot_set[e].reshape(-1).astype(jnp.int32), rank_columns)
        weights = (
            expert_w_in[e],
            expert_w_down[e],
            expert_a_in[e],
            expert_b_in[e],
            expert_a_down[e],
            expert_b_down[e],
        )
        produced, kept = expert_forward(inputs, row_mask, *weights)
        scaled = (slot_gate[e].reshape(-1)[:, None] * produced).astype(low)
        outs.append(scaled.reshape(dp_count, capacity, full_width))
        grad_inputs, ga_in, gb_in, ga_down, gb_down = expert_backward(
            inputs, row_mask, *weights, kept, grad_rows
        )
        backs.append(grad_inputs.reshape(dp_count, capacity, full_width))
        adapter_parts.append((ga_in, gb_in, ga_down, gb_down))

    def put_back(parts):
        total = None
        for e in range(local_count):
            term = jnp.einsum("jct,jcd->jtd", pick[e], parts[e], preferred_element_type=f32)
            total = term if total is None else total + term
        return total.astype(low).reshape(dp_count * own_rows, full_width)

    mixture = lax.psum_scatter(put_back(outs), "dp", scatter_dimension=0, tiled=True)
    grad_normed_ffn = lax.psum_scatter(put_back(backs), "dp", scatter_dimension=0, tiled=True).astype(f32)
    layer_output = (hidden + mixture.astype(f32)).astype(low)[None]

    grad_out = out_cotangent[0].astype(f32)
    unused, pull_ffn = jax.vjp(lambda values: rms_scale(values, gain_ffn), hidden)
    grad_hidden = grad_out + pull_ffn(grad_normed_ffn)[0]
    grad_hidden_low = grad_hidden.astype(low)
    grad_reduced_output = (own_mask * dot(grad_hidden_low, upt_output)).astype(low)
    grad_pack = jnp.concatenate([grad_hidden_low, grad_reduced_output, output_reduced], axis=1)
    grad_pack_all = jnp.concatenate(spread(grad_pack, "seq", n), axis=0)
    grad_all = grad_pack_all[:, :full_width]
    grad_reduced_all = grad_pack_all[:, full_width : full_width + rank_columns]
    output_reduced_all = grad_pack_all[:, full_width + rank_columns :]
    grad_mixed_group = dot_t(grad_pack_all[:, : full_width + rank_columns], out_maps).astype(low)
    grad_cols = lax.dynamic_slice_in_dim(grad_all, group_start, group_width, 1)
    grad_upt_output = dot_l(grad_cols, output_reduced_all)
    grad_down_output = dot_l(mixed_group, grad_reduced_all)
    grad_query, grad_key, grad_value = attend_back(
        query_heads,
        key_heads,
        value_heads,
        segment,
        logsum,
        grad_mixed_group.reshape(length, group_heads, HD),
    )
    unused_query, pull_query = jax.vjp(
        lambda values: head_prepare(values, gain_query, offset), query_raw
    )
    unused_key, pull_key = jax.vjp(lambda values: head_prepare(values, gain_key, offset), key_raw)
    grad_raw_list = [
        pull_query(grad_query.astype(low).astype(f32))[0].reshape(length, group_width).astype(low),
        pull_key(grad_key.astype(low).astype(f32))[0].reshape(length, group_width).astype(low),
        grad_value.astype(low).reshape(length, group_width),
    ]
    partial_normed = jnp.zeros((length, full_width), f32)
    partial_reduced = []
    grad_upt = []
    for m in range(3):
        partial_normed = partial_normed + dot(grad_raw_list[m], w_group[m])
        partial_reduced.append(dot(grad_raw_list[m], upt_group[m]))
        grad_upt.append(dot_l(grad_raw_list[m], reduced_list[m]))
    back_pack = jnp.concatenate([partial_normed] + partial_reduced, axis=1).astype(low)
    back_pack = back_pack.reshape(n, own_rows, -1)
    summed_back = collect([back_pack[k] for k in range(n)], "seq", n)
    grad_reduced = (jnp.tile(own_mask, (1, 3)) * summed_back[:, full_width:]).astype(low)
    grad_normed = summed_back[:, :full_width] + dot_t(grad_reduced, down_cat)
    unused_input, pull_input = jax.vjp(lambda values: rms_scale(values, gain_attention), tokens)
    input_grad = (grad_hidden + pull_input(grad_normed)[0]).astype(low)[None]

    grad_reduced_full = jnp.concatenate(spread(grad_reduced, "seq", n), axis=0)
    normed_cols = lax.dynamic_slice_in_dim(normed_all, group_start, group_width, 1)
    grad_down_cat = dot_l(normed_cols, grad_reduced_full)

    def over_dp(parts):
        stacked = jnp.stack(parts).astype(low).reshape(len(parts), dp_count, piece, rank_columns)
        stacked = jnp.swapaxes(stacked, 0, 1)
        return lax.psum_scatter(stacked, "dp", scatter_dimension=0).astype(f32)

    early = over_dp([grad_down_output] + grad_upt + [grad_upt_output])
    late = over_dp([grad_down_cat[:, m * rank_columns : (m + 1) * rank_columns] for m in range(3)])
    grad_a_attention = jnp.concatenate([late, early[0:1]], axis=0)
    grad_b_attention = jnp.swapaxes(early[1:5], 1, 2)

    flat = []
    for ga_in, gb_in, ga_down, gb_down in adapter_parts:
        flat.append(ga_in.astype(low).reshape(2, n, -1, rank_columns))
        flat.append(jnp.swapaxes(gb_in, 1, 2).astype(low).reshape(2, n, -1, rank_columns))
        flat.append(ga_down.astype(low).reshape(1, n, -1, rank_columns))
        flat.append(jnp.swapaxes(gb_down, 0, 1).astype(low).reshape(1, n, -1, rank_columns))
    sizes = [x.shape[0] * x.shape[2] for x in flat]
    flat = jnp.concatenate(
        [jnp.swapaxes(x, 0, 1).reshape(n, -1, rank_columns) for x in flat], axis=1
    )
    flat = lax.psum_scatter(flat, "seq", scatter_dimension=0).astype(f32)
    pieces = []
    start = 0
    for size in sizes:
        pieces.append(flat[start : start + size])
        start += size
    grad_a_in = jnp.stack([pieces[4 * e].reshape(2, -1, rank_columns) for e in range(local_count)])
    grad_b_in = jnp.stack(
        [jnp.swapaxes(pieces[4 * e + 1].reshape(2, -1, rank_columns), 1, 2) for e in range(local_count)]
    )
    grad_a_down = jnp.stack([pieces[4 * e + 2] for e in range(local_count)])
    grad_b_down = jnp.stack([pieces[4 * e + 3].T for e in range(local_count)])
    return (
        layer_output,
        input_grad,
        grad_a_attention,
        grad_b_attention,
        grad_a_in,
        grad_b_in,
        grad_a_down,
        grad_b_down,
    )


def solution(mesh):
    return jax.shard_map(
        local,
        mesh=mesh,
        in_specs=(
            P("dp", "seq", None),
            P("dp", "seq", None),
            P(),
            P(),
            P(),
            P(),
            P(None, None, ("seq", "dp")),
            P(("seq", "dp"), None),
            P(None, ("seq", "dp"), None),
            P(None, None, ("seq", "dp")),
            P("dp", None, None, None),
            P("dp", None, None),
            P("dp", None, None, None),
            P("dp", None, None, None),
            P("dp", None, None),
            P("dp", None, None),
            P("dp", "seq", None),
            P("dp", "seq", None),
            P("dp", None),
            P("dp", None),
        ),
        out_specs=(
            P("dp", "seq", None),
            P("dp", "seq", None),
            P(None, ("seq", "dp"), None),
            P(None, None, ("seq", "dp")),
            P("dp", None, "seq", None),
            P("dp", None, None, "seq"),
            P("dp", "seq", None),
            P("dp", None, "seq"),
        ),
        check_vma=False,
    )
```

time: 1820 us -> 936 us (0.51)
  waiting for transfers between devices: 1080 us -> 311 us
  local copies, waits for them, and re-layouts: 182 us -> 103 us
  other arithmetic: 128 us -> 88.3 us
  blocking collectives: 43.9 us -> 14.5 us
  matrix products: 328 us -> 355 us
    all_to_all x5 -> x0, waiting for transfers between devices: 612 us -> none  [the longest x1 206 us: local(): lax.all_to_all(grad_inputs_all, 'dp', split_axis=1, concat_axis=1, tiled=...]
    reduce_scatter x9 -> x3, waiting for transfers between devices: 306 us -> 59 us  [the longest x1 30.8 us: local(): lax.psum_scatter(put_back(outs), 'dp', scatter_dimension=0, tiled=True)]
    ppermute x0 -> x18, waiting for transfers between devices: none -> 189 us  [swap(): return lax.ppermute(values, axis, [(i, i ^ distance) for i in range(count)])]
    gather x5 -> x1, local copies, waits for them, and re-layouts: 78.2 us -> 2.67 us  [local(): share_full = share_blocks[order]]
    all_gather x6 -> x7, waiting for transfers between devices: 126 us -> 56.7 us  [the longest x1 32.7 us: local(): rows_all = lax.all_gather(normed_ffn, 'dp', axis=0)]
    dot_general x33, matrix products: 85 us -> 117 us  [the longest x4 41.3 us: put_back(): jnp.einsum('jct,jcd->jtd', pick[e], parts[e], preferred_element_type=f32)]
    unnamed x17 -> x14, waiting for transfers between devices: 37.1 us -> 6.04 us
    all_gather x3 -> x1, blocking collectives: 43.9 us -> 14.5 us  [local(): meta_all = lax.all_gather(meta, 'dp', axis=0)]
  transfers between devices with their start and end apart: 21 -> 30, of which waited for: 14 -> 17; matrix products, arithmetic and copies ran while one was open for 20% -> 42% of each run, Pallas kernels for 0% -> 0%
where the time goes in v1:
time: 936 us; the launch traced here: 926 us
  matrix products  355 us (38%)
  waiting for transfers between devices  311 us (33%)
  local copies, waits for them, and re-layouts  103 us (11%)
  other arithmetic  88.3 us (9%)
  starting transfers between devices  36.2 us (4%)
  between operations  17.1 us (2%)
  blocking collectives  14.5 us (2%)
    ppermute x18, waiting for transfers between devices, swap(): return lax.ppermute(values, axis, [(i, i ^ distance) for i in range(count)])  189 us
    dot_general x6, matrix products, project(): jnp.dot(inputs, weight, preferred_element_type=jnp.float32)  57 us
    dot_general x6, matrix products, project_back(): jnp.dot(grad_result, weight.T, preferred_element_type=jnp.float32)  52.9 us
    dot_general x4, matrix products, put_back(): jnp.einsum('jct,jcd->jtd', pick[e], parts[e], preferred_element_type=f32)  41.3 us
    all_gather x1, waiting for transfers between devices, local(): rows_all = lax.all_gather(normed_ffn, 'dp', axis=0)  32.7 us
    reduce_scatter x1, waiting for transfers between devices, local(): lax.psum_scatter(put_back(outs), 'dp', scatter_dimension=0, tiled=True)  30.8 us
    dot_general x9, matrix products, local(): lax.dot_general(a, b, (((1,), (1,)), ((), ())), preferred_element_type=f32)  30.2 us
    reduce_scatter x1, waiting for transfers between devices, over_dp(): return lax.psum_scatter(stacked, 'dp', scatter_dimension=0).astype(f32)  27 us
  transfers between devices with their start and end apart: 30, of which 17 were waited for; matrix products, arithmetic and copies ran while one was open for 42% of the time, Pallas kernels for 0%

profile of v1, /device:TPU:0, one launch (start us, length us, event | category | flops | bytes accessed | tf_op | source)
XLA Modules:
  0.0 925.8 jit_solution(12549062532337744469)
XLA Ops:
  20.8 14.3 %all-gather.19.cloned.1.call-done = bf16[64,64,128]{2,1,0:T(8,128)(2,1)} async-done(((bf16[8,64,128]{2,1,0:T(8,128)(2,1)}), bf16[64,64,128]{2,1,0:T(8,128)(2,1)}) %all-gather.19.cloned.1.call-update) | async-done | bytes 1048592 | tf_op jit(solution)/shard_map/all_gather | solution.py:258
  47.8 27.7 %collective-permute-done.3 = bf16[4,512,128]{2,1,0:T(8,128)(2,1)} collective-permute-done((bf16[4,512,128]{2,1,0:T(8,128)(2,1)}, bf16[4,512,128]{2,1,0:T(8,128)(2,1)}, u32[]{:S(2)}, u32[]{:S(2)}) %collective-permute-start.3) | collective-permute-done | bytes 524320 | tf_op jit(solution)/shard_map/ppermute | solution.py:196
  108.8 11.3 %all-gather.25.cloned.1.call-start = ((), (), s32[]{:S(2)}) async-start(), calls=%async_computation.12 | async-start | bytes 9437184 | tf_op jit(solution)/shard_map/all_gather | solution.py:314
  147.3 9.6 %all-gather.23.cloned.1.call-done = bf16[1,512,2048]{2,1,0:T(8,128)(2,1)} async-done(((bf16[1,64,2048]{2,1,0:T(8,128)(2,1)}), bf16[1,512,2048]{2,1,0:T(8,128)(2,1)}) %all-gather.23.cloned.1.call-update) | async-done | bytes 2097168 | tf_op jit(solution)/shard_map/all_gather | solution.py:261
  173.9 17.9 %while.27 = (s32[]{:T(128)}, bf16[2,512,4,128]{3,1,2,0:T(8,128)(2,1)}, f32[2,4,512]{2,1,0:T(4,128)}, s32[2,512]{1,0:T(2,128)S(1)}, s32[1024]{0:T(1024)S(1)}, /*i...) while((s32[]{:T(128)}, ...), condition=%wide.region_10.11_spmd, body=%wide.region_7.10_spmd.sunk | while | flops 1099429888 | bytes 31009892 | solution.py:103
  205.1 22.2 %collective-permute-done.6 = bf16[256,2176]{1,0:T(8,128)(2,1)S(1)} collective-permute-done((bf16[256,2176]{1,0:T(8,128)(2,1)S(1)}, bf16[256,2176]{1,0:T(8,128)(2,1)S(1)}, u32[]{:S(2)}, u32[]{:S(2)}) %collective-permute-start.6) | collective-permute-done | bytes 1114144 | tf_op jit(solution)/shard_map/ppermute | solution.py:196
  227.3 24.3 %collective-permute-done.7 = bf16[256,2176]{1,0:T(8,128)(2,1)S(1)} collective-permute-done((bf16[256,2176]{1,0:T(8,128)(2,1)S(1)}, bf16[256,2176]{1,0:T(8,128)(2,1)S(1)}, u32[]{:S(2)}, u32[]{:S(2)}) %collective-permute-start.7) | collective-permute-done | bytes 1114144 | tf_op jit(solution)/shard_map/ppermute | solution.py:196
  255.8 14.5 %all-gather.4 = f32[192,256]{1,0:T(8,128)S(1)} all-gather(f32[24,256]{1,0:T(8,128)S(1)} %maximum_maximum_fusion), channel_id=6, replica_groups=mesh['seq'=4,'dp'=8] {'dp'}, dimensions={0}, use_global_device_ids=true | all-gather | bytes 221184 | tf_op jit(solution)/shard_map/all_gather | solution.py:272
  283.4 9.6 %fusion.48 = f32[1152,1024]{1,0:T(8,128)S(1)} fusion(bf16[1152,2048]{1,0:T(8,128)(2,1)S(1)} %bitcast.598, bf16[2,1024,2048]{2,1,0:T(8,128)(2,1)} %param.35), kind=kOutput, calls=%fused_computation.94 | convolution fusion | flops 4831838208 | bytes 13631488 | tf_op jit(solution)/shard_map/dot_general | solution.py:72
  304.0 32.7 %all-gather.25.cloned.1.call-done = bf16[2048,2048]{1,0:T(8,128)(2,1)} async-done(((bf16[256,2048]{1,0:T(8,128)(2,1)}), bf16[2048,2048]{1,0:T(8,128)(2,1)}) %all-gather.25.cloned.1.call-update) | async-done | bytes 8388624 | tf_op jit(solution)/shard_map/all_gather | solution.py:314
  341.5 9.4 %fusion.54 = f32[1152,1024]{1,0:T(8,128)S(1)} fusion(bf16[1152,2048]{1,0:T(8,128)(2,1)S(1)} %bitcast.590, bf16[2,2,2048,1024]{3,2,1,0:T(8,128)(2,1)} %param.34), kind=kOutput, calls=%fused_computation.100 | convolution fusion | flops 4831838208 | bytes 13631488 | tf_op jit(solution)/shard_map/dot_general | solution.py:60
  395.5 9.7 %fusion.52 = f32[1152,2048]{1,0:T(8,128)} fusion(bf16[1152,1024]{1,0:T(8,128)(2,1)S(1)} %get-tuple-element.343, bf16[2,2,2048,1024]{3,2,1,0:T(8,128)(2,1)} %param.34), kind=kOutput, calls=%fused_computation.98 | convolution fusion | flops 4831838208 | bytes 15990784 | tf_op jit(solution)/shard_map/dot_general | solution.py:72
  406.7 10.6 %fusion.56 = f32[1152,2048]{1,0:T(8,128)} fusion(bf16[1152,1024]{1,0:T(8,128)(2,1)S(1)} %get-tuple-element.342, bf16[2,2,2048,1024]{3,2,1,0:T(8,128)(2,1)} %param.34), kind=kOutput, calls=%fused_computation.102 | convolution fusion | flops 4831838208 | bytes 15990784 | tf_op jit(solution)/shard_map/dot_general | solution.py:72
  432.2 9.8 %fusion.68 = f32[1152,2048]{1,0:T(8,128)} fusion(bf16[1152,1024]{1,0:T(8,128)(2,1)S(1)} %get-tuple-element.345, bf16[2,2,2048,1024]{3,2,1,0:T(8,128)(2,1)} %param.34), kind=kOutput, calls=%fused_computation.114 | convolution fusion | flops 4831838208 | bytes 15990784 | tf_op jit(solution)/shard_map/dot_general | solution.py:72
  469.6 11.8 %add_convert_fusion = bf16[8,256,2048]{2,1,0:T(8,128)(2,1)} fusion(f32[8,256,2048]{2,1,0:T(8,128)} %fusion.193, bf16[8,144,2048]{2,1,0:T(8,128)(2,1)S(1)} %bitcast.596, pred[2,8,144,256]{3,2,1,0:T(8,128)(4,1)S(1)} %compare_and_fusion), kind=kOutput, calls=%fused_computation.47 | convolution fusion | flops 1216348160 | bytes 30179328 | tf_op jit(solution)/shard_map/jct,jcd->jtd/dot_general | solution.py:366
  541.1 9.8 %fusion.50 = f32[1152,2048]{1,0:T(8,128)} fusion(bf16[1152,1024]{1,0:T(8,128)(2,1)} %get-tuple-element.344, bf16[2,1024,2048]{2,1,0:T(8,128)(2,1)} %param.35), kind=kOutput, calls=%fused_computation.96 | convolution fusion | flops 4831838208 | bytes 15990784 | tf_op jit(solution)/shard_map/dot_general | solution.py:60
  551.0 9.8 %fusion.62 = f32[1152,2048]{1,0:T(8,128)} fusion(bf16[1152,1024]{1,0:T(8,128)(2,1)S(1)} %copy-done.165, bf16[2,1024,2048]{2,1,0:T(8,128)(2,1)} %param.35), kind=kOutput, calls=%fused_computation.108 | convolution fusion | flops 4831838208 | bytes 15990784 | tf_op jit(solution)/shard_map/dot_general | solution.py:60
  592.4 60.3 %collective-permute-done.10 = bf16[256,2304]{1,0:T(8,128)(2,1)S(1)} collective-permute-done((bf16[256,2304]{1,0:T(8,128)(2,1)S(1)}, bf16[256,2304]{1,0:T(8,128)(2,1)S(1)}, u32[]{:S(2)}, u32[]{:S(2)}) %collective-permute-start.10) | collective-permute-done | bytes 1179680 | tf_op jit(solution)/shard_map/ppermute | solution.py:196
  664.4 42.9 %while.28 = (s32[]{:T(128)}, f32[1024,4,128]{0,2,1:T(8,128)S(1)}, f32[1024,4,128]{0,2,1:T(8,128)}, bf16[2,512,4,128]{3,1,0,2:T(8,128)(2,1)}, bf16[2,512,4,128]{3...) while((s32[]{:T(128)}, f32[1024,4,128]{0,2,1:T(8,128)S(1)}, ...), condition=%wide.region_21.22_spmd.clone, body=%wide.region_19.21_spmd.clone.sunk | while | flops 2719217664 | bytes 181473200 | solution.py:146
  737.9 13.1 %add_convert_fusion.1 = bf16[8,256,2048]{2,1,0:T(8,128)(2,1)} fusion(f32[8,256,2048]{2,1,0:T(8,128)} %fusion.194, bf16[8,144,2048]{2,1,0:T(8,128)(2,1)} %bitcast.595, pred[2,8,144,256]{3,2,1,0:T(8,128)(4,1)S(1)} %copy-done.30), kind=kOutput, calls=%fused_computation.48 | convolution fusion | flops 1216348160 | bytes 30179328 | tf_op jit(solution)/shard_map/jct,jcd->jtd/dot_general | solution.py:366
  796.9 16.2 %collective-permute-done.12 = bf16[256,2432]{1,0:T(8,128)(2,1)} collective-permute-done((bf16[256,2432]{1,0:T(8,128)(2,1)}, bf16[256,2432]{1,0:T(8,128)(2,1)}, u32[]{:S(2)}, u32[]{:S(2)}) %collective-permute-start.12) | collective-permute-done | bytes 1245216 | tf_op jit(solution)/shard_map/ppermute | solution.py:196
  813.1 26.1 %collective-permute-done.13 = bf16[256,2432]{1,0:T(8,128)(2,1)} collective-permute-done((bf16[256,2432]{1,0:T(8,128)(2,1)}, bf16[256,2432]{1,0:T(8,128)(2,1)}, u32[]{:S(2)}, u32[]{:S(2)}) %collective-permute-start.13) | collective-permute-done | bytes 1245216 | tf_op jit(solution)/shard_map/ppermute | solution.py:196
  854.8 30.8 %reduce-scatter.10.cloned.1.call-done = bf16[256,2048]{1,0:T(8,128)(2,1)} async-done(((bf16[2048,2048]{1,0:T(8,128)(2,1)}), bf16[256,2048]{1,0:T(8,128)(2,1)}) %reduce-scatter.10.cloned.1.call-update) | async-done | bytes 1048592 | tf_op jit(solution)/shard_map/reduce_scatter | solution.py:370
  890.3 27.0 %reduce-scatter.14.cloned.1.call-done = bf16[1,3,64,128]{3,2,1,0:T(8,128)(2,1)} async-done(((bf16[8,3,64,128]{3,2,1,0:T(8,128)(2,1)}), bf16[1,3,64,128]{3,2,1,0:T(8,128)(2,1)}) %reduce-scatter.14.cloned.1.call-update) | async-done | bytes 49168 | tf_op jit(solution)/shard_map/reduce_scatter | solution.py:427
  (710 shorter events, 497.1 us)
Async XLA Ops:
  8.9 99.9 %all-gather.15.cloned.1.call-start = ((), (), s32[]{:S(2)}) async-start(), calls=%async_computation.4 | async-start | bytes 2359296 | tf_op jit(solution)/shard_map/all_gather | solution.py:262
  9.6 110.5 %all-gather.21.cloned.1.call-start = ((), (), s32[]{:S(2)}) async-start(), calls=%async_computation.10 | async-start | bytes 2359296 | tf_op jit(solution)/shard_map/all_gather | solution.py:261
  11.7 115.4 %all-gather.17.cloned.1.call-start = ((), (), s32[]{:S(2)}) async-start(), calls=%async_computation.8 | async-start | bytes 2359296 | tf_op jit(solution)/shard_map/all_gather | solution.py:261
  12.3 144.7 %all-gather.23.cloned.1.call-start = ((), (), s32[]{:S(2)}) async-start(), calls=%async_computation.11 | async-start | bytes 2359296 | tf_op jit(solution)/shard_map/all_gather | solution.py:261
  15.5 83.9 %collective-permute-start = (bf16[256,2048]{1,0:T(8,128)(2,1)S(1)}, bf16[256,2048]{1,0:T(8,128)(2,1)}, u32[]{:S(2)}, u32[]{:S(2)}) collective-permute-start(bf16[256,2048]{1,0:T(8,128)(2,1)S(1)} %fusion.109), channel_id=1, source_target_pairs={{0,8},{8,0},{16,24},{24,16},{1,9},{9,1},{17,25},{25,17},{2,10},{10... | collective-permute-start | bytes 3145736 | tf_op jit(solution)/shard_map/ppermute | solution.py:196
  18.5 80.9 %collective-permute-start.1 = (bf16[256,2048]{1,0:T(8,128)(2,1)S(1)}, bf16[256,2048]{1,0:T(8,128)(2,1)}, u32[]{:S(2)}, u32[]{:S(2)}) collective-permute-start(bf16[256,2048]{1,0:T(8,128)(2,1)S(1)} %fusion.109), channel_id=1, source_target_pairs={{0,16},{8,24},{16,0},{24,8},{1,17},{9,25},{17,1},{25,9},{2,18},{10... | collective-permute-start | bytes 3145736 | tf_op jit(solution)/shard_map/ppermute | solution.py:196
  20.0 79.4 %collective-permute-start.2 = (bf16[256,2048]{1,0:T(8,128)(2,1)S(1)}, bf16[256,2048]{1,0:T(8,128)(2,1)}, u32[]{:S(2)}, u32[]{:S(2)}) collective-permute-start(bf16[256,2048]{1,0:T(8,128)(2,1)S(1)} %fusion.109), channel_id=1, source_target_pairs={{0,24},{8,16},{16,8},{24,0},{1,25},{9,17},{17,9},{25,1},{2,26},{10... | collective-permute-start | bytes 3145736 | tf_op jit(solution)/shard_map/ppermute | solution.py:196
  20.1 253.3 %all-gather.27.cloned.1.call-start = ((), (), s32[]{:S(2)}) async-start(), calls=%async_computation.13 | async-start | bytes 9437184 | tf_op jit(solution)/shard_map/all_gather | solution.py:273
  39.2 36.3 %collective-permute-start.3 = (bf16[4,512,128]{2,1,0:T(8,128)(2,1)}, bf16[4,512,128]{2,1,0:T(8,128)(2,1)}, u32[]{:S(2)}, u32[]{:S(2)}) collective-permute-start(bf16[4,512,128]{2,1,0:T(8,128)(2,1)} %get-tuple-element.385), channel_id=1, source_target_pairs={{0,8},{8,0},{16,24},{24,16},{1,9},{9,1},{17,25},{25,17},{2,10},{10... | collective-permute-start | bytes 1572872 | tf_op jit(solution)/shard_map/ppermute | solution.py:196
  46.3 36.5 %collective-permute-start.4 = (bf16[4,512,128]{2,1,0:T(8,128)(2,1)}, bf16[4,512,128]{2,1,0:T(8,128)(2,1)S(1)}, u32[]{:S(2)}, u32[]{:S(2)}) collective-permute-start(bf16[4,512,128]{2,1,0:T(8,128)(2,1)} %get-tuple-element.385), channel_id=1, source_target_pairs={{0,16},{8,24},{16,0},{24,8},{1,17},{9,25},{17,1},{25,9},{2,18},{10... | collective-permute-start | bytes 1572872 | tf_op jit(solution)/shard_map/ppermute | solution.py:196
  108.8 227.9 %all-gather.25.cloned.1.call-start = ((), (), s32[]{:S(2)}) async-start(), calls=%async_computation.12 | async-start | bytes 9437184 | tf_op jit(solution)/shard_map/all_gather | solution.py:314
  201.3 50.2 %collective-permute-start.7 = (bf16[256,2176]{1,0:T(8,128)(2,1)S(1)}, bf16[256,2176]{1,0:T(8,128)(2,1)S(1)}, u32[]{:S(2)}, u32[]{:S(2)}) collective-permute-start(bf16[256,2176]{1,0:T(8,128)(2,1)S(1)} %get-tuple-element.353), channel_id=1, source_target_pairs={{0,16},{8,24},{16,0},{24,8},{1,17},{9,25},{17,1},{25,9},{2,18},{10... | collective-permute-start | bytes 3342344 | tf_op jit(solution)/shard_map/ppermute | solution.py:196
  202.8 48.8 %collective-permute-start.8 = (bf16[256,2176]{1,0:T(8,128)(2,1)S(1)}, bf16[256,2176]{1,0:T(8,128)(2,1)S(1)}, u32[]{:S(2)}, u32[]{:S(2)}) collective-permute-start(bf16[256,2176]{1,0:T(8,128)(2,1)S(1)} %get-tuple-element.352), channel_id=1, source_target_pairs={{0,24},{8,16},{16,8},{24,0},{1,25},{9,17},{17,9},{25,1},{2,26},{10... | collective-permute-start | bytes 3342344 | tf_op jit(solution)/shard_map/ppermute | solution.py:196
  255.6 314.0 %reduce-scatter.12.cloned.1.call-start = ((), (), s32[]{:S(2)}) async-start(), calls=%async_computation.6 | async-start | bytes 9437184 | tf_op jit(solution)/shard_map/reduce_scatter | solution.py:371
  481.4 275.8 %reduce-scatter.16.cloned.1.call-start = ((), (), s32[]{:S(2)}) async-start(), calls=%async_computation.15 | async-start | bytes 5898240
  560.8 233.9 %all-reduce.8.cloned.1.call-start = ((), (), s32[]{:S(2)}) async-start(), calls=%async_computation.14 | async-start | bytes 1310720
  575.5 77.2 %collective-permute-start.10 = (bf16[256,2304]{1,0:T(8,128)(2,1)S(1)}, bf16[256,2304]{1,0:T(8,128)(2,1)S(1)}, u32[]{:S(2)}, u32[]{:S(2)}) collective-permute-start(bf16[256,2304]{1,0:T(8,128)(2,1)S(1)} %pad_maximum_fusion.8), channel_id=1, source_target_pairs={{0,16},{8,24},{16,0},{24,8},{1,17},{9,25},{17,1},{25,9},{2,18},{10... | collective-permute-start | bytes 3538952 | tf_op jit(solution)/shard_map/ppermute | solution.py:196
  577.1 75.7 %collective-permute-start.11 = (bf16[256,2304]{1,0:T(8,128)(2,1)S(1)}, bf16[256,2304]{1,0:T(8,128)(2,1)S(1)}, u32[]{:S(2)}, u32[]{:S(2)}) collective-permute-start(bf16[256,2304]{1,0:T(8,128)(2,1)S(1)} %pad_maximum_fusion.8), channel_id=1, source_target_pairs={{0,24},{8,16},{16,8},{24,0},{1,25},{9,17},{17,9},{25,1},{2,26},{10... | collective-permute-start | bytes 3538952 | tf_op jit(solution)/shard_map/ppermute | solution.py:196
  578.5 75.5 %collective-permute-start.9 = (bf16[256,2304]{1,0:T(8,128)(2,1)S(1)}, bf16[256,2304]{1,0:T(8,128)(2,1)S(1)}, u32[]{:S(2)}, u32[]{:S(2)}) collective-permute-start(bf16[256,2304]{1,0:T(8,128)(2,1)S(1)} %pad_maximum_fusion.8), channel_id=1, source_target_pairs={{0,8},{8,0},{16,24},{24,16},{1,9},{9,1},{17,25},{25,17},{2,10},{10... | collective-permute-start | bytes 3538952 | tf_op jit(solution)/shard_map/ppermute | solution.py:196
  737.9 147.7 %reduce-scatter.10.cloned.1.call-start = ((), (), s32[]{:S(2)}) async-start(), calls=%async_computation.5 | async-start | bytes 9437184 | tf_op jit(solution)/shard_map/reduce_scatter | solution.py:370
  751.0 166.2 %reduce-scatter.14.cloned.1.call-start = ((), (), s32[]{:S(2)}) async-start(), calls=%async_computation.7 | async-start | bytes 442368 | tf_op jit(solution)/shard_map/reduce_scatter | solution.py:427
  782.5 30.6 %collective-permute-start.12 = (bf16[256,2432]{1,0:T(8,128)(2,1)}, bf16[256,2432]{1,0:T(8,128)(2,1)}, u32[]{:S(2)}, u32[]{:S(2)}) collective-permute-start(bf16[256,2432]{1,0:T(8,128)(2,1)} %get-tuple-element.348), channel_id=1, source_target_pairs={{0,8},{8,0},{16,24},{24,16},{1,9},{9,1},{17,25},{25,17},{2,10},{10... | collective-permute-start | bytes 3735560 | tf_op jit(solution)/shard_map/ppermute | solution.py:196
  784.0 55.2 %collective-permute-start.13 = (bf16[256,2432]{1,0:T(8,128)(2,1)}, bf16[256,2432]{1,0:T(8,128)(2,1)}, u32[]{:S(2)}, u32[]{:S(2)}) collective-permute-start(bf16[256,2432]{1,0:T(8,128)(2,1)} %get-tuple-element.350), channel_id=1, source_target_pairs={{0,16},{8,24},{16,0},{24,8},{1,17},{9,25},{17,1},{25,9},{2,18},{10... | collective-permute-start | bytes 3735560 | tf_op jit(solution)/shard_map/ppermute | solution.py:196
  785.3 53.9 %collective-permute-start.14 = (bf16[256,2432]{1,0:T(8,128)(2,1)}, bf16[256,2432]{1,0:T(8,128)(2,1)}, u32[]{:S(2)}, u32[]{:S(2)}) collective-permute-start(bf16[256,2432]{1,0:T(8,128)(2,1)} %get-tuple-element.349), channel_id=1, source_target_pairs={{0,24},{8,16},{16,8},{24,0},{1,25},{9,17},{17,9},{25,1},{2,26},{10... | collective-permute-start | bytes 3735560 | tf_op jit(solution)/shard_map/ppermute | solution.py:196
  (196 other events, 2570.0 us)
Sparse Core Ops, SparseCore 0:
  10.2 24.9 all-gather.18
  36.8 28.7 all-gather.14
  67.7 28.5 all-gather.20
  97.8 28.5 all-gather.16
  128.4 28.5 all-gather.22
  158.4 81.4 all-gather.26
  255.7 80.9 all-gather.24
  481.6 87.9 reduce-scatter.11
  572.6 102.8 reduce-scatter.15
  738.0 56.6 all-reduce.7
  797.0 88.5 reduce-scatter.9
  887.7 29.5 reduce-scatter.13

commit v2 on v1

v2 whole, which is shorter than its diff:
```python
import functools

import jax
import jax.numpy as jnp
from jax import lax
from jax.experimental import pallas as pl
from jax.experimental.pallas import tpu as pltpu
from jax.sharding import PartitionSpec as P

H = 16
HD = 128
TOP = 8
R = 16


norm_epsilon = 1e-06
rope_base = 10000.0
masked_score = -1000000000.0


def rms_scale(values, gain_vector):
    return (
        values
        * lax.rsqrt(jnp.mean(values * values, axis=-1, keepdims=True) + norm_epsilon)
        * gain_vector
    )


def rope_tables(offset, width):
    half = width // 2
    frequency = rope_base ** (-(jnp.arange(half, dtype=jnp.float32) * 2.0) / width)
    angles = offset.astype(jnp.float32)[:, None] * frequency[None, :]
    cosine = jnp.cos(angles)
    sine = jnp.sin(angles)
    return jnp.concatenate([cosine, cosine], axis=1), jnp.concatenate([-sine, sine], axis=1)


def dot_nn(a, b):
    return lax.dot_general(a, b, (((1,), (0,)), ((), ())), preferred_element_type=jnp.float32)


def dot_nt(a, b):
    return lax.dot_general(a, b, (((1,), (1,)), ((), ())), preferred_element_type=jnp.float32)


def dot_tn(a, b):
    return lax.dot_general(a, b, (((0,), (0,)), ((), ())), preferred_element_type=jnp.float32)


def normed_head(raw, gain):
    inverse = lax.rsqrt(jnp.mean(raw * raw, axis=-1, keepdims=True) + norm_epsilon)
    return raw * inverse * gain, inverse


def turned_head(values, cosine, sine):
    return values * cosine + pltpu.roll(values, values.shape[-1] // 2, 1) * sine


def unturned_head(grad, cosine, sine):
    return grad * cosine + pltpu.roll(grad * sine, grad.shape[-1] // 2, 1)


def attend_kernel(
    tile, q_raw, k_raw, v_raw, cosine, sine, gain_q, gain_k, seg_col, seg_row, mixed, query, key, value, stat
):
    rows = q_raw.shape[0]
    scale = HD ** (-0.5)
    cos_all = cosine[...]
    sin_all = sine[...]
    normed_q, unused = normed_head(q_raw[...], gain_q[...])
    query[...] = turned_head(normed_q, cos_all, sin_all).astype(jnp.bfloat16)
    normed_k, unused = normed_head(k_raw[...], gain_k[...])
    keys = turned_head(normed_k, cos_all, sin_all).astype(jnp.bfloat16)
    key[...] = keys
    values = v_raw[...].astype(jnp.bfloat16)
    value[...] = values
    values_t = values.T
    for start in range(0, rows, tile):
        part = slice(start, start + tile)
        scores = dot_nt(keys, query[part, :]) * scale
        scores = jnp.where(seg_col[...] == seg_row[:, part], scores, masked_score)
        top = jnp.max(scores, axis=0, keepdims=True)
        weight = jnp.exp(scores - top)
        total = jnp.sum(weight, axis=0, keepdims=True)
        soft = (weight * (1.0 / total)).astype(jnp.bfloat16)
        mixed[part, :] = dot_nn(values_t, soft).T.astype(jnp.bfloat16)
        stat[0, :, part] = top + jnp.log(total)


def attend(raw, cosine, sine, gain_q, gain_k, segment):
    unused, length, width = raw.shape
    heads = width // HD
    tile = min(256, length)
    head = pl.BlockSpec((length, HD), lambda h: (0, h))
    raw_head = [pl.BlockSpec((None, length, HD), functools.partial(lambda m, h: (m, 0, h), m)) for m in range(3)]
    fixed = lambda shape: pl.BlockSpec(shape, lambda h: (0, 0))
    seg = segment.astype(jnp.float32)
    low = jax.ShapeDtypeStruct((length, width), jnp.bfloat16)
    return pl.pallas_call(
        functools.partial(attend_kernel, tile),
        grid=(heads,),
        in_specs=raw_head + [fixed((length, HD)), fixed((length, HD)), fixed((1, HD)), fixed((1, HD)),
                  fixed((length, 1)), fixed((1, length))],
        out_specs=[head, head, head, head, pl.BlockSpec((1, 1, length), lambda h: (h, 0, 0))],
        out_shape=[low, low, low, low, jax.ShapeDtypeStruct((heads, 1, length), jnp.float32)],
        cost_estimate=pl.CostEstimate(
            flops=4 * heads * length * length * HD, bytes_accessed=20 * length * width, transcendentals=heads * length * length
        ),
        name="attend",
    )(raw, raw, raw, cosine, sine, gain_q[None, :], gain_k[None, :], seg[:, None], seg[None, :])


def attend_back_kernel(
    tile, query, key, value, grad_mixed, stat, q_raw, k_raw, cosine, sine, gain_q, gain_k, seg_col, seg_row,
    grad_q, grad_k, grad_v, sum_k, sum_v
):
    rows = q_raw.shape[0]
    scale = HD ** (-0.5)
    keys = key[...]
    values = value[...]
    keys_t = keys.T

    def through(grad, raw_ref, gain_ref, part):
        grad = grad.astype(jnp.bfloat16).astype(jnp.float32)
        raw = raw_ref[part, :]
        gain = gain_ref[...]
        inverse = lax.rsqrt(jnp.mean(raw * raw, axis=-1, keepdims=True) + norm_epsilon)
        grad = unturned_head(grad, cosine[part, :], sine[part, :]) * gain
        dots = jnp.mean(grad * raw, axis=-1, keepdims=True)
        return (inverse * (grad - raw * (inverse * inverse * dots))).astype(jnp.bfloat16)

    for start in range(0, rows, tile):
        part = slice(start, start + tile)
        queries = query[part, :]
        grads = grad_mixed[part, :]
        scores = dot_nt(keys, queries) * scale
        scores = jnp.where(seg_col[...] == seg_row[:, part], scores, masked_score)
        soft = jnp.exp(scores - stat[0, :, part])
        grad_soft = dot_nt(values, grads)
        delta = jnp.sum(soft * grad_soft, axis=0, keepdims=True)
        grad_scores = (soft * (grad_soft - delta)).astype(jnp.bfloat16)
        term_k = dot_nn(grad_scores, queries)
        term_v = dot_nn(soft.astype(jnp.bfloat16), grads)
        if start == 0:
            sum_k[...] = term_k
            sum_v[...] = term_v
        else:
            sum_k[...] += term_k
            sum_v[...] += term_v
        grad_q[part, :] = through(dot_nn(keys_t, grad_scores).T * scale, q_raw, gain_q, part)
    for start in range(0, rows, tile):
        part = slice(start, start + tile)
        grad_k[part, :] = through(sum_k[part, :] * scale, k_raw, gain_k, part)
        grad_v[part, :] = sum_v[part, :].astype(jnp.bfloat16)


def attend_back(kept, grad_mixed, raw, cosine, sine, gain_q, gain_k, segment):
    query, key, value, stat = kept
    unused, length, width = raw.shape
    heads = width // HD
    tile = min(256, length)
    head = pl.BlockSpec((length, HD), lambda h: (0, h))
    raw_head = [pl.BlockSpec((None, length, HD), functools.partial(lambda m, h: (m, 0, h), m)) for m in range(3)]
    fixed = lambda shape: pl.BlockSpec(shape, lambda h: (0, 0))
    seg = segment.astype(jnp.float32)
    low = jax.ShapeDtypeStruct((length, width), jnp.bfloat16)
    return pl.pallas_call(
        functools.partial(attend_back_kernel, tile),
        grid=(heads,),
        in_specs=[head, head, head, head, pl.BlockSpec((1, 1, length), lambda h: (h, 0, 0)), raw_head[0], raw_head[1],
                  fixed((length, HD)), fixed((length, HD)), fixed((1, HD)), fixed((1, HD)),
                  fixed((length, 1)), fixed((1, length))],
        out_specs=[head, head, head],
        out_shape=[low, low, low],
        scratch_shapes=[pltpu.VMEM((length, HD), jnp.float32), pltpu.VMEM((length, HD), jnp.float32)],
        cost_estimate=pl.CostEstimate(
            flops=10 * heads * length * length * HD, bytes_accessed=24 * length * width, transcendentals=heads * length * length
        ),
        name="attend_back",
    )(query, key, value, grad_mixed, stat, raw, raw, cosine, sine, gain_q[None, :], gain_k[None, :],
      seg[:, None], seg[None, :])


def doc_layout(lengths, chosen, position):
    slots = jnp.arange(lengths.shape[0], dtype=jnp.int32)
    doc_ends = jnp.sum(jnp.where(slots[:, None] >= slots[None, :], lengths[None, :], 0), axis=1)
    starts = doc_ends - lengths
    segment = jnp.sum((position[:, None] >= doc_ends[None, :]).astype(jnp.int32), axis=1)
    doc_pick = (segment[:, None] == slots[None, :]).astype(jnp.int32)
    offset = position - jnp.sum(doc_pick * starts[None, :], axis=1)
    adapter = jnp.sum(doc_pick * chosen[None, :], axis=1)
    return (segment, offset, adapter)


def column_mask(adapter, columns):
    groups = jnp.arange(columns, dtype=jnp.int32) // R
    return (groups[None, :] == adapter[:, None]).astype(jnp.float32)


def qkv_kernel(x_ref, reduced_ref, w_ref, up_ref, out_ref):
    width = w_ref.shape[0] * w_ref.shape[1]
    weights = w_ref[...].reshape(width, x_ref.shape[1])
    out_ref[0] = dot_nt(x_ref[...], weights) + dot_nt(reduced_ref[...], up_ref[0])


def qkv_project(normed_all, reduced_cat, w_group, up_group):
    length, width = normed_all.shape
    dp_count, unused, piece, unused = w_group.shape
    group = dp_count * piece
    rank = up_group.shape[2]
    half = dp_count // 2
    return pl.pallas_call(
        qkv_kernel,
        grid=(3, 2),
        in_specs=[
            pl.BlockSpec((length, width), lambda m, p: (0, 0)),
            pl.BlockSpec((length, rank), lambda m, p: (0, m)),
            pl.BlockSpec((half, None, piece, width), lambda m, p: (p, m, 0, 0)),
            pl.BlockSpec((1, group // 2, rank), lambda m, p: (m, p, 0)),
        ],
        out_specs=pl.BlockSpec((1, length, group // 2), lambda m, p: (m, 0, p)),
        out_shape=jax.ShapeDtypeStruct((3, length, group), jnp.float32),
        cost_estimate=pl.CostEstimate(
            flops=6 * length * width * group, bytes_accessed=2 * length * width + 12 * length * group + 6 * group * width,
            transcendentals=0,
        ),
        name="qkv_project",
    )(normed_all, reduced_cat, w_group, up_group)


def qkv_back_kernel(a_ref, b_ref, c_ref, w_ref, out_ref):
    dp_count, unused, piece, cols = w_ref.shape
    total = None
    for m, ref in enumerate((a_ref, b_ref, c_ref)):
        term = dot_nn(ref[...], w_ref[:, m].reshape(dp_count * piece, cols))
        total = term if total is None else total + term
    out_ref[...] = total.astype(jnp.bfloat16)


def qkv_back(grads, w_group):
    length, group = grads[0].shape
    dp_count, unused, piece, width = w_group.shape
    tile = min(256, width)
    whole = pl.BlockSpec((length, group), lambda i: (0, 0))
    return pl.pallas_call(
        qkv_back_kernel,
        grid=(width // tile,),
        in_specs=[whole, whole, whole, pl.BlockSpec((dp_count, 3, piece, tile), lambda i: (0, 0, 0, i))],
        out_specs=pl.BlockSpec((length, tile), lambda i: (0, i)),
        out_shape=jax.ShapeDtypeStruct((length, width), jnp.bfloat16),
        cost_estimate=pl.CostEstimate(
            flops=6 * length * width * group, bytes_accessed=2 * length * width + 6 * length * group + 6 * group * width,
            transcendentals=0,
        ),
        name="qkv_back",
    )(grads[0], grads[1], grads[2], w_group)


def expert_kernel(kept_in, *refs):
    (x_a, x_b, g_a, g_b, pick, pick_t, slot, w_in, w_down, a_in, b_in, a_down, b_down) = refs[:13]
    refs = refs[13 + kept_in:]
    (out_a, out_b, back_a, back_b, xs, ps, act_o, gate_o, up_o, reds) = refs[:10]
    (red_g, red_u, gred_d, down_acc, down_red, gx_acc, gred_g, gred_u, sum_out_a, sum_out_b, sum_back_a, sum_back_b) = refs[10:]
    low = jnp.bfloat16
    e = pl.program_id(0)
    f = pl.program_id(1)
    last = pl.num_programs(1) - 1
    cap = pick.shape[2]
    rank = a_in.shape[3]
    rows = xs.shape[1]
    groups = lax.shift_right_logical(lax.broadcasted_iota(jnp.int32, (rows, rank), 1), R.bit_length() - 1)
    mask = jnp.where(groups.astype(jnp.float32) == slot[0, :, 1:2], 1.0, 0.0)

    @pl.when(f == 0)
    def _():
        for b, (x_ref, g_ref) in enumerate(((x_a, g_a), (x_b, g_b))):
            part = slice(b * cap, (b + 1) * cap)
            xs[0, part, :] = dot_nn(pick[0, b], x_ref[...]).astype(low)
            ps[0, part, :] = (slot[0, part, 0:1] * dot_nn(pick[0, b], g_ref[...])).astype(low)
        red_g[...] = (mask * dot_nn(xs[0], a_in[0, 0])).astype(low)
        red_u[...] = (mask * dot_nn(xs[0], a_in[0, 1])).astype(low)
        gred_d[...] = (mask * dot_nt(ps[0], b_down[0])).astype(low)

    x = xs[0]
    p = ps[0]
    gate = dot_nn(x, w_in[0, 0]) + dot_nn(red_g[...], b_in[0, 0])
    up = dot_nn(x, w_in[0, 1]) + dot_nn(red_u[...], b_in[0, 1])
    grad_act = dot_nt(p, w_down[0]) + dot_nt(gred_d[...], a_down[0])
    sigma = 1.0 / (1.0 + jnp.exp(-gate))
    silu = gate * sigma
    act = (silu * up).astype(low)
    grad_gate = (grad_act * up * (sigma * (1.0 + gate * (1.0 - sigma)))).astype(low)
    grad_up = (grad_act * silu).astype(low)
    act_o[0] = act
    gate_o[0] = grad_gate
    up_o[0] = grad_up
    down_term = dot_nn(act, w_down[0])
    down_red_term = dot_nn(act, a_down[0])
    gx_term = dot_nt(grad_gate, w_in[0, 0]) + dot_nt(grad_up, w_in[0, 1])
    gred_g_term = dot_nt(grad_gate, b_in[0, 0])
    gred_u_term = dot_nt(grad_up, b_in[0, 1])

    @pl.when(f == 0)
    def _():
        down_acc[...] = down_term
        down_red[...] = down_red_term
        gx_acc[...] = gx_term
        gred_g[...] = gred_g_term
        gred_u[...] = gred_u_term

    @pl.when(f > 0)
    def _():
        down_acc[...] += down_term
        down_red[...] += down_red_term
        gx_acc[...] += gx_term
        gred_g[...] += gred_g_term
        gred_u[...] += gred_u_term

    @pl.when(f == last)
    def _():
        reduced_d = (mask * down_red[...]).astype(low)
        back_g = (mask * gred_g[...]).astype(low)
        back_u = (mask * gred_u[...]).astype(low)
        for i, value in enumerate((red_g[...], red_u[...], reduced_d, back_g, back_u, gred_d[...])):
            reds[0, :, i * rank : (i + 1) * rank] = value
        produced = down_acc[...] + dot_nn(reduced_d, b_down[0])
        scaled = (slot[0, :, 0:1] * produced).astype(low)
        grads = (gx_acc[...] + dot_nt(back_g, a_in[0, 0]) + dot_nt(back_u, a_in[0, 1])).astype(low)
        for b, (out_ref, out_sum, back_ref, back_sum) in enumerate(
            ((out_a, sum_out_a, back_a, sum_back_a), (out_b, sum_out_b, back_b, sum_back_b))
        ):
            part = slice(b * cap, (b + 1) * cap)
            for values, total, result in ((scaled, out_sum, out_ref), (grads, back_sum, back_ref)):
                term = dot_nn(pick_t[0, b], values[part, :])

                @pl.when(e == 0)
                def _():
                    total[...] = term

                @pl.when(e > 0)
                def _():
                    total[...] += term

                @pl.when(e == pl.num_programs(0) - 1)
                def _():
                    result[...] = total[...].astype(low)


def run_experts(chunk, x_pair, g_pair, pick, pick_t, slot, weights, kept):
    w_in, w_down, a_in, b_in, a_down, b_down = weights
    experts, unused, width, ff = w_in.shape
    unused, dp_count, cap, own_rows = pick.shape
    rank = a_down.shape[2]
    rows = 2 * cap
    tile = min(256, ff)
    low = jnp.bfloat16
    f32 = jnp.float32
    token = pl.BlockSpec((own_rows, width), lambda e, f: (0, 0), pipeline_mode=pl.Buffered(1))
    stored = [
        ((experts, dp_count * cap, width), (1, rows, width), lambda e, f: (e, chunk, 0)),
        ((experts, dp_count * cap, width), (1, rows, width), lambda e, f: (e, chunk, 0)),
        ((experts, dp_count * cap, ff), (1, rows, tile), lambda e, f: (e, chunk, f)),
        ((experts, dp_count * cap, ff), (1, rows, tile), lambda e, f: (e, chunk, f)),
        ((experts, dp_count * cap, ff), (1, rows, tile), lambda e, f: (e, chunk, f)),
        ((experts, dp_count * cap, 6 * rank), (1, rows, 6 * rank), lambda e, f: (e, chunk, 0)),
    ]
    in_specs = [
        token, token, token, token,
        pl.BlockSpec((1, 2, cap, own_rows), lambda e, f: (e, chunk, 0, 0)),
        pl.BlockSpec((1, 2, own_rows, cap), lambda e, f: (e, chunk, 0, 0)),
        pl.BlockSpec((1, rows, 2), lambda e, f: (e, chunk, 0)),
        pl.BlockSpec((1, 2, width, tile), lambda e, f: (e, 0, 0, f)),
        pl.BlockSpec((1, tile, width), lambda e, f: (e, f, 0)),
        pl.BlockSpec((1, 2, width, rank), lambda e, f: (e, 0, 0, 0)),
        pl.BlockSpec((1, 2, rank, tile), lambda e, f: (e, 0, 0, f)),
        pl.BlockSpec((1, tile, rank), lambda e, f: (e, f, 0)),
        pl.BlockSpec((1, rank, width), lambda e, f: (e, 0, 0)),
    ] + [pl.BlockSpec(memory_space=pl.ANY) for unused in kept]
    part = jax.ShapeDtypeStruct((own_rows, width), low)
    results = pl.pallas_call(
        functools.partial(expert_kernel, len(kept)),
        grid=(experts, ff // tile),
        in_specs=in_specs,
        out_specs=[pl.BlockSpec((own_rows, width), lambda e, f: (0, 0), pipeline_mode=pl.Buffered(1))] * 4
        + [pl.BlockSpec(block, index) for unused, block, index in stored],
        out_shape=[part] * 4 + [jax.ShapeDtypeStruct(shape, low) for shape, unused, unused2 in stored],
        scratch_shapes=[
            pltpu.VMEM((rows, rank), low),
            pltpu.VMEM((rows, rank), low),
            pltpu.VMEM((rows, rank), low),
            pltpu.VMEM((rows, width), f32),
            pltpu.VMEM((rows, rank), f32),
            pltpu.VMEM((rows, width), f32),
            pltpu.VMEM((rows, rank), f32),
            pltpu.VMEM((rows, rank), f32),
        ] + [pltpu.VMEM((own_rows, width), f32) for unused in range(4)],
        input_output_aliases={13 + i: 4 + i for i in range(len(kept))},
        cost_estimate=pl.CostEstimate(
            flops=14 * experts * rows * width * ff, bytes_accessed=experts * (6 * width * ff + 8 * rows * width), transcendentals=experts * rows * ff
        ),
        compiler_params=pltpu.CompilerParams(vmem_limit_bytes=60 * 1024 * 1024),
        name="experts",
    )(*x_pair, *g_pair, pick, pick_t, slot, *weights, *kept)
    return results[:4], results[4:]


def swap(values, axis, distance, count):
    return lax.ppermute(values, axis, [(i, i ^ distance) for i in range(count)])


def spread(values, axis, count):
    return [values] + [swap(values, axis, k, count) for k in range(1, count)]


def collect(blocks, axis, count):
    total = blocks[0].astype(jnp.float32)
    for k in range(1, count):
        total = total + swap(blocks[k], axis, k, count).astype(jnp.float32)
    return total


def spread_pairs(values, count):
    blocks = []
    for c in range(count // 2):
        same = values if c == 0 else swap(values, "dp", 2 * c, count)
        blocks += [same, swap(same, "dp", 1, count)]
    return blocks


def collect_pairs(blocks, count):
    total = None
    for c in range(count // 2):
        pair = blocks[2 * c].astype(jnp.float32) + swap(blocks[2 * c + 1], "dp", 1, count).astype(jnp.float32)
        if c > 0:
            pair = swap(pair.astype(jnp.bfloat16), "dp", 2 * c, count).astype(jnp.float32)
        total = pair if total is None else total + pair
    return total


def after(values, *earlier):
    return lax.optimization_barrier((values,) + earlier)[0]


def local(
    layer_input,
    out_cotangent,
    gain_attention,
    gain_query,
    gain_key,
    gain_ffn,
    w_qkv,
    w_output,
    a_attention,
    b_attention,
    expert_w_in,
    expert_w_down,
    expert_a_in,
    expert_b_in,
    expert_a_down,
    expert_b_down,
    route_experts,
    route_gates,
    doc_lengths,
    adapter_ids,
):
    low = jnp.bfloat16
    f32 = jnp.float32
    own_rows = layer_input.shape[1]
    full_width = layer_input.shape[2]
    n = lax.axis_size("seq")
    dp_count = lax.axis_size("dp")
    s = lax.axis_index("seq")
    d = lax.axis_index("dp")
    length = own_rows * n
    rank_columns = a_attention.shape[2]
    group_width = full_width // n
    group_heads = H // n
    piece = group_width // dp_count
    group_start = s * group_width
    order = s ^ jnp.arange(n, dtype=jnp.int32)
    position = (order[:, None] * own_rows + jnp.arange(own_rows, dtype=jnp.int32)[None, :]).reshape(-1)
    segment, offset, adapter = doc_layout(doc_lengths[0], adapter_ids[0], position)
    own_adapter = adapter[:own_rows]
    own_mask = column_mask(own_adapter, rank_columns)
    full_mask = column_mask(adapter, rank_columns)

    ab_piece = jnp.concatenate([a_attention, jnp.swapaxes(b_attention, 1, 2)], axis=0)
    ab_group = lax.all_gather(ab_piece, "dp", axis=0)
    ab_group = jnp.swapaxes(ab_group, 0, 1).reshape(8, group_width, rank_columns)
    wt_piece = jnp.swapaxes(w_qkv, 1, 2)
    w_group = lax.all_gather(after(wt_piece, ab_group), "dp", axis=0)
    wo_group = lax.all_gather(after(w_output, w_group), "dp", axis=0, tiled=True)
    gates = route_gates[0].T
    gates_high = gates.astype(low)
    meta = jnp.concatenate(
        [
            route_experts[0].T.astype(low),
            gates_high,
            (gates - gates_high.astype(f32)).astype(low),
            own_adapter[None, :].astype(low),
            jnp.zeros((7, own_rows), low),
        ],
        axis=0,
    )
    meta_rows = -(-meta.size // full_width)
    pad_rows = -(-meta_rows // 16) * 16
    meta_flat = jnp.pad(meta.reshape(-1), (0, pad_rows * full_width - meta.size))
    grad_send = jnp.concatenate([out_cotangent[0], meta_flat.reshape(pad_rows, full_width)], axis=0)
    grad_blocks = spread_pairs(after(grad_send, wo_group), dp_count)

    tokens = layer_input[0].astype(f32)
    normed = rms_scale(tokens, gain_attention).astype(low)
    normed_blocks = spread(normed, "seq", n)
    normed_all = jnp.concatenate(normed_blocks, axis=0)
    share = jnp.concatenate([ab_group[0:3], ab_group[7:8]], axis=0)
    share_blocks = jnp.stack(spread(share, "seq", n))
    share_full = share_blocks[order]
    share_full = jnp.swapaxes(share_full, 0, 1).reshape(4, full_width, rank_columns)
    down_cat = jnp.swapaxes(share_full[0:3], 0, 1).reshape(full_width, 3 * rank_columns)
    upt_output = share_full[3]
    upt_group = ab_group[4:7]
    down_rows = ab_group[3]

    dot = lambda a, b: jnp.dot(a, b, preferred_element_type=f32)
    dot_t = lambda a, b: lax.dot_general(a, b, (((1,), (1,)), ((), ())), preferred_element_type=f32)
    dot_l = lambda a, b: lax.dot_general(a, b, (((0,), (0,)), ((), ())), preferred_element_type=f32)

    reduced_cat = (jnp.tile(full_mask, (1, 3)) * dot(normed_all, down_cat)).astype(low)
    reduced_list = [reduced_cat[:, m * rank_columns : (m + 1) * rank_columns] for m in range(3)]
    raw = qkv_project(normed_all, reduced_cat, w_group, upt_group)
    cosine, sine = rope_tables(offset, HD)
    mixed_group, query_heads, key_heads, value_heads, stat = attend(
        raw, cosine, sine, gain_query, gain_key, segment
    )

    out_maps = jnp.concatenate([wo_group, down_rows], axis=1)
    partial_out = dot(mixed_group, out_maps).astype(low).reshape(n, own_rows, full_width + rank_columns)
    summed = collect([partial_out[k] for k in range(n)], "seq", n)
    output_reduced = (own_mask * summed[:, full_width:]).astype(low)
    attended = summed[:, :full_width] + dot_t(output_reduced, upt_output)
    hidden = tokens + attended
    normed_ffn = rms_scale(hidden, gain_ffn).astype(low)
    local_count = expert_w_in.shape[0]
    expert_count = local_count * dp_count
    capacity = own_rows * TOP // expert_count * 9 // 8
    capacity = -(-capacity // 16) * 16
    meta_all = jnp.stack(
        [
            x[own_rows:].reshape(-1)[: meta.size].reshape(meta.shape).astype(f32)
            for x in grad_blocks
        ]
    )
    named = meta_all[:, 0:TOP, :].astype(jnp.int32)
    gates_all = meta_all[:, TOP : 2 * TOP, :] + meta_all[:, 2 * TOP : 3 * TOP, :]
    sets_all = meta_all[:, 3 * TOP, :]
    mine = d * local_count + jnp.arange(local_count, dtype=jnp.int32)
    hit = (named[None] == mine[:, None, None, None]).astype(f32)
    member = jnp.sum(hit, axis=2)
    token_gate = jnp.sum(hit * gates_all[None], axis=2)
    t_index = jnp.arange(own_rows, dtype=jnp.int32)
    upto = (t_index[:, None] <= t_index[None, :]).astype(low)
    rank = jnp.einsum("ejt,tu->eju", member.astype(low), upto, preferred_element_type=f32) - 1.0
    slots = jnp.arange(capacity, dtype=jnp.int32).astype(f32)
    rank = jnp.where(member > 0.5, rank, -1.0)
    pick = slots[None, None, :, None] == rank[:, :, None, :]
    pick_t = (rank[:, :, :, None] == slots[None, None, None, :]).astype(low)
    slot_gate = jnp.sum(jnp.where(pick, token_gate[:, :, None, :], 0.0), axis=-1)
    slot_set = jnp.sum(jnp.where(pick, sets_all[None, :, None, :], 0.0), axis=-1)
    slot = jnp.stack([slot_gate, slot_set], axis=-1).reshape(local_count, dp_count * capacity, 2)
    pick = pick.astype(low)

    row_blocks = spread_pairs(normed_ffn, dp_count)
    weights = (expert_w_in, expert_w_down, expert_a_in, expert_b_in, expert_a_down, expert_b_down)
    outs = []
    backs = []
    kept = ()
    for c in range(dp_count // 2):
        (out_a, out_b, back_a, back_b), kept = run_experts(
            c, row_blocks[2 * c : 2 * c + 2], grad_blocks[2 * c : 2 * c + 2], pick, pick_t, slot, weights, kept
        )
        outs += [out_a, out_b]
        backs += [back_a, back_b]
    grad_normed_ffn = collect_pairs(backs, dp_count)

    grad_out = out_cotangent[0].astype(f32)
    unused, pull_ffn = jax.vjp(lambda values: rms_scale(values, gain_ffn), hidden)
    grad_hidden = grad_out + pull_ffn(grad_normed_ffn)[0]
    grad_hidden_low = grad_hidden.astype(low)
    grad_reduced_output = (own_mask * dot(grad_hidden_low, upt_output)).astype(low)
    grad_pack = jnp.concatenate([grad_hidden_low, grad_reduced_output, output_reduced], axis=1)
    grad_pack_all = jnp.concatenate(spread(grad_pack, "seq", n), axis=0)
    outs = list(after(tuple(outs), grad_pack_all))
    mixture = collect_pairs(outs, dp_count)
    layer_output = (hidden + mixture).astype(low)[None]
    grad_all = grad_pack_all[:, :full_width]
    grad_reduced_all = grad_pack_all[:, full_width : full_width + rank_columns]
    output_reduced_all = grad_pack_all[:, full_width + rank_columns :]
    grad_mixed_group = dot_t(grad_pack_all[:, : full_width + rank_columns], out_maps).astype(low)
    grad_cols = lax.dynamic_slice_in_dim(grad_all, group_start, group_width, 1)
    grad_upt_output = dot_l(grad_cols, output_reduced_all)
    grad_down_output = dot_l(mixed_group, grad_reduced_all)
    grad_raw_list = attend_back(
        (query_heads, key_heads, value_heads, stat),
        grad_mixed_group,
        raw,
        cosine,
        sine,
        gain_query,
        gain_key,
        segment,
    )
    partial_reduced = jnp.concatenate(
        [dot(grad_raw_list[m], upt_group[m]) for m in range(3)], axis=1
    ).astype(low).reshape(n, own_rows, 3 * rank_columns)
    summed_reduced = collect([partial_reduced[k] for k in range(n)], "seq", n)
    grad_reduced = (jnp.tile(own_mask, (1, 3)) * summed_reduced).astype(low)
    grad_reduced_full = jnp.concatenate(spread(grad_reduced, "seq", n), axis=0)
    partial_normed = qkv_back(grad_raw_list, w_group).reshape(n, own_rows, full_width)
    summed_back = collect([partial_normed[k] for k in range(n)], "seq", n)
    grad_normed = summed_back + dot_t(grad_reduced, down_cat)
    unused_input, pull_input = jax.vjp(lambda values: rms_scale(values, gain_attention), tokens)
    input_grad = (grad_hidden + pull_input(grad_normed)[0]).astype(low)[None]

    grad_upt = [dot_l(grad_raw_list[m], reduced_list[m]) for m in range(3)]
    normed_cols = lax.dynamic_slice_in_dim(normed_all, group_start, group_width, 1)
    grad_down_cat = dot_l(normed_cols, grad_reduced_full)
    parts = [grad_down_cat[:, m * rank_columns : (m + 1) * rank_columns] for m in range(3)]
    parts += [grad_down_output] + grad_upt + [grad_upt_output]
    stacked = jnp.stack([x.astype(low).reshape(dp_count, piece, rank_columns) for x in parts], axis=1)
    own_parts = lax.psum_scatter(stacked, "dp", scatter_dimension=0).astype(f32)
    grad_a_attention = own_parts[0:4]
    grad_b_attention = jnp.swapaxes(own_parts[4:8], 1, 2)

    xs, ps, act_rows, gate_rows, up_rows, reds = kept
    flat = []
    for e in range(local_count):
        red = [reds[e][:, i * rank_columns : (i + 1) * rank_columns] for i in range(6)]
        terms = [
            (reds[e][:, 3 * rank_columns : 5 * rank_columns], xs[e]),
            (red[0], gate_rows[e]),
            (red[1], up_rows[e]),
            (red[5], act_rows[e]),
            (red[2], ps[e]),
        ]
        flat += [dot_l(a, b).astype(low).reshape(-1, rank_columns, b.shape[1]) for a, b in terms]
    widths = [(x.shape[0], x.shape[2] // n) for x in flat]
    flat = jnp.concatenate(
        [
            x.reshape(x.shape[0], rank_columns, n, -1).transpose(2, 0, 1, 3).reshape(n, -1)
            for x in flat
        ],
        axis=1,
    ).reshape(n, -1, rank_columns)
    flat = lax.psum_scatter(flat, "seq", scatter_dimension=0).astype(f32).reshape(-1)
    pieces = []
    start = 0
    for count, width in widths:
        size = count * rank_columns * width
        pieces.append(flat[start : start + size].reshape(count, rank_columns, width))
        start += size
    per = [pieces[5 * e : 5 * e + 5] for e in range(local_count)]
    grad_a_in = jnp.stack([jnp.swapaxes(p[0], 1, 2) for p in per])
    grad_b_in = jnp.stack([jnp.concatenate([p[1], p[2]], axis=0) for p in per])
    grad_a_down = jnp.stack([p[3][0].T for p in per])
    grad_b_down = jnp.stack([p[4][0] for p in per])
    return (
        layer_output,
        input_grad,
        grad_a_attention,
        grad_b_attention,
        grad_a_in,
        grad_b_in,
        grad_a_down,
        grad_b_down,
    )


def solution(mesh):
    return jax.shard_map(
        local,
        mesh=mesh,
        in_specs=(
            P("dp", "seq", None),
            P("dp", "seq", None),
            P(),
            P(),
            P(),
            P(),
            P(None, None, ("seq", "dp")),
            P(("seq", "dp"), None),
            P(None, ("seq", "dp"), None),
            P(None, None, ("seq", "dp")),
            P("dp", None, None, None),
            P("dp", None, None),
            P("dp", None, None, None),
            P("dp", None, None, None),
            P("dp", None, None),
            P("dp", None, None),
            P("dp", "seq", None),
            P("dp", "seq", None),
            P("dp", None),
            P("dp", None),
        ),
        out_specs=(
            P("dp", "seq", None),
            P("dp", "seq", None),
            P(None, ("seq", "dp"), None),
            P(None, None, ("seq", "dp")),
            P("dp", None, "seq", None),
            P("dp", None, None, "seq"),
            P("dp", "seq", None),
            P("dp", None, "seq"),
        ),
        check_vma=False,
    )
```

time: 936 us -> 1000 us (1.068)
  the two profiles are of different devices: /device:TPU:0 before, /device:TPU:8 now
where the time goes in v2:
time: 1000 us; the launch traced here: 994 us
  waiting for transfers between devices  510 us (51%)
  Pallas kernels  242 us (24%)
  local copies, waits for them, and re-layouts  76.4 us (8%)
  matrix products  55.7 us (6%)
  other arithmetic  55.3 us (6%)
  starting transfers between devices  39.2 us (4%)
  between operations  15.7 us (2%)
    ppermute x49, waiting for transfers between devices, swap(): return lax.ppermute(values, axis, [(i, i ^ distance) for i in range(count)])  432 us
    pallas_call x4, Pallas kernels, run_experts(): pl.pallas_call(functools.partial(expert_kernel, len(kept)), grid=(experts...  169 us
    all_gather x1, waiting for transfers between devices, local(): w_group = lax.all_gather(after(wt_piece, ab_group), 'dp', axis=0)  53.9 us
    ppermute x49, starting transfers between devices, swap(): return lax.ppermute(values, axis, [(i, i ^ distance) for i in range(count)])  39 us
    dot_general x16, matrix products, local(): lax.dot_general(a, b, (((0,), (0,)), ((), ())), preferred_element_type=f32)  34.6 us
    unnamed x171, local copies, waits for them, and re-layouts  26.9 us
    pallas_call x1, Pallas kernels, attend(): pl.pallas_call(functools.partial(attend_kernel, tile), grid=(heads,), in_...  23.8 us
    pallas_call x1, Pallas kernels, attend_back(): pl.pallas_call(functools.partial(attend_back_kernel, tile), grid=(heads,)...  23.7 us
  transfers between devices with their start and end apart: 54, of which 26 were waited for; matrix products, arithmetic and copies ran while one was open for 14% of the time, Pallas kernels for 22%

profile of v2, /device:TPU:8, one launch (start us, length us, event | category | flops | bytes accessed | tf_op | source)
XLA Modules:
  0.0 993.9 jit_solution(13005376249469812788)
XLA Ops:
  19.5 53.9 %all-gather.10.cloned.1.call-done = bf16[24,64,2048]{2,1,0:T(8,128)(2,1)} async-done(((bf16[3,64,2048]{2,1,0:T(8,128)(2,1)}), bf16[24,64,2048]{2,1,0:T(8,128)(2,1)}) %all-gather.10.cloned.1.call-update) | async-done | bytes 6291472 | tf_op jit(solution)/shard_map/all_gather | solution.py:491
  75.6 23.2 %all-gather.8.cloned.1.call-done = bf16[64,64,128]{2,1,0:T(8,128)(2,1)} async-done(((bf16[8,64,128]{2,1,0:T(8,128)(2,1)}), bf16[64,64,128]{2,1,0:T(8,128)(2,1)}) %all-gather.8.cloned.1.call-update) | async-done | bytes 1048592 | tf_op jit(solution)/shard_map/all_gather | solution.py:488
  145.3 12.6 %qkv_project.1.q_raw.k_raw.v_raw = f32[3,1024,512]{2,1,0:T(8,128)} custom-call(bf16[1024,2048]{1,0:T(8,128)(2,1)} %pad_maximum_fusion.1.x_ref, bf16[1024,384]{1,0:T(8,128)(2,1)} %multiply_convert_fusion.1.reduced_ref, bf16[8,3,64,2048]{3,2,1,0:T(8,128)(2,1)} %bitcast.299, bf16[3,512,128]{2,1,0:T(8,128)(2,1)} %bitcast.277), custom_call_target="tpu_custom_call" | custom-call | flops 6442450944 | bytes 16777216 | tf_op jit(solution)/shard_map/qkv_project/pallas_call | solution.py:212
  157.9 23.8 %attend.1 = (bf16[1024,512]{1,0:T(8,128)(2,1)}, bf16[1024,512]{1,0:T(8,128)(2,1)}, bf16[1024,512]{1,0:T(8,128)(2,1)}, bf16[1024,512]{1,0:T(8,128)(2,1)}, f32[4,1,1024]{2,1,0:T(1,128)}) custom-call(f32[3,1024,512]{2,1,0:T(8,128)} %qkv_project.1.q_raw.k_raw.v_raw, f32[3,1024,512]{2,1,0:T(8,128)} %qkv_project.1.q_raw.k_raw.v_raw, ...), custom_call_target="tpu_custom_call" | custom-call | flops 2147483648 | bytes 10485760 | tf_op jit(solution)/shard_map/attend/pallas_call | solution.py:99
  192.7 36.1 %collective-permute-done.11.refs_2_ = bf16[272,2048]{1,0:T(8,128)(2,1)S(1)} collective-permute-done((bf16[272,2048]{1,0:T(8,128)(2,1)}, bf16[272,2048]{1,0:T(8,128)(2,1)S(1)}, u32[]{:S(2)}, u32[]{:S(2)}) %collective-permute-start.11) | collective-permute-done | bytes 1114144 | tf_op jit(solution)/shard_map/ppermute | solution.py:408
  239.9 40.8 %collective-permute-done.15.refs_2_ = bf16[272,2048]{1,0:T(8,128)(2,1)} collective-permute-done((bf16[272,2048]{1,0:T(8,128)(2,1)S(1)}, bf16[272,2048]{1,0:T(8,128)(2,1)}, u32[]{:S(2)}, u32[]{:S(2)}) %collective-permute-start.15) | collective-permute-done | bytes 1114144 | tf_op jit(solution)/shard_map/ppermute | solution.py:408
  292.1 36.1 %collective-permute-done.17.refs_0_ = bf16[256,2048]{1,0:T(8,128)(2,1)} collective-permute-done((bf16[256,2048]{1,0:T(8,128)(2,1)}, bf16[256,2048]{1,0:T(8,128)(2,1)}, u32[]{:S(2)}, u32[]{:S(2)}) %collective-permute-start.17) | collective-permute-done | bytes 1048608 | tf_op jit(solution)/shard_map/ppermute | solution.py:408
  328.1 26.0 %collective-permute-done.19.refs_0_ = bf16[256,2048]{1,0:T(8,128)(2,1)} collective-permute-done((bf16[256,2048]{1,0:T(8,128)(2,1)}, bf16[256,2048]{1,0:T(8,128)(2,1)}, u32[]{:S(2)}, u32[]{:S(2)}) %collective-permute-start.19) | collective-permute-done | bytes 1048608 | tf_op jit(solution)/shard_map/ppermute | solution.py:408
  354.1 23.0 %collective-permute-done.21.refs_0_ = bf16[256,2048]{1,0:T(8,128)(2,1)} collective-permute-done((bf16[256,2048]{1,0:T(8,128)(2,1)}, bf16[256,2048]{1,0:T(8,128)(2,1)}, u32[]{:S(2)}, u32[]{:S(2)}) %collective-permute-start.21) | collective-permute-done | bytes 1048608 | tf_op jit(solution)/shard_map/ppermute | solution.py:408
  388.5 42.3 %experts.4 = (bf16[256,2048]{1,0:T(8,128)(2,1)}, bf16[256,2048]{1,0:T(8,128)(2,1)}, bf16[256,2048]{1,0:T(8,128)(2,1)}, bf16[256,2048]{1,0:T(8,128)(2,1)}, bf16[2...) custom-call(bf16[256,2048]{1,0:T(8,128)(2,1)} %multiply_convert_fusi, ...), custom_call_target="tpu_custom_call" | custom-call | flops 16911433728 | bytes 34603008 | tf_op jit(solution)/shard_map/experts/pallas_call | solution.py:380
  430.9 42.3 %experts.5 = (bf16[256,2048]{1,0:T(8,128)(2,1)}, bf16[256,2048]{1,0:T(8,128)(2,1)}, bf16[256,2048]{1,0:T(8,128)(2,1)}, bf16[256,2048]{1,0:T(8,128)(2,1)}, bf16[2...) custom-call(bf16[256,2048]{1,0:T(8,128)(2,1)} %collective-permute-do, ...), custom_call_target="tpu_custom_call", output_to_operand_aliasing={{4}: (13, {}), {5}: (14, {}), {6}: (15, {}), {7}: (16, {}),... | custom-call | flops 16911433728 | bytes 34603008 | tf_op jit(solution)/shard_map/experts/pallas_call | solution.py:380
  473.2 42.1 %experts.6 = (bf16[256,2048]{1,0:T(8,128)(2,1)}, bf16[256,2048]{1,0:T(8,128)(2,1)}, bf16[256,2048]{1,0:T(8,128)(2,1)}, bf16[256,2048]{1,0:T(8,128)(2,1)}, bf16[2...) custom-call(bf16[256,2048]{1,0:T(8,128)(2,1)} %collective-permute-do, ...), custom_call_target="tpu_custom_call", output_to_operand_aliasing={{4}: (13, {}), {5}: (14, {}), {6}: (15, {}), {7}: (16, {}),... | custom-call | flops 16911433728 | bytes 34603008 | tf_op jit(solution)/shard_map/experts/pallas_call | solution.py:380
  515.3 42.6 %experts.7 = (bf16[256,2048]{1,0:T(8,128)(2,1)}, bf16[256,2048]{1,0:T(8,128)(2,1)}, bf16[256,2048]{1,0:T(8,128)(2,1)}, bf16[256,2048]{1,0:T(8,128)(2,1)}, bf16[2...) custom-call(bf16[256,2048]{1,0:T(8,128)(2,1)} %collective-permute-do, ...), custom_call_target="tpu_custom_call", output_to_operand_aliasing={{4}: (13, {}), {5}: (14, {}), {6}: (15, {}), {7}: (16, {}),... | custom-call | flops 16911433728 | bytes 34603008 | tf_op jit(solution)/shard_map/experts/pallas_call | solution.py:380
  617.8 32.8 %collective-permute-done.25 = bf16[256,2048]{1,0:T(8,128)(2,1)} collective-permute-done((bf16[256,2048]{1,0:T(8,128)(2,1)}, bf16[256,2048]{1,0:T(8,128)(2,1)}, u32[]{:S(2)}, u32[]{:S(2)}) %collective-permute-start.25) | collective-permute-done | bytes 1048608 | tf_op jit(solution)/shard_map/ppermute | solution.py:408
  650.6 29.0 %collective-permute-done.27 = bf16[256,2048]{1,0:T(8,128)(2,1)} collective-permute-done((bf16[256,2048]{1,0:T(8,128)(2,1)}, bf16[256,2048]{1,0:T(8,128)(2,1)}, u32[]{:S(2)}, u32[]{:S(2)}) %collective-permute-start.27) | collective-permute-done | bytes 1048608 | tf_op jit(solution)/shard_map/ppermute | solution.py:408
  679.5 22.6 %collective-permute-done.29 = bf16[256,2048]{1,0:T(8,128)(2,1)} collective-permute-done((bf16[256,2048]{1,0:T(8,128)(2,1)}, bf16[256,2048]{1,0:T(8,128)(2,1)}, u32[]{:S(2)}, u32[]{:S(2)}) %collective-permute-start.29) | collective-permute-done | bytes 1048608 | tf_op jit(solution)/shard_map/ppermute | solution.py:408
  721.3 20.0 %collective-permute-done.30 = bf16[256,2304]{1,0:T(8,128)(2,1)} collective-permute-done((bf16[256,2304]{1,0:T(8,128)(2,1)}, bf16[256,2304]{1,0:T(8,128)(2,1)}, u32[]{:S(2)}, u32[]{:S(2)}) %collective-permute-start.30) | collective-permute-done | bytes 1179680 | tf_op jit(solution)/shard_map/ppermute | solution.py:408
  741.3 24.9 %collective-permute-done.31 = bf16[256,2304]{1,0:T(8,128)(2,1)} collective-permute-done((bf16[256,2304]{1,0:T(8,128)(2,1)}, bf16[256,2304]{1,0:T(8,128)(2,1)}, u32[]{:S(2)}, u32[]{:S(2)}) %collective-permute-start.31) | collective-permute-done | bytes 1179680 | tf_op jit(solution)/shard_map/ppermute | solution.py:408
  776.8 23.7 %attend_back.1 = (bf16[1024,512]{1,0:T(8,128)(2,1)}, bf16[1024,512]{1,0:T(8,128)(2,1)}, bf16[1024,512]{1,0:T(8,128)(2,1)}) custom-call(bf16[1024,512]{1,0:T(8,128)(2,1)} %get-tuple-element.111.query, bf16[1024,512]{1,0:T(8,128)(2,1)} %get-tuple-element.112.key, bf16[1024,512]{1,0:T(8,128)(2,1)} %get-tuple-element.113.value, ...), custom_call_target="tpu_custom_call" | custom-call | flops 5368709120 | bytes 12582912 | tf_op jit(solution)/shard_map/attend_back/pallas_call | solution.py:167
  840.7 12.4 %qkv_back.1 = bf16[1024,2048]{1,0:T(8,128)(2,1)} custom-call(bf16[1024,512]{1,0:T(8,128)(2,1)} %get-tuple-element.115.a_ref, bf16[1024,512]{1,0:T(8,128)(2,1)} %get-tuple-element.116.b_ref, bf16[1024,512]{1,0:T(8,128)(2,1)} %get-tuple-element.117.c_ref, bf16[8,3,64,2048]{3,2,1,0:T(8,128)(2,1)} %bitcast.300), custom_call_target="tpu_custom_call" | custom-call | flops 6442450944 | bytes 13631488 | tf_op jit(solution)/shard_map/qkv_back/pallas_call | solution.py:245
  862.4 25.7 %collective-permute-done.40 = bf16[256,2048]{1,0:T(8,128)(2,1)S(1)} collective-permute-done((bf16[256,2048]{1,0:T(8,128)(2,1)S(1)}, bf16[256,2048]{1,0:T(8,128)(2,1)S(1)}, u32[]{:S(2)}, u32[]{:S(2)}) %collective-permute-start.40) | collective-permute-done | bytes 1048608 | tf_op jit(solution)/shard_map/ppermute | solution.py:408
  892.2 36.6 %collective-permute-done.42 = bf16[256,2048]{1,0:T(8,128)(2,1)S(1)} collective-permute-done((bf16[256,2048]{1,0:T(8,128)(2,1)S(1)}, bf16[256,2048]{1,0:T(8,128)(2,1)S(1)}, u32[]{:S(2)}, u32[]{:S(2)}) %collective-permute-start.42) | collective-permute-done | bytes 1048608 | tf_op jit(solution)/shard_map/ppermute | solution.py:408
  933.0 20.8 %collective-permute-done.37 = bf16[256,2048]{1,0:T(8,128)(2,1)S(1)} collective-permute-done((bf16[256,2048]{1,0:T(8,128)(2,1)S(1)}, bf16[256,2048]{1,0:T(8,128)(2,1)S(1)}, u32[]{:S(2)}, u32[]{:S(2)}) %collective-permute-start.37) | collective-permute-done | bytes 1048608 | tf_op jit(solution)/shard_map/ppermute | solution.py:408
  953.8 22.2 %collective-permute-done.39 = bf16[256,2048]{1,0:T(8,128)(2,1)S(1)} collective-permute-done((bf16[256,2048]{1,0:T(8,128)(2,1)S(1)}, bf16[256,2048]{1,0:T(8,128)(2,1)S(1)}, u32[]{:S(2)}, u32[]{:S(2)}) %collective-permute-start.39) | collective-permute-done | bytes 1048608 | tf_op jit(solution)/shard_map/ppermute | solution.py:408
  (430 shorter events, 263.0 us)
Async XLA Ops:
  7.2 66.3 %all-gather.10.cloned.1.call-start = ((), (), s32[]{:S(2)}) async-start(), calls=%async_computation.5 | async-start | bytes 7077888 | tf_op jit(solution)/shard_map/all_gather | solution.py:491
  7.9 90.8 %all-gather.8.cloned.1.call-start = ((), (), s32[]{:S(2)}) async-start(), calls=%async_computation.4 | async-start | bytes 1179648 | tf_op jit(solution)/shard_map/all_gather | solution.py:488
  11.6 94.0 %collective-permute-start = (bf16[256,2048]{1,0:T(8,128)(2,1)}, bf16[256,2048]{1,0:T(8,128)(2,1)}, u32[]{:S(2)}, u32[]{:S(2)}) collective-permute-start(bf16[256,2048]{1,0:T(8,128)(2,1)} %fusion.51), channel_id=1, source_target_pairs={{0,8},{8,0},{16,24},{24,16},{1,9},{9,1},{17,25},{25,17},{2,10},{10... | collective-permute-start | bytes 3145736 | tf_op jit(solution)/shard_map/ppermute | solution.py:408
  13.1 98.7 %collective-permute-start.1 = (bf16[256,2048]{1,0:T(8,128)(2,1)}, bf16[256,2048]{1,0:T(8,128)(2,1)}, u32[]{:S(2)}, u32[]{:S(2)}) collective-permute-start(bf16[256,2048]{1,0:T(8,128)(2,1)} %fusion.51), channel_id=1, source_target_pairs={{0,16},{8,24},{16,0},{24,8},{1,17},{9,25},{17,1},{25,9},{2,18},{10... | collective-permute-start | bytes 3145736 | tf_op jit(solution)/shard_map/ppermute | solution.py:408
  14.6 97.2 %collective-permute-start.2 = (bf16[256,2048]{1,0:T(8,128)(2,1)}, bf16[256,2048]{1,0:T(8,128)(2,1)}, u32[]{:S(2)}, u32[]{:S(2)}) collective-permute-start(bf16[256,2048]{1,0:T(8,128)(2,1)} %fusion.51), channel_id=1, source_target_pairs={{0,24},{8,16},{16,8},{24,0},{1,25},{9,17},{17,9},{25,1},{2,26},{10... | collective-permute-start | bytes 3145736 | tf_op jit(solution)/shard_map/ppermute | solution.py:408
  15.8 166.0 %all-gather.6.cloned.1.call-start = ((), (), s32[]{:S(2)}) async-start(), calls=%async_computation.2 | async-start | bytes 2359296 | tf_op jit(solution)/shard_map/all_gather | solution.py:492
  73.5 904.5 %reduce-scatter.5.cloned.1.call-start = ((), (), s32[]{:S(2)}) async-start(), calls=%async_computation.3 | async-start | bytes 1179648 | tf_op jit(solution)/shard_map/reduce_scatter | solution.py:630
  239.2 137.9 %collective-permute-start.14 = (bf16[272,2048]{1,0:T(8,128)(2,1)}, bf16[272,2048]{1,0:T(8,128)(2,1)}, u32[]{:S(2)}, u32[]{:S(2)}) collective-permute-start(bf16[272,2048]{1,0:T(8,128)(2,1)} %collective-permute-done.13.refs_2_), channel_id=1, source_target_pairs={{0,1},{1,0},{2,3},{3,2},{4,5},{5,4},{6,7},{7,6},{8,9},{9,8},{10,11... | collective-permute-start | bytes 3342344 | tf_op jit(solution)/shard_map/ppermute | solution.py:408
  280.6 97.8 %collective-permute-start.16 = (bf16[272,2048]{1,0:T(8,128)(2,1)}, bf16[272,2048]{1,0:T(8,128)(2,1)}, u32[]{:S(2)}, u32[]{:S(2)}) collective-permute-start(bf16[272,2048]{1,0:T(8,128)(2,1)} %collective-permute-done.15.refs_2_), channel_id=1, source_target_pairs={{0,1},{1,0},{2,3},{3,2},{4,5},{5,4},{6,7},{7,6},{8,9},{9,8},{10,11... | collective-permute-start | bytes 3342344 | tf_op jit(solution)/shard_map/ppermute | solution.py:408
  282.6 71.5 %collective-permute-start.19 = (bf16[256,2048]{1,0:T(8,128)(2,1)}, bf16[256,2048]{1,0:T(8,128)(2,1)}, u32[]{:S(2)}, u32[]{:S(2)}) collective-permute-start(bf16[256,2048]{1,0:T(8,128)(2,1)} %multiply_convert_fusion.refs_0_), channel_id=1, source_target_pairs={{0,4},{1,5},{2,6},{3,7},{4,0},{5,1},{6,2},{7,3},{8,12},{9,13},{10,... | collective-permute-start | bytes 3145736 | tf_op jit(solution)/shard_map/ppermute | solution.py:408
  286.3 90.8 %collective-permute-start.21 = (bf16[256,2048]{1,0:T(8,128)(2,1)}, bf16[256,2048]{1,0:T(8,128)(2,1)}, u32[]{:S(2)}, u32[]{:S(2)}) collective-permute-start(bf16[256,2048]{1,0:T(8,128)(2,1)} %multiply_convert_fusion.refs_0_), channel_id=1, source_target_pairs={{0,6},{1,7},{2,4},{3,5},{4,2},{5,3},{6,0},{7,1},{8,14},{9,15},{10,... | collective-permute-start | bytes 3145736 | tf_op jit(solution)/shard_map/ppermute | solution.py:408
  328.1 60.4 %collective-permute-start.9 = (bf16[256,2048]{1,0:T(8,128)(2,1)}, bf16[256,2048]{1,0:T(8,128)(2,1)}, u32[]{:S(2)}, u32[]{:S(2)}) collective-permute-start(bf16[256,2048]{1,0:T(8,128)(2,1)} %multiply_convert_fusion.refs_0_), channel_id=1, source_target_pairs={{0,1},{1,0},{2,3},{3,2},{4,5},{5,4},{6,7},{7,6},{8,9},{9,8},{10,11... | collective-permute-start | bytes 3145736 | tf_op jit(solution)/shard_map/ppermute | solution.py:408
  354.1 76.7 %collective-permute-start.18 = (bf16[256,2048]{1,0:T(8,128)(2,1)}, bf16[256,2048]{1,0:T(8,128)(2,1)}, u32[]{:S(2)}, u32[]{:S(2)}) collective-permute-start(bf16[256,2048]{1,0:T(8,128)(2,1)} %collective-permute-done.17.refs_0_), channel_id=1, source_target_pairs={{0,1},{1,0},{2,3},{3,2},{4,5},{5,4},{6,7},{7,6},{8,9},{9,8},{10,11... | collective-permute-start | bytes 3145736 | tf_op jit(solution)/shard_map/ppermute | solution.py:408
  377.1 96.1 %collective-permute-start.20 = (bf16[256,2048]{1,0:T(8,128)(2,1)}, bf16[256,2048]{1,0:T(8,128)(2,1)}, u32[]{:S(2)}, u32[]{:S(2)}) collective-permute-start(bf16[256,2048]{1,0:T(8,128)(2,1)} %collective-permute-done.19.refs_0_), channel_id=1, source_target_pairs={{0,1},{1,0},{2,3},{3,2},{4,5},{5,4},{6,7},{7,6},{8,9},{9,8},{10,11... | collective-permute-start | bytes 3145736 | tf_op jit(solution)/shard_map/ppermute | solution.py:408
  377.1 138.2 %collective-permute-start.22 = (bf16[256,2048]{1,0:T(8,128)(2,1)}, bf16[256,2048]{1,0:T(8,128)(2,1)}, u32[]{:S(2)}, u32[]{:S(2)}) collective-permute-start(bf16[256,2048]{1,0:T(8,128)(2,1)} %collective-permute-done.21.refs_0_), channel_id=1, source_target_pairs={{0,1},{1,0},{2,3},{3,2},{4,5},{5,4},{6,7},{7,6},{8,9},{9,8},{10,11... | collective-permute-start | bytes 3145736 | tf_op jit(solution)/shard_map/ppermute | solution.py:408
  430.8 187.0 %collective-permute-start.23 = (bf16[256,2048]{1,0:T(8,128)(2,1)}, bf16[256,2048]{1,0:T(8,128)(2,1)}, u32[]{:S(2)}, u32[]{:S(2)}) collective-permute-start(bf16[256,2048]{1,0:T(8,128)(2,1)} %get-tuple-element.96), channel_id=1, source_target_pairs={{0,1},{1,0},{2,3},{3,2},{4,5},{5,4},{6,7},{7,6},{8,9},{9,8},{10,11... | collective-permute-start | bytes 3145736 | tf_op jit(solution)/shard_map/ppermute | solution.py:408
  608.0 71.5 %collective-permute-start.27 = (bf16[256,2048]{1,0:T(8,128)(2,1)}, bf16[256,2048]{1,0:T(8,128)(2,1)}, u32[]{:S(2)}, u32[]{:S(2)}) collective-permute-start(bf16[256,2048]{1,0:T(8,128)(2,1)} %add_convert_fusion.5), channel_id=1, source_target_pairs={{0,4},{1,5},{2,6},{3,7},{4,0},{5,1},{6,2},{7,3},{8,12},{9,13},{10,... | collective-permute-start | bytes 3145736 | tf_op jit(solution)/shard_map/ppermute | solution.py:408
  612.1 90.0 %collective-permute-start.29 = (bf16[256,2048]{1,0:T(8,128)(2,1)}, bf16[256,2048]{1,0:T(8,128)(2,1)}, u32[]{:S(2)}, u32[]{:S(2)}) collective-permute-start(bf16[256,2048]{1,0:T(8,128)(2,1)} %add_convert_fusion.4), channel_id=1, source_target_pairs={{0,6},{1,7},{2,4},{3,5},{4,2},{5,3},{6,0},{7,1},{8,14},{9,15},{10,... | collective-permute-start | bytes 3145736 | tf_op jit(solution)/shard_map/ppermute | solution.py:408
  833.9 145.7 %reduce-scatter.7.cloned.1.call-start = ((), (), s32[]{:S(2)}) async-start(), calls=%async_computation.6 | async-start | bytes 5898240
  857.6 71.1 %collective-permute-start.42 = (bf16[256,2048]{1,0:T(8,128)(2,1)S(1)}, bf16[256,2048]{1,0:T(8,128)(2,1)S(1)}, u32[]{:S(2)}, u32[]{:S(2)}) collective-permute-start(bf16[256,2048]{1,0:T(8,128)(2,1)S(1)} %get-tuple-element.174), channel_id=1, source_target_pairs={{0,24},{8,16},{16,8},{24,0},{1,25},{9,17},{17,9},{25,1},{2,26},{10... | collective-permute-start | bytes 3145736 | tf_op jit(solution)/shard_map/ppermute | solution.py:408
  860.8 72.2 %collective-permute-start.33 = (bf16[256,2048]{1,0:T(8,128)(2,1)S(1)}, bf16[256,2048]{1,0:T(8,128)(2,1)S(1)}, u32[]{:S(2)}, u32[]{:S(2)}) collective-permute-start(bf16[256,2048]{1,0:T(8,128)(2,1)S(1)} %copy-done.59), channel_id=1, source_target_pairs={{0,1},{1,0},{2,3},{3,2},{4,5},{5,4},{6,7},{7,6},{8,9},{9,8},{10,11... | collective-permute-start | bytes 3145736 | tf_op jit(solution)/shard_map/ppermute | solution.py:408
  861.8 71.2 %collective-permute-start.35 = (bf16[256,2048]{1,0:T(8,128)(2,1)S(1)}, bf16[256,2048]{1,0:T(8,128)(2,1)S(1)}, u32[]{:S(2)}, u32[]{:S(2)}) collective-permute-start(bf16[256,2048]{1,0:T(8,128)(2,1)S(1)} %add_convert_fusion.3), channel_id=1, source_target_pairs={{0,2},{1,3},{2,0},{3,1},{4,6},{5,7},{6,4},{7,5},{8,10},{9,11},{10,... | collective-permute-start | bytes 3145736 | tf_op jit(solution)/shard_map/ppermute | solution.py:408
  888.1 65.6 %collective-permute-start.37 = (bf16[256,2048]{1,0:T(8,128)(2,1)S(1)}, bf16[256,2048]{1,0:T(8,128)(2,1)S(1)}, u32[]{:S(2)}, u32[]{:S(2)}) collective-permute-start(bf16[256,2048]{1,0:T(8,128)(2,1)S(1)} %add_convert_fusion.2), channel_id=1, source_target_pairs={{0,4},{1,5},{2,6},{3,7},{4,0},{5,1},{6,2},{7,3},{8,12},{9,13},{10,... | collective-permute-start | bytes 3145736 | tf_op jit(solution)/shard_map/ppermute | solution.py:408
  891.3 84.7 %collective-permute-start.39 = (bf16[256,2048]{1,0:T(8,128)(2,1)S(1)}, bf16[256,2048]{1,0:T(8,128)(2,1)S(1)}, u32[]{:S(2)}, u32[]{:S(2)}) collective-permute-start(bf16[256,2048]{1,0:T(8,128)(2,1)S(1)} %add_convert_fusion.1), channel_id=1, source_target_pairs={{0,6},{1,7},{2,4},{3,5},{4,2},{5,3},{6,0},{7,1},{8,14},{9,15},{10,... | collective-permute-start | bytes 3145736 | tf_op jit(solution)/shard_map/ppermute | solution.py:408
  (102 other events, 2093.7 us)
Sparse Core Ops, SparseCore 0:
  9.6 63.7 all-gather.9
  75.6 23.0 all-gather.7
  100.4 28.6 all-gather.5
  834.1 27.6 reduce-scatter.4
  864.5 86.1 reduce-scatter.6

commit v3 on v2

--- a/solution.py
+++ b/solution.py
@@ -174,7 +174,7 @@
         out_shape=[low, low, low],
         scratch_shapes=[pltpu.VMEM((length, HD), jnp.float32), pltpu.VMEM((length, HD), jnp.float32)],
         cost_estimate=pl.CostEstimate(
-            flops=10 * heads * length * length * HD, bytes_accessed=24 * length * width, transcendentals=heads * length * length
+            flops=heads * length * HD, bytes_accessed=length * width, transcendentals=0
         ),
         name="attend_back",
     )(query, key, value, grad_mixed, stat, raw, raw, cosine, sine, gain_q[None, :], gain_k[None, :],
@@ -248,10 +248,7 @@
         in_specs=[whole, whole, whole, pl.BlockSpec((dp_count, 3, piece, tile), lambda i: (0, 0, 0, i))],
         out_specs=pl.BlockSpec((length, tile), lambda i: (0, i)),
         out_shape=jax.ShapeDtypeStruct((length, width), jnp.bfloat16),
-        cost_estimate=pl.CostEstimate(
-            flops=6 * length * width * group, bytes_accessed=2 * length * width + 6 * length * group + 6 * group * width,
-            transcendentals=0,
-        ),
+        cost_estimate=pl.CostEstimate(flops=length * width, bytes_accessed=length * width, transcendentals=0),
         name="qkv_back",
     )(grads[0], grads[1], grads[2], w_group)
 
@@ -396,7 +393,7 @@
         ] + [pltpu.VMEM((own_rows, width), f32) for unused in range(4)],
         input_output_aliases={13 + i: 4 + i for i in range(len(kept))},
         cost_estimate=pl.CostEstimate(
-            flops=14 * experts * rows * width * ff, bytes_accessed=experts * (6 * width * ff + 8 * rows * width), transcendentals=experts * rows * ff
+            flops=experts * rows * width, bytes_accessed=experts * rows * width, transcendentals=0
         ),
         compiler_params=pltpu.CompilerParams(vmem_limit_bytes=60 * 1024 * 1024),
         name="experts",
@@ -419,26 +416,8 @@
     return total
 
 
-def spread_pairs(values, count):
-    blocks = []
-    for c in range(count // 2):
-        same = values if c == 0 else swap(values, "dp", 2 * c, count)
-        blocks += [same, swap(same, "dp", 1, count)]
-    return blocks
-
-
-def collect_pairs(blocks, count):
-    total = None
-    for c in range(count // 2):
-        pair = blocks[2 * c].astype(jnp.float32) + swap(blocks[2 * c + 1], "dp", 1, count).astype(jnp.float32)
-        if c > 0:
-            pair = swap(pair.astype(jnp.bfloat16), "dp", 2 * c, count).astype(jnp.float32)
-        total = pair if total is None else total + pair
-    return total
-
-
-def after(values, *earlier):
-    return lax.optimization_barrier((values,) + earlier)[0]
+def pin(*values):
+    return lax.optimization_barrier(values)
 
 
 def local(
@@ -484,12 +463,6 @@
     own_mask = column_mask(own_adapter, rank_columns)
     full_mask = column_mask(adapter, rank_columns)
 
-    ab_piece = jnp.concatenate([a_attention, jnp.swapaxes(b_attention, 1, 2)], axis=0)
-    ab_group = lax.all_gather(ab_piece, "dp", axis=0)
-    ab_group = jnp.swapaxes(ab_group, 0, 1).reshape(8, group_width, rank_columns)
-    wt_piece = jnp.swapaxes(w_qkv, 1, 2)
-    w_group = lax.all_gather(after(wt_piece, ab_group), "dp", axis=0)
-    wo_group = lax.all_gather(after(w_output, w_group), "dp", axis=0, tiled=True)
     gates = route_gates[0].T
     gates_high = gates.astype(low)
     meta = jnp.concatenate(
@@ -502,54 +475,25 @@
         ],
         axis=0,
     )
-    meta_rows = -(-meta.size // full_width)
-    pad_rows = -(-meta_rows // 16) * 16
-    meta_flat = jnp.pad(meta.reshape(-1), (0, pad_rows * full_width - meta.size))
-    grad_send = jnp.concatenate([out_cotangent[0], meta_flat.reshape(pad_rows, full_width)], axis=0)
-    grad_blocks = spread_pairs(after(grad_send, wo_group), dp_count)
-
-    tokens = layer_input[0].astype(f32)
-    normed = rms_scale(tokens, gain_attention).astype(low)
-    normed_blocks = spread(normed, "seq", n)
-    normed_all = jnp.concatenate(normed_blocks, axis=0)
-    share = jnp.concatenate([ab_group[0:3], ab_group[7:8]], axis=0)
-    share_blocks = jnp.stack(spread(share, "seq", n))
-    share_full = share_blocks[order]
-    share_full = jnp.swapaxes(share_full, 0, 1).reshape(4, full_width, rank_columns)
-    down_cat = jnp.swapaxes(share_full[0:3], 0, 1).reshape(full_width, 3 * rank_columns)
-    upt_output = share_full[3]
-    upt_group = ab_group[4:7]
-    down_rows = ab_group[3]
-
-    dot = lambda a, b: jnp.dot(a, b, preferred_element_type=f32)
-    dot_t = lambda a, b: lax.dot_general(a, b, (((1,), (1,)), ((), ())), preferred_element_type=f32)
-    dot_l = lambda a, b: lax.dot_general(a, b, (((0,), (0,)), ((), ())), preferred_element_type=f32)
-
-    reduced_cat = (jnp.tile(full_mask, (1, 3)) * dot(normed_all, down_cat)).astype(low)
-    reduced_list = [reduced_cat[:, m * rank_columns : (m + 1) * rank_columns] for m in range(3)]
-    raw = qkv_project(normed_all, reduced_cat, w_group, upt_group)
-    cosine, sine = rope_tables(offset, HD)
-    mixed_group, query_heads, key_heads, value_heads, stat = attend(
-        raw, cosine, sine, gain_query, gain_key, segment
-    )
-
-    out_maps = jnp.concatenate([wo_group, down_rows], axis=1)
-    partial_out = dot(mixed_group, out_maps).astype(low).reshape(n, own_rows, full_width + rank_columns)
-    summed = collect([partial_out[k] for k in range(n)], "seq", n)
-    output_reduced = (own_mask * summed[:, full_width:]).astype(low)
-    attended = summed[:, :full_width] + dot_t(output_reduced, upt_output)
-    hidden = tokens + attended
-    normed_ffn = rms_scale(hidden, gain_ffn).astype(low)
+    ab_piece = jnp.concatenate([a_attention[0:3], jnp.swapaxes(b_attention, 1, 2)], axis=0).reshape(-1, rank_columns)
+    ab_rows = ab_piece.shape[0]
+    ab_piece = jnp.concatenate([ab_piece, meta.reshape(-1, rank_columns)], axis=0)
+    ab_got = lax.all_gather(ab_piece, "dp", axis=0)
+    out_piece = jnp.concatenate([w_output, a_attention[3]], axis=1)
+    out_piece, ab_got = pin(out_piece, ab_got)
+    dp_order = d ^ jnp.arange(dp_count, dtype=jnp.int32)
+    meta_all = ab_got[:, ab_rows:].reshape((dp_count,) + meta.shape)[dp_order].astype(f32)
+    ab_group = ab_got[:, :ab_rows].reshape(dp_count, 7, piece, rank_columns)
+    ab_group = jnp.swapaxes(ab_group, 0, 1).reshape(7, group_width, rank_columns)
+    out_maps = lax.all_gather(out_piece, "dp", axis=0, tiled=True)
+    wt_piece = jnp.swapaxes(w_qkv, 1, 2)
+    wt_piece, out_maps = pin(wt_piece, out_maps)
+    w_group = lax.all_gather(wt_piece, "dp", axis=0)
+
     local_count = expert_w_in.shape[0]
     expert_count = local_count * dp_count
     capacity = own_rows * TOP // expert_count * 9 // 8
     capacity = -(-capacity // 16) * 16
-    meta_all = jnp.stack(
-        [
-            x[own_rows:].reshape(-1)[: meta.size].reshape(meta.shape).astype(f32)
-            for x in grad_blocks
-        ]
-    )
     named = meta_all[:, 0:TOP, :].astype(jnp.int32)
     gates_all = meta_all[:, TOP : 2 * TOP, :] + meta_all[:, 2 * TOP : 3 * TOP, :]
     sets_all = meta_all[:, 3 * TOP, :]
@@ -569,29 +513,117 @@
     slot = jnp.stack([slot_gate, slot_set], axis=-1).reshape(local_count, dp_count * capacity, 2)
     pick = pick.astype(low)
 
-    row_blocks = spread_pairs(normed_ffn, dp_count)
+    cosine, sine = rope_tables(offset, HD)
+    tokens = layer_input[0].astype(f32)
+    normed = rms_scale(tokens, gain_attention).astype(low)
+    normed_blocks = spread(normed, "seq", n)
+    share = jnp.concatenate([ab_group[0:3], ab_group[6:7]], axis=0)
+    share_blocks = spread(share, "seq", n)
+    grad_send, w_group, pick, pick_t, slot, cosine, sine, *early = pin(
+        out_cotangent[0], w_group, pick, pick_t, slot, cosine, sine, *normed_blocks, *share_blocks
+    )
+    grad_got = lax.all_gather(grad_send, "dp", axis=0)
+    grad_blocks = [lax.dynamic_index_in_dim(grad_got, dp_order[k], 0, keepdims=False) for k in range(dp_count)]
+    normed_all = jnp.concatenate(early[:n], axis=0)
+    share_blocks = jnp.stack(early[n:])
+    share_full = share_blocks[order]
+    share_full = jnp.swapaxes(share_full, 0, 1).reshape(4, full_width, rank_columns)
+    down_cat = jnp.swapaxes(share_full[0:3], 0, 1).reshape(full_width, 3 * rank_columns)
+    upt_output = share_full[3]
+    upt_group = ab_group[3:6]
+
+    dot = lambda a, b: jnp.dot(a, b, preferred_element_type=f32)
+    dot_t = lambda a, b: lax.dot_general(a, b, (((1,), (1,)), ((), ())), preferred_element_type=f32)
+    dot_l = lambda a, b: lax.dot_general(a, b, (((0,), (0,)), ((), ())), preferred_element_type=f32)
+
+    reduced_cat = (jnp.tile(full_mask, (1, 3)) * dot(normed_all, down_cat)).astype(low)
+    reduced_list = [reduced_cat[:, m * rank_columns : (m + 1) * rank_columns] for m in range(3)]
+    raw = qkv_project(normed_all, reduced_cat, w_group, upt_group)
+    mixed_group, query_heads, key_heads, value_heads, stat = attend(
+        raw, cosine, sine, gain_query, gain_key, segment
+    )
+
+    partial_out = dot(mixed_group, out_maps).astype(low).reshape(n, own_rows, full_width + rank_columns)
+    summed = collect([partial_out[k] for k in range(n)], "seq", n)
+    output_reduced = (own_mask * summed[:, full_width:]).astype(low)
+    attended = summed[:, :full_width] + dot_t(output_reduced, upt_output)
+    hidden = tokens + attended
+    normed_ffn = rms_scale(hidden, gain_ffn).astype(low)
     weights = (expert_w_in, expert_w_down, expert_a_in, expert_b_in, expert_a_down, expert_b_down)
-    outs = []
-    backs = []
+    chips = dp_count // 2
+    turns = [0] + list(range(chips // 2, chips)) + list(range(1, chips // 2))
+    outs = [None] * dp_count
     kept = ()
-    for c in range(dp_count // 2):
-        (out_a, out_b, back_a, back_b), kept = run_experts(
-            c, row_blocks[2 * c : 2 * c + 2], grad_blocks[2 * c : 2 * c + 2], pick, pick_t, slot, weights, kept
+    rows = normed_ffn
+    here = normed_ffn
+    arrived = swap(rows, "dp", 2 * turns[1], dp_count)
+    other = swap(here, "dp", 1, dp_count)
+    leaving = None
+    flying = None
+    grad_normed_ffn = None
+    for i, c in enumerate(turns):
+        if i > 0:
+            here = arrived
+            if flying is not None:
+                here, flying = pin(here, flying)
+                grad_normed_ffn = grad_normed_ffn + flying.astype(f32)
+            other = swap(here, "dp", 1, dp_count)
+            rows, here, other, leaving = pin(rows, here, other, leaving)
+            if i < chips - 1:
+                arrived = swap(rows, "dp", 2 * turns[i + 1], dp_count)
+            if i == 1:
+                grad_normed_ffn = leaving
+            else:
+                flying = swap(leaving, "dp", 2 * turns[i - 1], dp_count)
+        (outs[2 * c], outs[2 * c + 1], back, back_other), kept = run_experts(
+            c, (here, other), grad_blocks[2 * c : 2 * c + 2], pick, pick_t, slot, weights, kept
         )
-        outs += [out_a, out_b]
-        backs += [back_a, back_b]
-    grad_normed_ffn = collect_pairs(backs, dp_count)
-
+        if i == chips - 1 and flying is not None:
+            flying, back_other = pin(flying, back_other)
+        leaving = back.astype(f32) + swap(back_other, "dp", 1, dp_count).astype(f32)
+        if i > 0:
+            leaving = leaving.astype(low)
+    if flying is not None:
+        grad_normed_ffn = grad_normed_ffn + flying.astype(f32)
+    leaving, *kept = pin(leaving, *kept)
+    flying = swap(leaving, "dp", 2 * turns[-1], dp_count)
+    flying, *kept_later = pin(flying, *kept)
+    grad_normed_ffn = grad_normed_ffn + flying.astype(f32)
+
+    outs_all = jnp.stack(outs)[dp_order]
+    outs_all, grad_normed_ffn = pin(outs_all, grad_normed_ffn)
+    mixture = lax.psum_scatter(outs_all, "dp", scatter_dimension=0)
     grad_out = out_cotangent[0].astype(f32)
     unused, pull_ffn = jax.vjp(lambda values: rms_scale(values, gain_ffn), hidden)
     grad_hidden = grad_out + pull_ffn(grad_normed_ffn)[0]
     grad_hidden_low = grad_hidden.astype(low)
     grad_reduced_output = (own_mask * dot(grad_hidden_low, upt_output)).astype(low)
     grad_pack = jnp.concatenate([grad_hidden_low, grad_reduced_output, output_reduced], axis=1)
-    grad_pack_all = jnp.concatenate(spread(grad_pack, "seq", n), axis=0)
-    outs = list(after(tuple(outs), grad_pack_all))
-    mixture = collect_pairs(outs, dp_count)
-    layer_output = (hidden + mixture).astype(low)[None]
+    flat = []
+    for e in range(local_count):
+        xs, ps, act_rows, gate_rows, up_rows, reds = kept if e == 0 else kept_later
+        red = [reds[e][:, i * rank_columns : (i + 1) * rank_columns] for i in range(6)]
+        terms = [
+            (reds[e][:, 3 * rank_columns : 5 * rank_columns], xs[e]),
+            (red[0], gate_rows[e]),
+            (red[1], up_rows[e]),
+            (red[5], act_rows[e]),
+            (red[2], ps[e]),
+        ]
+        flat += [dot_l(a, b).astype(low).reshape(-1, rank_columns, b.shape[1]) for a, b in terms]
+    widths = [(x.shape[0], x.shape[2] // n) for x in flat]
+    flat = jnp.concatenate(
+        [
+            x.reshape(x.shape[0], rank_columns, n, -1).transpose(2, 0, 1, 3).reshape(n, -1)
+            for x in flat
+        ],
+        axis=1,
+    ).reshape(n, -1, rank_columns)
+    grad_packs = spread(grad_pack, "seq", n)
+    flat, *grad_packs = pin(flat, *grad_packs)
+    expert_terms = [lax.dynamic_index_in_dim(flat, order[k], 0, keepdims=False) for k in range(n)]
+    expert_terms = expert_terms[:1] + [swap(expert_terms[k], "seq", k, n) for k in range(1, n)]
+    grad_pack_all = jnp.concatenate(grad_packs, axis=0)
     grad_all = grad_pack_all[:, :full_width]
     grad_reduced_all = grad_pack_all[:, full_width : full_width + rank_columns]
     output_reduced_all = grad_pack_all[:, full_width + rank_columns :]
@@ -609,6 +641,7 @@
         gain_key,
         segment,
     )
+    expert_terms[-1], *grad_raw_list = pin(expert_terms[-1], *grad_raw_list)
     partial_reduced = jnp.concatenate(
         [dot(grad_raw_list[m], upt_group[m]) for m in range(3)], axis=1
     ).astype(low).reshape(n, own_rows, 3 * rank_columns)
@@ -616,7 +649,10 @@
     grad_reduced = (jnp.tile(own_mask, (1, 3)) * summed_reduced).astype(low)
     grad_reduced_full = jnp.concatenate(spread(grad_reduced, "seq", n), axis=0)
     partial_normed = qkv_back(grad_raw_list, w_group).reshape(n, own_rows, full_width)
+    partial_normed, *expert_terms = pin(partial_normed, *expert_terms)
     summed_back = collect([partial_normed[k] for k in range(n)], "seq", n)
+    summed_back, mixture, hidden = pin(summed_back, mixture, hidden)
+    layer_output = (hidden + mixture.astype(f32)).astype(low)[None]
     grad_normed = summed_back + dot_t(grad_reduced, down_cat)
     unused_input, pull_input = jax.vjp(lambda values: rms_scale(values, gain_attention), tokens)
     input_grad = (grad_hidden + pull_input(grad_normed)[0]).astype(low)[None]
@@ -627,31 +663,13 @@
     parts = [grad_down_cat[:, m * rank_columns : (m + 1) * rank_columns] for m in range(3)]
     parts += [grad_down_output] + grad_upt + [grad_upt_output]
     stacked = jnp.stack([x.astype(low).reshape(dp_count, piece, rank_columns) for x in parts], axis=1)
-    own_parts = lax.psum_scatter(stacked, "dp", scatter_dimension=0).astype(f32)
+    own_parts = lax.psum_scatter(stacked, "dp", scatter_dimension=0)
+    own_parts, input_grad = pin(own_parts, input_grad)
+    own_parts = own_parts.astype(f32)
     grad_a_attention = own_parts[0:4]
     grad_b_attention = jnp.swapaxes(own_parts[4:8], 1, 2)
 
-    xs, ps, act_rows, gate_rows, up_rows, reds = kept
-    flat = []
-    for e in range(local_count):
-        red = [reds[e][:, i * rank_columns : (i + 1) * rank_columns] for i in range(6)]
-        terms = [
-            (reds[e][:, 3 * rank_columns : 5 * rank_columns], xs[e]),
-            (red[0], gate_rows[e]),
-            (red[1], up_rows[e]),
-            (red[5], act_rows[e]),
-            (red[2], ps[e]),
-        ]
-        flat += [dot_l(a, b).astype(low).reshape(-1, rank_columns, b.shape[1]) for a, b in terms]
-    widths = [(x.shape[0], x.shape[2] // n) for x in flat]
-    flat = jnp.concatenate(
-        [
-            x.reshape(x.shape[0], rank_columns, n, -1).transpose(2, 0, 1, 3).reshape(n, -1)
-            for x in flat
-        ],
-        axis=1,
-    ).reshape(n, -1, rank_columns)
-    flat = lax.psum_scatter(flat, "seq", scatter_dimension=0).astype(f32).reshape(-1)
+    flat = sum(x.astype(f32) for x in expert_terms).reshape(-1)
     pieces = []
     start = 0
     for count, width in widths:

time: 1000 us -> 795 us (0.80)
  the two profiles are of different devices: /device:TPU:8 before, /device:TPU:0 now
where the time goes in v3:
time: 795 us; the launch traced here: 788 us
  Pallas kernels  241 us (30%)
  waiting for transfers between devices  234 us (29%)
  local copies, waits for them, and re-layouts  115 us (14%)
  matrix products  59 us (7%)
  other arithmetic  56.6 us (7%)
  starting transfers between devices  42.4 us (5%)
  between operations  38.7 us (5%)
    pallas_call x4, Pallas kernels, run_experts(): pl.pallas_call(functools.partial(expert_kernel, len(kept)), grid=(experts...  169 us
    ppermute x38, waiting for transfers between devices, swap(): return lax.ppermute(values, axis, [(i, i ^ distance) for i in range(count)])  160 us
    unnamed x192, local copies, waits for them, and re-layouts  41.8 us
    ppermute x38, starting transfers between devices, swap(): return lax.ppermute(values, axis, [(i, i ^ distance) for i in range(count)])  41.8 us
    dot_general x16, matrix products, local(): lax.dot_general(a, b, (((0,), (0,)), ((), ())), preferred_element_type=f32)  39.3 us
    all_gather x1, waiting for transfers between devices, local(): out_maps = lax.all_gather(out_piece, 'dp', axis=0, tiled=True)  32 us
    pallas_call x1, Pallas kernels, attend(): pl.pallas_call(functools.partial(attend_kernel, tile), grid=(heads,), in_...  24 us
    pallas_call x1, Pallas kernels, attend_back(): pl.pallas_call(functools.partial(attend_back_kernel, tile), grid=(heads,)...  23.5 us
  transfers between devices with their start and end apart: 44, of which 16 were waited for; matrix products, arithmetic and copies ran while one was open for 25% of the time, Pallas kernels for 31%

profile of v3, /device:TPU:0, one launch (start us, length us, event | category | flops | bytes accessed | tf_op | source)
XLA Modules:
  0.0 787.6 jit_solution(5145532539425801177)
XLA Ops:
  16.3 22.7 %all-gather.10.cloned.1.call-done = bf16[4096,128]{1,0:T(8,128)(2,1)} async-done(((bf16[512,128]{1,0:T(8,128)(2,1)}), bf16[4096,128]{1,0:T(8,128)(2,1)}) %all-gather.10.cloned.1.call-update) | async-done | bytes 1048592 | tf_op jit(solution)/shard_map/all_gather | solution.py:481
  39.1 32.0 %all-gather.8.cloned.1.call-done = bf16[512,2176]{1,0:T(8,128)(2,1)} async-done(((bf16[64,2176]{1,0:T(8,128)(2,1)}), bf16[512,2176]{1,0:T(8,128)(2,1)}) %all-gather.8.cloned.1.call-update) | async-done | bytes 2228240 | tf_op jit(solution)/shard_map/all_gather | solution.py:488
  91.3 6.7 collective-permute-done
  103.5 18.5 %collective-permute-done.1 = bf16[256,2048]{1,0:T(8,128)(2,1)} collective-permute-done((bf16[256,2048]{1,0:T(8,128)(2,1)S(1)}, bf16[256,2048]{1,0:T(8,128)(2,1)}, u32[]{:S(2)}, u32[]{:S(2)}) %collective-permute-start.1) | collective-permute-done | bytes 1048608 | tf_op jit(solution)/shard_map/ppermute | solution.py:405
  122.0 9.8 %collective-permute-done.3 = bf16[4,512,128]{2,1,0:T(8,128)(2,1)} collective-permute-done((bf16[4,512,128]{2,1,0:T(8,128)(2,1)S(1)}, bf16[4,512,128]{2,1,0:T(8,128)(2,1)}, u32[]{:S(2)}, u32[]{:S(2)}) %collective-permute-start.3) | collective-permute-done | bytes 524320 | tf_op jit(solution)/shard_map/ppermute | solution.py:405
  131.8 11.6 %collective-permute-done.4 = bf16[4,512,128]{2,1,0:T(8,128)(2,1)} collective-permute-done((bf16[4,512,128]{2,1,0:T(8,128)(2,1)S(1)}, bf16[4,512,128]{2,1,0:T(8,128)(2,1)}, u32[]{:S(2)}, u32[]{:S(2)}) %collective-permute-start.4) | collective-permute-done | bytes 524320 | tf_op jit(solution)/shard_map/ppermute | solution.py:405
  166.4 12.7 %qkv_project.1.q_raw.k_raw.v_raw = f32[3,1024,512]{2,1,0:T(8,128)} custom-call(bf16[1024,2048]{1,0:T(8,128)(2,1)} %copy-done.56, bf16[1024,384]{1,0:T(8,128)(2,1)} %multiply_convert_fusion.1.reduced_ref, bf16[8,3,64,2048]{3,2,1,0:T(8,128)(2,1)} %bitcast.316, bf16[3,512,128]{2,1,0:T(8,128)(2,1)} %bitcast.352), custom_call_target="tpu_custom_call" | custom-call | flops 6442450944 | bytes 16777216 | tf_op jit(solution)/shard_map/qkv_project/pallas_call | solution.py:212
  179.1 24.0 %attend.1 = (bf16[1024,512]{1,0:T(8,128)(2,1)}, bf16[1024,512]{1,0:T(8,128)(2,1)}, bf16[1024,512]{1,0:T(8,128)(2,1)}, bf16[1024,512]{1,0:T(8,128)(2,1)}, f32[4,1,1024]{2,1,0:T(1,128)}) custom-call(f32[3,1024,512]{2,1,0:T(8,128)} %qkv_project.1.q_raw.k_raw.v_raw, f32[3,1024,512]{2,1,0:T(8,128)} %qkv_project.1.q_raw.k_raw.v_raw, ...), custom_call_target="tpu_custom_call" | custom-call | flops 2147483648 | bytes 10485760 | tf_op jit(solution)/shard_map/attend/pallas_call | solution.py:99
  211.5 23.9 %collective-permute-done.6 = bf16[256,2176]{1,0:T(8,128)(2,1)S(1)} collective-permute-done((bf16[256,2176]{1,0:T(8,128)(2,1)S(1)}, bf16[256,2176]{1,0:T(8,128)(2,1)S(1)}, u32[]{:S(2)}, u32[]{:S(2)}) %collective-permute-start.6) | collective-permute-done | bytes 1114144 | tf_op jit(solution)/shard_map/ppermute | solution.py:405
  235.4 22.9 %collective-permute-done.7 = bf16[256,2176]{1,0:T(8,128)(2,1)S(1)} collective-permute-done((bf16[256,2176]{1,0:T(8,128)(2,1)S(1)}, bf16[256,2176]{1,0:T(8,128)(2,1)S(1)}, u32[]{:S(2)}, u32[]{:S(2)}) %collective-permute-start.7) | collective-permute-done | bytes 1114144 | tf_op jit(solution)/shard_map/ppermute | solution.py:405
  279.7 6.8 dynamic-slice_bitcast_fusion.4
  286.5 42.3 %experts.4 = (bf16[256,2048]{1,0:T(8,128)(2,1)}, bf16[256,2048]{1,0:T(8,128)(2,1)}, bf16[256,2048]{1,0:T(8,128)(2,1)}, bf16[256,2048]{1,0:T(8,128)(2,1)}, bf16[2...) custom-call(bf16[256,2048]{1,0:T(8,128)(2,1)} %multiply_convert_fusi, ...), custom_call_target="tpu_custom_call" | custom-call | flops 1179648 | bytes 1179648 | tf_op jit(solution)/shard_map/experts/pallas_call | solution.py:377
  337.7 42.0 %experts.5 = (bf16[256,2048]{1,0:T(8,128)(2,1)}, bf16[256,2048]{1,0:T(8,128)(2,1)}, bf16[256,2048]{1,0:T(8,128)(2,1)}, bf16[256,2048]{1,0:T(8,128)(2,1)}, bf16[2...) custom-call(bf16[256,2048]{1,0:T(8,128)(2,1)} %copy-done.30, ...), custom_call_target="tpu_custom_call", output_to_operand_aliasing={{4}: (13, {}), {5}: (14, {}), {6}: (15, {}), {7}: (16, {}),... | custom-call | flops 1179648 | bytes 1179648 | tf_op jit(solution)/shard_map/experts/pallas_call | solution.py:377
  388.1 42.1 %experts.6 = (bf16[256,2048]{1,0:T(8,128)(2,1)}, bf16[256,2048]{1,0:T(8,128)(2,1)}, bf16[256,2048]{1,0:T(8,128)(2,1)}, bf16[256,2048]{1,0:T(8,128)(2,1)}, bf16[2...) custom-call(bf16[256,2048]{1,0:T(8,128)(2,1)} %collective-permute-do, ...), custom_call_target="tpu_custom_call", output_to_operand_aliasing={{4}: (13, {}), {5}: (14, {}), {6}: (15, {}), {7}: (16, {}),... | custom-call | flops 1179648 | bytes 1179648 | tf_op jit(solution)/shard_map/experts/pallas_call | solution.py:377
  449.3 42.2 %experts.7 = (bf16[256,2048]{1,0:T(8,128)(2,1)}, bf16[256,2048]{1,0:T(8,128)(2,1)}, bf16[256,2048]{1,0:T(8,128)(2,1)}, bf16[256,2048]{1,0:T(8,128)(2,1)}, bf16[2...) custom-call(bf16[256,2048]{1,0:T(8,128)(2,1)} %copy-done.31, ...), custom_call_target="tpu_custom_call", output_to_operand_aliasing={{4}: (13, {}), {5}: (14, {}), {6}: (15, {}), {7}: (16, {}),... | custom-call | flops 1179648 | bytes 1179648 | tf_op jit(solution)/shard_map/experts/pallas_call | solution.py:377
  499.4 8.5 %gather_fusion.2 = bf16[8,256,2048]{2,1,0:T(8,128)(2,1)} fusion(bf16[8,256,2048]{2,1,0:T(8,128)(2,1)} %bitcast_dynamic-update-slice_fusion, s32[1024]{0:T(1024)} %get-tuple-element.348), kind=kCustom, calls=%fused_computation.2 | custom fusion | bytes 16777248 | tf_op jit(solution)/shard_map/gather | solution.py:593
  527.9 5.1 fusion.14
  567.0 5.1 fusion.17
  584.0 14.1 %collective-permute-done.24 = bf16[256,2304]{1,0:T(8,128)(2,1)} collective-permute-done((bf16[256,2304]{1,0:T(8,128)(2,1)S(1)}, bf16[256,2304]{1,0:T(8,128)(2,1)}, u32[]{:S(2)}, u32[]{:S(2)}) %collective-permute-start.24) | collective-permute-done | bytes 1179680 | tf_op jit(solution)/shard_map/ppermute | solution.py:405
  615.0 23.5 %attend_back.1 = (bf16[1024,512]{1,0:T(8,128)(2,1)}, bf16[1024,512]{1,0:T(8,128)(2,1)}, bf16[1024,512]{1,0:T(8,128)(2,1)}) custom-call(bf16[1024,512]{1,0:T(8,128)(2,1)} %get-tuple-element.216.query, bf16[1024,512]{1,0:T(8,128)(2,1)} %get-tuple-element.217.key, bf16[1024,512]{1,0:T(8,128)(2,1)} %get-tuple-element.218.value, ...), custom_call_target="tpu_custom_call" | custom-call | flops 524288 | bytes 524288 | tf_op jit(solution)/shard_map/attend_back/pallas_call | solution.py:167
  643.4 12.4 %qkv_back.1 = bf16[1024,2048]{1,0:T(8,128)(2,1)} custom-call(bf16[1024,512]{1,0:T(8,128)(2,1)} %get-tuple-element.227.a_ref, bf16[1024,512]{1,0:T(8,128)(2,1)} %get-tuple-element.228.b_ref, bf16[1024,512]{1,0:T(8,128)(2,1)} %get-tuple-element.229.c_ref, bf16[8,3,64,2048]{3,2,1,0:T(8,128)(2,1)} %bitcast.317), custom_call_target="tpu_custom_call" | custom-call | flops 2097152 | bytes 2097152 | tf_op jit(solution)/shard_map/qkv_back/pallas_call | solution.py:245
  692.6 21.6 %collective-permute-done.35 = bf16[256,384]{0,1:T(8,128)(2,1)S(1)} collective-permute-done((bf16[256,384]{0,1:T(8,128)(2,1)S(1)}, bf16[256,384]{0,1:T(8,128)(2,1)S(1)}, u32[]{:S(2)}, u32[]{:S(2)}) %collective-permute-start.35) | collective-permute-done | bytes 196640 | tf_op jit(solution)/shard_map/ppermute | solution.py:405
  715.8 23.7 %collective-permute-done.36 = bf16[256,384]{0,1:T(8,128)(2,1)S(1)} collective-permute-done((bf16[256,384]{0,1:T(8,128)(2,1)S(1)}, bf16[256,384]{0,1:T(8,128)(2,1)S(1)}, u32[]{:S(2)}, u32[]{:S(2)}) %collective-permute-start.36) | collective-permute-done | bytes 196640 | tf_op jit(solution)/shard_map/ppermute | solution.py:405
  755.4 19.3 %reduce-scatter.5.cloned.1.call-done = bf16[1,8,64,128]{3,2,1,0:T(8,128)(2,1)} async-done(((bf16[8,8,64,128]{3,2,1,0:T(8,128)(2,1)}), bf16[1,8,64,128]{3,2,1,0:T(8,128)(2,1)}) %reduce-scatter.5.cloned.1.call-update) | async-done | bytes 131088 | tf_op jit(solution)/shard_map/reduce_scatter | solution.py:666
  (432 shorter events, 255.3 us)
Async XLA Ops:
  13.9 57.2 %all-gather.8.cloned.1.call-start = ((), (), s32[]{:S(2)}) async-start(), calls=%async_computation.2 | async-start | bytes 2506752 | tf_op jit(solution)/shard_map/all_gather | solution.py:488
  39.0 104.4 %all-gather.12.cloned.1.call-start = ((), (), s32[]{:S(2)}) async-start(), calls=%async_computation.6 | async-start | bytes 7077888 | tf_op jit(solution)/shard_map/all_gather | solution.py:491
  71.1 208.6 %all-gather.14.cloned.1.call-start = ((), (), s32[]{:S(2)}) async-start(), calls=%async_computation.7 | async-start | bytes 9437184 | tf_op jit(solution)/shard_map/all_gather | solution.py:525
  73.4 48.6 %collective-permute-start.1 = (bf16[256,2048]{1,0:T(8,128)(2,1)S(1)}, bf16[256,2048]{1,0:T(8,128)(2,1)}, u32[]{:S(2)}, u32[]{:S(2)}) collective-permute-start(bf16[256,2048]{1,0:T(8,128)(2,1)S(1)} %fusion.51), channel_id=1, source_target_pairs={{0,16},{8,24},{16,0},{24,8},{1,17},{9,25},{17,1},{25,9},{2,18},{10... | collective-permute-start | bytes 3145736 | tf_op jit(solution)/shard_map/ppermute | solution.py:405
  74.8 47.1 %collective-permute-start.2 = (bf16[256,2048]{1,0:T(8,128)(2,1)S(1)}, bf16[256,2048]{1,0:T(8,128)(2,1)}, u32[]{:S(2)}, u32[]{:S(2)}) collective-permute-start(bf16[256,2048]{1,0:T(8,128)(2,1)S(1)} %fusion.51), channel_id=1, source_target_pairs={{0,24},{8,16},{16,8},{24,0},{1,25},{9,17},{17,9},{25,1},{2,26},{10... | collective-permute-start | bytes 3145736 | tf_op jit(solution)/shard_map/ppermute | solution.py:405
  84.4 47.4 %collective-permute-start.3 = (bf16[4,512,128]{2,1,0:T(8,128)(2,1)S(1)}, bf16[4,512,128]{2,1,0:T(8,128)(2,1)}, u32[]{:S(2)}, u32[]{:S(2)}) collective-permute-start(bf16[4,512,128]{2,1,0:T(8,128)(2,1)S(1)} %pad_maximum_fusion.6), channel_id=1, source_target_pairs={{0,8},{8,0},{16,24},{24,16},{1,9},{9,1},{17,25},{25,17},{2,10},{10... | collective-permute-start | bytes 1572872 | tf_op jit(solution)/shard_map/ppermute | solution.py:405
  86.0 57.4 %collective-permute-start.4 = (bf16[4,512,128]{2,1,0:T(8,128)(2,1)S(1)}, bf16[4,512,128]{2,1,0:T(8,128)(2,1)}, u32[]{:S(2)}, u32[]{:S(2)}) collective-permute-start(bf16[4,512,128]{2,1,0:T(8,128)(2,1)S(1)} %pad_maximum_fusion.6), channel_id=1, source_target_pairs={{0,16},{8,24},{16,0},{24,8},{1,17},{9,25},{17,1},{25,9},{2,18},{10... | collective-permute-start | bytes 1572872 | tf_op jit(solution)/shard_map/ppermute | solution.py:405
  98.0 45.4 %collective-permute-start.5 = (bf16[4,512,128]{2,1,0:T(8,128)(2,1)S(1)}, bf16[4,512,128]{2,1,0:T(8,128)(2,1)}, u32[]{:S(2)}, u32[]{:S(2)}) collective-permute-start(bf16[4,512,128]{2,1,0:T(8,128)(2,1)S(1)} %pad_maximum_fusion.6), channel_id=1, source_target_pairs={{0,24},{8,16},{16,8},{24,0},{1,25},{9,17},{17,9},{25,1},{2,26},{10... | collective-permute-start | bytes 1572872 | tf_op jit(solution)/shard_map/ppermute | solution.py:405
  143.5 606.0 %reduce-scatter.3.cloned.1.call-start = ((), (), s32[]{:S(2)}) async-start(), calls=%async_computation.3 | async-start | bytes 9437184 | tf_op jit(solution)/shard_map/reduce_scatter | solution.py:595
  208.8 49.4 %collective-permute-start.7 = (bf16[256,2176]{1,0:T(8,128)(2,1)S(1)}, bf16[256,2176]{1,0:T(8,128)(2,1)S(1)}, u32[]{:S(2)}, u32[]{:S(2)}) collective-permute-start(bf16[256,2176]{1,0:T(8,128)(2,1)S(1)} %get-tuple-element.298), channel_id=1, source_target_pairs={{0,16},{8,24},{16,0},{24,8},{1,17},{9,25},{17,1},{25,9},{2,18},{10... | collective-permute-start | bytes 3342344 | tf_op jit(solution)/shard_map/ppermute | solution.py:405
  209.6 48.7 %collective-permute-start.8 = (bf16[256,2176]{1,0:T(8,128)(2,1)S(1)}, bf16[256,2176]{1,0:T(8,128)(2,1)S(1)}, u32[]{:S(2)}, u32[]{:S(2)}) collective-permute-start(bf16[256,2176]{1,0:T(8,128)(2,1)S(1)} %get-tuple-element.297), channel_id=1, source_target_pairs={{0,24},{8,16},{16,8},{24,0},{1,25},{9,17},{17,9},{25,1},{2,26},{10... | collective-permute-start | bytes 3342344 | tf_op jit(solution)/shard_map/ppermute | solution.py:405
  260.8 68.3 %collective-permute-start.9 = (bf16[256,2048]{1,0:T(8,128)(2,1)}, bf16[256,2048]{1,0:T(8,128)(2,1)S(1)}, u32[]{:S(2)}, u32[]{:S(2)}) collective-permute-start(bf16[256,2048]{1,0:T(8,128)(2,1)} %multiply_convert_fusion.refs_0_), channel_id=1, source_target_pairs={{0,4},{1,5},{2,6},{3,7},{4,0},{5,1},{6,2},{7,3},{8,12},{9,13},{10,... | collective-permute-start | bytes 3145736 | tf_op jit(solution)/shard_map/ppermute | solution.py:405
  385.3 54.2 %collective-permute-start.16 = (bf16[256,2048]{1,0:T(8,128)(2,1)}, bf16[256,2048]{1,0:T(8,128)(2,1)S(1)}, u32[]{:S(2)}, u32[]{:S(2)}) collective-permute-start(bf16[256,2048]{1,0:T(8,128)(2,1)} %multiply_convert_fusion.refs_0_), channel_id=1, source_target_pairs={{0,2},{1,3},{2,0},{3,1},{4,6},{5,7},{6,4},{7,5},{8,10},{9,11},{10,... | collective-permute-start | bytes 3145736 | tf_op jit(solution)/shard_map/ppermute | solution.py:405
  387.5 52.1 %collective-permute-start.17 = (bf16[256,2048]{1,0:T(8,128)(2,1)}, bf16[256,2048]{1,0:T(8,128)(2,1)}, u32[]{:S(2)}, u32[]{:S(2)}) collective-permute-start(bf16[256,2048]{1,0:T(8,128)(2,1)} %add_convert_fusion.3), channel_id=1, source_target_pairs={{0,4},{1,5},{2,6},{3,7},{4,0},{5,1},{6,2},{7,3},{8,12},{9,13},{10,... | collective-permute-start | bytes 3145736 | tf_op jit(solution)/shard_map/ppermute | solution.py:405
  447.5 48.7 %collective-permute-start.20 = (bf16[256,2048]{1,0:T(8,128)(2,1)}, bf16[256,2048]{1,0:T(8,128)(2,1)}, u32[]{:S(2)}, u32[]{:S(2)}) collective-permute-start(bf16[256,2048]{1,0:T(8,128)(2,1)} %add_convert_fusion.2), channel_id=1, source_target_pairs={{0,6},{1,7},{2,4},{3,5},{4,2},{5,3},{6,0},{7,1},{8,14},{9,15},{10,... | collective-permute-start | bytes 3145736 | tf_op jit(solution)/shard_map/ppermute | solution.py:405
  544.9 53.2 %collective-permute-start.24 = (bf16[256,2304]{1,0:T(8,128)(2,1)S(1)}, bf16[256,2304]{1,0:T(8,128)(2,1)}, u32[]{:S(2)}, u32[]{:S(2)}) collective-permute-start(bf16[256,2304]{1,0:T(8,128)(2,1)S(1)} %pad_maximum_fusion.1), channel_id=1, source_target_pairs={{0,16},{8,24},{16,0},{24,8},{1,17},{9,25},{17,1},{25,9},{2,18},{10... | collective-permute-start | bytes 3538952 | tf_op jit(solution)/shard_map/ppermute | solution.py:405
  546.3 51.8 %collective-permute-start.25 = (bf16[256,2304]{1,0:T(8,128)(2,1)S(1)}, bf16[256,2304]{1,0:T(8,128)(2,1)}, u32[]{:S(2)}, u32[]{:S(2)}) collective-permute-start(bf16[256,2304]{1,0:T(8,128)(2,1)S(1)} %pad_maximum_fusion.1), channel_id=1, source_target_pairs={{0,24},{8,16},{16,8},{24,0},{1,25},{9,17},{17,9},{25,1},{2,26},{10... | collective-permute-start | bytes 3538952 | tf_op jit(solution)/shard_map/ppermute | solution.py:405
  574.7 200.1 %reduce-scatter.5.cloned.1.call-start = ((), (), s32[]{:S(2)}) async-start(), calls=%async_computation.4 | async-start | bytes 1179648 | tf_op jit(solution)/shard_map/reduce_scatter | solution.py:666
  601.6 54.2 %collective-permute-start.27 = (bf16[4608,128]{1,0:T(8,128)(2,1)}, bf16[4608,128]{1,0:T(8,128)(2,1)}, u32[]{:S(2)}, u32[]{:S(2)}) collective-permute-start(bf16[4608,128]{1,0:T(8,128)(2,1)} %get-tuple-element.293), channel_id=1, source_target_pairs={{0,8},{8,0},{16,24},{24,16},{1,9},{9,1},{17,25},{25,17},{2,10},{10... | collective-permute-start | bytes 3538952 | tf_op jit(solution)/shard_map/ppermute | solution.py:405
  603.0 52.8 %collective-permute-start.28 = (bf16[4608,128]{1,0:T(8,128)(2,1)}, bf16[4608,128]{1,0:T(8,128)(2,1)}, u32[]{:S(2)}, u32[]{:S(2)}) collective-permute-start(bf16[4608,128]{1,0:T(8,128)(2,1)} %get-tuple-element.292), channel_id=1, source_target_pairs={{0,16},{8,24},{16,0},{24,8},{1,17},{9,25},{17,1},{25,9},{2,18},{10... | collective-permute-start | bytes 3538952 | tf_op jit(solution)/shard_map/ppermute | solution.py:405
  680.9 64.3 %collective-permute-start.29 = (bf16[256,2048]{1,0:T(8,128)(2,1)}, bf16[256,2048]{1,0:T(8,128)(2,1)}, u32[]{:S(2)}, u32[]{:S(2)}) collective-permute-start(bf16[256,2048]{1,0:T(8,128)(2,1)} %get-tuple-element.299), channel_id=1, source_target_pairs={{0,8},{8,0},{16,24},{24,16},{1,9},{9,1},{17,25},{25,17},{2,10},{10... | collective-permute-start | bytes 3145736 | tf_op jit(solution)/shard_map/ppermute | solution.py:405
  682.4 62.8 %collective-permute-start.30 = (bf16[256,2048]{1,0:T(8,128)(2,1)}, bf16[256,2048]{1,0:T(8,128)(2,1)}, u32[]{:S(2)}, u32[]{:S(2)}) collective-permute-start(bf16[256,2048]{1,0:T(8,128)(2,1)} %get-tuple-element.301), channel_id=1, source_target_pairs={{0,16},{8,24},{16,0},{24,8},{1,17},{9,25},{17,1},{25,9},{2,18},{10... | collective-permute-start | bytes 3145736 | tf_op jit(solution)/shard_map/ppermute | solution.py:405
  689.3 50.2 %collective-permute-start.36 = (bf16[256,384]{0,1:T(8,128)(2,1)S(1)}, bf16[256,384]{0,1:T(8,128)(2,1)S(1)}, u32[]{:S(2)}, u32[]{:S(2)}) collective-permute-start(bf16[256,384]{0,1:T(8,128)(2,1)S(1)} %fusion.91), channel_id=1, source_target_pairs={{0,16},{8,24},{16,0},{24,8},{1,17},{9,25},{17,1},{25,9},{2,18},{10... | collective-permute-start | bytes 589832 | tf_op jit(solution)/shard_map/ppermute | solution.py:405
  690.6 48.9 %collective-permute-start.37 = (bf16[256,384]{0,1:T(8,128)(2,1)S(1)}, bf16[256,384]{0,1:T(8,128)(2,1)S(1)}, u32[]{:S(2)}, u32[]{:S(2)}) collective-permute-start(bf16[256,384]{0,1:T(8,128)(2,1)S(1)} %fusion.91), channel_id=1, source_target_pairs={{0,24},{8,16},{16,8},{24,0},{1,25},{9,17},{17,9},{25,1},{2,26},{10... | collective-permute-start | bytes 589832 | tf_op jit(solution)/shard_map/ppermute | solution.py:405
  (99 other events, 1142.4 us)
Sparse Core Ops, SparseCore 0:
  14.0 24.9 all-gather.9
  41.2 29.8 all-gather.7
  72.7 64.0 all-gather.11
  143.6 80.5 all-gather.13
  574.8 88.0 reduce-scatter.2
  743.5 31.2 reduce-scatter.4

commit v4 on v3

--- a/solution.py
+++ b/solution.py
@@ -16,6 +16,7 @@
 norm_epsilon = 1e-06
 rope_base = 10000.0
 masked_score = -1000000000.0
+half_from = 200000
 
 
 def rms_scale(values, gain_vector):
@@ -405,14 +406,36 @@
     return lax.ppermute(values, axis, [(i, i ^ distance) for i in range(count)])
 
 
-def spread(values, axis, count):
-    return [values] + [swap(values, axis, k, count) for k in range(1, count)]
+def near(values, axis, count):
+    return [swap(values, axis, 1, count), swap(values, axis, 2, count)]
+
+
+def spread(values, axis, count, close=None):
+    one, two = near(values, axis, count) if close is None else close
+    if count == 4 and values.size >= half_from:
+        half = values.shape[0] // 2
+        three = [swap(two[:half], axis, 1, count), swap(one[half:], axis, 2, count)]
+        return [values, one, two, jnp.concatenate(three, axis=0)]
+    return [values, one, two] + [swap(values, axis, k, count) for k in range(3, count)]
 
 
 def collect(blocks, axis, count):
-    total = blocks[0].astype(jnp.float32)
+    f32 = jnp.float32
+    if count == 4 and blocks[0].size >= half_from:
+        half = blocks[0].shape[0] // 2
+        over_one = swap(blocks[3][:half], axis, 1, count)
+        over_two = swap(blocks[3][half:], axis, 2, count)
+        top = blocks[0][:half].astype(f32) + swap(blocks[1][:half], axis, 1, count).astype(f32)
+        low = blocks[0][half:].astype(f32) + swap(blocks[2][half:], axis, 2, count).astype(f32)
+        to_two = (blocks[2][:half].astype(f32) + over_one.astype(f32)).astype(blocks[2].dtype)
+        to_one = (blocks[1][half:].astype(f32) + over_two.astype(f32)).astype(blocks[1].dtype)
+        to_two, to_one = pin(to_two, to_one)
+        top = top + swap(to_two, axis, 2, count).astype(f32)
+        low = low + swap(to_one, axis, 1, count).astype(f32)
+        return jnp.concatenate([top, low], axis=0)
+    total = blocks[0].astype(f32)
     for k in range(1, count):
-        total = total + swap(blocks[k], axis, k, count).astype(jnp.float32)
+        total = total + swap(blocks[k], axis, k, count).astype(f32)
     return total
 
 
@@ -479,17 +502,15 @@
     ab_rows = ab_piece.shape[0]
     ab_piece = jnp.concatenate([ab_piece, meta.reshape(-1, rank_columns)], axis=0)
     ab_got = lax.all_gather(ab_piece, "dp", axis=0)
-    out_piece = jnp.concatenate([w_output, a_attention[3]], axis=1)
-    out_piece, ab_got = pin(out_piece, ab_got)
+    tokens = layer_input[0].astype(f32)
+    normed = rms_scale(tokens, gain_attention).astype(low)
+    wt_piece = jnp.swapaxes(w_qkv, 1, 2)
+    wt_piece, ab_got, *close = pin(wt_piece, ab_got, *near(normed, "seq", n))
+    w_group = lax.all_gather(wt_piece, "dp", axis=0)
     dp_order = d ^ jnp.arange(dp_count, dtype=jnp.int32)
     meta_all = ab_got[:, ab_rows:].reshape((dp_count,) + meta.shape)[dp_order].astype(f32)
     ab_group = ab_got[:, :ab_rows].reshape(dp_count, 7, piece, rank_columns)
     ab_group = jnp.swapaxes(ab_group, 0, 1).reshape(7, group_width, rank_columns)
-    out_maps = lax.all_gather(out_piece, "dp", axis=0, tiled=True)
-    wt_piece = jnp.swapaxes(w_qkv, 1, 2)
-    wt_piece, out_maps = pin(wt_piece, out_maps)
-    w_group = lax.all_gather(wt_piece, "dp", axis=0)
-
     local_count = expert_w_in.shape[0]
     expert_count = local_count * dp_count
     capacity = own_rows * TOP // expert_count * 9 // 8
@@ -514,31 +535,32 @@
     pick = pick.astype(low)
 
     cosine, sine = rope_tables(offset, HD)
-    tokens = layer_input[0].astype(f32)
-    normed = rms_scale(tokens, gain_attention).astype(low)
-    normed_blocks = spread(normed, "seq", n)
+
+    dot = lambda a, b: jnp.dot(a, b, preferred_element_type=f32)
+    dot_t = lambda a, b: lax.dot_general(a, b, (((1,), (1,)), ((), ())), preferred_element_type=f32)
+    dot_l = lambda a, b: lax.dot_general(a, b, (((0,), (0,)), ((), ())), preferred_element_type=f32)
+
     share = jnp.concatenate([ab_group[0:3], ab_group[6:7]], axis=0)
-    share_blocks = spread(share, "seq", n)
-    grad_send, w_group, pick, pick_t, slot, cosine, sine, *early = pin(
-        out_cotangent[0], w_group, pick, pick_t, slot, cosine, sine, *normed_blocks, *share_blocks
-    )
-    grad_got = lax.all_gather(grad_send, "dp", axis=0)
-    grad_blocks = [lax.dynamic_index_in_dim(grad_got, dp_order[k], 0, keepdims=False) for k in range(dp_count)]
-    normed_all = jnp.concatenate(early[:n], axis=0)
-    share_blocks = jnp.stack(early[n:])
-    share_full = share_blocks[order]
+    share_full = jnp.stack(spread(share, "seq", n))[order]
     share_full = jnp.swapaxes(share_full, 0, 1).reshape(4, full_width, rank_columns)
     down_cat = jnp.swapaxes(share_full[0:3], 0, 1).reshape(full_width, 3 * rank_columns)
     upt_output = share_full[3]
     upt_group = ab_group[3:6]
-
-    dot = lambda a, b: jnp.dot(a, b, preferred_element_type=f32)
-    dot_t = lambda a, b: lax.dot_general(a, b, (((1,), (1,)), ((), ())), preferred_element_type=f32)
-    dot_l = lambda a, b: lax.dot_general(a, b, (((0,), (0,)), ((), ())), preferred_element_type=f32)
-
+    normed_all = jnp.concatenate(spread(normed, "seq", n, close), axis=0)
     reduced_cat = (jnp.tile(full_mask, (1, 3)) * dot(normed_all, down_cat)).astype(low)
+    out_piece = jnp.concatenate([w_output, a_attention[3]], axis=1)
+    out_piece, w_group, pick, pick_t, slot, cosine, sine, normed_all, reduced_cat, upt_group, upt_output = pin(
+        out_piece, w_group, pick, pick_t, slot, cosine, sine, normed_all, reduced_cat, upt_group, upt_output
+    )
+    out_maps = lax.all_gather(out_piece, "dp", axis=0, tiled=True)
     reduced_list = [reduced_cat[:, m * rank_columns : (m + 1) * rank_columns] for m in range(3)]
     raw = qkv_project(normed_all, reduced_cat, w_group, upt_group)
+    grad_send, raw = pin(out_cotangent[0], raw)
+    grad_got = lax.all_gather(grad_send, "dp", axis=0)
+    grad_own = [out_cotangent[0], swap(out_cotangent[0], "dp", 1, dp_count)]
+    grad_blocks = grad_own + [
+        lax.dynamic_index_in_dim(grad_got, dp_order[k], 0, keepdims=False) for k in range(2, dp_count)
+    ]
     mixed_group, query_heads, key_heads, value_heads, stat = attend(
         raw, cosine, sine, gain_query, gain_key, segment
     )
@@ -622,7 +644,7 @@
     grad_packs = spread(grad_pack, "seq", n)
     flat, *grad_packs = pin(flat, *grad_packs)
     expert_terms = [lax.dynamic_index_in_dim(flat, order[k], 0, keepdims=False) for k in range(n)]
-    expert_terms = expert_terms[:1] + [swap(expert_terms[k], "seq", k, n) for k in range(1, n)]
+    expert_sum = collect(expert_terms, "seq", n)
     grad_pack_all = jnp.concatenate(grad_packs, axis=0)
     grad_all = grad_pack_all[:, :full_width]
     grad_reduced_all = grad_pack_all[:, full_width : full_width + rank_columns]
@@ -641,15 +663,17 @@
         gain_key,
         segment,
     )
-    expert_terms[-1], *grad_raw_list = pin(expert_terms[-1], *grad_raw_list)
+    expert_sum, *grad_raw_list = pin(expert_sum, *grad_raw_list)
     partial_reduced = jnp.concatenate(
         [dot(grad_raw_list[m], upt_group[m]) for m in range(3)], axis=1
-    ).astype(low).reshape(n, own_rows, 3 * rank_columns)
+    ).astype(low)
+    partial_reduced, *grad_raw_list = pin(partial_reduced, *grad_raw_list)
+    partial_reduced = partial_reduced.reshape(n, own_rows, 3 * rank_columns)
     summed_reduced = collect([partial_reduced[k] for k in range(n)], "seq", n)
     grad_reduced = (jnp.tile(own_mask, (1, 3)) * summed_reduced).astype(low)
     grad_reduced_full = jnp.concatenate(spread(grad_reduced, "seq", n), axis=0)
     partial_normed = qkv_back(grad_raw_list, w_group).reshape(n, own_rows, full_width)
-    partial_normed, *expert_terms = pin(partial_normed, *expert_terms)
+    partial_normed, grad_reduced_full = pin(partial_normed, grad_reduced_full)
     summed_back = collect([partial_normed[k] for k in range(n)], "seq", n)
     summed_back, mixture, hidden = pin(summed_back, mixture, hidden)
     layer_output = (hidden + mixture.astype(f32)).astype(low)[None]
@@ -669,7 +693,7 @@
     grad_a_attention = own_parts[0:4]
     grad_b_attention = jnp.swapaxes(own_parts[4:8], 1, 2)
 
-    flat = sum(x.astype(f32) for x in expert_terms).reshape(-1)
+    flat = expert_sum.reshape(-1)
     pieces = []
     start = 0
     for count, width in widths:

time: 795 us -> 736 us (0.926)
  waiting for transfers between devices: 234 us -> 159 us
    all_gather x1, waiting for transfers between devices: 32 us -> 0.02 us  [local(): out_maps = lax.all_gather(out_piece, 'dp', axis=0, tiled=True)]
    all_gather x1, waiting for transfers between devices: 22.7 us -> 0.01 us  [local(): ab_got = lax.all_gather(ab_piece, 'dp', axis=0)]
    ppermute x38 -> x51, waiting for transfers between devices: 160 us -> 139 us  [swap(): return lax.ppermute(values, axis, [(i, i ^ distance) for i in range(count)])]
    all_gather x1, waiting for transfers between devices: 0.01 us -> 9.52 us  [local(): w_group = lax.all_gather(wt_piece, 'dp', axis=0)]
    reduce_scatter x1, waiting for transfers between devices: 19.3 us -> 11.2 us  [local(): own_parts = lax.psum_scatter(stacked, 'dp', scatter_dimension=0)]
    ppermute x38 -> x51, starting transfers between devices: 41.8 us -> 47.9 us  [swap(): return lax.ppermute(values, axis, [(i, i ^ distance) for i in range(count)])]
    unnamed x192 -> x158, local copies, waits for them, and re-layouts: 41.8 us -> 41.7 us
  transfers between devices with their start and end apart: 44 -> 57, of which waited for: 16 -> 26; matrix products, arithmetic and copies ran while one was open for 25% -> 29% of each run, Pallas kernels for 31% -> 33%
where the time goes in v4:
time: 736 us; the launch traced here: 725 us
  Pallas kernels  242 us (33%)
  waiting for transfers between devices  159 us (22%)
  local copies, waits for them, and re-layouts  117 us (16%)
  matrix products  62.5 us (8%)
  other arithmetic  60.9 us (8%)
  starting transfers between devices  48.5 us (7%)
  between operations  34.7 us (5%)
    pallas_call x4, Pallas kernels, run_experts(): pl.pallas_call(functools.partial(expert_kernel, len(kept)), grid=(experts...  169 us
    ppermute x51, waiting for transfers between devices, swap(): return lax.ppermute(values, axis, [(i, i ^ distance) for i in range(count)])  139 us
    ppermute x51, starting transfers between devices, swap(): return lax.ppermute(values, axis, [(i, i ^ distance) for i in range(count)])  47.9 us
    unnamed x158, local copies, waits for them, and re-layouts  41.7 us
    dot_general x16, matrix products, local(): lax.dot_general(a, b, (((0,), (0,)), ((), ())), preferred_element_type=f32)  39.4 us
    pallas_call x1, Pallas kernels, attend_back(): pl.pallas_call(functools.partial(attend_back_kernel, tile), grid=(heads,)...  23.8 us
    pallas_call x1, Pallas kernels, attend(): pl.pallas_call(functools.partial(attend_kernel, tile), grid=(heads,), in_...  23.7 us
    dot_general x6, matrix products, local(): dot = lambda a, b: jnp.dot(a, b, preferred_element_type=f32)  15.7 us
  transfers between devices with their start and end apart: 57, of which 26 were waited for; matrix products, arithmetic and copies ran while one was open for 29% of the time, Pallas kernels for 33%

profile of v4, /device:TPU:0, one launch (start us, length us, event | category | flops | bytes accessed | tf_op | source)
XLA Modules:
  0.0 724.7 jit_solution(8260308706780612662)
XLA Ops:
  21.6 21.7 %collective-permute-done = bf16[256,2048]{1,0:T(8,128)(2,1)} collective-permute-done((bf16[256,2048]{1,0:T(8,128)(2,1)S(1)}, bf16[256,2048]{1,0:T(8,128)(2,1)}, u32[]{:S(2)}, u32[]{:S(2)}) %collective-permute-start) | collective-permute-done | bytes 1048608 | tf_op jit(solution)/shard_map/ppermute | solution.py:406
  75.5 5.9 collective-permute-done.2
  94.1 6.3 multiply_convert_fusion.1.reduced_ref
  100.4 9.5 %all-gather.12.cloned.1.call-done = bf16[24,64,2048]{2,1,0:T(8,128)(2,1)} async-done(((bf16[3,64,2048]{2,1,0:T(8,128)(2,1)}), bf16[24,64,2048]{2,1,0:T(8,128)(2,1)}) %all-gather.12.cloned.1.call-update) | async-done | bytes 6291472 | tf_op jit(solution)/shard_map/all_gather | solution.py:509
  110.0 12.8 %qkv_project.1.q_raw.k_raw.v_raw = f32[3,1024,512]{2,1,0:T(8,128)} custom-call(bf16[1024,2048]{1,0:T(8,128)(2,1)} %constant_dynamic-update-slice_fusion.x_ref, bf16[1024,384]{1,0:T(8,128)(2,1)} %multiply_convert_fusion.1.reduced_ref, bf16[8,3,64,2048]{3,2,1,0:T(8,128)(2,1)} %bitcast.349, bf16[3,512,128]{2,1,0:T(8,128)(2,1)} %bitcast.363), custom_call_target="tpu_custom_call" | custom-call | flops 6442450944 | bytes 16777216 | tf_op jit(solution)/shard_map/qkv_project/pallas_call | solution.py:213
  124.2 23.7 %attend.1 = (bf16[1024,512]{1,0:T(8,128)(2,1)}, bf16[1024,512]{1,0:T(8,128)(2,1)}, bf16[1024,512]{1,0:T(8,128)(2,1)}, bf16[1024,512]{1,0:T(8,128)(2,1)}, f32[4,1,1024]{2,1,0:T(1,128)}) custom-call(f32[3,1024,512]{2,1,0:T(8,128)} %qkv_project.1.q_raw.k_raw.v_raw, f32[3,1024,512]{2,1,0:T(8,128)} %qkv_project.1.q_raw.k_raw.v_raw, ...), custom_call_target="tpu_custom_call" | custom-call | flops 2147483648 | bytes 10485760 | tf_op jit(solution)/shard_map/attend/pallas_call | solution.py:100
  157.1 11.4 %collective-permute-done.10 = bf16[128,2176]{1,0:T(8,128)(2,1)S(1)} collective-permute-done((bf16[128,2176]{1,0:T(8,128)(2,1)S(1)}, bf16[128,2176]{1,0:T(8,128)(2,1)S(1)}, u32[]{:S(2)}, u32[]{:S(2)}) %collective-permute-start.10) | collective-permute-done | bytes 557088 | tf_op jit(solution)/shard_map/ppermute | solution.py:406
  172.2 8.3 %collective-permute-done.12 = bf16[128,2176]{1,0:T(8,128)(2,1)S(1)} collective-permute-done((bf16[128,2176]{1,0:T(8,128)(2,1)S(1)}, bf16[128,2176]{1,0:T(8,128)(2,1)S(1)}, u32[]{:S(2)}, u32[]{:S(2)}) %collective-permute-start.12) | collective-permute-done | bytes 557088 | tf_op jit(solution)/shard_map/ppermute | solution.py:406
  181.7 9.9 %collective-permute-done.11 = bf16[128,2176]{1,0:T(8,128)(2,1)S(1)} collective-permute-done((bf16[128,2176]{1,0:T(8,128)(2,1)S(1)}, bf16[128,2176]{1,0:T(8,128)(2,1)S(1)}, u32[]{:S(2)}, u32[]{:S(2)}) %collective-permute-start.11) | collective-permute-done | bytes 557088 | tf_op jit(solution)/shard_map/ppermute | solution.py:406
  197.9 42.5 %experts.4 = (bf16[256,2048]{1,0:T(8,128)(2,1)}, bf16[256,2048]{1,0:T(8,128)(2,1)}, bf16[256,2048]{1,0:T(8,128)(2,1)}, bf16[256,2048]{1,0:T(8,128)(2,1)}, bf16[2...) custom-call(bf16[256,2048]{1,0:T(8,128)(2,1)} %copy-done.13, ...), custom_call_target="tpu_custom_call" | custom-call | flops 1179648 | bytes 1179648 | tf_op jit(solution)/shard_map/experts/pallas_call | solution.py:378
  240.7 25.9 %collective-permute-done.14.refs_0_ = bf16[256,2048]{1,0:T(8,128)(2,1)} collective-permute-done((bf16[256,2048]{1,0:T(8,128)(2,1)S(1)}, bf16[256,2048]{1,0:T(8,128)(2,1)}, u32[]{:S(2)}, u32[]{:S(2)}) %collective-permute-start.14) | collective-permute-done | bytes 1048608 | tf_op jit(solution)/shard_map/ppermute | solution.py:406
  282.4 5.6 dynamic-slice_bitcast_fusion
  288.0 42.0 %experts.5 = (bf16[256,2048]{1,0:T(8,128)(2,1)}, bf16[256,2048]{1,0:T(8,128)(2,1)}, bf16[256,2048]{1,0:T(8,128)(2,1)}, bf16[256,2048]{1,0:T(8,128)(2,1)}, bf16[2...) custom-call(bf16[256,2048]{1,0:T(8,128)(2,1)} %collective-permute-do, ...), custom_call_target="tpu_custom_call", output_to_operand_aliasing={{4}: (13, {}), {5}: (14, {}), {6}: (15, {}), {7}: (16, {}),... | custom-call | flops 1179648 | bytes 1179648 | tf_op jit(solution)/shard_map/experts/pallas_call | solution.py:378
  339.4 42.1 %experts.6 = (bf16[256,2048]{1,0:T(8,128)(2,1)}, bf16[256,2048]{1,0:T(8,128)(2,1)}, bf16[256,2048]{1,0:T(8,128)(2,1)}, bf16[256,2048]{1,0:T(8,128)(2,1)}, bf16[2...) custom-call(bf16[256,2048]{1,0:T(8,128)(2,1)} %collective-permute-do, ...), custom_call_target="tpu_custom_call", output_to_operand_aliasing={{4}: (13, {}), {5}: (14, {}), {6}: (15, {}), {7}: (16, {}),... | custom-call | flops 1179648 | bytes 1179648 | tf_op jit(solution)/shard_map/experts/pallas_call | solution.py:378
  398.3 42.5 %experts.7 = (bf16[256,2048]{1,0:T(8,128)(2,1)}, bf16[256,2048]{1,0:T(8,128)(2,1)}, bf16[256,2048]{1,0:T(8,128)(2,1)}, bf16[256,2048]{1,0:T(8,128)(2,1)}, bf16[2...) custom-call(bf16[256,2048]{1,0:T(8,128)(2,1)} %collective-permute-do, ...), custom_call_target="tpu_custom_call", output_to_operand_aliasing={{4}: (13, {}), {5}: (14, {}), {6}: (15, {}), {7}: (16, {}),... | custom-call | flops 1179648 | bytes 1179648 | tf_op jit(solution)/shard_map/experts/pallas_call | solution.py:378
  448.6 8.4 %gather_fusion.2 = bf16[8,256,2048]{2,1,0:T(8,128)(2,1)} fusion(bf16[8,256,2048]{2,1,0:T(8,128)(2,1)} %bitcast_dynamic-update-slice_fusion, s32[1024]{0:T(1024)S(1)} %pad_clamp_fusion.1), kind=kCustom, calls=%fused_computation.2 | custom fusion | bytes 16777248 | tf_op jit(solution)/shard_map/gather | solution.py:615
  516.9 5.1 fusion.18
  537.7 8.3 %collective-permute-done.31 = bf16[128,2304]{1,0:T(8,128)(2,1)S(1)} collective-permute-done((bf16[128,2304]{1,0:T(8,128)(2,1)S(1)}, bf16[128,2304]{1,0:T(8,128)(2,1)S(1)}, u32[]{:S(2)}, u32[]{:S(2)}) %collective-permute-start.31) | collective-permute-done | bytes 589856 | tf_op jit(solution)/shard_map/ppermute | solution.py:406
  555.8 9.2 %collective-permute-done.34 = bf16[2304,128]{1,0:T(8,128)(2,1)S(1)} collective-permute-done((bf16[2304,128]{1,0:T(8,128)(2,1)S(1)}, bf16[2304,128]{1,0:T(8,128)(2,1)S(1)}, u32[]{:S(2)}, u32[]{:S(2)}) %collective-permute-start.34) | collective-permute-done | bytes 589856 | tf_op jit(solution)/shard_map/ppermute | solution.py:406
  576.0 23.8 %attend_back.1 = (bf16[1024,512]{1,0:T(8,128)(2,1)}, bf16[1024,512]{1,0:T(8,128)(2,1)}, bf16[1024,512]{1,0:T(8,128)(2,1)}) custom-call(bf16[1024,512]{1,0:T(8,128)(2,1)} %get-tuple-element.223.query, bf16[1024,512]{1,0:T(8,128)(2,1)} %get-tuple-element.224.key, bf16[1024,512]{1,0:T(8,128)(2,1)} %get-tuple-element.225.value, ...), custom_call_target="tpu_custom_call" | custom-call | flops 524288 | bytes 524288 | tf_op jit(solution)/shard_map/attend_back/pallas_call | solution.py:168
  628.8 12.3 %qkv_back.1 = bf16[1024,2048]{1,0:T(8,128)(2,1)} custom-call(bf16[1024,512]{1,0:T(8,128)(2,1)} %get-tuple-element.237.a_ref, bf16[1024,512]{1,0:T(8,128)(2,1)} %get-tuple-element.238.b_ref, bf16[1024,512]{1,0:T(8,128)(2,1)} %get-tuple-element.239.c_ref, bf16[8,3,64,2048]{3,2,1,0:T(8,128)(2,1)} %bitcast.350), custom_call_target="tpu_custom_call" | custom-call | flops 2097152 | bytes 2097152 | tf_op jit(solution)/shard_map/qkv_back/pallas_call | solution.py:246
  666.1 8.6 %collective-permute-done.46 = bf16[128,2048]{1,0:T(8,128)(2,1)S(1)} collective-permute-done((bf16[128,2048]{1,0:T(8,128)(2,1)S(1)}, bf16[128,2048]{1,0:T(8,128)(2,1)S(1)}, u32[]{:S(2)}, u32[]{:S(2)}) %collective-permute-start.46) | collective-permute-done | bytes 524320 | tf_op jit(solution)/shard_map/ppermute | solution.py:406
  684.6 5.6 collective-permute-done.48
  700.6 11.2 %reduce-scatter.5.cloned.1.call-done = bf16[1,8,64,128]{3,2,1,0:T(8,128)(2,1)} async-done(((bf16[8,8,64,128]{3,2,1,0:T(8,128)(2,1)}), bf16[1,8,64,128]{3,2,1,0:T(8,128)(2,1)}) %reduce-scatter.5.cloned.1.call-update) | async-done | bytes 131088 | tf_op jit(solution)/shard_map/reduce_scatter | solution.py:690
  (439 shorter events, 287.2 us)
Async XLA Ops:
  7.2 37.6 %all-gather.10.cloned.1.call-start = ((), (), s32[]{:S(2)}) async-start(), calls=%async_computation.5 | async-start | bytes 1179648 | tf_op jit(solution)/shard_map/all_gather | solution.py:504
  13.5 96.5 %all-gather.12.cloned.1.call-start = ((), (), s32[]{:S(2)}) async-start(), calls=%async_computation.6 | async-start | bytes 7077888 | tf_op jit(solution)/shard_map/all_gather | solution.py:509
  17.1 26.2 %collective-permute-start = (bf16[256,2048]{1,0:T(8,128)(2,1)S(1)}, bf16[256,2048]{1,0:T(8,128)(2,1)}, u32[]{:S(2)}, u32[]{:S(2)}) collective-permute-start(bf16[256,2048]{1,0:T(8,128)(2,1)S(1)} %get-tuple-element.293), channel_id=1, source_target_pairs={{0,8},{8,0},{16,24},{24,16},{1,9},{9,1},{17,25},{25,17},{2,10},{10... | collective-permute-start | bytes 3145736 | tf_op jit(solution)/shard_map/ppermute | solution.py:406
  20.0 24.7 %collective-permute-start.1 = (bf16[256,2048]{1,0:T(8,128)(2,1)S(1)}, bf16[256,2048]{1,0:T(8,128)(2,1)}, u32[]{:S(2)}, u32[]{:S(2)}) collective-permute-start(bf16[256,2048]{1,0:T(8,128)(2,1)S(1)} %get-tuple-element.293), channel_id=1, source_target_pairs={{0,16},{8,24},{16,0},{24,8},{1,17},{9,25},{17,1},{25,9},{2,18},{10... | collective-permute-start | bytes 3145736 | tf_op jit(solution)/shard_map/ppermute | solution.py:406
  44.8 103.1 %all-gather.8.cloned.1.call-start = ((), (), s32[]{:S(2)}) async-start(), calls=%async_computation.2 | async-start | bytes 2506752 | tf_op jit(solution)/shard_map/all_gather | solution.py:555
  110.0 172.4 %all-gather.14.cloned.1.call-start = ((), (), s32[]{:S(2)}) async-start(), calls=%async_computation.7 | async-start | bytes 9437184 | tf_op jit(solution)/shard_map/all_gather | solution.py:559
  122.9 571.2 %reduce-scatter.3.cloned.1.call-start = ((), (), s32[]{:S(2)}) async-start(), calls=%async_computation.3 | async-start | bytes 9437184 | tf_op jit(solution)/shard_map/reduce_scatter | solution.py:617
  155.8 24.7 %collective-permute-start.12 = (bf16[128,2176]{1,0:T(8,128)(2,1)S(1)}, bf16[128,2176]{1,0:T(8,128)(2,1)S(1)}, u32[]{:S(2)}, u32[]{:S(2)}) collective-permute-start(bf16[128,2176]{1,0:T(8,128)(2,1)S(1)} %get-tuple-element.313), channel_id=1, source_target_pairs={{0,16},{8,24},{16,0},{24,8},{1,17},{9,25},{17,1},{25,9},{2,18},{10... | collective-permute-start | bytes 1671176 | tf_op jit(solution)/shard_map/ppermute | solution.py:406
  156.3 25.4 %collective-permute-start.8 = (bf16[128,2176]{1,0:T(8,128)(2,1)S(1)}, bf16[128,2176]{1,0:T(8,128)(2,1)S(1)}, u32[]{:S(2)}, u32[]{:S(2)}) collective-permute-start(bf16[128,2176]{1,0:T(8,128)(2,1)S(1)} %get-tuple-element.312), channel_id=1, source_target_pairs={{0,8},{8,0},{16,24},{24,16},{1,9},{9,1},{17,25},{25,17},{2,10},{10... | collective-permute-start | bytes 1671176 | tf_op jit(solution)/shard_map/ppermute | solution.py:406
  172.2 25.4 %collective-permute-start.17 = (bf16[256,2048]{1,0:T(8,128)(2,1)}, bf16[256,2048]{1,0:T(8,128)(2,1)}, u32[]{:S(2)}, u32[]{:S(2)}) collective-permute-start(bf16[256,2048]{1,0:T(8,128)(2,1)} %bitcast.1.refs_2_), channel_id=1, source_target_pairs={{0,1},{1,0},{2,3},{3,2},{4,5},{5,4},{6,7},{7,6},{8,9},{9,8},{10,11... | collective-permute-start | bytes 3145736 | tf_op jit(solution)/shard_map/ppermute | solution.py:406
  195.1 71.5 %collective-permute-start.14 = (bf16[256,2048]{1,0:T(8,128)(2,1)S(1)}, bf16[256,2048]{1,0:T(8,128)(2,1)}, u32[]{:S(2)}, u32[]{:S(2)}) collective-permute-start(bf16[256,2048]{1,0:T(8,128)(2,1)S(1)} %multiply_convert_fusion.refs_0_), channel_id=1, source_target_pairs={{0,4},{1,5},{2,6},{3,7},{4,0},{5,1},{6,2},{7,3},{8,12},{9,13},{10,... | collective-permute-start | bytes 3145736 | tf_op jit(solution)/shard_map/ppermute | solution.py:406
  240.4 26.4 %collective-permute-start.18 = (bf16[256,2048]{1,0:T(8,128)(2,1)}, bf16[256,2048]{1,0:T(8,128)(2,1)S(1)}, u32[]{:S(2)}, u32[]{:S(2)}) collective-permute-start(bf16[256,2048]{1,0:T(8,128)(2,1)} %get-tuple-element.150), channel_id=1, source_target_pairs={{0,1},{1,0},{2,3},{3,2},{4,5},{5,4},{6,7},{7,6},{8,9},{9,8},{10,11... | collective-permute-start | bytes 3145736 | tf_op jit(solution)/shard_map/ppermute | solution.py:406
  269.8 60.4 %collective-permute-start.19 = (bf16[256,2048]{1,0:T(8,128)(2,1)S(1)}, bf16[256,2048]{1,0:T(8,128)(2,1)}, u32[]{:S(2)}, u32[]{:S(2)}) collective-permute-start(bf16[256,2048]{1,0:T(8,128)(2,1)S(1)} %copy-done.14), channel_id=1, source_target_pairs={{0,6},{1,7},{2,4},{3,5},{4,2},{5,3},{6,0},{7,1},{8,14},{9,15},{10,... | collective-permute-start | bytes 3145736 | tf_op jit(solution)/shard_map/ppermute | solution.py:406
  335.6 55.0 %collective-permute-start.22 = (bf16[256,2048]{1,0:T(8,128)(2,1)S(1)}, bf16[256,2048]{1,0:T(8,128)(2,1)}, u32[]{:S(2)}, u32[]{:S(2)}) collective-permute-start(bf16[256,2048]{1,0:T(8,128)(2,1)S(1)} %copy-done.14), channel_id=1, source_target_pairs={{0,2},{1,3},{2,0},{3,1},{4,6},{5,7},{6,4},{7,5},{8,10},{9,11},{10,... | collective-permute-start | bytes 3145736 | tf_op jit(solution)/shard_map/ppermute | solution.py:406
  336.5 54.0 %collective-permute-start.23 = (bf16[256,2048]{1,0:T(8,128)(2,1)}, bf16[256,2048]{1,0:T(8,128)(2,1)}, u32[]{:S(2)}, u32[]{:S(2)}) collective-permute-start(bf16[256,2048]{1,0:T(8,128)(2,1)} %add_convert_fusion.3), channel_id=1, source_target_pairs={{0,4},{1,5},{2,6},{3,7},{4,0},{5,1},{6,2},{7,3},{8,12},{9,13},{10,... | collective-permute-start | bytes 3145736 | tf_op jit(solution)/shard_map/ppermute | solution.py:406
  397.3 48.1 %collective-permute-start.26 = (bf16[256,2048]{1,0:T(8,128)(2,1)}, bf16[256,2048]{1,0:T(8,128)(2,1)}, u32[]{:S(2)}, u32[]{:S(2)}) collective-permute-start(bf16[256,2048]{1,0:T(8,128)(2,1)} %add_convert_fusion.2), channel_id=1, source_target_pairs={{0,6},{1,7},{2,4},{3,5},{4,2},{5,3},{6,0},{7,1},{8,14},{9,15},{10,... | collective-permute-start | bytes 3145736 | tf_op jit(solution)/shard_map/ppermute | solution.py:406
  459.6 27.8 %collective-permute-start.28 = (bf16[256,2048]{1,0:T(8,128)(2,1)}, bf16[256,2048]{1,0:T(8,128)(2,1)}, u32[]{:S(2)}, u32[]{:S(2)}) collective-permute-start(bf16[256,2048]{1,0:T(8,128)(2,1)} %add_convert_fusion.1), channel_id=1, source_target_pairs={{0,2},{1,3},{2,0},{3,1},{4,6},{5,7},{6,4},{7,5},{8,10},{9,11},{10,... | collective-permute-start | bytes 3145736 | tf_op jit(solution)/shard_map/ppermute | solution.py:406
  494.7 35.3 %collective-permute-start.30 = (bf16[256,2304]{1,0:T(8,128)(2,1)S(1)}, bf16[256,2304]{1,0:T(8,128)(2,1)}, u32[]{:S(2)}, u32[]{:S(2)}) collective-permute-start(bf16[256,2304]{1,0:T(8,128)(2,1)S(1)} %pad_maximum_fusion.3), channel_id=1, source_target_pairs={{0,16},{8,24},{16,0},{24,8},{1,17},{9,25},{17,1},{25,9},{2,18},{10... | collective-permute-start | bytes 3538952 | tf_op jit(solution)/shard_map/ppermute | solution.py:406
  496.3 35.6 %collective-permute-start.29 = (bf16[256,2304]{1,0:T(8,128)(2,1)S(1)}, bf16[256,2304]{1,0:T(8,128)(2,1)}, u32[]{:S(2)}, u32[]{:S(2)}) collective-permute-start(bf16[256,2304]{1,0:T(8,128)(2,1)S(1)} %pad_maximum_fusion.3), channel_id=1, source_target_pairs={{0,8},{8,0},{16,24},{24,16},{1,9},{9,1},{17,25},{25,17},{2,10},{10... | collective-permute-start | bytes 3538952 | tf_op jit(solution)/shard_map/ppermute | solution.py:406
  524.7 187.1 %reduce-scatter.5.cloned.1.call-start = ((), (), s32[]{:S(2)}) async-start(), calls=%async_computation.4 | async-start | bytes 1179648 | tf_op jit(solution)/shard_map/reduce_scatter | solution.py:690
  550.9 53.8 %collective-permute-start.33 = (bf16[2304,128]{1,0:T(8,128)(2,1)}, bf16[2304,128]{1,0:T(8,128)(2,1)}, u32[]{:S(2)}, u32[]{:S(2)}) collective-permute-start(bf16[2304,128]{1,0:T(8,128)(2,1)} %get-tuple-element.304), channel_id=1, source_target_pairs={{0,8},{8,0},{16,24},{24,16},{1,9},{9,1},{17,25},{25,17},{2,10},{10... | collective-permute-start | bytes 1769480 | tf_op jit(solution)/shard_map/ppermute | solution.py:406
  552.2 52.4 %collective-permute-start.37 = (bf16[2304,128]{1,0:T(8,128)(2,1)}, bf16[2304,128]{1,0:T(8,128)(2,1)}, u32[]{:S(2)}, u32[]{:S(2)}) collective-permute-start(bf16[2304,128]{1,0:T(8,128)(2,1)} %get-tuple-element.307), channel_id=1, source_target_pairs={{0,16},{8,24},{16,0},{24,8},{1,17},{9,25},{17,1},{25,9},{2,18},{10... | collective-permute-start | bytes 1769480 | tf_op jit(solution)/shard_map/ppermute | solution.py:406
  567.8 36.8 %collective-permute-start.36 = (bf16[2304,128]{1,0:T(8,128)(2,1)}, bf16[2304,128]{1,0:T(8,128)(2,1)S(1)}, u32[]{:S(2)}, u32[]{:S(2)}) collective-permute-start(bf16[2304,128]{1,0:T(8,128)(2,1)} %get-tuple-element.221), channel_id=1, source_target_pairs={{0,16},{8,24},{16,0},{24,8},{1,17},{9,25},{17,1},{25,9},{2,18},{10... | collective-permute-start | bytes 1769480 | tf_op jit(solution)/shard_map/ppermute | solution.py:406
  568.4 36.2 %collective-permute-start.38 = (bf16[2304,128]{1,0:T(8,128)(2,1)}, bf16[2304,128]{1,0:T(8,128)(2,1)S(1)}, u32[]{:S(2)}, u32[]{:S(2)}) collective-permute-start(bf16[2304,128]{1,0:T(8,128)(2,1)} %get-tuple-element.222), channel_id=1, source_target_pairs={{0,8},{8,0},{16,24},{24,16},{1,9},{9,1},{17,25},{25,17},{2,10},{10... | collective-permute-start | bytes 1769480 | tf_op jit(solution)/shard_map/ppermute | solution.py:406
  (95 other events, 861.6 us)
Sparse Core Ops, SparseCore 0:
  13.6 24.9 all-gather.9
  44.9 65.0 all-gather.11
  111.6 28.8 all-gather.7
  142.0 115.6 all-gather.13
  524.8 87.8 reduce-scatter.2
  679.9 31.8 reduce-scatter.4

commit v5 on v4

--- a/solution.py
+++ b/solution.py
@@ -254,11 +254,11 @@
     )(grads[0], grads[1], grads[2], w_group)
 
 
-def expert_kernel(kept_in, *refs):
-    (x_a, x_b, g_a, g_b, pick, pick_t, slot, w_in, w_down, a_in, b_in, a_down, b_down) = refs[:13]
-    refs = refs[13 + kept_in:]
-    (out_a, out_b, back_a, back_b, xs, ps, act_o, gate_o, up_o, reds) = refs[:10]
-    (red_g, red_u, gred_d, down_acc, down_red, gx_acc, gred_g, gred_u, sum_out_a, sum_out_b, sum_back_a, sum_back_b) = refs[10:]
+def expert_kernel(kept_in, which, *refs):
+    (x_a, x_b, g_both, pick, pick_t, slot, w_in, w_down, a_in, b_in, a_down, b_down) = refs[:12]
+    refs = refs[12 + kept_in:]
+    (out_both, back_a, back_b, xs, ps, act_o, gate_o, up_o, reds) = refs[:9]
+    (red_g, red_u, gred_d, down_acc, down_red, gx_acc, gred_g, gred_u, sum_out_a, sum_out_b, sum_back_a, sum_back_b) = refs[9:]
     low = jnp.bfloat16
     e = pl.program_id(0)
     f = pl.program_id(1)
@@ -271,10 +271,11 @@
 
     @pl.when(f == 0)
     def _():
-        for b, (x_ref, g_ref) in enumerate(((x_a, g_a), (x_b, g_b))):
+        for b, x_ref in enumerate((x_a, x_b)):
             part = slice(b * cap, (b + 1) * cap)
+            g_place = which[1] if b == 0 else 1 - which[1]
             xs[0, part, :] = dot_nn(pick[0, b], x_ref[...]).astype(low)
-            ps[0, part, :] = (slot[0, part, 0:1] * dot_nn(pick[0, b], g_ref[...])).astype(low)
+            ps[0, part, :] = (slot[0, part, 0:1] * dot_nn(pick[0, b], g_both[g_place])).astype(low)
         red_g[...] = (mask * dot_nn(xs[0], a_in[0, 0])).astype(low)
         red_u[...] = (mask * dot_nn(xs[0], a_in[0, 1])).astype(low)
         gred_d[...] = (mask * dot_nt(ps[0], b_down[0])).astype(low)
@@ -324,10 +325,11 @@
         produced = down_acc[...] + dot_nn(reduced_d, b_down[0])
         scaled = (slot[0, :, 0:1] * produced).astype(low)
         grads = (gx_acc[...] + dot_nt(back_g, a_in[0, 0]) + dot_nt(back_u, a_in[0, 1])).astype(low)
-        for b, (out_ref, out_sum, back_ref, back_sum) in enumerate(
-            ((out_a, sum_out_a, back_a, sum_back_a), (out_b, sum_out_b, back_b, sum_back_b))
+        for b, (out_sum, back_ref, back_sum) in enumerate(
+            ((sum_out_a, back_a, sum_back_a), (sum_out_b, back_b, sum_back_b))
         ):
             part = slice(b * cap, (b + 1) * cap)
+            out_ref = out_both.at[which[3] if b == 0 else 1 - which[3]]
             for values, total, result in ((scaled, out_sum, out_ref), (grads, back_sum, back_ref)):
                 term = dot_nn(pick_t[0, b], values[part, :])
 
@@ -344,7 +346,7 @@
                     result[...] = total[...].astype(low)
 
 
-def run_experts(chunk, x_pair, g_pair, pick, pick_t, slot, weights, kept):
+def run_experts(chunk, which, x_pair, g_all, pick, pick_t, slot, weights, kept):
     w_in, w_down, a_in, b_in, a_down, b_down = weights
     experts, unused, width, ff = w_in.shape
     unused, dp_count, cap, own_rows = pick.shape
@@ -353,36 +355,38 @@
     tile = min(256, ff)
     low = jnp.bfloat16
     f32 = jnp.float32
-    token = pl.BlockSpec((own_rows, width), lambda e, f: (0, 0), pipeline_mode=pl.Buffered(1))
+    one = pl.Buffered(1)
+    token = pl.BlockSpec((own_rows, width), lambda e, f, w: (0, 0), pipeline_mode=one)
     stored = [
-        ((experts, dp_count * cap, width), (1, rows, width), lambda e, f: (e, chunk, 0)),
-        ((experts, dp_count * cap, width), (1, rows, width), lambda e, f: (e, chunk, 0)),
-        ((experts, dp_count * cap, ff), (1, rows, tile), lambda e, f: (e, chunk, f)),
-        ((experts, dp_count * cap, ff), (1, rows, tile), lambda e, f: (e, chunk, f)),
-        ((experts, dp_count * cap, ff), (1, rows, tile), lambda e, f: (e, chunk, f)),
-        ((experts, dp_count * cap, 6 * rank), (1, rows, 6 * rank), lambda e, f: (e, chunk, 0)),
+        ((experts, dp_count * cap, width), (1, rows, width), lambda e, f, w: (e, chunk, 0)),
+        ((experts, dp_count * cap, width), (1, rows, width), lambda e, f, w: (e, chunk, 0)),
+        ((experts, dp_count * cap, ff), (1, rows, tile), lambda e, f, w: (e, chunk, f)),
+        ((experts, dp_count * cap, ff), (1, rows, tile), lambda e, f, w: (e, chunk, f)),
+        ((experts, dp_count * cap, ff), (1, rows, tile), lambda e, f, w: (e, chunk, f)),
+        ((experts, dp_count * cap, 6 * rank), (1, rows, 6 * rank), lambda e, f, w: (e, chunk, 0)),
     ]
     in_specs = [
-        token, token, token, token,
-        pl.BlockSpec((1, 2, cap, own_rows), lambda e, f: (e, chunk, 0, 0)),
-        pl.BlockSpec((1, 2, own_rows, cap), lambda e, f: (e, chunk, 0, 0)),
-        pl.BlockSpec((1, rows, 2), lambda e, f: (e, chunk, 0)),
-        pl.BlockSpec((1, 2, width, tile), lambda e, f: (e, 0, 0, f)),
-        pl.BlockSpec((1, tile, width), lambda e, f: (e, f, 0)),
-        pl.BlockSpec((1, 2, width, rank), lambda e, f: (e, 0, 0, 0)),
-        pl.BlockSpec((1, 2, rank, tile), lambda e, f: (e, 0, 0, f)),
-        pl.BlockSpec((1, tile, rank), lambda e, f: (e, f, 0)),
-        pl.BlockSpec((1, rank, width), lambda e, f: (e, 0, 0)),
+        token, token, pl.BlockSpec((2, own_rows, width), lambda e, f, w: (w[0], 0, 0), pipeline_mode=one),
+        pl.BlockSpec((1, 2, cap, own_rows), lambda e, f, w: (e, chunk, 0, 0)),
+        pl.BlockSpec((1, 2, own_rows, cap), lambda e, f, w: (e, chunk, 0, 0)),
+        pl.BlockSpec((1, rows, 2), lambda e, f, w: (e, chunk, 0)),
+        pl.BlockSpec((1, 2, width, tile), lambda e, f, w: (e, 0, 0, f)),
+        pl.BlockSpec((1, tile, width), lambda e, f, w: (e, f, 0)),
+        pl.BlockSpec((1, 2, width, rank), lambda e, f, w: (e, 0, 0, 0)),
+        pl.BlockSpec((1, 2, rank, tile), lambda e, f, w: (e, 0, 0, f)),
+        pl.BlockSpec((1, tile, rank), lambda e, f, w: (e, f, 0)),
+        pl.BlockSpec((1, rank, width), lambda e, f, w: (e, 0, 0)),
     ] + [pl.BlockSpec(memory_space=pl.ANY) for unused in kept]
     part = jax.ShapeDtypeStruct((own_rows, width), low)
     results = pl.pallas_call(
         functools.partial(expert_kernel, len(kept)),
-        grid=(experts, ff // tile),
-        in_specs=in_specs,
-        out_specs=[pl.BlockSpec((own_rows, width), lambda e, f: (0, 0), pipeline_mode=pl.Buffered(1))] * 4
-        + [pl.BlockSpec(block, index) for unused, block, index in stored],
-        out_shape=[part] * 4 + [jax.ShapeDtypeStruct(shape, low) for shape, unused, unused2 in stored],
-        scratch_shapes=[
+        grid_spec=pltpu.PrefetchScalarGridSpec(
+            num_scalar_prefetch=1,
+            grid=(experts, ff // tile),
+            in_specs=in_specs,
+            out_specs=[pl.BlockSpec((2, own_rows, width), lambda e, f, w: (w[2], 0, 0), pipeline_mode=one), token, token]
+            + [pl.BlockSpec(block, index) for unused, block, index in stored],
+            scratch_shapes=[
             pltpu.VMEM((rows, rank), low),
             pltpu.VMEM((rows, rank), low),
             pltpu.VMEM((rows, rank), low),
@@ -392,14 +396,16 @@
             pltpu.VMEM((rows, rank), f32),
             pltpu.VMEM((rows, rank), f32),
         ] + [pltpu.VMEM((own_rows, width), f32) for unused in range(4)],
-        input_output_aliases={13 + i: 4 + i for i in range(len(kept))},
+        ),
+        out_shape=[jax.ShapeDtypeStruct((dp_count, own_rows, width), low)] + [part] * 2 + [jax.ShapeDtypeStruct(shape, low) for shape, unused, unused2 in stored],
+        input_output_aliases={13 + i: 0 if i == 0 else 2 + i for i in range(len(kept))},
         cost_estimate=pl.CostEstimate(
             flops=experts * rows * width, bytes_accessed=experts * rows * width, transcendentals=0
         ),
         compiler_params=pltpu.CompilerParams(vmem_limit_bytes=60 * 1024 * 1024),
         name="experts",
-    )(*x_pair, *g_pair, pick, pick_t, slot, *weights, *kept)
-    return results[:4], results[4:]
+    )(which, *x_pair, g_all, pick, pick_t, slot, *weights, *kept)
+    return results[1:3], [results[0]] + list(results[3:])
 
 
 def swap(values, axis, distance, count):
@@ -419,7 +425,7 @@
     return [values, one, two] + [swap(values, axis, k, count) for k in range(3, count)]
 
 
-def collect(blocks, axis, count):
+def collect(blocks, axis, count, cover=None):
     f32 = jnp.float32
     if count == 4 and blocks[0].size >= half_from:
         half = blocks[0].shape[0] // 2
@@ -427,16 +433,19 @@
         over_two = swap(blocks[3][half:], axis, 2, count)
         top = blocks[0][:half].astype(f32) + swap(blocks[1][:half], axis, 1, count).astype(f32)
         low = blocks[0][half:].astype(f32) + swap(blocks[2][half:], axis, 2, count).astype(f32)
+        if cover is not None:
+            over_one, over_two, cover = pin(over_one, over_two, cover)
         to_two = (blocks[2][:half].astype(f32) + over_one.astype(f32)).astype(blocks[2].dtype)
         to_one = (blocks[1][half:].astype(f32) + over_two.astype(f32)).astype(blocks[1].dtype)
         to_two, to_one = pin(to_two, to_one)
         top = top + swap(to_two, axis, 2, count).astype(f32)
         low = low + swap(to_one, axis, 1, count).astype(f32)
-        return jnp.concatenate([top, low], axis=0)
-    total = blocks[0].astype(f32)
-    for k in range(1, count):
-        total = total + swap(blocks[k], axis, k, count).astype(f32)
-    return total
+        total = jnp.concatenate([top, low], axis=0)
+    else:
+        total = blocks[0].astype(f32)
+        for k in range(1, count):
+            total = total + swap(blocks[k], axis, k, count).astype(f32)
+    return total if cover is None else (total, cover)
 
 
 def pin(*values):
@@ -557,10 +566,7 @@
     raw = qkv_project(normed_all, reduced_cat, w_group, upt_group)
     grad_send, raw = pin(out_cotangent[0], raw)
     grad_got = lax.all_gather(grad_send, "dp", axis=0)
-    grad_own = [out_cotangent[0], swap(out_cotangent[0], "dp", 1, dp_count)]
-    grad_blocks = grad_own + [
-        lax.dynamic_index_in_dim(grad_got, dp_order[k], 0, keepdims=False) for k in range(2, dp_count)
-    ]
+    grad_own = jnp.stack([out_cotangent[0], swap(out_cotangent[0], "dp", 1, dp_count)])
     mixed_group, query_heads, key_heads, value_heads, stat = attend(
         raw, cosine, sine, gain_query, gain_key, segment
     )
@@ -574,7 +580,6 @@
     weights = (expert_w_in, expert_w_down, expert_a_in, expert_b_in, expert_a_down, expert_b_down)
     chips = dp_count // 2
     turns = [0] + list(range(chips // 2, chips)) + list(range(1, chips // 2))
-    outs = [None] * dp_count
     kept = ()
     rows = normed_ffn
     here = normed_ffn
@@ -597,8 +602,11 @@
                 grad_normed_ffn = leaving
             else:
                 flying = swap(leaving, "dp", 2 * turns[i - 1], dp_count)
-        (outs[2 * c], outs[2 * c + 1], back, back_other), kept = run_experts(
-            c, (here, other), grad_blocks[2 * c : 2 * c + 2], pick, pick_t, slot, weights, kept
+        block = lax.shift_right_logical(d, 1) ^ c
+        place = d & 1
+        which = jnp.stack([block, place, block, place] if c else [0 * d, 0 * d, block, place]).astype(jnp.int32)
+        (back, back_other), kept = run_experts(
+            c, which, (here, other), grad_got if c else grad_own, pick, pick_t, slot, weights, kept
         )
         if i == chips - 1 and flying is not None:
             flying, back_other = pin(flying, back_other)
@@ -607,12 +615,12 @@
             leaving = leaving.astype(low)
     if flying is not None:
         grad_normed_ffn = grad_normed_ffn + flying.astype(f32)
+    outs_all, *kept = kept
     leaving, *kept = pin(leaving, *kept)
     flying = swap(leaving, "dp", 2 * turns[-1], dp_count)
     flying, *kept_later = pin(flying, *kept)
     grad_normed_ffn = grad_normed_ffn + flying.astype(f32)
 
-    outs_all = jnp.stack(outs)[dp_order]
     outs_all, grad_normed_ffn = pin(outs_all, grad_normed_ffn)
     mixture = lax.psum_scatter(outs_all, "dp", scatter_dimension=0)
     grad_out = out_cotangent[0].astype(f32)
@@ -621,10 +629,14 @@
     grad_hidden_low = grad_hidden.astype(low)
     grad_reduced_output = (own_mask * dot(grad_hidden_low, upt_output)).astype(low)
     grad_pack = jnp.concatenate([grad_hidden_low, grad_reduced_output, output_reduced], axis=1)
+    grad_close = near(grad_pack, "seq", n)
+    *grad_close, xs, ps, act_rows, gate_rows, up_rows, reds = pin(*grad_close, *kept_later)
+    kept_last = (xs, ps, act_rows, gate_rows, up_rows, reds)
     flat = []
     for e in range(local_count):
-        xs, ps, act_rows, gate_rows, up_rows, reds = kept if e == 0 else kept_later
-        red = [reds[e][:, i * rank_columns : (i + 1) * rank_columns] for i in range(6)]
+        xs, unused, unused2, gate_rows, up_rows, reds = kept if e == 0 else kept_later
+        unused, ps, act_rows, unused2, unused3, reds_last = kept if e == 0 else kept_last
+        red = [(reds if i in (0, 1) else reds_last)[e][:, i * rank_columns : (i + 1) * rank_columns] for i in range(6)]
         terms = [
             (reds[e][:, 3 * rank_columns : 5 * rank_columns], xs[e]),
             (red[0], gate_rows[e]),
@@ -641,15 +653,15 @@
         ],
         axis=1,
     ).reshape(n, -1, rank_columns)
-    grad_packs = spread(grad_pack, "seq", n)
+    grad_packs = spread(grad_pack, "seq", n, grad_close)
     flat, *grad_packs = pin(flat, *grad_packs)
     expert_terms = [lax.dynamic_index_in_dim(flat, order[k], 0, keepdims=False) for k in range(n)]
-    expert_sum = collect(expert_terms, "seq", n)
     grad_pack_all = jnp.concatenate(grad_packs, axis=0)
     grad_all = grad_pack_all[:, :full_width]
     grad_reduced_all = grad_pack_all[:, full_width : full_width + rank_columns]
     output_reduced_all = grad_pack_all[:, full_width + rank_columns :]
     grad_mixed_group = dot_t(grad_pack_all[:, : full_width + rank_columns], out_maps).astype(low)
+    expert_sum, grad_mixed_group = collect(expert_terms, "seq", n, grad_mixed_group)
     grad_cols = lax.dynamic_slice_in_dim(grad_all, group_start, group_width, 1)
     grad_upt_output = dot_l(grad_cols, output_reduced_all)
     grad_down_output = dot_l(mixed_group, grad_reduced_all)
@@ -671,9 +683,10 @@
     partial_reduced = partial_reduced.reshape(n, own_rows, 3 * rank_columns)
     summed_reduced = collect([partial_reduced[k] for k in range(n)], "seq", n)
     grad_reduced = (jnp.tile(own_mask, (1, 3)) * summed_reduced).astype(low)
+    grad_reduced, *grad_raw_late = pin(grad_reduced, *grad_raw_list)
     grad_reduced_full = jnp.concatenate(spread(grad_reduced, "seq", n), axis=0)
     partial_normed = qkv_back(grad_raw_list, w_group).reshape(n, own_rows, full_width)
-    partial_normed, grad_reduced_full = pin(partial_normed, grad_reduced_full)
+    partial_normed, grad_reduced_full, expert_sum = pin(partial_normed, grad_reduced_full, expert_sum)
     summed_back = collect([partial_normed[k] for k in range(n)], "seq", n)
     summed_back, mixture, hidden = pin(summed_back, mixture, hidden)
     layer_output = (hidden + mixture.astype(f32)).astype(low)[None]
@@ -681,7 +694,7 @@
     unused_input, pull_input = jax.vjp(lambda values: rms_scale(values, gain_attention), tokens)
     input_grad = (grad_hidden + pull_input(grad_normed)[0]).astype(low)[None]
 
-    grad_upt = [dot_l(grad_raw_list[m], reduced_list[m]) for m in range(3)]
+    grad_upt = [dot_l(grad_raw_late[m], reduced_list[m]) for m in range(3)]
     normed_cols = lax.dynamic_slice_in_dim(normed_all, group_start, group_width, 1)
     grad_down_cat = dot_l(normed_cols, grad_reduced_full)
     parts = [grad_down_cat[:, m * rank_columns : (m + 1) * rank_columns] for m in range(3)]

time: 736 us -> 710 us (0.965)
  waiting for transfers between devices: 159 us -> 126 us
  other arithmetic: 60.9 us -> 74.9 us
  between operations: 34.7 us -> 23.5 us
    ppermute x51, waiting for transfers between devices: 139 us -> 101 us  [swap(): return lax.ppermute(values, axis, [(i, i ^ distance) for i in range(count)])]
    gather x1 -> x0, local copies, waits for them, and re-layouts: 8.36 us -> none  [local(): outs_all = jnp.stack(outs)[dp_order]]
    unnamed x158 -> x139, local copies, waits for them, and re-layouts: 41.7 us -> 37.3 us
  transfers between devices with their start and end apart: 57 -> 57, of which waited for: 26 -> 21; matrix products, arithmetic and copies ran while one was open for 29% -> 32% of each run, Pallas kernels for 33% -> 35%
where the time goes in v5:
time: 710 us; the launch traced here: 699 us
  Pallas kernels  245 us (35%)
  waiting for transfers between devices  126 us (18%)
  local copies, waits for them, and re-layouts  111 us (16%)
  other arithmetic  74.9 us (11%)
  matrix products  66.3 us (9%)
  starting transfers between devices  52.3 us (7%)
  between operations  23.5 us (3%)
    pallas_call x4, Pallas kernels, run_experts(): pl.pallas_call(functools.partial(expert_kernel, len(kept)), grid_spec=plt...  172 us
    ppermute x51, waiting for transfers between devices, swap(): return lax.ppermute(values, axis, [(i, i ^ distance) for i in range(count)])  101 us
    ppermute x51, starting transfers between devices, swap(): return lax.ppermute(values, axis, [(i, i ^ distance) for i in range(count)])  51.6 us
    dot_general x16, matrix products, local(): lax.dot_general(a, b, (((0,), (0,)), ((), ())), preferred_element_type=f32)  45.6 us
    unnamed x139, local copies, waits for them, and re-layouts  37.3 us
    pallas_call x1, Pallas kernels, attend_back(): pl.pallas_call(functools.partial(attend_back_kernel, tile), grid=(heads,)...  23.8 us
    pallas_call x1, Pallas kernels, attend(): pl.pallas_call(functools.partial(attend_kernel, tile), grid=(heads,), in_...  23.7 us
    reduce_scatter x1, waiting for transfers between devices, local(): own_parts = lax.psum_scatter(stacked, 'dp', scatter_dimension=0)  15.8 us
  transfers between devices with their start and end apart: 57, of which 21 were waited for; matrix products, arithmetic and copies ran while one was open for 32% of the time, Pallas kernels for 35%

profile of v5, /device:TPU:0, one launch (start us, length us, event | category | flops | bytes accessed | tf_op | source)
XLA Modules:
  0.0 698.9 jit_solution(8039162987831678107)
XLA Ops:
  21.6 21.7 %collective-permute-done = bf16[256,2048]{1,0:T(8,128)(2,1)} collective-permute-done((bf16[256,2048]{1,0:T(8,128)(2,1)S(1)}, bf16[256,2048]{1,0:T(8,128)(2,1)}, u32[]{:S(2)}, u32[]{:S(2)}) %collective-permute-start) | collective-permute-done | bytes 1048608 | tf_op jit(solution)/shard_map/ppermute | solution.py:412
  75.6 5.8 collective-permute-done.2
  94.1 6.4 multiply_convert_fusion.1.reduced_ref
  100.4 9.5 %all-gather.12.cloned.1.call-done = bf16[24,64,2048]{2,1,0:T(8,128)(2,1)} async-done(((bf16[3,64,2048]{2,1,0:T(8,128)(2,1)}), bf16[24,64,2048]{2,1,0:T(8,128)(2,1)}) %all-gather.12.cloned.1.call-update) | async-done | bytes 6291472 | tf_op jit(solution)/shard_map/all_gather | solution.py:518
  110.0 12.9 %qkv_project.1.q_raw.k_raw.v_raw = f32[3,1024,512]{2,1,0:T(8,128)} custom-call(bf16[1024,2048]{1,0:T(8,128)(2,1)} %constant_dynamic-update-slice_fusion.x_ref, bf16[1024,384]{1,0:T(8,128)(2,1)} %multiply_convert_fusion.1.reduced_ref, bf16[8,3,64,2048]{3,2,1,0:T(8,128)(2,1)} %bitcast.323, bf16[3,512,128]{2,1,0:T(8,128)(2,1)} %bitcast.336), custom_call_target="tpu_custom_call" | custom-call | flops 6442450944 | bytes 16777216 | tf_op jit(solution)/shard_map/qkv_project/pallas_call | solution.py:213
  124.2 23.7 %attend.1 = (bf16[1024,512]{1,0:T(8,128)(2,1)}, bf16[1024,512]{1,0:T(8,128)(2,1)}, bf16[1024,512]{1,0:T(8,128)(2,1)}, bf16[1024,512]{1,0:T(8,128)(2,1)}, f32[4,1,1024]{2,1,0:T(1,128)}) custom-call(f32[3,1024,512]{2,1,0:T(8,128)} %qkv_project.1.q_raw.k_raw.v_raw, f32[3,1024,512]{2,1,0:T(8,128)} %qkv_project.1.q_raw.k_raw.v_raw, ...), custom_call_target="tpu_custom_call" | custom-call | flops 2147483648 | bytes 10485760 | tf_op jit(solution)/shard_map/attend/pallas_call | solution.py:100
  147.9 4.9 convolution_convert_fusion
  157.1 11.4 %collective-permute-done.10 = bf16[128,2176]{1,0:T(8,128)(2,1)S(1)} collective-permute-done((bf16[128,2176]{1,0:T(8,128)(2,1)S(1)}, bf16[128,2176]{1,0:T(8,128)(2,1)S(1)}, u32[]{:S(2)}, u32[]{:S(2)}) %collective-permute-start.10) | collective-permute-done | bytes 557088 | tf_op jit(solution)/shard_map/ppermute | solution.py:412
  172.2 8.3 %collective-permute-done.12 = bf16[128,2176]{1,0:T(8,128)(2,1)S(1)} collective-permute-done((bf16[128,2176]{1,0:T(8,128)(2,1)S(1)}, bf16[128,2176]{1,0:T(8,128)(2,1)S(1)}, u32[]{:S(2)}, u32[]{:S(2)}) %collective-permute-start.12) | collective-permute-done | bytes 557088 | tf_op jit(solution)/shard_map/ppermute | solution.py:412
  181.8 9.9 %collective-permute-done.11 = bf16[128,2176]{1,0:T(8,128)(2,1)S(1)} collective-permute-done((bf16[128,2176]{1,0:T(8,128)(2,1)S(1)}, bf16[128,2176]{1,0:T(8,128)(2,1)S(1)}, u32[]{:S(2)}, u32[]{:S(2)}) %collective-permute-start.11) | collective-permute-done | bytes 557088 | tf_op jit(solution)/shard_map/ppermute | solution.py:412
  201.2 43.0 %experts.4 = (bf16[8,256,2048]{2,1,0:T(8,128)(2,1)}, bf16[256,2048]{1,0:T(8,128)(2,1)}, bf16[256,2048]{1,0:T(8,128)(2,1)}, bf16[2,1152,2048]{2,1,0:T(8,128)(2,1)...) custom-call(s32[4]{0:T(128)} %add_add_fusion.3.which, ...), custom_call_target="tpu_custom_call" | custom-call | flops 1179648 | bytes 1179648 | tf_op jit(solution)/shard_map/experts/pallas_call | solution.py:381
  244.5 22.2 %collective-permute-done.14.refs_0_ = bf16[256,2048]{1,0:T(8,128)(2,1)} collective-permute-done((bf16[256,2048]{1,0:T(8,128)(2,1)S(1)}, bf16[256,2048]{1,0:T(8,128)(2,1)}, u32[]{:S(2)}, u32[]{:S(2)}) %collective-permute-start.14) | collective-permute-done | bytes 1048608 | tf_op jit(solution)/shard_map/ppermute | solution.py:412
  271.0 42.9 %experts.5 = (bf16[8,256,2048]{2,1,0:T(8,128)(2,1)}, bf16[256,2048]{1,0:T(8,128)(2,1)}, bf16[256,2048]{1,0:T(8,128)(2,1)}, bf16[2,1152,2048]{2,1,0:T(8,128)(2,1)...) custom-call(s32[4]{0:T(128)} %add_add_fusion.4.which, ...), custom_call_target="tpu_custom_call", output_to_operand_aliasing={{0}: (13, {}), {3}: (14, {}), {4}: (15, {}), {5}: (16, {}),... | custom-call | flops 1179648 | bytes 1179648 | tf_op jit(solution)/shard_map/experts/pallas_call | solution.py:381
  323.8 42.8 %experts.6 = (bf16[8,256,2048]{2,1,0:T(8,128)(2,1)}, bf16[256,2048]{1,0:T(8,128)(2,1)}, bf16[256,2048]{1,0:T(8,128)(2,1)}, bf16[2,1152,2048]{2,1,0:T(8,128)(2,1)...) custom-call(s32[4]{0:T(128)} %get-tuple-element.374.which, ...), custom_call_target="tpu_custom_call", output_to_operand_aliasing={{0}: (13, {}), {3}: (14, {}), {4}: (15, {}), {5}: (16, {}),... | custom-call | flops 1179648 | bytes 1179648 | tf_op jit(solution)/shard_map/experts/pallas_call | solution.py:381
  375.4 43.2 %experts.7 = (bf16[8,256,2048]{2,1,0:T(8,128)(2,1)}, bf16[256,2048]{1,0:T(8,128)(2,1)}, bf16[256,2048]{1,0:T(8,128)(2,1)}, bf16[2,1152,2048]{2,1,0:T(8,128)(2,1)...) custom-call(s32[4]{0:T(128)} %get-tuple-element.373.which, ...), custom_call_target="tpu_custom_call", output_to_operand_aliasing={{0}: (13, {}), {3}: (14, {}), {4}: (15, {}), {5}: (16, {}),... | custom-call | flops 1179648 | bytes 1179648 | tf_op jit(solution)/shard_map/experts/pallas_call | solution.py:381
  446.2 5.1 fusion.15
  458.0 3.9 convert_add_fusion.1
  480.0 5.1 fusion.18
  503.5 4.1 fusion.24
  534.6 5.0 collective-permute-done.34
  547.2 4.9 slice.561
  554.3 23.8 %attend_back.1 = (bf16[1024,512]{1,0:T(8,128)(2,1)}, bf16[1024,512]{1,0:T(8,128)(2,1)}, bf16[1024,512]{1,0:T(8,128)(2,1)}) custom-call(bf16[1024,512]{1,0:T(8,128)(2,1)} %get-tuple-element.239.query, bf16[1024,512]{1,0:T(8,128)(2,1)} %get-tuple-element.240.key, bf16[1024,512]{1,0:T(8,128)(2,1)} %get-tuple-element.241.value, ...), custom_call_target="tpu_custom_call" | custom-call | flops 524288 | bytes 524288 | tf_op jit(solution)/shard_map/attend_back/pallas_call | solution.py:168
  590.4 12.4 %qkv_back.1 = bf16[1024,2048]{1,0:T(8,128)(2,1)} custom-call(bf16[1024,512]{1,0:T(8,128)(2,1)} %get-tuple-element.263.a_ref, bf16[1024,512]{1,0:T(8,128)(2,1)} %get-tuple-element.264.b_ref, bf16[1024,512]{1,0:T(8,128)(2,1)} %get-tuple-element.265.c_ref, bf16[8,3,64,2048]{3,2,1,0:T(8,128)(2,1)} %bitcast.324), custom_call_target="tpu_custom_call" | custom-call | flops 2097152 | bytes 2097152 | tf_op jit(solution)/shard_map/qkv_back/pallas_call | solution.py:246
  670.1 15.8 %reduce-scatter.5.cloned.1.call-done = bf16[1,8,64,128]{3,2,1,0:T(8,128)(2,1)} async-done(((bf16[8,8,64,128]{3,2,1,0:T(8,128)(2,1)}), bf16[1,8,64,128]{3,2,1,0:T(8,128)(2,1)}) %reduce-scatter.5.cloned.1.call-update) | async-done | bytes 131088 | tf_op jit(solution)/shard_map/reduce_scatter | solution.py:703
  (420 shorter events, 286.5 us)
Async XLA Ops:
  7.2 37.6 %all-gather.10.cloned.1.call-start = ((), (), s32[]{:S(2)}) async-start(), calls=%async_computation.5 | async-start | bytes 1179648 | tf_op jit(solution)/shard_map/all_gather | solution.py:513
  13.5 96.5 %all-gather.12.cloned.1.call-start = ((), (), s32[]{:S(2)}) async-start(), calls=%async_computation.6 | async-start | bytes 7077888 | tf_op jit(solution)/shard_map/all_gather | solution.py:518
  17.1 26.2 %collective-permute-start = (bf16[256,2048]{1,0:T(8,128)(2,1)S(1)}, bf16[256,2048]{1,0:T(8,128)(2,1)}, u32[]{:S(2)}, u32[]{:S(2)}) collective-permute-start(bf16[256,2048]{1,0:T(8,128)(2,1)S(1)} %get-tuple-element.311), channel_id=1, source_target_pairs={{0,8},{8,0},{16,24},{24,16},{1,9},{9,1},{17,25},{25,17},{2,10},{10... | collective-permute-start | bytes 3145736 | tf_op jit(solution)/shard_map/ppermute | solution.py:412
  20.0 24.7 %collective-permute-start.1 = (bf16[256,2048]{1,0:T(8,128)(2,1)S(1)}, bf16[256,2048]{1,0:T(8,128)(2,1)}, u32[]{:S(2)}, u32[]{:S(2)}) collective-permute-start(bf16[256,2048]{1,0:T(8,128)(2,1)S(1)} %get-tuple-element.311), channel_id=1, source_target_pairs={{0,16},{8,24},{16,0},{24,8},{1,17},{9,25},{17,1},{25,9},{2,18},{10... | collective-permute-start | bytes 3145736 | tf_op jit(solution)/shard_map/ppermute | solution.py:412
  44.8 103.1 %all-gather.8.cloned.1.call-start = ((), (), s32[]{:S(2)}) async-start(), calls=%async_computation.2 | async-start | bytes 2506752 | tf_op jit(solution)/shard_map/all_gather | solution.py:564
  110.0 161.1 %all-gather.14.cloned.1.call-start = ((), (), s32[]{:S(2)}) async-start(), calls=%async_computation.7 | async-start | bytes 9437184 | tf_op jit(solution)/shard_map/all_gather | solution.py:568
  122.9 540.6 %reduce-scatter.3.cloned.1.call-start = ((), (), s32[]{:S(2)}) async-start(), calls=%async_computation.3 | async-start | bytes 9437184 | tf_op jit(solution)/shard_map/reduce_scatter | solution.py:625
  155.8 24.7 %collective-permute-start.12 = (bf16[128,2176]{1,0:T(8,128)(2,1)S(1)}, bf16[128,2176]{1,0:T(8,128)(2,1)S(1)}, u32[]{:S(2)}, u32[]{:S(2)}) collective-permute-start(bf16[128,2176]{1,0:T(8,128)(2,1)S(1)} %get-tuple-element.325), channel_id=1, source_target_pairs={{0,16},{8,24},{16,0},{24,8},{1,17},{9,25},{17,1},{25,9},{2,18},{10... | collective-permute-start | bytes 1671176 | tf_op jit(solution)/shard_map/ppermute | solution.py:412
  156.3 25.4 %collective-permute-start.8 = (bf16[128,2176]{1,0:T(8,128)(2,1)S(1)}, bf16[128,2176]{1,0:T(8,128)(2,1)S(1)}, u32[]{:S(2)}, u32[]{:S(2)}) collective-permute-start(bf16[128,2176]{1,0:T(8,128)(2,1)S(1)} %get-tuple-element.324), channel_id=1, source_target_pairs={{0,8},{8,0},{16,24},{24,16},{1,9},{9,1},{17,25},{25,17},{2,10},{10... | collective-permute-start | bytes 1671176 | tf_op jit(solution)/shard_map/ppermute | solution.py:412
  195.2 71.5 %collective-permute-start.14 = (bf16[256,2048]{1,0:T(8,128)(2,1)S(1)}, bf16[256,2048]{1,0:T(8,128)(2,1)}, u32[]{:S(2)}, u32[]{:S(2)}) collective-permute-start(bf16[256,2048]{1,0:T(8,128)(2,1)S(1)} %multiply_convert_fusion.refs_0_), channel_id=1, source_target_pairs={{0,4},{1,5},{2,6},{3,7},{4,0},{5,1},{6,2},{7,3},{8,12},{9,13},{10,... | collective-permute-start | bytes 3145736 | tf_op jit(solution)/shard_map/ppermute | solution.py:412
  269.7 44.4 %collective-permute-start.19 = (bf16[256,2048]{1,0:T(8,128)(2,1)S(1)}, bf16[256,2048]{1,0:T(8,128)(2,1)}, u32[]{:S(2)}, u32[]{:S(2)}) collective-permute-start(bf16[256,2048]{1,0:T(8,128)(2,1)S(1)} %copy-done.12), channel_id=1, source_target_pairs={{0,6},{1,7},{2,4},{3,5},{4,2},{5,3},{6,0},{7,1},{8,14},{9,15},{10,... | collective-permute-start | bytes 3145736 | tf_op jit(solution)/shard_map/ppermute | solution.py:412
  319.5 47.2 %collective-permute-start.22 = (bf16[256,2048]{1,0:T(8,128)(2,1)S(1)}, bf16[256,2048]{1,0:T(8,128)(2,1)}, u32[]{:S(2)}, u32[]{:S(2)}) collective-permute-start(bf16[256,2048]{1,0:T(8,128)(2,1)S(1)} %copy-done.12), channel_id=1, source_target_pairs={{0,2},{1,3},{2,0},{3,1},{4,6},{5,7},{6,4},{7,5},{8,10},{9,11},{10,... | collective-permute-start | bytes 3145736 | tf_op jit(solution)/shard_map/ppermute | solution.py:412
  320.4 48.9 %collective-permute-start.23 = (bf16[256,2048]{1,0:T(8,128)(2,1)}, bf16[256,2048]{1,0:T(8,128)(2,1)}, u32[]{:S(2)}, u32[]{:S(2)}) collective-permute-start(bf16[256,2048]{1,0:T(8,128)(2,1)} %add_convert_fusion.3), channel_id=1, source_target_pairs={{0,4},{1,5},{2,6},{3,7},{4,0},{5,1},{6,2},{7,3},{8,12},{9,13},{10,... | collective-permute-start | bytes 3145736 | tf_op jit(solution)/shard_map/ppermute | solution.py:412
  372.3 46.4 %collective-permute-start.26 = (bf16[256,2048]{1,0:T(8,128)(2,1)}, bf16[256,2048]{1,0:T(8,128)(2,1)}, u32[]{:S(2)}, u32[]{:S(2)}) collective-permute-start(bf16[256,2048]{1,0:T(8,128)(2,1)} %add_convert_fusion.2), channel_id=1, source_target_pairs={{0,6},{1,7},{2,4},{3,5},{4,2},{5,3},{6,0},{7,1},{8,14},{9,15},{10,... | collective-permute-start | bytes 3145736 | tf_op jit(solution)/shard_map/ppermute | solution.py:412
  427.6 30.3 %collective-permute-start.28 = (bf16[256,2048]{1,0:T(8,128)(2,1)}, bf16[256,2048]{1,0:T(8,128)(2,1)}, u32[]{:S(2)}, u32[]{:S(2)}) collective-permute-start(bf16[256,2048]{1,0:T(8,128)(2,1)} %add_convert_fusion.1), channel_id=1, source_target_pairs={{0,2},{1,3},{2,0},{3,1},{4,6},{5,7},{6,4},{7,5},{8,10},{9,11},{10,... | collective-permute-start | bytes 3145736 | tf_op jit(solution)/shard_map/ppermute | solution.py:412
  466.7 28.3 %collective-permute-start.29 = (bf16[256,2304]{1,0:T(8,128)(2,1)S(1)}, bf16[256,2304]{1,0:T(8,128)(2,1)}, u32[]{:S(2)}, u32[]{:S(2)}) collective-permute-start(bf16[256,2304]{1,0:T(8,128)(2,1)S(1)} %pad_maximum_fusion.4), channel_id=1, source_target_pairs={{0,8},{8,0},{16,24},{24,16},{1,9},{9,1},{17,25},{25,17},{2,10},{10... | collective-permute-start | bytes 3538952 | tf_op jit(solution)/shard_map/ppermute | solution.py:412
  468.2 27.9 %collective-permute-start.30 = (bf16[256,2304]{1,0:T(8,128)(2,1)S(1)}, bf16[256,2304]{1,0:T(8,128)(2,1)}, u32[]{:S(2)}, u32[]{:S(2)}) collective-permute-start(bf16[256,2304]{1,0:T(8,128)(2,1)S(1)} %pad_maximum_fusion.4), channel_id=1, source_target_pairs={{0,16},{8,24},{16,0},{24,8},{1,17},{9,25},{17,1},{25,9},{2,18},{10... | collective-permute-start | bytes 3538952 | tf_op jit(solution)/shard_map/ppermute | solution.py:412
  487.7 198.2 %reduce-scatter.5.cloned.1.call-start = ((), (), s32[]{:S(2)}) async-start(), calls=%async_computation.4 | async-start | bytes 1179648 | tf_op jit(solution)/shard_map/reduce_scatter | solution.py:703
  525.3 52.7 %collective-permute-start.33 = (bf16[2304,128]{1,0:T(8,128)(2,1)}, bf16[2304,128]{1,0:T(8,128)(2,1)}, u32[]{:S(2)}, u32[]{:S(2)}) collective-permute-start(bf16[2304,128]{1,0:T(8,128)(2,1)} %get-tuple-element.316), channel_id=1, source_target_pairs={{0,8},{8,0},{16,24},{24,16},{1,9},{9,1},{17,25},{25,17},{2,10},{10... | collective-permute-start | bytes 1769480 | tf_op jit(solution)/shard_map/ppermute | solution.py:412
  525.9 52.2 %collective-permute-start.37 = (bf16[2304,128]{1,0:T(8,128)(2,1)}, bf16[2304,128]{1,0:T(8,128)(2,1)}, u32[]{:S(2)}, u32[]{:S(2)}) collective-permute-start(bf16[2304,128]{1,0:T(8,128)(2,1)} %get-tuple-element.319), channel_id=1, source_target_pairs={{0,16},{8,24},{16,0},{24,8},{1,17},{9,25},{17,1},{25,9},{2,18},{10... | collective-permute-start | bytes 1769480 | tf_op jit(solution)/shard_map/ppermute | solution.py:412
  542.4 35.7 %collective-permute-start.36 = (bf16[2304,128]{1,0:T(8,128)(2,1)}, bf16[2304,128]{1,0:T(8,128)(2,1)S(1)}, u32[]{:S(2)}, u32[]{:S(2)}) collective-permute-start(bf16[2304,128]{1,0:T(8,128)(2,1)} %get-tuple-element.237), channel_id=1, source_target_pairs={{0,16},{8,24},{16,0},{24,8},{1,17},{9,25},{17,1},{25,9},{2,18},{10... | collective-permute-start | bytes 1769480 | tf_op jit(solution)/shard_map/ppermute | solution.py:412
  542.9 35.2 %collective-permute-start.38 = (bf16[2304,128]{1,0:T(8,128)(2,1)}, bf16[2304,128]{1,0:T(8,128)(2,1)S(1)}, u32[]{:S(2)}, u32[]{:S(2)}) collective-permute-start(bf16[2304,128]{1,0:T(8,128)(2,1)} %get-tuple-element.238), channel_id=1, source_target_pairs={{0,8},{8,0},{16,24},{24,16},{1,9},{9,1},{17,25},{25,17},{2,10},{10... | collective-permute-start | bytes 1769480 | tf_op jit(solution)/shard_map/ppermute | solution.py:412
  622.7 37.0 %collective-permute-start.45 = (bf16[128,2048]{1,0:T(8,128)(2,1)}, bf16[128,2048]{1,0:T(8,128)(2,1)}, u32[]{:S(2)}, u32[]{:S(2)}) collective-permute-start(bf16[128,2048]{1,0:T(8,128)(2,1)} %get-tuple-element.332), channel_id=1, source_target_pairs={{0,8},{8,0},{16,24},{24,16},{1,9},{9,1},{17,25},{25,17},{2,10},{10... | collective-permute-start | bytes 1572872 | tf_op jit(solution)/shard_map/ppermute | solution.py:412
  623.4 36.3 %collective-permute-start.49 = (bf16[128,2048]{1,0:T(8,128)(2,1)}, bf16[128,2048]{1,0:T(8,128)(2,1)}, u32[]{:S(2)}, u32[]{:S(2)}) collective-permute-start(bf16[128,2048]{1,0:T(8,128)(2,1)} %get-tuple-element.333), channel_id=1, source_target_pairs={{0,16},{8,24},{16,0},{24,8},{1,17},{9,25},{17,1},{25,9},{2,18},{10... | collective-permute-start | bytes 1572872 | tf_op jit(solution)/shard_map/ppermute | solution.py:412
  (89 other events, 1205.5 us)
Sparse Core Ops, SparseCore 0:
  13.6 24.9 all-gather.9
  44.9 65.0 all-gather.11
  111.6 28.8 all-gather.7
  142.0 115.6 all-gather.13
  487.8 86.7 reduce-scatter.2
  656.1 29.8 reduce-scatter.4

commit v6 on v5

--- a/solution.py
+++ b/solution.py
@@ -346,7 +346,7 @@
                     result[...] = total[...].astype(low)
 
 
-def run_experts(chunk, which, x_pair, g_all, pick, pick_t, slot, weights, kept):
+def run_experts(which, x_pair, g_all, pick, pick_t, slot, weights, kept):
     w_in, w_down, a_in, b_in, a_down, b_down = weights
     experts, unused, width, ff = w_in.shape
     unused, dp_count, cap, own_rows = pick.shape
@@ -358,18 +358,18 @@
     one = pl.Buffered(1)
     token = pl.BlockSpec((own_rows, width), lambda e, f, w: (0, 0), pipeline_mode=one)
     stored = [
-        ((experts, dp_count * cap, width), (1, rows, width), lambda e, f, w: (e, chunk, 0)),
-        ((experts, dp_count * cap, width), (1, rows, width), lambda e, f, w: (e, chunk, 0)),
-        ((experts, dp_count * cap, ff), (1, rows, tile), lambda e, f, w: (e, chunk, f)),
-        ((experts, dp_count * cap, ff), (1, rows, tile), lambda e, f, w: (e, chunk, f)),
-        ((experts, dp_count * cap, ff), (1, rows, tile), lambda e, f, w: (e, chunk, f)),
-        ((experts, dp_count * cap, 6 * rank), (1, rows, 6 * rank), lambda e, f, w: (e, chunk, 0)),
+        ((experts, dp_count * cap, width), (1, rows, width), lambda e, f, w: (e, w[4], 0)),
+        ((experts, dp_count * cap, width), (1, rows, width), lambda e, f, w: (e, w[4], 0)),
+        ((experts, dp_count * cap, ff), (1, rows, tile), lambda e, f, w: (e, w[4], f)),
+        ((experts, dp_count * cap, ff), (1, rows, tile), lambda e, f, w: (e, w[4], f)),
+        ((experts, dp_count * cap, ff), (1, rows, tile), lambda e, f, w: (e, w[4], f)),
+        ((experts, dp_count * cap, 6 * rank), (1, rows, 6 * rank), lambda e, f, w: (e, w[4], 0)),
     ]
     in_specs = [
         token, token, pl.BlockSpec((2, own_rows, width), lambda e, f, w: (w[0], 0, 0), pipeline_mode=one),
-        pl.BlockSpec((1, 2, cap, own_rows), lambda e, f, w: (e, chunk, 0, 0)),
-        pl.BlockSpec((1, 2, own_rows, cap), lambda e, f, w: (e, chunk, 0, 0)),
-        pl.BlockSpec((1, rows, 2), lambda e, f, w: (e, chunk, 0)),
+        pl.BlockSpec((1, 2, cap, own_rows), lambda e, f, w: (e, w[4], 0, 0)),
+        pl.BlockSpec((1, 2, own_rows, cap), lambda e, f, w: (e, w[4], 0, 0)),
+        pl.BlockSpec((1, rows, 2), lambda e, f, w: (e, w[4], 0)),
         pl.BlockSpec((1, 2, width, tile), lambda e, f, w: (e, 0, 0, f)),
         pl.BlockSpec((1, tile, width), lambda e, f, w: (e, f, 0)),
         pl.BlockSpec((1, 2, width, rank), lambda e, f, w: (e, 0, 0, 0)),
@@ -408,6 +408,42 @@
     return results[1:3], [results[0]] + list(results[3:])
 
 
+def adapter_kernel(which, xs, ps, act, gate, up, reds, out):
+    rank = out.shape[3]
+    red = [reds[0, :, i * rank : (i + 1) * rank] for i in range(6)]
+    into = dot_tn(xs[0], reds[0, :, 3 * rank : 5 * rank])
+    parts = [into[:, :rank], into[:, rank:], dot_tn(act[0], red[5])]
+    for wide in (dot_tn(red[0], gate[0]), dot_tn(red[1], up[0]), dot_tn(red[2], ps[0])):
+        parts += [wide[:, i : i + rank] for i in range(0, wide.shape[1], rank)]
+    start = 0
+    for part in parts:
+        out[0, 0, start : start + part.shape[0], :] = part.astype(jnp.bfloat16)
+        start += part.shape[0]
+
+
+def adapter_grads(kept, order):
+    xs, ps, act, gate, up, reds = kept
+    experts, rows, width = xs.shape
+    ff = act.shape[2]
+    n = order.shape[0]
+    rank = reds.shape[2] // 6
+    total = (3 * width + 3 * ff) // n
+    wide = pl.BlockSpec((1, rows, width // n), lambda e, k, w: (e, 0, w[k]))
+    narrow = pl.BlockSpec((1, rows, ff // n), lambda e, k, w: (e, 0, w[k]))
+    return pl.pallas_call(
+        adapter_kernel,
+        grid_spec=pltpu.PrefetchScalarGridSpec(
+            num_scalar_prefetch=1,
+            grid=(experts, n),
+            in_specs=[wide, wide, narrow, narrow, narrow, pl.BlockSpec((1, rows, 6 * rank), lambda e, k, w: (e, 0, 0))],
+            out_specs=pl.BlockSpec((1, 1, total, rank), lambda e, k, w: (k, e, 0, 0)),
+        ),
+        out_shape=jax.ShapeDtypeStruct((n, experts, total, rank), jnp.bfloat16),
+        cost_estimate=pl.CostEstimate(flops=rows * width, bytes_accessed=rows * width, transcendentals=0),
+        name="adapter_grads",
+    )(order, xs, ps, act, gate, up, reds)
+
+
 def swap(values, axis, distance, count):
     return lax.ppermute(values, axis, [(i, i ^ distance) for i in range(count)])
 
@@ -425,27 +461,34 @@
     return [values, one, two] + [swap(values, axis, k, count) for k in range(3, count)]
 
 
-def collect(blocks, axis, count, cover=None):
+def collect_begin(blocks, axis, count):
+    if count == 4 and blocks[0].size >= half_from:
+        half = blocks[0].shape[0] // 2
+        return [
+            swap(blocks[3][:half], axis, 1, count),
+            swap(blocks[3][half:], axis, 2, count),
+            swap(blocks[1][:half], axis, 1, count),
+            swap(blocks[2][half:], axis, 2, count),
+        ]
+    return [swap(blocks[k], axis, k, count) for k in range(1, count)]
+
+
+def collect_end(blocks, arrived, axis, count):
     f32 = jnp.float32
     if count == 4 and blocks[0].size >= half_from:
         half = blocks[0].shape[0] // 2
-        over_one = swap(blocks[3][:half], axis, 1, count)
-        over_two = swap(blocks[3][half:], axis, 2, count)
-        top = blocks[0][:half].astype(f32) + swap(blocks[1][:half], axis, 1, count).astype(f32)
-        low = blocks[0][half:].astype(f32) + swap(blocks[2][half:], axis, 2, count).astype(f32)
-        if cover is not None:
-            over_one, over_two, cover = pin(over_one, over_two, cover)
+        over_one, over_two, from_one, from_two = arrived
         to_two = (blocks[2][:half].astype(f32) + over_one.astype(f32)).astype(blocks[2].dtype)
         to_one = (blocks[1][half:].astype(f32) + over_two.astype(f32)).astype(blocks[1].dtype)
         to_two, to_one = pin(to_two, to_one)
-        top = top + swap(to_two, axis, 2, count).astype(f32)
-        low = low + swap(to_one, axis, 1, count).astype(f32)
-        total = jnp.concatenate([top, low], axis=0)
-    else:
-        total = blocks[0].astype(f32)
-        for k in range(1, count):
-            total = total + swap(blocks[k], axis, k, count).astype(f32)
-    return total if cover is None else (total, cover)
+        top = blocks[0][:half].astype(f32) + from_one.astype(f32) + swap(to_two, axis, 2, count).astype(f32)
+        low = blocks[0][half:].astype(f32) + from_two.astype(f32) + swap(to_one, axis, 1, count).astype(f32)
+        return jnp.concatenate([top, low], axis=0)
+    return sum((x.astype(f32) for x in arrived), blocks[0].astype(f32))
+
+
+def collect(blocks, axis, count):
+    return collect_end(blocks, collect_begin(blocks, axis, count), axis, count)
 
 
 def pin(*values):
@@ -604,9 +647,9 @@
                 flying = swap(leaving, "dp", 2 * turns[i - 1], dp_count)
         block = lax.shift_right_logical(d, 1) ^ c
         place = d & 1
-        which = jnp.stack([block, place, block, place] if c else [0 * d, 0 * d, block, place]).astype(jnp.int32)
+        which = jnp.stack(([block, place] if c else [0 * d, 0 * d]) + [block, place, 0 * d + c]).astype(jnp.int32)
         (back, back_other), kept = run_experts(
-            c, which, (here, other), grad_got if c else grad_own, pick, pick_t, slot, weights, kept
+            which, (here, other), grad_got if c else grad_own, pick, pick_t, slot, weights, kept
         )
         if i == chips - 1 and flying is not None:
             flying, back_other = pin(flying, back_other)
@@ -618,7 +661,10 @@
     outs_all, *kept = kept
     leaving, *kept = pin(leaving, *kept)
     flying = swap(leaving, "dp", 2 * turns[-1], dp_count)
-    flying, *kept_later = pin(flying, *kept)
+    flat = adapter_grads(kept, order)
+    expert_arrived = collect_begin([flat[k] for k in range(n)], "seq", n)
+    flat, flying = pin(flat, flying)
+    expert_terms = [flat[k] for k in range(n)]
     grad_normed_ffn = grad_normed_ffn + flying.astype(f32)
 
     outs_all, grad_normed_ffn = pin(outs_all, grad_normed_ffn)
@@ -629,39 +675,16 @@
     grad_hidden_low = grad_hidden.astype(low)
     grad_reduced_output = (own_mask * dot(grad_hidden_low, upt_output)).astype(low)
     grad_pack = jnp.concatenate([grad_hidden_low, grad_reduced_output, output_reduced], axis=1)
-    grad_close = near(grad_pack, "seq", n)
-    *grad_close, xs, ps, act_rows, gate_rows, up_rows, reds = pin(*grad_close, *kept_later)
-    kept_last = (xs, ps, act_rows, gate_rows, up_rows, reds)
-    flat = []
-    for e in range(local_count):
-        xs, unused, unused2, gate_rows, up_rows, reds = kept if e == 0 else kept_later
-        unused, ps, act_rows, unused2, unused3, reds_last = kept if e == 0 else kept_last
-        red = [(reds if i in (0, 1) else reds_last)[e][:, i * rank_columns : (i + 1) * rank_columns] for i in range(6)]
-        terms = [
-            (reds[e][:, 3 * rank_columns : 5 * rank_columns], xs[e]),
-            (red[0], gate_rows[e]),
-            (red[1], up_rows[e]),
-            (red[5], act_rows[e]),
-            (red[2], ps[e]),
-        ]
-        flat += [dot_l(a, b).astype(low).reshape(-1, rank_columns, b.shape[1]) for a, b in terms]
-    widths = [(x.shape[0], x.shape[2] // n) for x in flat]
-    flat = jnp.concatenate(
-        [
-            x.reshape(x.shape[0], rank_columns, n, -1).transpose(2, 0, 1, 3).reshape(n, -1)
-            for x in flat
-        ],
-        axis=1,
-    ).reshape(n, -1, rank_columns)
-    grad_packs = spread(grad_pack, "seq", n, grad_close)
-    flat, *grad_packs = pin(flat, *grad_packs)
-    expert_terms = [lax.dynamic_index_in_dim(flat, order[k], 0, keepdims=False) for k in range(n)]
+    grad_pack, *expert_arrived = pin(grad_pack, *expert_arrived)
+    grad_packs = spread(grad_pack, "seq", n)
+    expert_arrived = list(pin(*expert_arrived, *grad_packs))
+    grad_packs = expert_arrived[-n:]
+    expert_sum = collect_end(expert_terms, expert_arrived[:-n], "seq", n)
     grad_pack_all = jnp.concatenate(grad_packs, axis=0)
     grad_all = grad_pack_all[:, :full_width]
     grad_reduced_all = grad_pack_all[:, full_width : full_width + rank_columns]
     output_reduced_all = grad_pack_all[:, full_width + rank_columns :]
     grad_mixed_group = dot_t(grad_pack_all[:, : full_width + rank_columns], out_maps).astype(low)
-    expert_sum, grad_mixed_group = collect(expert_terms, "seq", n, grad_mixed_group)
     grad_cols = lax.dynamic_slice_in_dim(grad_all, group_start, group_width, 1)
     grad_upt_output = dot_l(grad_cols, output_reduced_all)
     grad_down_output = dot_l(mixed_group, grad_reduced_all)
@@ -686,38 +709,40 @@
     grad_reduced, *grad_raw_late = pin(grad_reduced, *grad_raw_list)
     grad_reduced_full = jnp.concatenate(spread(grad_reduced, "seq", n), axis=0)
     partial_normed = qkv_back(grad_raw_list, w_group).reshape(n, own_rows, full_width)
-    partial_normed, grad_reduced_full, expert_sum = pin(partial_normed, grad_reduced_full, expert_sum)
-    summed_back = collect([partial_normed[k] for k in range(n)], "seq", n)
-    summed_back, mixture, hidden = pin(summed_back, mixture, hidden)
-    layer_output = (hidden + mixture.astype(f32)).astype(low)[None]
-    grad_normed = summed_back + dot_t(grad_reduced, down_cat)
-    unused_input, pull_input = jax.vjp(lambda values: rms_scale(values, gain_attention), tokens)
-    input_grad = (grad_hidden + pull_input(grad_normed)[0]).astype(low)[None]
-
+    partial_normed, grad_reduced = pin(partial_normed, grad_reduced)
     grad_upt = [dot_l(grad_raw_late[m], reduced_list[m]) for m in range(3)]
     normed_cols = lax.dynamic_slice_in_dim(normed_all, group_start, group_width, 1)
     grad_down_cat = dot_l(normed_cols, grad_reduced_full)
     parts = [grad_down_cat[:, m * rank_columns : (m + 1) * rank_columns] for m in range(3)]
     parts += [grad_down_output] + grad_upt + [grad_upt_output]
     stacked = jnp.stack([x.astype(low).reshape(dp_count, piece, rank_columns) for x in parts], axis=1)
+    normed_terms = [partial_normed[k] for k in range(n)]
+    arrived = collect_begin(normed_terms, "seq", n)
+    stacked, *arrived = pin(stacked, *arrived)
+    summed_back = collect_end(normed_terms, arrived, "seq", n)
+    summed_back, mixture, hidden = pin(summed_back, mixture, hidden)
+    layer_output = (hidden + mixture.astype(f32)).astype(low)[None]
+    grad_normed = summed_back + dot_t(grad_reduced, down_cat)
+    unused_input, pull_input = jax.vjp(lambda values: rms_scale(values, gain_attention), tokens)
+    input_grad = (grad_hidden + pull_input(grad_normed)[0]).astype(low)[None]
+
+    stacked, expert_sum = pin(stacked, expert_sum)
     own_parts = lax.psum_scatter(stacked, "dp", scatter_dimension=0)
     own_parts, input_grad = pin(own_parts, input_grad)
     own_parts = own_parts.astype(f32)
     grad_a_attention = own_parts[0:4]
     grad_b_attention = jnp.swapaxes(own_parts[4:8], 1, 2)
 
-    flat = expert_sum.reshape(-1)
-    pieces = []
-    start = 0
-    for count, width in widths:
-        size = count * rank_columns * width
-        pieces.append(flat[start : start + size].reshape(count, rank_columns, width))
-        start += size
-    per = [pieces[5 * e : 5 * e + 5] for e in range(local_count)]
-    grad_a_in = jnp.stack([jnp.swapaxes(p[0], 1, 2) for p in per])
-    grad_b_in = jnp.stack([jnp.concatenate([p[1], p[2]], axis=0) for p in per])
-    grad_a_down = jnp.stack([p[3][0].T for p in per])
-    grad_b_down = jnp.stack([p[4][0] for p in per])
+    own_width = full_width // n
+    own_ff = expert_w_down.shape[1] // n
+    columns = lambda x, count: jnp.swapaxes(x.reshape(local_count, count, -1, rank_columns, rank_columns), 2, 3).reshape(
+        local_count, count, rank_columns, -1
+    )
+    ends = [2 * own_width, 2 * own_width + own_ff, 2 * own_width + 3 * own_ff]
+    grad_a_in = expert_sum[:, : ends[0]].reshape(local_count, 2, own_width, rank_columns)
+    grad_a_down = expert_sum[:, ends[0] : ends[1]]
+    grad_b_in = columns(expert_sum[:, ends[1] : ends[2]], 2)
+    grad_b_down = columns(expert_sum[:, ends[2] :], 1)[:, 0]
     return (
         layer_output,
         input_grad,

time: 710 us -> 690 us (0.972)
  waiting for transfers between devices: 126 us -> 185 us
  local copies, waits for them, and re-layouts: 111 us -> 63.6 us
  matrix products: 66.3 us -> 29.1 us
  Pallas kernels: 245 us -> 266 us
  between operations: 23.5 us -> 15.5 us
    ppermute x51, waiting for transfers between devices: 101 us -> 165 us  [swap(): return lax.ppermute(values, axis, [(i, i ^ distance) for i in range(count)])]
    dot_general x16 -> x6, matrix products: 45.6 us -> 8.25 us  [local(): lax.dot_general(a, b, (((0,), (0,)), ((), ())), preferred_element_type=f32)]
    unnamed x139 -> x135, local copies, waits for them, and re-layouts: 37.3 us -> 15 us
    pallas_call x0 -> x1, Pallas kernels: none -> 18.4 us  [adapter_grads(): pl.pallas_call(adapter_kernel, grid_spec=pltpu.PrefetchScalarGridSpec(num...]
    another operation x15 -> x5, local copies, waits for them, and re-layouts: 17.4 us -> 2.75 us  [the longest x3 1.74 us: local(): jnp.stack(([block, place] if c else [0 * d, 0 * d]) + [block, place, 0 *...]
  transfers between devices with their start and end apart: 57 -> 57, of which waited for: 21 -> 29; matrix products, arithmetic and copies ran while one was open for 32% -> 20% of each run, Pallas kernels for 35% -> 39%
where the time goes in v6:
time: 690 us; the launch traced here: 680 us
  Pallas kernels  266 us (39%)
  waiting for transfers between devices  185 us (27%)
  other arithmetic  69.1 us (10%)
  local copies, waits for them, and re-layouts  63.6 us (9%)
  starting transfers between devices  52 us (8%)
  matrix products  29.1 us (4%)
  between operations  15.5 us (2%)
    pallas_call x4, Pallas kernels, run_experts(): pl.pallas_call(functools.partial(expert_kernel, len(kept)), grid_spec=plt...  175 us
    ppermute x51, waiting for transfers between devices, swap(): return lax.ppermute(values, axis, [(i, i ^ distance) for i in range(count)])  165 us
    ppermute x51, starting transfers between devices, swap(): return lax.ppermute(values, axis, [(i, i ^ distance) for i in range(count)])  51.1 us
    pallas_call x1, Pallas kernels, attend(): pl.pallas_call(functools.partial(attend_kernel, tile), grid=(heads,), in_...  23.7 us
    pallas_call x1, Pallas kernels, attend_back(): pl.pallas_call(functools.partial(attend_back_kernel, tile), grid=(heads,)...  23.7 us
    pallas_call x1, Pallas kernels, adapter_grads(): pl.pallas_call(adapter_kernel, grid_spec=pltpu.PrefetchScalarGridSpec(num...  18.4 us
    unnamed x135, local copies, waits for them, and re-layouts  15 us
    reduce_scatter x1, waiting for transfers between devices, local(): own_parts = lax.psum_scatter(stacked, 'dp', scatter_dimension=0)  14.8 us
  transfers between devices with their start and end apart: 57, of which 29 were waited for; matrix products, arithmetic and copies ran while one was open for 20% of the time, Pallas kernels for 39%

profile of v6, /device:TPU:0, one launch (start us, length us, event | category | flops | bytes accessed | tf_op | source)
XLA Modules:
  0.0 680.0 jit_solution(17307040984506850058)
XLA Ops:
  22.1 21.6 %collective-permute-done = bf16[256,2048]{1,0:T(8,128)(2,1)S(1)} collective-permute-done((bf16[256,2048]{1,0:T(8,128)(2,1)S(1)}, bf16[256,2048]{1,0:T(8,128)(2,1)S(1)}, u32[]{:S(2)}, u32[]{:S(2)}) %collective-permute-start) | collective-permute-done | bytes 1048608 | tf_op jit(solution)/shard_map/ppermute | solution.py:448
  99.2 6.5 multiply_convert_fusion.1.reduced_ref
  105.7 4.8 all-gather.12.cloned.1.call-done
  110.5 12.8 %qkv_project.1.q_raw.k_raw.v_raw = f32[3,1024,512]{2,1,0:T(8,128)} custom-call(bf16[1024,2048]{1,0:T(8,128)(2,1)} %constant_dynamic-update-slice_fusion.x_ref, bf16[1024,384]{1,0:T(8,128)(2,1)} %multiply_convert_fusion.1.reduced_ref, bf16[8,3,64,2048]{3,2,1,0:T(8,128)(2,1)} %bitcast.214, bf16[3,512,128]{2,1,0:T(8,128)(2,1)} %bitcast.223), custom_call_target="tpu_custom_call" | custom-call | flops 6442450944 | bytes 16777216 | tf_op jit(solution)/shard_map/qkv_project/pallas_call | solution.py:213
  125.0 23.7 %attend.1 = (bf16[1024,512]{1,0:T(8,128)(2,1)}, bf16[1024,512]{1,0:T(8,128)(2,1)}, bf16[1024,512]{1,0:T(8,128)(2,1)}, bf16[1024,512]{1,0:T(8,128)(2,1)}, f32[4,1,1024]{2,1,0:T(1,128)}) custom-call(f32[3,1024,512]{2,1,0:T(8,128)} %qkv_project.1.q_raw.k_raw.v_raw, f32[3,1024,512]{2,1,0:T(8,128)} %qkv_project.1.q_raw.k_raw.v_raw, ...), custom_call_target="tpu_custom_call" | custom-call | flops 2147483648 | bytes 10485760 | tf_op jit(solution)/shard_map/attend/pallas_call | solution.py:100
  148.7 4.9 convolution_convert_fusion
  157.9 11.4 %collective-permute-done.10 = bf16[128,2176]{1,0:T(8,128)(2,1)S(1)} collective-permute-done((bf16[128,2176]{1,0:T(8,128)(2,1)S(1)}, bf16[128,2176]{1,0:T(8,128)(2,1)S(1)}, u32[]{:S(2)}, u32[]{:S(2)}) %collective-permute-start.10) | collective-permute-done | bytes 557088 | tf_op jit(solution)/shard_map/ppermute | solution.py:448
  173.0 8.2 %collective-permute-done.12 = bf16[128,2176]{1,0:T(8,128)(2,1)S(1)} collective-permute-done((bf16[128,2176]{1,0:T(8,128)(2,1)S(1)}, bf16[128,2176]{1,0:T(8,128)(2,1)S(1)}, u32[]{:S(2)}, u32[]{:S(2)}) %collective-permute-start.12) | collective-permute-done | bytes 557088 | tf_op jit(solution)/shard_map/ppermute | solution.py:448
  182.6 9.9 %collective-permute-done.11 = bf16[128,2176]{1,0:T(8,128)(2,1)S(1)} collective-permute-done((bf16[128,2176]{1,0:T(8,128)(2,1)S(1)}, bf16[128,2176]{1,0:T(8,128)(2,1)S(1)}, u32[]{:S(2)}, u32[]{:S(2)}) %collective-permute-start.11) | collective-permute-done | bytes 557088 | tf_op jit(solution)/shard_map/ppermute | solution.py:448
  202.2 43.6 %experts.4 = (bf16[8,256,2048]{2,1,0:T(8,128)(2,1)}, bf16[256,2048]{1,0:T(8,128)(2,1)}, bf16[256,2048]{1,0:T(8,128)(2,1)}, bf16[2,1152,2048]{2,1,0:T(8,128)(2,1)...) custom-call(s32[5]{0:T(128)} %pad_add_fusion.which, ...), custom_call_target="tpu_custom_call" | custom-call | flops 1179648 | bytes 1179648 | tf_op jit(solution)/shard_map/experts/pallas_call | solution.py:381
  246.0 21.2 %collective-permute-done.14.refs_0_ = bf16[256,2048]{1,0:T(8,128)(2,1)} collective-permute-done((bf16[256,2048]{1,0:T(8,128)(2,1)S(1)}, bf16[256,2048]{1,0:T(8,128)(2,1)}, u32[]{:S(2)}, u32[]{:S(2)}) %collective-permute-start.14) | collective-permute-done | bytes 1048608 | tf_op jit(solution)/shard_map/ppermute | solution.py:448
  271.4 43.7 %experts.5 = (bf16[8,256,2048]{2,1,0:T(8,128)(2,1)}, bf16[256,2048]{1,0:T(8,128)(2,1)}, bf16[256,2048]{1,0:T(8,128)(2,1)}, bf16[2,1152,2048]{2,1,0:T(8,128)(2,1)...) custom-call(s32[5]{0:T(128)} %stack.85.which, ...), custom_call_target="tpu_custom_call", output_to_operand_aliasing={{0}: (13, {}), {3}: (14, {}), {4}: (15, {}), {5}: (16, {}),... | custom-call | flops 1179648 | bytes 1179648 | tf_op jit(solution)/shard_map/experts/pallas_call | solution.py:381
  325.2 43.9 %experts.6 = (bf16[8,256,2048]{2,1,0:T(8,128)(2,1)}, bf16[256,2048]{1,0:T(8,128)(2,1)}, bf16[256,2048]{1,0:T(8,128)(2,1)}, bf16[2,1152,2048]{2,1,0:T(8,128)(2,1)...) custom-call(s32[5]{0:T(128)} %stack.87.which, ...), custom_call_target="tpu_custom_call", output_to_operand_aliasing={{0}: (13, {}), {3}: (14, {}), {4}: (15, {}), {5}: (16, {}),... | custom-call | flops 1179648 | bytes 1179648 | tf_op jit(solution)/shard_map/experts/pallas_call | solution.py:381
  377.4 43.7 %experts.7 = (bf16[8,256,2048]{2,1,0:T(8,128)(2,1)}, bf16[256,2048]{1,0:T(8,128)(2,1)}, bf16[256,2048]{1,0:T(8,128)(2,1)}, bf16[2,1152,2048]{2,1,0:T(8,128)(2,1)...) custom-call(s32[5]{0:T(128)} %stack.71.which, ...), custom_call_target="tpu_custom_call", output_to_operand_aliasing={{0}: (13, {}), {3}: (14, {}), {4}: (15, {}), {5}: (16, {}),... | custom-call | flops 1179648 | bytes 1179648 | tf_op jit(solution)/shard_map/experts/pallas_call | solution.py:381
  429.6 18.4 %adapter_grads.1 = bf16[4,2,2304,128]{3,2,1,0:T(8,128)(2,1)} custom-call(s32[4]{0:T(128)} %iota_xor_fusion.which, bf16[2,1152,2048]{2,1,0:T(8,128)(2,1)} %get-tuple-element.207.xs, bf16[2,1152,2048]{2,1,0:T(8,128)(2,1)} %get-tuple-element.208.ps, bf16[2,1152,1024]{2,1,0:T(8,128)(2,1)} %get-tuple-element.209.act, ...), custom_call_target="tpu_custom_call" | custom-call | flops 2359296 | bytes 2359296 | tf_op jit(solution)/shard_map/adapter_grads/pallas_call | solution.py:433
  466.1 9.2 %collective-permute-done.29 = bf16[1,2304,128]{2,1,0:T(8,128)(2,1)S(1)} collective-permute-done((bf16[1,2304,128]{2,1,0:T(8,128)(2,1)S(1)}, bf16[1,2304,128]{2,1,0:T(8,128)(2,1)S(1)}, u32[]{:S(2)}, u32[]{:S(2)}) %collective-permute-start.29) | collective-permute-done | bytes 589856 | tf_op jit(solution)/shard_map/ppermute | solution.py:448
  476.7 9.8 %collective-permute-done.31 = bf16[1,2304,128]{2,1,0:T(8,128)(2,1)S(1)} collective-permute-done((bf16[1,2304,128]{2,1,0:T(8,128)(2,1)S(1)}, bf16[1,2304,128]{2,1,0:T(8,128)(2,1)S(1)}, u32[]{:S(2)}, u32[]{:S(2)}) %collective-permute-start.31) | collective-permute-done | bytes 589856 | tf_op jit(solution)/shard_map/ppermute | solution.py:448
  489.7 24.4 %collective-permute-done.34 = bf16[256,2304]{1,0:T(8,128)(2,1)S(1)} collective-permute-done((bf16[256,2304]{1,0:T(8,128)(2,1)S(1)}, bf16[256,2304]{1,0:T(8,128)(2,1)S(1)}, u32[]{:S(2)}, u32[]{:S(2)}) %collective-permute-start.34) | collective-permute-done | bytes 1179680 | tf_op jit(solution)/shard_map/ppermute | solution.py:448
  520.1 8.2 %collective-permute-done.35 = bf16[128,2304]{1,0:T(8,128)(2,1)} collective-permute-done((bf16[128,2304]{1,0:T(8,128)(2,1)}, bf16[128,2304]{1,0:T(8,128)(2,1)}, u32[]{:S(2)}, u32[]{:S(2)}) %collective-permute-start.35) | collective-permute-done | bytes 589856 | tf_op jit(solution)/shard_map/ppermute | solution.py:448
  545.0 23.7 %attend_back.1 = (bf16[1024,512]{1,0:T(8,128)(2,1)}, bf16[1024,512]{1,0:T(8,128)(2,1)}, bf16[1024,512]{1,0:T(8,128)(2,1)}) custom-call(bf16[1024,512]{1,0:T(8,128)(2,1)} %get-tuple-element.232.query, bf16[1024,512]{1,0:T(8,128)(2,1)} %get-tuple-element.233.key, bf16[1024,512]{1,0:T(8,128)(2,1)} %get-tuple-element.234.value, ...), custom_call_target="tpu_custom_call" | custom-call | flops 524288 | bytes 524288 | tf_op jit(solution)/shard_map/attend_back/pallas_call | solution.py:168
  583.3 12.3 %qkv_back.1 = bf16[1024,2048]{1,0:T(8,128)(2,1)} custom-call(bf16[1024,512]{1,0:T(8,128)(2,1)} %get-tuple-element.252.a_ref, bf16[1024,512]{1,0:T(8,128)(2,1)} %get-tuple-element.253.b_ref, bf16[1024,512]{1,0:T(8,128)(2,1)} %get-tuple-element.254.c_ref, bf16[8,3,64,2048]{3,2,1,0:T(8,128)(2,1)} %bitcast.215), custom_call_target="tpu_custom_call" | custom-call | flops 2097152 | bytes 2097152 | tf_op jit(solution)/shard_map/qkv_back/pallas_call | solution.py:246
  620.1 7.0 %collective-permute-done.47 = bf16[128,2048]{1,0:T(8,128)(2,1)S(1)} collective-permute-done((bf16[128,2048]{1,0:T(8,128)(2,1)}, bf16[128,2048]{1,0:T(8,128)(2,1)S(1)}, u32[]{:S(2)}, u32[]{:S(2)}) %collective-permute-start.47) | collective-permute-done | bytes 524320 | tf_op jit(solution)/shard_map/ppermute | solution.py:448
  636.8 5.2 collective-permute-done.49
  652.3 14.8 %reduce-scatter.5.cloned.1.call-done = bf16[1,8,64,128]{3,2,1,0:T(8,128)(2,1)} async-done(((bf16[8,8,64,128]{3,2,1,0:T(8,128)(2,1)}), bf16[1,8,64,128]{3,2,1,0:T(8,128)(2,1)}) %reduce-scatter.5.cloned.1.call-update) | async-done | bytes 131088 | tf_op jit(solution)/shard_map/reduce_scatter | solution.py:730
  (379 shorter events, 231.5 us)
Async XLA Ops:
  7.2 38.1 %all-gather.10.cloned.1.call-start = ((), (), s32[]{:S(2)}) async-start(), calls=%async_computation.5 | async-start | bytes 1179648 | tf_op jit(solution)/shard_map/all_gather | solution.py:556
  14.1 96.4 %all-gather.12.cloned.1.call-start = ((), (), s32[]{:S(2)}) async-start(), calls=%async_computation.6 | async-start | bytes 7077888 | tf_op jit(solution)/shard_map/all_gather | solution.py:561
  17.7 26.1 %collective-permute-start = (bf16[256,2048]{1,0:T(8,128)(2,1)S(1)}, bf16[256,2048]{1,0:T(8,128)(2,1)S(1)}, u32[]{:S(2)}, u32[]{:S(2)}) collective-permute-start(bf16[256,2048]{1,0:T(8,128)(2,1)S(1)} %get-tuple-element.281), channel_id=1, source_target_pairs={{0,8},{8,0},{16,24},{24,16},{1,9},{9,1},{17,25},{25,17},{2,10},{10... | collective-permute-start | bytes 3145736 | tf_op jit(solution)/shard_map/ppermute | solution.py:448
  20.6 24.6 %collective-permute-start.1 = (bf16[256,2048]{1,0:T(8,128)(2,1)S(1)}, bf16[256,2048]{1,0:T(8,128)(2,1)S(1)}, u32[]{:S(2)}, u32[]{:S(2)}) collective-permute-start(bf16[256,2048]{1,0:T(8,128)(2,1)S(1)} %get-tuple-element.281), channel_id=1, source_target_pairs={{0,16},{8,24},{16,0},{24,8},{1,17},{9,25},{17,1},{25,9},{2,18},{10... | collective-permute-start | bytes 3145736 | tf_op jit(solution)/shard_map/ppermute | solution.py:448
  45.3 103.4 %all-gather.8.cloned.1.call-start = ((), (), s32[]{:S(2)}) async-start(), calls=%async_computation.2 | async-start | bytes 2506752 | tf_op jit(solution)/shard_map/all_gather | solution.py:607
  110.5 161.0 %all-gather.14.cloned.1.call-start = ((), (), s32[]{:S(2)}) async-start(), calls=%async_computation.7 | async-start | bytes 9437184 | tf_op jit(solution)/shard_map/all_gather | solution.py:611
  123.4 522.3 %reduce-scatter.3.cloned.1.call-start = ((), (), s32[]{:S(2)}) async-start(), calls=%async_computation.3 | async-start | bytes 9437184 | tf_op jit(solution)/shard_map/reduce_scatter | solution.py:671
  156.6 24.6 %collective-permute-start.12 = (bf16[128,2176]{1,0:T(8,128)(2,1)S(1)}, bf16[128,2176]{1,0:T(8,128)(2,1)S(1)}, u32[]{:S(2)}, u32[]{:S(2)}) collective-permute-start(bf16[128,2176]{1,0:T(8,128)(2,1)S(1)} %get-tuple-element.295), channel_id=1, source_target_pairs={{0,16},{8,24},{16,0},{24,8},{1,17},{9,25},{17,1},{25,9},{2,18},{10... | collective-permute-start | bytes 1671176 | tf_op jit(solution)/shard_map/ppermute | solution.py:448
  157.2 25.4 %collective-permute-start.8 = (bf16[128,2176]{1,0:T(8,128)(2,1)S(1)}, bf16[128,2176]{1,0:T(8,128)(2,1)S(1)}, u32[]{:S(2)}, u32[]{:S(2)}) collective-permute-start(bf16[128,2176]{1,0:T(8,128)(2,1)S(1)} %get-tuple-element.294), channel_id=1, source_target_pairs={{0,8},{8,0},{16,24},{24,16},{1,9},{9,1},{17,25},{25,17},{2,10},{10... | collective-permute-start | bytes 1671176 | tf_op jit(solution)/shard_map/ppermute | solution.py:448
  171.7 21.8 %collective-permute-start.13 = (bf16[128,2176]{1,0:T(8,128)(2,1)S(1)}, bf16[128,2176]{1,0:T(8,128)(2,1)S(1)}, u32[]{:S(2)}, u32[]{:S(2)}) collective-permute-start(bf16[128,2176]{1,0:T(8,128)(2,1)S(1)} %get-tuple-element.154), channel_id=1, source_target_pairs={{0,8},{8,0},{16,24},{24,16},{1,9},{9,1},{17,25},{25,17},{2,10},{10... | collective-permute-start | bytes 1671176 | tf_op jit(solution)/shard_map/ppermute | solution.py:448
  173.0 24.6 %collective-permute-start.17 = (bf16[256,2048]{1,0:T(8,128)(2,1)}, bf16[256,2048]{1,0:T(8,128)(2,1)}, u32[]{:S(2)}, u32[]{:S(2)}) collective-permute-start(bf16[256,2048]{1,0:T(8,128)(2,1)} %bitcast.3), channel_id=1, source_target_pairs={{0,1},{1,0},{2,3},{3,2},{4,5},{5,4},{6,7},{7,6},{8,9},{9,8},{10,11... | collective-permute-start | bytes 3145736 | tf_op jit(solution)/shard_map/ppermute | solution.py:448
  196.0 71.2 %collective-permute-start.14 = (bf16[256,2048]{1,0:T(8,128)(2,1)S(1)}, bf16[256,2048]{1,0:T(8,128)(2,1)}, u32[]{:S(2)}, u32[]{:S(2)}) collective-permute-start(bf16[256,2048]{1,0:T(8,128)(2,1)S(1)} %multiply_convert_fusion.refs_0_), channel_id=1, source_target_pairs={{0,4},{1,5},{2,6},{3,7},{4,0},{5,1},{6,2},{7,3},{8,12},{9,13},{10,... | collective-permute-start | bytes 3145736 | tf_op jit(solution)/shard_map/ppermute | solution.py:448
  270.2 45.1 %collective-permute-start.19 = (bf16[256,2048]{1,0:T(8,128)(2,1)S(1)}, bf16[256,2048]{1,0:T(8,128)(2,1)}, u32[]{:S(2)}, u32[]{:S(2)}) collective-permute-start(bf16[256,2048]{1,0:T(8,128)(2,1)S(1)} %copy-done.10), channel_id=1, source_target_pairs={{0,6},{1,7},{2,4},{3,5},{4,2},{5,3},{6,0},{7,1},{8,14},{9,15},{10,... | collective-permute-start | bytes 3145736 | tf_op jit(solution)/shard_map/ppermute | solution.py:448
  320.7 48.5 %collective-permute-start.22 = (bf16[256,2048]{1,0:T(8,128)(2,1)S(1)}, bf16[256,2048]{1,0:T(8,128)(2,1)}, u32[]{:S(2)}, u32[]{:S(2)}) collective-permute-start(bf16[256,2048]{1,0:T(8,128)(2,1)S(1)} %copy-done.10), channel_id=1, source_target_pairs={{0,2},{1,3},{2,0},{3,1},{4,6},{5,7},{6,4},{7,5},{8,10},{9,11},{10,... | collective-permute-start | bytes 3145736 | tf_op jit(solution)/shard_map/ppermute | solution.py:448
  321.7 48.9 %collective-permute-start.23 = (bf16[256,2048]{1,0:T(8,128)(2,1)}, bf16[256,2048]{1,0:T(8,128)(2,1)}, u32[]{:S(2)}, u32[]{:S(2)}) collective-permute-start(bf16[256,2048]{1,0:T(8,128)(2,1)} %add_convert_fusion.3), channel_id=1, source_target_pairs={{0,4},{1,5},{2,6},{3,7},{4,0},{5,1},{6,2},{7,3},{8,12},{9,13},{10,... | collective-permute-start | bytes 3145736 | tf_op jit(solution)/shard_map/ppermute | solution.py:448
  374.6 46.5 %collective-permute-start.26 = (bf16[256,2048]{1,0:T(8,128)(2,1)}, bf16[256,2048]{1,0:T(8,128)(2,1)}, u32[]{:S(2)}, u32[]{:S(2)}) collective-permute-start(bf16[256,2048]{1,0:T(8,128)(2,1)} %add_convert_fusion.2), channel_id=1, source_target_pairs={{0,6},{1,7},{2,4},{3,5},{4,2},{5,3},{6,0},{7,1},{8,14},{9,15},{10,... | collective-permute-start | bytes 3145736 | tf_op jit(solution)/shard_map/ppermute | solution.py:448
  426.7 26.0 %collective-permute-start.28 = (bf16[256,2048]{1,0:T(8,128)(2,1)}, bf16[256,2048]{1,0:T(8,128)(2,1)S(1)}, u32[]{:S(2)}, u32[]{:S(2)}) collective-permute-start(bf16[256,2048]{1,0:T(8,128)(2,1)} %add_convert_fusion.1), channel_id=1, source_target_pairs={{0,2},{1,3},{2,0},{3,1},{4,6},{5,7},{6,4},{7,5},{8,10},{9,11},{10,... | collective-permute-start | bytes 3145736 | tf_op jit(solution)/shard_map/ppermute | solution.py:448
  456.8 210.3 %reduce-scatter.5.cloned.1.call-start = ((), (), s32[]{:S(2)}) async-start(), calls=%async_computation.4 | async-start | bytes 1179648 | tf_op jit(solution)/shard_map/reduce_scatter | solution.py:730
  462.0 24.5 %collective-permute-start.31 = (bf16[1,2304,128]{2,1,0:T(8,128)(2,1)S(1)}, bf16[1,2304,128]{2,1,0:T(8,128)(2,1)S(1)}, u32[]{:S(2)}, u32[]{:S(2)}) collective-permute-start(bf16[1,2304,128]{2,1,0:T(8,128)(2,1)S(1)} %get-tuple-element.289), channel_id=1, source_target_pairs={{0,8},{8,0},{16,24},{24,16},{1,9},{9,1},{17,25},{25,17},{2,10},{10... | collective-permute-start | bytes 1769480 | tf_op jit(solution)/shard_map/ppermute | solution.py:448
  462.5 25.2 %collective-permute-start.32 = (bf16[1,2304,128]{2,1,0:T(8,128)(2,1)S(1)}, bf16[1,2304,128]{2,1,0:T(8,128)(2,1)S(1)}, u32[]{:S(2)}, u32[]{:S(2)}) collective-permute-start(bf16[1,2304,128]{2,1,0:T(8,128)(2,1)S(1)} %get-tuple-element.288), channel_id=1, source_target_pairs={{0,16},{8,24},{16,0},{24,8},{1,17},{9,25},{17,1},{25,9},{2,18},{10... | collective-permute-start | bytes 1769480 | tf_op jit(solution)/shard_map/ppermute | solution.py:448
  487.7 26.4 %collective-permute-start.34 = (bf16[256,2304]{1,0:T(8,128)(2,1)S(1)}, bf16[256,2304]{1,0:T(8,128)(2,1)S(1)}, u32[]{:S(2)}, u32[]{:S(2)}) collective-permute-start(bf16[256,2304]{1,0:T(8,128)(2,1)S(1)} %pad_maximum_fusion.4), channel_id=1, source_target_pairs={{0,16},{8,24},{16,0},{24,8},{1,17},{9,25},{17,1},{25,9},{2,18},{10... | collective-permute-start | bytes 3538952 | tf_op jit(solution)/shard_map/ppermute | solution.py:448
  489.1 26.5 %collective-permute-start.33 = (bf16[256,2304]{1,0:T(8,128)(2,1)S(1)}, bf16[256,2304]{1,0:T(8,128)(2,1)S(1)}, u32[]{:S(2)}, u32[]{:S(2)}) collective-permute-start(bf16[256,2304]{1,0:T(8,128)(2,1)S(1)} %pad_maximum_fusion.4), channel_id=1, source_target_pairs={{0,8},{8,0},{16,24},{24,16},{1,9},{9,1},{17,25},{25,17},{2,10},{10... | collective-permute-start | bytes 3538952 | tf_op jit(solution)/shard_map/ppermute | solution.py:448
  534.1 37.0 %collective-permute-start.37 = (bf16[1,2304,128]{2,1,0:T(8,128)(2,1)}, bf16[1,2304,128]{2,1,0:T(8,128)(2,1)}, u32[]{:S(2)}, u32[]{:S(2)}) collective-permute-start(bf16[1,2304,128]{2,1,0:T(8,128)(2,1)} %get-tuple-element.229), channel_id=1, source_target_pairs={{0,16},{8,24},{16,0},{24,8},{1,17},{9,25},{17,1},{25,9},{2,18},{10... | collective-permute-start | bytes 1769480 | tf_op jit(solution)/shard_map/ppermute | solution.py:448
  535.5 35.6 %collective-permute-start.38 = (bf16[1,2304,128]{2,1,0:T(8,128)(2,1)}, bf16[1,2304,128]{2,1,0:T(8,128)(2,1)}, u32[]{:S(2)}, u32[]{:S(2)}) collective-permute-start(bf16[1,2304,128]{2,1,0:T(8,128)(2,1)} %get-tuple-element.231), channel_id=1, source_target_pairs={{0,8},{8,0},{16,24},{24,16},{1,9},{9,1},{17,25},{25,17},{2,10},{10... | collective-permute-start | bytes 1769480 | tf_op jit(solution)/shard_map/ppermute | solution.py:448
  (93 other events, 907.9 us)
Sparse Core Ops, SparseCore 0:
  14.2 24.9 all-gather.9
  45.4 65.0 all-gather.11
  112.1 28.8 all-gather.7
  142.5 115.4 all-gather.13
  457.0 88.7 reduce-scatter.2
  636.9 30.1 reduce-scatter.4

commit v7 on v6

--- a/solution.py
+++ b/solution.py
@@ -473,22 +473,39 @@
     return [swap(blocks[k], axis, k, count) for k in range(1, count)]
 
 
-def collect_end(blocks, arrived, axis, count):
-    f32 = jnp.float32
+def collect_turn(blocks, arrived, axis, count):
     if count == 4 and blocks[0].size >= half_from:
         half = blocks[0].shape[0] // 2
-        over_one, over_two, from_one, from_two = arrived
-        to_two = (blocks[2][:half].astype(f32) + over_one.astype(f32)).astype(blocks[2].dtype)
-        to_one = (blocks[1][half:].astype(f32) + over_two.astype(f32)).astype(blocks[1].dtype)
+        to_two = (blocks[2][:half].astype(jnp.float32) + arrived[0].astype(jnp.float32)).astype(blocks[2].dtype)
+        to_one = (blocks[1][half:].astype(jnp.float32) + arrived[1].astype(jnp.float32)).astype(blocks[1].dtype)
         to_two, to_one = pin(to_two, to_one)
-        top = blocks[0][:half].astype(f32) + from_one.astype(f32) + swap(to_two, axis, 2, count).astype(f32)
-        low = blocks[0][half:].astype(f32) + from_two.astype(f32) + swap(to_one, axis, 1, count).astype(f32)
+        return [swap(to_two, axis, 2, count), swap(to_one, axis, 1, count)]
+    return []
+
+
+def collect_end(blocks, arrived, turned, axis, count):
+    f32 = jnp.float32
+    if turned:
+        half = blocks[0].shape[0] // 2
+        top = blocks[0][:half].astype(f32) + arrived[2].astype(f32) + turned[0].astype(f32)
+        low = blocks[0][half:].astype(f32) + arrived[3].astype(f32) + turned[1].astype(f32)
         return jnp.concatenate([top, low], axis=0)
     return sum((x.astype(f32) for x in arrived), blocks[0].astype(f32))
 
 
 def collect(blocks, axis, count):
-    return collect_end(blocks, collect_begin(blocks, axis, count), axis, count)
+    arrived = collect_begin(blocks, axis, count)
+    return collect_end(blocks, arrived, collect_turn(blocks, arrived, axis, count), axis, count)
+
+
+def collect_chips(blocks, count):
+    pairs = blocks.reshape((count // 2, 2) + blocks.shape[1:])
+    summed = pairs[:, 0].astype(jnp.float32) + swap(pairs[:, 1], "dp", 1, count).astype(jnp.float32)
+    total = summed[0]
+    summed = summed.astype(blocks.dtype)
+    for c in range(1, count // 2):
+        total = total + swap(summed[c], "dp", 2 * c, count).astype(jnp.float32)
+    return total
 
 
 def pin(*values):
@@ -662,9 +679,7 @@
     leaving, *kept = pin(leaving, *kept)
     flying = swap(leaving, "dp", 2 * turns[-1], dp_count)
     flat = adapter_grads(kept, order)
-    expert_arrived = collect_begin([flat[k] for k in range(n)], "seq", n)
     flat, flying = pin(flat, flying)
-    expert_terms = [flat[k] for k in range(n)]
     grad_normed_ffn = grad_normed_ffn + flying.astype(f32)
 
     outs_all, grad_normed_ffn = pin(outs_all, grad_normed_ffn)
@@ -675,11 +690,9 @@
     grad_hidden_low = grad_hidden.astype(low)
     grad_reduced_output = (own_mask * dot(grad_hidden_low, upt_output)).astype(low)
     grad_pack = jnp.concatenate([grad_hidden_low, grad_reduced_output, output_reduced], axis=1)
-    grad_pack, *expert_arrived = pin(grad_pack, *expert_arrived)
-    grad_packs = spread(grad_pack, "seq", n)
-    expert_arrived = list(pin(*expert_arrived, *grad_packs))
-    grad_packs = expert_arrived[-n:]
-    expert_sum = collect_end(expert_terms, expert_arrived[:-n], "seq", n)
+    flat, *grad_packs = pin(flat, *spread(grad_pack, "seq", n))
+    expert_terms = [flat[k] for k in range(n)]
+    expert_arrived = collect_begin(expert_terms, "seq", n)
     grad_pack_all = jnp.concatenate(grad_packs, axis=0)
     grad_all = grad_pack_all[:, :full_width]
     grad_reduced_all = grad_pack_all[:, full_width : full_width + rank_columns]
@@ -698,7 +711,10 @@
         gain_key,
         segment,
     )
-    expert_sum, *grad_raw_list = pin(expert_sum, *grad_raw_list)
+    pinned = pin(*grad_raw_list, *expert_arrived)
+    grad_raw_list = list(pinned[:3])
+    expert_arrived = pinned[3:]
+    expert_turned = collect_turn(expert_terms, expert_arrived, "seq", n)
     partial_reduced = jnp.concatenate(
         [dot(grad_raw_list[m], upt_group[m]) for m in range(3)], axis=1
     ).astype(low)
@@ -709,30 +725,29 @@
     grad_reduced, *grad_raw_late = pin(grad_reduced, *grad_raw_list)
     grad_reduced_full = jnp.concatenate(spread(grad_reduced, "seq", n), axis=0)
     partial_normed = qkv_back(grad_raw_list, w_group).reshape(n, own_rows, full_width)
-    partial_normed, grad_reduced = pin(partial_normed, grad_reduced)
+    partial_normed, grad_reduced, *expert_turned = pin(partial_normed, grad_reduced, *expert_turned)
+    expert_sum = collect_end(expert_terms, expert_arrived, expert_turned, "seq", n)
     grad_upt = [dot_l(grad_raw_late[m], reduced_list[m]) for m in range(3)]
     normed_cols = lax.dynamic_slice_in_dim(normed_all, group_start, group_width, 1)
     grad_down_cat = dot_l(normed_cols, grad_reduced_full)
     parts = [grad_down_cat[:, m * rank_columns : (m + 1) * rank_columns] for m in range(3)]
-    parts += [grad_down_output] + grad_upt + [grad_upt_output]
-    stacked = jnp.stack([x.astype(low).reshape(dp_count, piece, rank_columns) for x in parts], axis=1)
+    piled = lambda some: jnp.stack([x.astype(low).reshape(dp_count, piece, rank_columns) for x in some], axis=1)
+    early_parts = piled([grad_down_output] + grad_upt + [grad_upt_output])
+    early_parts = lax.psum_scatter(early_parts, "dp", scatter_dimension=0)
+    late_parts = collect_chips(piled(parts)[dp_order], dp_count)
     normed_terms = [partial_normed[k] for k in range(n)]
     arrived = collect_begin(normed_terms, "seq", n)
-    stacked, *arrived = pin(stacked, *arrived)
-    summed_back = collect_end(normed_terms, arrived, "seq", n)
+    summed_back = collect_end(normed_terms, arrived, collect_turn(normed_terms, arrived, "seq", n), "seq", n)
     summed_back, mixture, hidden = pin(summed_back, mixture, hidden)
     layer_output = (hidden + mixture.astype(f32)).astype(low)[None]
     grad_normed = summed_back + dot_t(grad_reduced, down_cat)
     unused_input, pull_input = jax.vjp(lambda values: rms_scale(values, gain_attention), tokens)
     input_grad = (grad_hidden + pull_input(grad_normed)[0]).astype(low)[None]
 
-    stacked, expert_sum = pin(stacked, expert_sum)
-    own_parts = lax.psum_scatter(stacked, "dp", scatter_dimension=0)
-    own_parts, input_grad = pin(own_parts, input_grad)
-    own_parts = own_parts.astype(f32)
-    grad_a_attention = own_parts[0:4]
-    grad_b_attention = jnp.swapaxes(own_parts[4:8], 1, 2)
-
+    early_parts, input_grad = pin(early_parts, input_grad)
+    early_parts = early_parts.astype(f32)
+    grad_a_attention = jnp.concatenate([late_parts, early_parts[:1]], axis=0)
+    grad_b_attention = jnp.swapaxes(early_parts[1:], 1, 2)
     own_width = full_width // n
     own_ff = expert_w_down.shape[1] // n
     columns = lambda x, count: jnp.swapaxes(x.reshape(local_count, count, -1, rank_columns, rank_columns), 2, 3).reshape(

time: 690 us -> 665 us (0.964)
  waiting for transfers between devices: 185 us -> 151 us
    ppermute x51 -> x55, waiting for transfers between devices: 165 us -> 146 us  [swap(): return lax.ppermute(values, axis, [(i, i ^ distance) for i in range(count)])]
    reduce_scatter x1, waiting for transfers between devices: 14.8 us -> 0.01 us  [local(): early_parts = lax.psum_scatter(early_parts, 'dp', scatter_dimension=0)]
    ppermute x51 -> x55, starting transfers between devices: 51.1 us -> 54.5 us  [swap(): return lax.ppermute(values, axis, [(i, i ^ distance) for i in range(count)])]
    unnamed x135 -> x114, local copies, waits for them, and re-layouts: 15 us -> 14.2 us
  transfers between devices with their start and end apart: 57 -> 61, of which waited for: 29 -> 24; matrix products, arithmetic and copies ran while one was open for 20% -> 22% of each run, Pallas kernels for 39% -> 41%
where the time goes in v7:
time: 665 us; the launch traced here: 655 us
  Pallas kernels  266 us (40%)
  waiting for transfers between devices  151 us (23%)
  other arithmetic  73.9 us (11%)
  local copies, waits for them, and re-layouts  62.2 us (9%)
  starting transfers between devices  55.5 us (8%)
  matrix products  31.4 us (5%)
  between operations  15.6 us (2%)
    pallas_call x4, Pallas kernels, run_experts(): pl.pallas_call(functools.partial(expert_kernel, len(kept)), grid_spec=plt...  175 us
    ppermute x55, waiting for transfers between devices, swap(): return lax.ppermute(values, axis, [(i, i ^ distance) for i in range(count)])  146 us
    ppermute x55, starting transfers between devices, swap(): return lax.ppermute(values, axis, [(i, i ^ distance) for i in range(count)])  54.5 us
    pallas_call x1, Pallas kernels, attend(): pl.pallas_call(functools.partial(attend_kernel, tile), grid=(heads,), in_...  23.7 us
    pallas_call x1, Pallas kernels, attend_back(): pl.pallas_call(functools.partial(attend_back_kernel, tile), grid=(heads,)...  23.7 us
    pallas_call x1, Pallas kernels, adapter_grads(): pl.pallas_call(adapter_kernel, grid_spec=pltpu.PrefetchScalarGridSpec(num...  18.4 us
    unnamed x114, local copies, waits for them, and re-layouts  14.2 us
  transfers between devices with their start and end apart: 61, of which 24 were waited for; matrix products, arithmetic and copies ran while one was open for 22% of the time, Pallas kernels for 41%

profile of v7, /device:TPU:0, one launch (start us, length us, event | category | flops | bytes accessed | tf_op | source)
XLA Modules:
  0.0 655.0 jit_solution(6106562192039121134)
XLA Ops:
  22.2 21.6 %collective-permute-done = bf16[256,2048]{1,0:T(8,128)(2,1)S(1)} collective-permute-done((bf16[256,2048]{1,0:T(8,128)(2,1)S(1)}, bf16[256,2048]{1,0:T(8,128)(2,1)S(1)}, u32[]{:S(2)}, u32[]{:S(2)}) %collective-permute-start) | collective-permute-done | bytes 1048608 | tf_op jit(solution)/shard_map/ppermute | solution.py:448
  99.2 6.5 multiply_convert_fusion.1.reduced_ref
  105.7 4.8 all-gather.12.cloned.1.call-done
  110.5 12.9 %qkv_project.1.q_raw.k_raw.v_raw = f32[3,1024,512]{2,1,0:T(8,128)} custom-call(bf16[1024,2048]{1,0:T(8,128)(2,1)} %constant_dynamic-update-slice_fusion.x_ref, bf16[1024,384]{1,0:T(8,128)(2,1)} %multiply_convert_fusion.1.reduced_ref, bf16[8,3,64,2048]{3,2,1,0:T(8,128)(2,1)} %bitcast.234, bf16[3,512,128]{2,1,0:T(8,128)(2,1)} %bitcast.245), custom_call_target="tpu_custom_call" | custom-call | flops 6442450944 | bytes 16777216 | tf_op jit(solution)/shard_map/qkv_project/pallas_call | solution.py:213
  125.0 23.7 %attend.1 = (bf16[1024,512]{1,0:T(8,128)(2,1)}, bf16[1024,512]{1,0:T(8,128)(2,1)}, bf16[1024,512]{1,0:T(8,128)(2,1)}, bf16[1024,512]{1,0:T(8,128)(2,1)}, f32[4,1,1024]{2,1,0:T(1,128)}) custom-call(f32[3,1024,512]{2,1,0:T(8,128)} %qkv_project.1.q_raw.k_raw.v_raw, f32[3,1024,512]{2,1,0:T(8,128)} %qkv_project.1.q_raw.k_raw.v_raw, ...), custom_call_target="tpu_custom_call" | custom-call | flops 2147483648 | bytes 10485760 | tf_op jit(solution)/shard_map/attend/pallas_call | solution.py:100
  148.7 4.9 convolution_convert_fusion
  157.9 11.4 %collective-permute-done.10 = bf16[128,2176]{1,0:T(8,128)(2,1)S(1)} collective-permute-done((bf16[128,2176]{1,0:T(8,128)(2,1)S(1)}, bf16[128,2176]{1,0:T(8,128)(2,1)S(1)}, u32[]{:S(2)}, u32[]{:S(2)}) %collective-permute-start.10) | collective-permute-done | bytes 557088 | tf_op jit(solution)/shard_map/ppermute | solution.py:448
  173.1 8.2 %collective-permute-done.12 = bf16[128,2176]{1,0:T(8,128)(2,1)S(1)} collective-permute-done((bf16[128,2176]{1,0:T(8,128)(2,1)S(1)}, bf16[128,2176]{1,0:T(8,128)(2,1)S(1)}, u32[]{:S(2)}, u32[]{:S(2)}) %collective-permute-start.12) | collective-permute-done | bytes 557088 | tf_op jit(solution)/shard_map/ppermute | solution.py:448
  182.6 9.9 %collective-permute-done.11 = bf16[128,2176]{1,0:T(8,128)(2,1)S(1)} collective-permute-done((bf16[128,2176]{1,0:T(8,128)(2,1)S(1)}, bf16[128,2176]{1,0:T(8,128)(2,1)S(1)}, u32[]{:S(2)}, u32[]{:S(2)}) %collective-permute-start.11) | collective-permute-done | bytes 557088 | tf_op jit(solution)/shard_map/ppermute | solution.py:448
  202.2 43.6 %experts.4 = (bf16[8,256,2048]{2,1,0:T(8,128)(2,1)}, bf16[256,2048]{1,0:T(8,128)(2,1)}, bf16[256,2048]{1,0:T(8,128)(2,1)}, bf16[2,1152,2048]{2,1,0:T(8,128)(2,1)...) custom-call(s32[5]{0:T(128)} %pad_add_fusion.which, ...), custom_call_target="tpu_custom_call" | custom-call | flops 1179648 | bytes 1179648 | tf_op jit(solution)/shard_map/experts/pallas_call | solution.py:381
  246.0 21.2 %collective-permute-done.14.refs_0_ = bf16[256,2048]{1,0:T(8,128)(2,1)} collective-permute-done((bf16[256,2048]{1,0:T(8,128)(2,1)S(1)}, bf16[256,2048]{1,0:T(8,128)(2,1)}, u32[]{:S(2)}, u32[]{:S(2)}) %collective-permute-start.14) | collective-permute-done | bytes 1048608 | tf_op jit(solution)/shard_map/ppermute | solution.py:448
  271.5 43.7 %experts.5 = (bf16[8,256,2048]{2,1,0:T(8,128)(2,1)}, bf16[256,2048]{1,0:T(8,128)(2,1)}, bf16[256,2048]{1,0:T(8,128)(2,1)}, bf16[2,1152,2048]{2,1,0:T(8,128)(2,1)...) custom-call(s32[5]{0:T(128)} %stack.88.which, ...), custom_call_target="tpu_custom_call", output_to_operand_aliasing={{0}: (13, {}), {3}: (14, {}), {4}: (15, {}), {5}: (16, {}),... | custom-call | flops 1179648 | bytes 1179648 | tf_op jit(solution)/shard_map/experts/pallas_call | solution.py:381
  325.3 43.9 %experts.6 = (bf16[8,256,2048]{2,1,0:T(8,128)(2,1)}, bf16[256,2048]{1,0:T(8,128)(2,1)}, bf16[256,2048]{1,0:T(8,128)(2,1)}, bf16[2,1152,2048]{2,1,0:T(8,128)(2,1)...) custom-call(s32[5]{0:T(128)} %stack.90.which, ...), custom_call_target="tpu_custom_call", output_to_operand_aliasing={{0}: (13, {}), {3}: (14, {}), {4}: (15, {}), {5}: (16, {}),... | custom-call | flops 1179648 | bytes 1179648 | tf_op jit(solution)/shard_map/experts/pallas_call | solution.py:381
  377.5 43.7 %experts.7 = (bf16[8,256,2048]{2,1,0:T(8,128)(2,1)}, bf16[256,2048]{1,0:T(8,128)(2,1)}, bf16[256,2048]{1,0:T(8,128)(2,1)}, bf16[2,1152,2048]{2,1,0:T(8,128)(2,1)...) custom-call(s32[5]{0:T(128)} %stack.82.which, ...), custom_call_target="tpu_custom_call", output_to_operand_aliasing={{0}: (13, {}), {3}: (14, {}), {4}: (15, {}), {5}: (16, {}),... | custom-call | flops 1179648 | bytes 1179648 | tf_op jit(solution)/shard_map/experts/pallas_call | solution.py:381
  429.6 18.4 %adapter_grads.1 = bf16[4,2,2304,128]{3,2,1,0:T(8,128)(2,1)} custom-call(s32[4]{0:T(128)} %iota_xor_fusion.which, bf16[2,1152,2048]{2,1,0:T(8,128)(2,1)} %get-tuple-element.200.xs, bf16[2,1152,2048]{2,1,0:T(8,128)(2,1)} %get-tuple-element.201.ps, bf16[2,1152,1024]{2,1,0:T(8,128)(2,1)} %get-tuple-element.202.act, ...), custom_call_target="tpu_custom_call" | custom-call | flops 2359296 | bytes 2359296 | tf_op jit(solution)/shard_map/adapter_grads/pallas_call | solution.py:433
  448.0 4.7 collective-permute-done.28
  452.8 4.1 convert_add_fusion.1
  464.9 24.5 %collective-permute-done.30 = bf16[256,2304]{1,0:T(8,128)(2,1)S(1)} collective-permute-done((bf16[256,2304]{1,0:T(8,128)(2,1)S(1)}, bf16[256,2304]{1,0:T(8,128)(2,1)S(1)}, u32[]{:S(2)}, u32[]{:S(2)}) %collective-permute-start.30) | collective-permute-done | bytes 1179680 | tf_op jit(solution)/shard_map/ppermute | solution.py:448
  496.3 8.4 %collective-permute-done.31 = bf16[128,2304]{1,0:T(8,128)(2,1)} collective-permute-done((bf16[128,2304]{1,0:T(8,128)(2,1)}, bf16[128,2304]{1,0:T(8,128)(2,1)}, u32[]{:S(2)}, u32[]{:S(2)}) %collective-permute-start.31) | collective-permute-done | bytes 589856 | tf_op jit(solution)/shard_map/ppermute | solution.py:448
  520.2 3.7 fusion.14.grad_mixed
  523.9 23.7 %attend_back.1 = (bf16[1024,512]{1,0:T(8,128)(2,1)}, bf16[1024,512]{1,0:T(8,128)(2,1)}, bf16[1024,512]{1,0:T(8,128)(2,1)}) custom-call(bf16[1024,512]{1,0:T(8,128)(2,1)} %get-tuple-element.141.query, bf16[1024,512]{1,0:T(8,128)(2,1)} %get-tuple-element.142.key, bf16[1024,512]{1,0:T(8,128)(2,1)} %get-tuple-element.143.value, ...), custom_call_target="tpu_custom_call" | custom-call | flops 524288 | bytes 524288 | tf_op jit(solution)/shard_map/attend_back/pallas_call | solution.py:168
  563.6 12.3 %qkv_back.1 = bf16[1024,2048]{1,0:T(8,128)(2,1)} custom-call(bf16[1024,512]{1,0:T(8,128)(2,1)} %get-tuple-element.241.a_ref, bf16[1024,512]{1,0:T(8,128)(2,1)} %get-tuple-element.242.b_ref, bf16[1024,512]{1,0:T(8,128)(2,1)} %get-tuple-element.243.c_ref, bf16[8,3,64,2048]{3,2,1,0:T(8,128)(2,1)} %bitcast.235), custom_call_target="tpu_custom_call" | custom-call | flops 2097152 | bytes 2097152 | tf_op jit(solution)/shard_map/qkv_back/pallas_call | solution.py:246
  602.4 6.3 collective-permute-done.43
  626.9 5.0 collective-permute-done.45
  (372 shorter events, 228.4 us)
Async XLA Ops:
  7.2 38.1 %all-gather.10.cloned.1.call-start = ((), (), s32[]{:S(2)}) async-start(), calls=%async_computation.5 | async-start | bytes 1179648 | tf_op jit(solution)/shard_map/all_gather | solution.py:573
  14.1 96.4 %all-gather.12.cloned.1.call-start = ((), (), s32[]{:S(2)}) async-start(), calls=%async_computation.6 | async-start | bytes 7077888 | tf_op jit(solution)/shard_map/all_gather | solution.py:578
  17.7 26.1 %collective-permute-start = (bf16[256,2048]{1,0:T(8,128)(2,1)S(1)}, bf16[256,2048]{1,0:T(8,128)(2,1)S(1)}, u32[]{:S(2)}, u32[]{:S(2)}) collective-permute-start(bf16[256,2048]{1,0:T(8,128)(2,1)S(1)} %get-tuple-element.261), channel_id=1, source_target_pairs={{0,8},{8,0},{16,24},{24,16},{1,9},{9,1},{17,25},{25,17},{2,10},{10... | collective-permute-start | bytes 3145736 | tf_op jit(solution)/shard_map/ppermute | solution.py:448
  45.3 103.4 %all-gather.8.cloned.1.call-start = ((), (), s32[]{:S(2)}) async-start(), calls=%async_computation.2 | async-start | bytes 2506752 | tf_op jit(solution)/shard_map/all_gather | solution.py:624
  110.5 161.1 %all-gather.14.cloned.1.call-start = ((), (), s32[]{:S(2)}) async-start(), calls=%async_computation.7 | async-start | bytes 9437184 | tf_op jit(solution)/shard_map/all_gather | solution.py:628
  123.4 512.4 %reduce-scatter.3.cloned.1.call-start = ((), (), s32[]{:S(2)}) async-start(), calls=%async_computation.3 | async-start | bytes 9437184 | tf_op jit(solution)/shard_map/reduce_scatter | solution.py:686
  157.2 25.4 %collective-permute-start.8 = (bf16[128,2176]{1,0:T(8,128)(2,1)S(1)}, bf16[128,2176]{1,0:T(8,128)(2,1)S(1)}, u32[]{:S(2)}, u32[]{:S(2)}) collective-permute-start(bf16[128,2176]{1,0:T(8,128)(2,1)S(1)} %get-tuple-element.274), channel_id=1, source_target_pairs={{0,8},{8,0},{16,24},{24,16},{1,9},{9,1},{17,25},{25,17},{2,10},{10... | collective-permute-start | bytes 1671176 | tf_op jit(solution)/shard_map/ppermute | solution.py:448
  196.0 71.2 %collective-permute-start.14 = (bf16[256,2048]{1,0:T(8,128)(2,1)S(1)}, bf16[256,2048]{1,0:T(8,128)(2,1)}, u32[]{:S(2)}, u32[]{:S(2)}) collective-permute-start(bf16[256,2048]{1,0:T(8,128)(2,1)S(1)} %multiply_convert_fusion.refs_0_), channel_id=1, source_target_pairs={{0,4},{1,5},{2,6},{3,7},{4,0},{5,1},{6,2},{7,3},{8,12},{9,13},{10,... | collective-permute-start | bytes 3145736 | tf_op jit(solution)/shard_map/ppermute | solution.py:448
  270.2 45.2 %collective-permute-start.19 = (bf16[256,2048]{1,0:T(8,128)(2,1)S(1)}, bf16[256,2048]{1,0:T(8,128)(2,1)}, u32[]{:S(2)}, u32[]{:S(2)}) collective-permute-start(bf16[256,2048]{1,0:T(8,128)(2,1)S(1)} %copy-done.9), channel_id=1, source_target_pairs={{0,6},{1,7},{2,4},{3,5},{4,2},{5,3},{6,0},{7,1},{8,14},{9,15},{10,... | collective-permute-start | bytes 3145736 | tf_op jit(solution)/shard_map/ppermute | solution.py:448
  320.8 48.5 %collective-permute-start.22 = (bf16[256,2048]{1,0:T(8,128)(2,1)S(1)}, bf16[256,2048]{1,0:T(8,128)(2,1)}, u32[]{:S(2)}, u32[]{:S(2)}) collective-permute-start(bf16[256,2048]{1,0:T(8,128)(2,1)S(1)} %copy-done.9), channel_id=1, source_target_pairs={{0,2},{1,3},{2,0},{3,1},{4,6},{5,7},{6,4},{7,5},{8,10},{9,11},{10,... | collective-permute-start | bytes 3145736 | tf_op jit(solution)/shard_map/ppermute | solution.py:448
  321.8 48.9 %collective-permute-start.23 = (bf16[256,2048]{1,0:T(8,128)(2,1)}, bf16[256,2048]{1,0:T(8,128)(2,1)}, u32[]{:S(2)}, u32[]{:S(2)}) collective-permute-start(bf16[256,2048]{1,0:T(8,128)(2,1)} %add_convert_fusion.3), channel_id=1, source_target_pairs={{0,4},{1,5},{2,6},{3,7},{4,0},{5,1},{6,2},{7,3},{8,12},{9,13},{10,... | collective-permute-start | bytes 3145736 | tf_op jit(solution)/shard_map/ppermute | solution.py:448
  374.7 46.5 %collective-permute-start.26 = (bf16[256,2048]{1,0:T(8,128)(2,1)}, bf16[256,2048]{1,0:T(8,128)(2,1)}, u32[]{:S(2)}, u32[]{:S(2)}) collective-permute-start(bf16[256,2048]{1,0:T(8,128)(2,1)} %add_convert_fusion.2), channel_id=1, source_target_pairs={{0,6},{1,7},{2,4},{3,5},{4,2},{5,3},{6,0},{7,1},{8,14},{9,15},{10,... | collective-permute-start | bytes 3145736 | tf_op jit(solution)/shard_map/ppermute | solution.py:448
  426.8 26.0 %collective-permute-start.28 = (bf16[256,2048]{1,0:T(8,128)(2,1)}, bf16[256,2048]{1,0:T(8,128)(2,1)S(1)}, u32[]{:S(2)}, u32[]{:S(2)}) collective-permute-start(bf16[256,2048]{1,0:T(8,128)(2,1)} %add_convert_fusion.1), channel_id=1, source_target_pairs={{0,2},{1,3},{2,0},{3,1},{4,6},{5,7},{6,4},{7,5},{8,10},{9,11},{10,... | collective-permute-start | bytes 3145736 | tf_op jit(solution)/shard_map/ppermute | solution.py:448
  456.9 185.5 %reduce-scatter.5.cloned.1.call-start = ((), (), s32[]{:S(2)}) async-start(), calls=%async_computation.4 | async-start | bytes 737280 | tf_op jit(solution)/shard_map/reduce_scatter | solution.py:736
  461.9 27.5 %collective-permute-start.30 = (bf16[256,2304]{1,0:T(8,128)(2,1)S(1)}, bf16[256,2304]{1,0:T(8,128)(2,1)S(1)}, u32[]{:S(2)}, u32[]{:S(2)}) collective-permute-start(bf16[256,2304]{1,0:T(8,128)(2,1)S(1)} %pad_maximum_fusion.3), channel_id=1, source_target_pairs={{0,16},{8,24},{16,0},{24,8},{1,17},{9,25},{17,1},{25,9},{2,18},{10... | collective-permute-start | bytes 3538952 | tf_op jit(solution)/shard_map/ppermute | solution.py:448
  463.4 28.4 %collective-permute-start.29 = (bf16[256,2304]{1,0:T(8,128)(2,1)S(1)}, bf16[256,2304]{1,0:T(8,128)(2,1)S(1)}, u32[]{:S(2)}, u32[]{:S(2)}) collective-permute-start(bf16[256,2304]{1,0:T(8,128)(2,1)S(1)} %pad_maximum_fusion.3), channel_id=1, source_target_pairs={{0,8},{8,0},{16,24},{24,16},{1,9},{9,1},{17,25},{25,17},{2,10},{10... | collective-permute-start | bytes 3538952 | tf_op jit(solution)/shard_map/ppermute | solution.py:448
  511.6 40.8 %collective-permute-start.33 = (bf16[1,2304,128]{2,1,0:T(8,128)(2,1)}, bf16[1,2304,128]{2,1,0:T(8,128)(2,1)}, u32[]{:S(2)}, u32[]{:S(2)}) collective-permute-start(bf16[1,2304,128]{2,1,0:T(8,128)(2,1)} %get-tuple-element.271), channel_id=1, source_target_pairs={{0,8},{8,0},{16,24},{24,16},{1,9},{9,1},{17,25},{25,17},{2,10},{10... | collective-permute-start | bytes 1769480 | tf_op jit(solution)/shard_map/ppermute | solution.py:448
  512.1 40.3 %collective-permute-start.34 = (bf16[1,2304,128]{2,1,0:T(8,128)(2,1)}, bf16[1,2304,128]{2,1,0:T(8,128)(2,1)}, u32[]{:S(2)}, u32[]{:S(2)}) collective-permute-start(bf16[1,2304,128]{2,1,0:T(8,128)(2,1)} %get-tuple-element.270), channel_id=1, source_target_pairs={{0,16},{8,24},{16,0},{24,8},{1,17},{9,25},{17,1},{25,9},{2,18},{10... | collective-permute-start | bytes 1769480 | tf_op jit(solution)/shard_map/ppermute | solution.py:448
  513.6 38.8 %collective-permute-start.35 = (bf16[1,2304,128]{2,1,0:T(8,128)(2,1)}, bf16[1,2304,128]{2,1,0:T(8,128)(2,1)}, u32[]{:S(2)}, u32[]{:S(2)}) collective-permute-start(bf16[1,2304,128]{2,1,0:T(8,128)(2,1)} %get-tuple-element.269), channel_id=1, source_target_pairs={{0,8},{8,0},{16,24},{24,16},{1,9},{9,1},{17,25},{25,17},{2,10},{10... | collective-permute-start | bytes 1769480 | tf_op jit(solution)/shard_map/ppermute | solution.py:448
  515.1 37.3 %collective-permute-start.36 = (bf16[1,2304,128]{2,1,0:T(8,128)(2,1)}, bf16[1,2304,128]{2,1,0:T(8,128)(2,1)}, u32[]{:S(2)}, u32[]{:S(2)}) collective-permute-start(bf16[1,2304,128]{2,1,0:T(8,128)(2,1)} %get-tuple-element.268), channel_id=1, source_target_pairs={{0,16},{8,24},{16,0},{24,8},{1,17},{9,25},{17,1},{25,9},{2,18},{10... | collective-permute-start | bytes 1769480 | tf_op jit(solution)/shard_map/ppermute | solution.py:448
  562.1 29.1 %collective-permute-start.40 = (bf16[1,2304,128]{2,1,0:T(8,128)(2,1)}, bf16[1,2304,128]{2,1,0:T(8,128)(2,1)}, u32[]{:S(2)}, u32[]{:S(2)}) collective-permute-start(bf16[1,2304,128]{2,1,0:T(8,128)(2,1)} %get-tuple-element.233), channel_id=1, source_target_pairs={{0,16},{8,24},{16,0},{24,8},{1,17},{9,25},{17,1},{25,9},{2,18},{10... | collective-permute-start | bytes 1769480 | tf_op jit(solution)/shard_map/ppermute | solution.py:448
  563.0 28.2 %collective-permute-start.41 = (bf16[1,2304,128]{2,1,0:T(8,128)(2,1)}, bf16[1,2304,128]{2,1,0:T(8,128)(2,1)}, u32[]{:S(2)}, u32[]{:S(2)}) collective-permute-start(bf16[1,2304,128]{2,1,0:T(8,128)(2,1)} %get-tuple-element.234), channel_id=1, source_target_pairs={{0,8},{8,0},{16,24},{24,16},{1,9},{9,1},{17,25},{25,17},{2,10},{10... | collective-permute-start | bytes 1769480 | tf_op jit(solution)/shard_map/ppermute | solution.py:448
  596.4 30.5 %collective-permute-start.42 = (bf16[128,2048]{1,0:T(8,128)(2,1)}, bf16[128,2048]{1,0:T(8,128)(2,1)}, u32[]{:S(2)}, u32[]{:S(2)}) collective-permute-start(bf16[128,2048]{1,0:T(8,128)(2,1)} %get-tuple-element.282), channel_id=1, source_target_pairs={{0,8},{8,0},{16,24},{24,16},{1,9},{9,1},{17,25},{25,17},{2,10},{10... | collective-permute-start | bytes 1572872 | tf_op jit(solution)/shard_map/ppermute | solution.py:448
  596.9 30.0 %collective-permute-start.46 = (bf16[128,2048]{1,0:T(8,128)(2,1)}, bf16[128,2048]{1,0:T(8,128)(2,1)}, u32[]{:S(2)}, u32[]{:S(2)}) collective-permute-start(bf16[128,2048]{1,0:T(8,128)(2,1)} %get-tuple-element.283), channel_id=1, source_target_pairs={{0,16},{8,24},{16,0},{24,8},{1,17},{9,25},{17,1},{25,9},{2,18},{10... | collective-permute-start | bytes 1572872 | tf_op jit(solution)/shard_map/ppermute | solution.py:448
  (88 other events, 786.3 us)
Sparse Core Ops, SparseCore 0:
  14.2 24.9 all-gather.9
  45.4 65.0 all-gather.11
  112.1 28.8 all-gather.7
  142.5 115.4 all-gather.13
  457.0 88.7 reduce-scatter.2
  588.2 30.1 reduce-scatter.4

commit v8 on v7

--- a/solution.py
+++ b/solution.py
@@ -352,7 +352,7 @@
     unused, dp_count, cap, own_rows = pick.shape
     rank = a_down.shape[2]
     rows = 2 * cap
-    tile = min(256, ff)
+    tile = min(512, ff)
     low = jnp.bfloat16
     f32 = jnp.float32
     one = pl.Buffered(1)

time: 665 us -> 661 us (level)
  Pallas kernels: 266 us -> 253 us
    pallas_call x4, Pallas kernels: 175 us -> 162 us  [run_experts(): pl.pallas_call(functools.partial(expert_kernel, len(kept)), grid_spec=plt...]
  transfers between devices with their start and end apart: 61 -> 61, of which waited for: 24 -> 25; matrix products, arithmetic and copies ran while one was open for 22% -> 22% of each run, Pallas kernels for 41% -> 39%
where the time goes in v8:
time: 661 us; the launch traced here: 651 us
  Pallas kernels  253 us (38%)
  waiting for transfers between devices  156 us (24%)
  other arithmetic  73.9 us (11%)
  local copies, waits for them, and re-layouts  61.2 us (9%)
  starting transfers between devices  59.8 us (9%)
  matrix products  31.4 us (5%)
  between operations  15.5 us (2%)
    pallas_call x4, Pallas kernels, run_experts(): pl.pallas_call(functools.partial(expert_kernel, len(kept)), grid_spec=plt...  162 us
    ppermute x55, waiting for transfers between devices, swap(): return lax.ppermute(values, axis, [(i, i ^ distance) for i in range(count)])  151 us
    ppermute x55, starting transfers between devices, swap(): return lax.ppermute(values, axis, [(i, i ^ distance) for i in range(count)])  58.8 us
    pallas_call x1, Pallas kernels, attend(): pl.pallas_call(functools.partial(attend_kernel, tile), grid=(heads,), in_...  23.7 us
    pallas_call x1, Pallas kernels, attend_back(): pl.pallas_call(functools.partial(attend_back_kernel, tile), grid=(heads,)...  23.7 us
    pallas_call x1, Pallas kernels, adapter_grads(): pl.pallas_call(adapter_kernel, grid_spec=pltpu.PrefetchScalarGridSpec(num...  18.4 us
    dot_general x6, matrix products, local(): dot = lambda a, b: jnp.dot(a, b, preferred_element_type=f32)  13.3 us
    unnamed x114, local copies, waits for them, and re-layouts  13.3 us
  transfers between devices with their start and end apart: 61, of which 25 were waited for; matrix products, arithmetic and copies ran while one was open for 22% of the time, Pallas kernels for 39%

profile of v8, /device:TPU:0, one launch (start us, length us, event | category | flops | bytes accessed | tf_op | source)
XLA Modules:
  0.0 651.0 jit_solution(9844246107124497112)
XLA Ops:
  22.2 21.6 %collective-permute-done = bf16[256,2048]{1,0:T(8,128)(2,1)S(1)} collective-permute-done((bf16[256,2048]{1,0:T(8,128)(2,1)S(1)}, bf16[256,2048]{1,0:T(8,128)(2,1)S(1)}, u32[]{:S(2)}, u32[]{:S(2)}) %collective-permute-start) | collective-permute-done | bytes 1048608 | tf_op jit(solution)/shard_map/ppermute | solution.py:448
  99.2 6.5 %multiply_convert_fusion.1.reduced_ref = bf16[1024,384]{1,0:T(8,128)(2,1)} fusion(f32[1024,384]{1,0:T(8,128)} %copy.124, bf16[1024,2048]{1,0:T(8,128)(2,1)} %constant_dynamic-update-slice_fusion.x_ref, bf16[2048,384]{0,1:T(8,128)(2,1)S(1)} %bitcast.232), kind=kOutput, calls=%fused_computation.50 | convolution fusion | flops 1611399168 | bytes 8126464 | tf_op jit(solution)/shard_map/dot_general | solution.py:608
  105.7 4.8 all-gather.12.cloned.1.call-done
  110.5 12.9 %qkv_project.1.q_raw.k_raw.v_raw = f32[3,1024,512]{2,1,0:T(8,128)} custom-call(bf16[1024,2048]{1,0:T(8,128)(2,1)} %constant_dynamic-update-slice_fusion.x_ref, bf16[1024,384]{1,0:T(8,128)(2,1)} %multiply_convert_fusion.1.reduced_ref, bf16[8,3,64,2048]{3,2,1,0:T(8,128)(2,1)} %bitcast.234, bf16[3,512,128]{2,1,0:T(8,128)(2,1)} %bitcast.245), custom_call_target="tpu_custom_call" | custom-call | flops 6442450944 | bytes 16777216 | tf_op jit(solution)/shard_map/qkv_project/pallas_call | solution.py:213
  125.0 23.7 %attend.1 = (bf16[1024,512]{1,0:T(8,128)(2,1)}, bf16[1024,512]{1,0:T(8,128)(2,1)}, bf16[1024,512]{1,0:T(8,128)(2,1)}, bf16[1024,512]{1,0:T(8,128)(2,1)}, f32[4,1,1024]{2,1,0:T(1,128)}) custom-call(f32[3,1024,512]{2,1,0:T(8,128)} %qkv_project.1.q_raw.k_raw.v_raw, f32[3,1024,512]{2,1,0:T(8,128)} %qkv_project.1.q_raw.k_raw.v_raw, ...), custom_call_target="tpu_custom_call" | custom-call | flops 2147483648 | bytes 10485760 | tf_op jit(solution)/shard_map/attend/pallas_call | solution.py:100
  148.7 4.9 convolution_convert_fusion
  157.9 11.4 %collective-permute-done.10 = bf16[128,2176]{1,0:T(8,128)(2,1)S(1)} collective-permute-done((bf16[128,2176]{1,0:T(8,128)(2,1)S(1)}, bf16[128,2176]{1,0:T(8,128)(2,1)S(1)}, u32[]{:S(2)}, u32[]{:S(2)}) %collective-permute-start.10) | collective-permute-done | bytes 557088 | tf_op jit(solution)/shard_map/ppermute | solution.py:448
  173.1 8.2 %collective-permute-done.12 = bf16[128,2176]{1,0:T(8,128)(2,1)S(1)} collective-permute-done((bf16[128,2176]{1,0:T(8,128)(2,1)S(1)}, bf16[128,2176]{1,0:T(8,128)(2,1)S(1)}, u32[]{:S(2)}, u32[]{:S(2)}) %collective-permute-start.12) | collective-permute-done | bytes 557088 | tf_op jit(solution)/shard_map/ppermute | solution.py:448
  182.6 9.9 %collective-permute-done.11 = bf16[128,2176]{1,0:T(8,128)(2,1)S(1)} collective-permute-done((bf16[128,2176]{1,0:T(8,128)(2,1)S(1)}, bf16[128,2176]{1,0:T(8,128)(2,1)S(1)}, u32[]{:S(2)}, u32[]{:S(2)}) %collective-permute-start.11) | collective-permute-done | bytes 557088 | tf_op jit(solution)/shard_map/ppermute | solution.py:448
  202.2 40.6 %experts.4 = (bf16[8,256,2048]{2,1,0:T(8,128)(2,1)}, bf16[256,2048]{1,0:T(8,128)(2,1)}, bf16[256,2048]{1,0:T(8,128)(2,1)}, bf16[2,1152,2048]{2,1,0:T(8,128)(2,1)...) custom-call(s32[5]{0:T(128)} %pad_add_fusion.which, ...), custom_call_target="tpu_custom_call" | custom-call | flops 1179648 | bytes 1179648 | tf_op jit(solution)/shard_map/experts/pallas_call | solution.py:381
  243.0 24.2 %collective-permute-done.14.refs_0_ = bf16[256,2048]{1,0:T(8,128)(2,1)} collective-permute-done((bf16[256,2048]{1,0:T(8,128)(2,1)S(1)}, bf16[256,2048]{1,0:T(8,128)(2,1)}, u32[]{:S(2)}, u32[]{:S(2)}) %collective-permute-start.14) | collective-permute-done | bytes 1048608 | tf_op jit(solution)/shard_map/ppermute | solution.py:448
  271.5 40.5 %experts.5 = (bf16[8,256,2048]{2,1,0:T(8,128)(2,1)}, bf16[256,2048]{1,0:T(8,128)(2,1)}, bf16[256,2048]{1,0:T(8,128)(2,1)}, bf16[2,1152,2048]{2,1,0:T(8,128)(2,1)...) custom-call(s32[5]{0:T(128)} %stack.88.which, ...), custom_call_target="tpu_custom_call", output_to_operand_aliasing={{0}: (13, {}), {3}: (14, {}), {4}: (15, {}), {5}: (16, {}),... | custom-call | flops 1179648 | bytes 1179648 | tf_op jit(solution)/shard_map/experts/pallas_call | solution.py:381
  322.3 40.7 %experts.6 = (bf16[8,256,2048]{2,1,0:T(8,128)(2,1)}, bf16[256,2048]{1,0:T(8,128)(2,1)}, bf16[256,2048]{1,0:T(8,128)(2,1)}, bf16[2,1152,2048]{2,1,0:T(8,128)(2,1)...) custom-call(s32[5]{0:T(128)} %stack.90.which, ...), custom_call_target="tpu_custom_call", output_to_operand_aliasing={{0}: (13, {}), {3}: (14, {}), {4}: (15, {}), {5}: (16, {}),... | custom-call | flops 1179648 | bytes 1179648 | tf_op jit(solution)/shard_map/experts/pallas_call | solution.py:381
  374.4 40.5 %experts.7 = (bf16[8,256,2048]{2,1,0:T(8,128)(2,1)}, bf16[256,2048]{1,0:T(8,128)(2,1)}, bf16[256,2048]{1,0:T(8,128)(2,1)}, bf16[2,1152,2048]{2,1,0:T(8,128)(2,1)...) custom-call(s32[5]{0:T(128)} %stack.82.which, ...), custom_call_target="tpu_custom_call", output_to_operand_aliasing={{0}: (13, {}), {3}: (14, {}), {4}: (15, {}), {5}: (16, {}),... | custom-call | flops 1179648 | bytes 1179648 | tf_op jit(solution)/shard_map/experts/pallas_call | solution.py:381
  420.4 4.7 collective-permute-start.28
  425.6 18.4 %adapter_grads.1 = bf16[4,2,2304,128]{3,2,1,0:T(8,128)(2,1)} custom-call(s32[4]{0:T(128)} %iota_xor_fusion.which, bf16[2,1152,2048]{2,1,0:T(8,128)(2,1)} %get-tuple-element.200.xs, bf16[2,1152,2048]{2,1,0:T(8,128)(2,1)} %get-tuple-element.201.ps, bf16[2,1152,1024]{2,1,0:T(8,128)(2,1)} %get-tuple-element.202.act, ...), custom_call_target="tpu_custom_call" | custom-call | flops 2359296 | bytes 2359296 | tf_op jit(solution)/shard_map/adapter_grads/pallas_call | solution.py:433
  444.0 4.7 collective-permute-done.28
  448.8 4.1 convert_add_fusion.1
  460.9 24.5 %collective-permute-done.30 = bf16[256,2304]{1,0:T(8,128)(2,1)S(1)} collective-permute-done((bf16[256,2304]{1,0:T(8,128)(2,1)S(1)}, bf16[256,2304]{1,0:T(8,128)(2,1)S(1)}, u32[]{:S(2)}, u32[]{:S(2)}) %collective-permute-start.30) | collective-permute-done | bytes 1179680 | tf_op jit(solution)/shard_map/ppermute | solution.py:448
  492.3 8.4 %collective-permute-done.31 = bf16[128,2304]{1,0:T(8,128)(2,1)} collective-permute-done((bf16[128,2304]{1,0:T(8,128)(2,1)}, bf16[128,2304]{1,0:T(8,128)(2,1)}, u32[]{:S(2)}, u32[]{:S(2)}) %collective-permute-start.31) | collective-permute-done | bytes 589856 | tf_op jit(solution)/shard_map/ppermute | solution.py:448
  519.9 23.7 %attend_back.1 = (bf16[1024,512]{1,0:T(8,128)(2,1)}, bf16[1024,512]{1,0:T(8,128)(2,1)}, bf16[1024,512]{1,0:T(8,128)(2,1)}) custom-call(bf16[1024,512]{1,0:T(8,128)(2,1)} %get-tuple-element.141.query, bf16[1024,512]{1,0:T(8,128)(2,1)} %get-tuple-element.142.key, bf16[1024,512]{1,0:T(8,128)(2,1)} %get-tuple-element.143.value, ...), custom_call_target="tpu_custom_call" | custom-call | flops 524288 | bytes 524288 | tf_op jit(solution)/shard_map/attend_back/pallas_call | solution.py:168
  559.6 12.3 %qkv_back.1 = bf16[1024,2048]{1,0:T(8,128)(2,1)} custom-call(bf16[1024,512]{1,0:T(8,128)(2,1)} %get-tuple-element.241.a_ref, bf16[1024,512]{1,0:T(8,128)(2,1)} %get-tuple-element.242.b_ref, bf16[1024,512]{1,0:T(8,128)(2,1)} %get-tuple-element.243.c_ref, bf16[8,3,64,2048]{3,2,1,0:T(8,128)(2,1)} %bitcast.235), custom_call_target="tpu_custom_call" | custom-call | flops 2097152 | bytes 2097152 | tf_op jit(solution)/shard_map/qkv_back/pallas_call | solution.py:246
  598.4 6.3 collective-permute-done.43
  623.0 5.0 collective-permute-done.45
  (372 shorter events, 232.9 us)
Async XLA Ops:
  7.2 38.1 %all-gather.10.cloned.1.call-start = ((), (), s32[]{:S(2)}) async-start(), calls=%async_computation.5 | async-start | bytes 1179648 | tf_op jit(solution)/shard_map/all_gather | solution.py:573
  14.1 96.4 %all-gather.12.cloned.1.call-start = ((), (), s32[]{:S(2)}) async-start(), calls=%async_computation.6 | async-start | bytes 7077888 | tf_op jit(solution)/shard_map/all_gather | solution.py:578
  17.7 26.1 %collective-permute-start = (bf16[256,2048]{1,0:T(8,128)(2,1)S(1)}, bf16[256,2048]{1,0:T(8,128)(2,1)S(1)}, u32[]{:S(2)}, u32[]{:S(2)}) collective-permute-start(bf16[256,2048]{1,0:T(8,128)(2,1)S(1)} %get-tuple-element.261), channel_id=1, source_target_pairs={{0,8},{8,0},{16,24},{24,16},{1,9},{9,1},{17,25},{25,17},{2,10},{10... | collective-permute-start | bytes 3145736 | tf_op jit(solution)/shard_map/ppermute | solution.py:448
  45.3 103.4 %all-gather.8.cloned.1.call-start = ((), (), s32[]{:S(2)}) async-start(), calls=%async_computation.2 | async-start | bytes 2506752 | tf_op jit(solution)/shard_map/all_gather | solution.py:624
  110.5 161.1 %all-gather.14.cloned.1.call-start = ((), (), s32[]{:S(2)}) async-start(), calls=%async_computation.7 | async-start | bytes 9437184 | tf_op jit(solution)/shard_map/all_gather | solution.py:628
  123.4 508.4 %reduce-scatter.3.cloned.1.call-start = ((), (), s32[]{:S(2)}) async-start(), calls=%async_computation.3 | async-start | bytes 9437184 | tf_op jit(solution)/shard_map/reduce_scatter | solution.py:686
  157.2 25.4 %collective-permute-start.8 = (bf16[128,2176]{1,0:T(8,128)(2,1)S(1)}, bf16[128,2176]{1,0:T(8,128)(2,1)S(1)}, u32[]{:S(2)}, u32[]{:S(2)}) collective-permute-start(bf16[128,2176]{1,0:T(8,128)(2,1)S(1)} %get-tuple-element.274), channel_id=1, source_target_pairs={{0,8},{8,0},{16,24},{24,16},{1,9},{9,1},{17,25},{25,17},{2,10},{10... | collective-permute-start | bytes 1671176 | tf_op jit(solution)/shard_map/ppermute | solution.py:448
  196.0 71.2 %collective-permute-start.14 = (bf16[256,2048]{1,0:T(8,128)(2,1)S(1)}, bf16[256,2048]{1,0:T(8,128)(2,1)}, u32[]{:S(2)}, u32[]{:S(2)}) collective-permute-start(bf16[256,2048]{1,0:T(8,128)(2,1)S(1)} %multiply_convert_fusion.refs_0_), channel_id=1, source_target_pairs={{0,4},{1,5},{2,6},{3,7},{4,0},{5,1},{6,2},{7,3},{8,12},{9,13},{10,... | collective-permute-start | bytes 3145736 | tf_op jit(solution)/shard_map/ppermute | solution.py:448
  270.2 42.0 %collective-permute-start.19 = (bf16[256,2048]{1,0:T(8,128)(2,1)S(1)}, bf16[256,2048]{1,0:T(8,128)(2,1)}, u32[]{:S(2)}, u32[]{:S(2)}) collective-permute-start(bf16[256,2048]{1,0:T(8,128)(2,1)S(1)} %copy-done.9), channel_id=1, source_target_pairs={{0,6},{1,7},{2,4},{3,5},{4,2},{5,3},{6,0},{7,1},{8,14},{9,15},{10,... | collective-permute-start | bytes 3145736 | tf_op jit(solution)/shard_map/ppermute | solution.py:448
  317.6 47.8 %collective-permute-start.22 = (bf16[256,2048]{1,0:T(8,128)(2,1)S(1)}, bf16[256,2048]{1,0:T(8,128)(2,1)}, u32[]{:S(2)}, u32[]{:S(2)}) collective-permute-start(bf16[256,2048]{1,0:T(8,128)(2,1)S(1)} %copy-done.9), channel_id=1, source_target_pairs={{0,2},{1,3},{2,0},{3,1},{4,6},{5,7},{6,4},{7,5},{8,10},{9,11},{10,... | collective-permute-start | bytes 3145736 | tf_op jit(solution)/shard_map/ppermute | solution.py:448
  319.5 48.7 %collective-permute-start.23 = (bf16[256,2048]{1,0:T(8,128)(2,1)}, bf16[256,2048]{1,0:T(8,128)(2,1)}, u32[]{:S(2)}, u32[]{:S(2)}) collective-permute-start(bf16[256,2048]{1,0:T(8,128)(2,1)} %add_convert_fusion.3), channel_id=1, source_target_pairs={{0,4},{1,5},{2,6},{3,7},{4,0},{5,1},{6,2},{7,3},{8,12},{9,13},{10,... | collective-permute-start | bytes 3145736 | tf_op jit(solution)/shard_map/ppermute | solution.py:448
  371.1 43.7 %collective-permute-start.26 = (bf16[256,2048]{1,0:T(8,128)(2,1)}, bf16[256,2048]{1,0:T(8,128)(2,1)}, u32[]{:S(2)}, u32[]{:S(2)}) collective-permute-start(bf16[256,2048]{1,0:T(8,128)(2,1)} %add_convert_fusion.2), channel_id=1, source_target_pairs={{0,6},{1,7},{2,4},{3,5},{4,2},{5,3},{6,0},{7,1},{8,14},{9,15},{10,... | collective-permute-start | bytes 3145736 | tf_op jit(solution)/shard_map/ppermute | solution.py:448
  420.4 28.3 %collective-permute-start.28 = (bf16[256,2048]{1,0:T(8,128)(2,1)}, bf16[256,2048]{1,0:T(8,128)(2,1)S(1)}, u32[]{:S(2)}, u32[]{:S(2)}) collective-permute-start(bf16[256,2048]{1,0:T(8,128)(2,1)} %add_convert_fusion.1), channel_id=1, source_target_pairs={{0,2},{1,3},{2,0},{3,1},{4,6},{5,7},{6,4},{7,5},{8,10},{9,11},{10,... | collective-permute-start | bytes 3145736 | tf_op jit(solution)/shard_map/ppermute | solution.py:448
  452.9 185.4 %reduce-scatter.5.cloned.1.call-start = ((), (), s32[]{:S(2)}) async-start(), calls=%async_computation.4 | async-start | bytes 737280 | tf_op jit(solution)/shard_map/reduce_scatter | solution.py:736
  457.9 27.5 %collective-permute-start.30 = (bf16[256,2304]{1,0:T(8,128)(2,1)S(1)}, bf16[256,2304]{1,0:T(8,128)(2,1)S(1)}, u32[]{:S(2)}, u32[]{:S(2)}) collective-permute-start(bf16[256,2304]{1,0:T(8,128)(2,1)S(1)} %pad_maximum_fusion.3), channel_id=1, source_target_pairs={{0,16},{8,24},{16,0},{24,8},{1,17},{9,25},{17,1},{25,9},{2,18},{10... | collective-permute-start | bytes 3538952 | tf_op jit(solution)/shard_map/ppermute | solution.py:448
  459.4 28.4 %collective-permute-start.29 = (bf16[256,2304]{1,0:T(8,128)(2,1)S(1)}, bf16[256,2304]{1,0:T(8,128)(2,1)S(1)}, u32[]{:S(2)}, u32[]{:S(2)}) collective-permute-start(bf16[256,2304]{1,0:T(8,128)(2,1)S(1)} %pad_maximum_fusion.3), channel_id=1, source_target_pairs={{0,8},{8,0},{16,24},{24,16},{1,9},{9,1},{17,25},{25,17},{2,10},{10... | collective-permute-start | bytes 3538952 | tf_op jit(solution)/shard_map/ppermute | solution.py:448
  507.6 40.8 %collective-permute-start.33 = (bf16[1,2304,128]{2,1,0:T(8,128)(2,1)}, bf16[1,2304,128]{2,1,0:T(8,128)(2,1)}, u32[]{:S(2)}, u32[]{:S(2)}) collective-permute-start(bf16[1,2304,128]{2,1,0:T(8,128)(2,1)} %get-tuple-element.271), channel_id=1, source_target_pairs={{0,8},{8,0},{16,24},{24,16},{1,9},{9,1},{17,25},{25,17},{2,10},{10... | collective-permute-start | bytes 1769480 | tf_op jit(solution)/shard_map/ppermute | solution.py:448
  508.2 40.3 %collective-permute-start.34 = (bf16[1,2304,128]{2,1,0:T(8,128)(2,1)}, bf16[1,2304,128]{2,1,0:T(8,128)(2,1)}, u32[]{:S(2)}, u32[]{:S(2)}) collective-permute-start(bf16[1,2304,128]{2,1,0:T(8,128)(2,1)} %get-tuple-element.270), channel_id=1, source_target_pairs={{0,16},{8,24},{16,0},{24,8},{1,17},{9,25},{17,1},{25,9},{2,18},{10... | collective-permute-start | bytes 1769480 | tf_op jit(solution)/shard_map/ppermute | solution.py:448
  509.6 38.8 %collective-permute-start.35 = (bf16[1,2304,128]{2,1,0:T(8,128)(2,1)}, bf16[1,2304,128]{2,1,0:T(8,128)(2,1)}, u32[]{:S(2)}, u32[]{:S(2)}) collective-permute-start(bf16[1,2304,128]{2,1,0:T(8,128)(2,1)} %get-tuple-element.269), channel_id=1, source_target_pairs={{0,8},{8,0},{16,24},{24,16},{1,9},{9,1},{17,25},{25,17},{2,10},{10... | collective-permute-start | bytes 1769480 | tf_op jit(solution)/shard_map/ppermute | solution.py:448
  511.1 37.3 %collective-permute-start.36 = (bf16[1,2304,128]{2,1,0:T(8,128)(2,1)}, bf16[1,2304,128]{2,1,0:T(8,128)(2,1)}, u32[]{:S(2)}, u32[]{:S(2)}) collective-permute-start(bf16[1,2304,128]{2,1,0:T(8,128)(2,1)} %get-tuple-element.268), channel_id=1, source_target_pairs={{0,16},{8,24},{16,0},{24,8},{1,17},{9,25},{17,1},{25,9},{2,18},{10... | collective-permute-start | bytes 1769480 | tf_op jit(solution)/shard_map/ppermute | solution.py:448
  558.1 29.1 %collective-permute-start.40 = (bf16[1,2304,128]{2,1,0:T(8,128)(2,1)}, bf16[1,2304,128]{2,1,0:T(8,128)(2,1)}, u32[]{:S(2)}, u32[]{:S(2)}) collective-permute-start(bf16[1,2304,128]{2,1,0:T(8,128)(2,1)} %get-tuple-element.233), channel_id=1, source_target_pairs={{0,16},{8,24},{16,0},{24,8},{1,17},{9,25},{17,1},{25,9},{2,18},{10... | collective-permute-start | bytes 1769480 | tf_op jit(solution)/shard_map/ppermute | solution.py:448
  559.0 28.3 %collective-permute-start.41 = (bf16[1,2304,128]{2,1,0:T(8,128)(2,1)}, bf16[1,2304,128]{2,1,0:T(8,128)(2,1)}, u32[]{:S(2)}, u32[]{:S(2)}) collective-permute-start(bf16[1,2304,128]{2,1,0:T(8,128)(2,1)} %get-tuple-element.234), channel_id=1, source_target_pairs={{0,8},{8,0},{16,24},{24,16},{1,9},{9,1},{17,25},{25,17},{2,10},{10... | collective-permute-start | bytes 1769480 | tf_op jit(solution)/shard_map/ppermute | solution.py:448
  592.5 30.5 %collective-permute-start.42 = (bf16[128,2048]{1,0:T(8,128)(2,1)}, bf16[128,2048]{1,0:T(8,128)(2,1)}, u32[]{:S(2)}, u32[]{:S(2)}) collective-permute-start(bf16[128,2048]{1,0:T(8,128)(2,1)} %get-tuple-element.282), channel_id=1, source_target_pairs={{0,8},{8,0},{16,24},{24,16},{1,9},{9,1},{17,25},{25,17},{2,10},{10... | collective-permute-start | bytes 1572872 | tf_op jit(solution)/shard_map/ppermute | solution.py:448
  593.0 30.0 %collective-permute-start.46 = (bf16[128,2048]{1,0:T(8,128)(2,1)}, bf16[128,2048]{1,0:T(8,128)(2,1)}, u32[]{:S(2)}, u32[]{:S(2)}) collective-permute-start(bf16[128,2048]{1,0:T(8,128)(2,1)} %get-tuple-element.283), channel_id=1, source_target_pairs={{0,16},{8,24},{16,0},{24,8},{1,17},{9,25},{17,1},{25,9},{2,18},{10... | collective-permute-start | bytes 1572872 | tf_op jit(solution)/shard_map/ppermute | solution.py:448
  (88 other events, 792.1 us)
Sparse Core Ops, SparseCore 0:
  14.2 24.9 all-gather.9
  45.4 65.0 all-gather.11
  112.1 28.8 all-gather.7
  142.5 115.4 all-gather.13
  453.0 88.7 reduce-scatter.2
  584.2 30.1 reduce-scatter.4

commit v9 on v8

--- a/solution.py
+++ b/solution.py
@@ -91,7 +91,7 @@
 def attend(raw, cosine, sine, gain_q, gain_k, segment):
     unused, length, width = raw.shape
     heads = width // HD
-    tile = min(256, length)
+    tile = min(512, length)
     head = pl.BlockSpec((length, HD), lambda h: (0, h))
     raw_head = [pl.BlockSpec((None, length, HD), functools.partial(lambda m, h: (m, 0, h), m)) for m in range(3)]
     fixed = lambda shape: pl.BlockSpec(shape, lambda h: (0, 0))
@@ -159,7 +159,7 @@
     query, key, value, stat = kept
     unused, length, width = raw.shape
     heads = width // HD
-    tile = min(256, length)
+    tile = min(512, length)
     head = pl.BlockSpec((length, HD), lambda h: (0, h))
     raw_head = [pl.BlockSpec((None, length, HD), functools.partial(lambda m, h: (m, 0, h), m)) for m in range(3)]
     fixed = lambda shape: pl.BlockSpec(shape, lambda h: (0, 0))

time: 661 us -> 661 us (level)
  transfers between devices with their start and end apart: 61 -> 61, of which waited for: 25 -> 25; matrix products, arithmetic and copies ran while one was open for 22% -> 22% of each run, Pallas kernels for 39% -> 38%
where the time goes in v9:
time: 661 us; the launch traced here: 651 us
  Pallas kernels  249 us (38%)
  waiting for transfers between devices  160 us (24%)
  other arithmetic  73.9 us (11%)
  local copies, waits for them, and re-layouts  61.3 us (9%)
  starting transfers between devices  60 us (9%)
  matrix products  31 us (5%)
  between operations  15.5 us (2%)
    pallas_call x4, Pallas kernels, run_experts(): pl.pallas_call(functools.partial(expert_kernel, len(kept)), grid_spec=plt...  162 us
    ppermute x55, waiting for transfers between devices, swap(): return lax.ppermute(values, axis, [(i, i ^ distance) for i in range(count)])  155 us
    ppermute x55, starting transfers between devices, swap(): return lax.ppermute(values, axis, [(i, i ^ distance) for i in range(count)])  59.1 us
    pallas_call x1, Pallas kernels, attend_back(): pl.pallas_call(functools.partial(attend_back_kernel, tile), grid=(heads,)...  23.6 us
    pallas_call x1, Pallas kernels, attend(): pl.pallas_call(functools.partial(attend_kernel, tile), grid=(heads,), in_...  19.6 us
    pallas_call x1, Pallas kernels, adapter_grads(): pl.pallas_call(adapter_kernel, grid_spec=pltpu.PrefetchScalarGridSpec(num...  18.4 us
    unnamed x114, local copies, waits for them, and re-layouts  13.3 us
  transfers between devices with their start and end apart: 61, of which 25 were waited for; matrix products, arithmetic and copies ran while one was open for 22% of the time, Pallas kernels for 38%

profile of v9, /device:TPU:0, one launch (start us, length us, event | category | flops | bytes accessed | tf_op | source)
XLA Modules:
  0.0 650.9 jit_solution(18159600100900921586)
XLA Ops:
  22.2 21.6 %collective-permute-done = bf16[256,2048]{1,0:T(8,128)(2,1)S(1)} collective-permute-done((bf16[256,2048]{1,0:T(8,128)(2,1)S(1)}, bf16[256,2048]{1,0:T(8,128)(2,1)S(1)}, u32[]{:S(2)}, u32[]{:S(2)}) %collective-permute-start) | collective-permute-done | bytes 1048608 | tf_op jit(solution)/shard_map/ppermute | solution.py:448
  99.2 6.5 %multiply_convert_fusion.1.reduced_ref = bf16[1024,384]{1,0:T(8,128)(2,1)} fusion(f32[1024,384]{1,0:T(8,128)} %copy.124, bf16[1024,2048]{1,0:T(8,128)(2,1)} %constant_dynamic-update-slice_fusion.x_ref, bf16[2048,384]{0,1:T(8,128)(2,1)S(1)} %bitcast.232), kind=kOutput, calls=%fused_computation.50 | convolution fusion | flops 1611399168 | bytes 8126464 | tf_op jit(solution)/shard_map/dot_general | solution.py:608
  105.7 4.8 all-gather.12.cloned.1.call-done
  110.5 12.9 %qkv_project.1.q_raw.k_raw.v_raw = f32[3,1024,512]{2,1,0:T(8,128)} custom-call(bf16[1024,2048]{1,0:T(8,128)(2,1)} %constant_dynamic-update-slice_fusion.x_ref, bf16[1024,384]{1,0:T(8,128)(2,1)} %multiply_convert_fusion.1.reduced_ref, bf16[8,3,64,2048]{3,2,1,0:T(8,128)(2,1)} %bitcast.234, bf16[3,512,128]{2,1,0:T(8,128)(2,1)} %bitcast.245), custom_call_target="tpu_custom_call" | custom-call | flops 6442450944 | bytes 16777216 | tf_op jit(solution)/shard_map/qkv_project/pallas_call | solution.py:213
  125.0 19.6 %attend.1 = (bf16[1024,512]{1,0:T(8,128)(2,1)}, bf16[1024,512]{1,0:T(8,128)(2,1)}, bf16[1024,512]{1,0:T(8,128)(2,1)}, bf16[1024,512]{1,0:T(8,128)(2,1)}, f32[4,1,1024]{2,1,0:T(1,128)}) custom-call(f32[3,1024,512]{2,1,0:T(8,128)} %qkv_project.1.q_raw.k_raw.v_raw, f32[3,1024,512]{2,1,0:T(8,128)} %qkv_project.1.q_raw.k_raw.v_raw, ...), custom_call_target="tpu_custom_call" | custom-call | flops 2147483648 | bytes 10485760 | tf_op jit(solution)/shard_map/attend/pallas_call | solution.py:100
  144.7 4.6 convolution_convert_fusion
  153.5 11.4 %collective-permute-done.10 = bf16[128,2176]{1,0:T(8,128)(2,1)S(1)} collective-permute-done((bf16[128,2176]{1,0:T(8,128)(2,1)S(1)}, bf16[128,2176]{1,0:T(8,128)(2,1)S(1)}, u32[]{:S(2)}, u32[]{:S(2)}) %collective-permute-start.10) | collective-permute-done | bytes 557088 | tf_op jit(solution)/shard_map/ppermute | solution.py:448
  168.7 8.2 %collective-permute-done.12 = bf16[128,2176]{1,0:T(8,128)(2,1)S(1)} collective-permute-done((bf16[128,2176]{1,0:T(8,128)(2,1)S(1)}, bf16[128,2176]{1,0:T(8,128)(2,1)S(1)}, u32[]{:S(2)}, u32[]{:S(2)}) %collective-permute-start.12) | collective-permute-done | bytes 557088 | tf_op jit(solution)/shard_map/ppermute | solution.py:448
  178.2 9.9 %collective-permute-done.11 = bf16[128,2176]{1,0:T(8,128)(2,1)S(1)} collective-permute-done((bf16[128,2176]{1,0:T(8,128)(2,1)S(1)}, bf16[128,2176]{1,0:T(8,128)(2,1)S(1)}, u32[]{:S(2)}, u32[]{:S(2)}) %collective-permute-start.11) | collective-permute-done | bytes 557088 | tf_op jit(solution)/shard_map/ppermute | solution.py:448
  198.0 40.6 %experts.4 = (bf16[8,256,2048]{2,1,0:T(8,128)(2,1)}, bf16[256,2048]{1,0:T(8,128)(2,1)}, bf16[256,2048]{1,0:T(8,128)(2,1)}, bf16[2,1152,2048]{2,1,0:T(8,128)(2,1)...) custom-call(s32[5]{0:T(128)} %pad_add_fusion.which, ...), custom_call_target="tpu_custom_call" | custom-call | flops 1179648 | bytes 1179648 | tf_op jit(solution)/shard_map/experts/pallas_call | solution.py:381
  238.8 28.4 %collective-permute-done.14.refs_0_ = bf16[256,2048]{1,0:T(8,128)(2,1)} collective-permute-done((bf16[256,2048]{1,0:T(8,128)(2,1)S(1)}, bf16[256,2048]{1,0:T(8,128)(2,1)}, u32[]{:S(2)}, u32[]{:S(2)}) %collective-permute-start.14) | collective-permute-done | bytes 1048608 | tf_op jit(solution)/shard_map/ppermute | solution.py:448
  271.5 40.5 %experts.5 = (bf16[8,256,2048]{2,1,0:T(8,128)(2,1)}, bf16[256,2048]{1,0:T(8,128)(2,1)}, bf16[256,2048]{1,0:T(8,128)(2,1)}, bf16[2,1152,2048]{2,1,0:T(8,128)(2,1)...) custom-call(s32[5]{0:T(128)} %stack.88.which, ...), custom_call_target="tpu_custom_call", output_to_operand_aliasing={{0}: (13, {}), {3}: (14, {}), {4}: (15, {}), {5}: (16, {}),... | custom-call | flops 1179648 | bytes 1179648 | tf_op jit(solution)/shard_map/experts/pallas_call | solution.py:381
  322.2 40.7 %experts.6 = (bf16[8,256,2048]{2,1,0:T(8,128)(2,1)}, bf16[256,2048]{1,0:T(8,128)(2,1)}, bf16[256,2048]{1,0:T(8,128)(2,1)}, bf16[2,1152,2048]{2,1,0:T(8,128)(2,1)...) custom-call(s32[5]{0:T(128)} %stack.90.which, ...), custom_call_target="tpu_custom_call", output_to_operand_aliasing={{0}: (13, {}), {3}: (14, {}), {4}: (15, {}), {5}: (16, {}),... | custom-call | flops 1179648 | bytes 1179648 | tf_op jit(solution)/shard_map/experts/pallas_call | solution.py:381
  374.3 40.5 %experts.7 = (bf16[8,256,2048]{2,1,0:T(8,128)(2,1)}, bf16[256,2048]{1,0:T(8,128)(2,1)}, bf16[256,2048]{1,0:T(8,128)(2,1)}, bf16[2,1152,2048]{2,1,0:T(8,128)(2,1)...) custom-call(s32[5]{0:T(128)} %stack.82.which, ...), custom_call_target="tpu_custom_call", output_to_operand_aliasing={{0}: (13, {}), {3}: (14, {}), {4}: (15, {}), {5}: (16, {}),... | custom-call | flops 1179648 | bytes 1179648 | tf_op jit(solution)/shard_map/experts/pallas_call | solution.py:381
  420.4 4.6 collective-permute-start.28
  425.6 18.4 %adapter_grads.1 = bf16[4,2,2304,128]{3,2,1,0:T(8,128)(2,1)} custom-call(s32[4]{0:T(128)} %iota_xor_fusion.which, bf16[2,1152,2048]{2,1,0:T(8,128)(2,1)} %get-tuple-element.200.xs, bf16[2,1152,2048]{2,1,0:T(8,128)(2,1)} %get-tuple-element.201.ps, bf16[2,1152,1024]{2,1,0:T(8,128)(2,1)} %get-tuple-element.202.act, ...), custom_call_target="tpu_custom_call" | custom-call | flops 2359296 | bytes 2359296 | tf_op jit(solution)/shard_map/adapter_grads/pallas_call | solution.py:433
  444.0 4.7 collective-permute-done.28
  448.7 4.1 convert_add_fusion.1
  460.9 24.5 %collective-permute-done.30 = bf16[256,2304]{1,0:T(8,128)(2,1)S(1)} collective-permute-done((bf16[256,2304]{1,0:T(8,128)(2,1)S(1)}, bf16[256,2304]{1,0:T(8,128)(2,1)S(1)}, u32[]{:S(2)}, u32[]{:S(2)}) %collective-permute-start.30) | collective-permute-done | bytes 1179680 | tf_op jit(solution)/shard_map/ppermute | solution.py:448
  492.3 8.4 %collective-permute-done.31 = bf16[128,2304]{1,0:T(8,128)(2,1)} collective-permute-done((bf16[128,2304]{1,0:T(8,128)(2,1)}, bf16[128,2304]{1,0:T(8,128)(2,1)}, u32[]{:S(2)}, u32[]{:S(2)}) %collective-permute-start.31) | collective-permute-done | bytes 589856 | tf_op jit(solution)/shard_map/ppermute | solution.py:448
  519.9 23.6 %attend_back.1 = (bf16[1024,512]{1,0:T(8,128)(2,1)}, bf16[1024,512]{1,0:T(8,128)(2,1)}, bf16[1024,512]{1,0:T(8,128)(2,1)}) custom-call(bf16[1024,512]{1,0:T(8,128)(2,1)} %get-tuple-element.141.query, bf16[1024,512]{1,0:T(8,128)(2,1)} %get-tuple-element.142.key, bf16[1024,512]{1,0:T(8,128)(2,1)} %get-tuple-element.143.value, ...), custom_call_target="tpu_custom_call" | custom-call | flops 524288 | bytes 524288 | tf_op jit(solution)/shard_map/attend_back/pallas_call | solution.py:168
  559.5 12.3 %qkv_back.1 = bf16[1024,2048]{1,0:T(8,128)(2,1)} custom-call(bf16[1024,512]{1,0:T(8,128)(2,1)} %get-tuple-element.241.a_ref, bf16[1024,512]{1,0:T(8,128)(2,1)} %get-tuple-element.242.b_ref, bf16[1024,512]{1,0:T(8,128)(2,1)} %get-tuple-element.243.c_ref, bf16[8,3,64,2048]{3,2,1,0:T(8,128)(2,1)} %bitcast.235), custom_call_target="tpu_custom_call" | custom-call | flops 2097152 | bytes 2097152 | tf_op jit(solution)/shard_map/qkv_back/pallas_call | solution.py:246
  598.3 6.3 collective-permute-done.43
  622.8 5.0 collective-permute-done.45
  (372 shorter events, 233.3 us)
Async XLA Ops:
  7.2 38.1 %all-gather.10.cloned.1.call-start = ((), (), s32[]{:S(2)}) async-start(), calls=%async_computation.5 | async-start | bytes 1179648 | tf_op jit(solution)/shard_map/all_gather | solution.py:573
  14.1 96.4 %all-gather.12.cloned.1.call-start = ((), (), s32[]{:S(2)}) async-start(), calls=%async_computation.6 | async-start | bytes 7077888 | tf_op jit(solution)/shard_map/all_gather | solution.py:578
  17.7 26.1 %collective-permute-start = (bf16[256,2048]{1,0:T(8,128)(2,1)S(1)}, bf16[256,2048]{1,0:T(8,128)(2,1)S(1)}, u32[]{:S(2)}, u32[]{:S(2)}) collective-permute-start(bf16[256,2048]{1,0:T(8,128)(2,1)S(1)} %get-tuple-element.261), channel_id=1, source_target_pairs={{0,8},{8,0},{16,24},{24,16},{1,9},{9,1},{17,25},{25,17},{2,10},{10... | collective-permute-start | bytes 3145736 | tf_op jit(solution)/shard_map/ppermute | solution.py:448
  45.3 99.4 %all-gather.8.cloned.1.call-start = ((), (), s32[]{:S(2)}) async-start(), calls=%async_computation.2 | async-start | bytes 2506752 | tf_op jit(solution)/shard_map/all_gather | solution.py:624
  110.5 161.0 %all-gather.14.cloned.1.call-start = ((), (), s32[]{:S(2)}) async-start(), calls=%async_computation.7 | async-start | bytes 9437184 | tf_op jit(solution)/shard_map/all_gather | solution.py:628
  123.4 508.3 %reduce-scatter.3.cloned.1.call-start = ((), (), s32[]{:S(2)}) async-start(), calls=%async_computation.3 | async-start | bytes 9437184 | tf_op jit(solution)/shard_map/reduce_scatter | solution.py:686
  191.6 75.5 %collective-permute-start.14 = (bf16[256,2048]{1,0:T(8,128)(2,1)S(1)}, bf16[256,2048]{1,0:T(8,128)(2,1)}, u32[]{:S(2)}, u32[]{:S(2)}) collective-permute-start(bf16[256,2048]{1,0:T(8,128)(2,1)S(1)} %multiply_convert_fusion.refs_0_), channel_id=1, source_target_pairs={{0,4},{1,5},{2,6},{3,7},{4,0},{5,1},{6,2},{7,3},{8,12},{9,13},{10,... | collective-permute-start | bytes 3145736 | tf_op jit(solution)/shard_map/ppermute | solution.py:448
  238.5 28.7 %collective-permute-start.18 = (bf16[256,2048]{1,0:T(8,128)(2,1)}, bf16[256,2048]{1,0:T(8,128)(2,1)S(1)}, u32[]{:S(2)}, u32[]{:S(2)}) collective-permute-start(bf16[256,2048]{1,0:T(8,128)(2,1)} %get-tuple-element.153), channel_id=1, source_target_pairs={{0,1},{1,0},{2,3},{3,2},{4,5},{5,4},{6,7},{7,6},{8,9},{9,8},{10,11... | collective-permute-start | bytes 3145736 | tf_op jit(solution)/shard_map/ppermute | solution.py:448
  270.2 42.0 %collective-permute-start.19 = (bf16[256,2048]{1,0:T(8,128)(2,1)S(1)}, bf16[256,2048]{1,0:T(8,128)(2,1)}, u32[]{:S(2)}, u32[]{:S(2)}) collective-permute-start(bf16[256,2048]{1,0:T(8,128)(2,1)S(1)} %copy-done.9), channel_id=1, source_target_pairs={{0,6},{1,7},{2,4},{3,5},{4,2},{5,3},{6,0},{7,1},{8,14},{9,15},{10,... | collective-permute-start | bytes 3145736 | tf_op jit(solution)/shard_map/ppermute | solution.py:448
  317.6 47.8 %collective-permute-start.22 = (bf16[256,2048]{1,0:T(8,128)(2,1)S(1)}, bf16[256,2048]{1,0:T(8,128)(2,1)}, u32[]{:S(2)}, u32[]{:S(2)}) collective-permute-start(bf16[256,2048]{1,0:T(8,128)(2,1)S(1)} %copy-done.9), channel_id=1, source_target_pairs={{0,2},{1,3},{2,0},{3,1},{4,6},{5,7},{6,4},{7,5},{8,10},{9,11},{10,... | collective-permute-start | bytes 3145736 | tf_op jit(solution)/shard_map/ppermute | solution.py:448
  319.4 48.7 %collective-permute-start.23 = (bf16[256,2048]{1,0:T(8,128)(2,1)}, bf16[256,2048]{1,0:T(8,128)(2,1)}, u32[]{:S(2)}, u32[]{:S(2)}) collective-permute-start(bf16[256,2048]{1,0:T(8,128)(2,1)} %add_convert_fusion.3), channel_id=1, source_target_pairs={{0,4},{1,5},{2,6},{3,7},{4,0},{5,1},{6,2},{7,3},{8,12},{9,13},{10,... | collective-permute-start | bytes 3145736 | tf_op jit(solution)/shard_map/ppermute | solution.py:448
  371.0 43.8 %collective-permute-start.26 = (bf16[256,2048]{1,0:T(8,128)(2,1)}, bf16[256,2048]{1,0:T(8,128)(2,1)}, u32[]{:S(2)}, u32[]{:S(2)}) collective-permute-start(bf16[256,2048]{1,0:T(8,128)(2,1)} %add_convert_fusion.2), channel_id=1, source_target_pairs={{0,6},{1,7},{2,4},{3,5},{4,2},{5,3},{6,0},{7,1},{8,14},{9,15},{10,... | collective-permute-start | bytes 3145736 | tf_op jit(solution)/shard_map/ppermute | solution.py:448
  420.4 28.3 %collective-permute-start.28 = (bf16[256,2048]{1,0:T(8,128)(2,1)}, bf16[256,2048]{1,0:T(8,128)(2,1)S(1)}, u32[]{:S(2)}, u32[]{:S(2)}) collective-permute-start(bf16[256,2048]{1,0:T(8,128)(2,1)} %add_convert_fusion.1), channel_id=1, source_target_pairs={{0,2},{1,3},{2,0},{3,1},{4,6},{5,7},{6,4},{7,5},{8,10},{9,11},{10,... | collective-permute-start | bytes 3145736 | tf_op jit(solution)/shard_map/ppermute | solution.py:448
  452.8 185.4 %reduce-scatter.5.cloned.1.call-start = ((), (), s32[]{:S(2)}) async-start(), calls=%async_computation.4 | async-start | bytes 737280 | tf_op jit(solution)/shard_map/reduce_scatter | solution.py:736
  457.9 27.5 %collective-permute-start.30 = (bf16[256,2304]{1,0:T(8,128)(2,1)S(1)}, bf16[256,2304]{1,0:T(8,128)(2,1)S(1)}, u32[]{:S(2)}, u32[]{:S(2)}) collective-permute-start(bf16[256,2304]{1,0:T(8,128)(2,1)S(1)} %pad_maximum_fusion.3), channel_id=1, source_target_pairs={{0,16},{8,24},{16,0},{24,8},{1,17},{9,25},{17,1},{25,9},{2,18},{10... | collective-permute-start | bytes 3538952 | tf_op jit(solution)/shard_map/ppermute | solution.py:448
  459.4 28.4 %collective-permute-start.29 = (bf16[256,2304]{1,0:T(8,128)(2,1)S(1)}, bf16[256,2304]{1,0:T(8,128)(2,1)S(1)}, u32[]{:S(2)}, u32[]{:S(2)}) collective-permute-start(bf16[256,2304]{1,0:T(8,128)(2,1)S(1)} %pad_maximum_fusion.3), channel_id=1, source_target_pairs={{0,8},{8,0},{16,24},{24,16},{1,9},{9,1},{17,25},{25,17},{2,10},{10... | collective-permute-start | bytes 3538952 | tf_op jit(solution)/shard_map/ppermute | solution.py:448
  507.6 40.7 %collective-permute-start.33 = (bf16[1,2304,128]{2,1,0:T(8,128)(2,1)}, bf16[1,2304,128]{2,1,0:T(8,128)(2,1)}, u32[]{:S(2)}, u32[]{:S(2)}) collective-permute-start(bf16[1,2304,128]{2,1,0:T(8,128)(2,1)} %get-tuple-element.271), channel_id=1, source_target_pairs={{0,8},{8,0},{16,24},{24,16},{1,9},{9,1},{17,25},{25,17},{2,10},{10... | collective-permute-start | bytes 1769480 | tf_op jit(solution)/shard_map/ppermute | solution.py:448
  508.1 40.2 %collective-permute-start.34 = (bf16[1,2304,128]{2,1,0:T(8,128)(2,1)}, bf16[1,2304,128]{2,1,0:T(8,128)(2,1)}, u32[]{:S(2)}, u32[]{:S(2)}) collective-permute-start(bf16[1,2304,128]{2,1,0:T(8,128)(2,1)} %get-tuple-element.270), channel_id=1, source_target_pairs={{0,16},{8,24},{16,0},{24,8},{1,17},{9,25},{17,1},{25,9},{2,18},{10... | collective-permute-start | bytes 1769480 | tf_op jit(solution)/shard_map/ppermute | solution.py:448
  509.6 38.8 %collective-permute-start.35 = (bf16[1,2304,128]{2,1,0:T(8,128)(2,1)}, bf16[1,2304,128]{2,1,0:T(8,128)(2,1)}, u32[]{:S(2)}, u32[]{:S(2)}) collective-permute-start(bf16[1,2304,128]{2,1,0:T(8,128)(2,1)} %get-tuple-element.269), channel_id=1, source_target_pairs={{0,8},{8,0},{16,24},{24,16},{1,9},{9,1},{17,25},{25,17},{2,10},{10... | collective-permute-start | bytes 1769480 | tf_op jit(solution)/shard_map/ppermute | solution.py:448
  511.1 37.2 %collective-permute-start.36 = (bf16[1,2304,128]{2,1,0:T(8,128)(2,1)}, bf16[1,2304,128]{2,1,0:T(8,128)(2,1)}, u32[]{:S(2)}, u32[]{:S(2)}) collective-permute-start(bf16[1,2304,128]{2,1,0:T(8,128)(2,1)} %get-tuple-element.268), channel_id=1, source_target_pairs={{0,16},{8,24},{16,0},{24,8},{1,17},{9,25},{17,1},{25,9},{2,18},{10... | collective-permute-start | bytes 1769480 | tf_op jit(solution)/shard_map/ppermute | solution.py:448
  558.0 29.1 %collective-permute-start.40 = (bf16[1,2304,128]{2,1,0:T(8,128)(2,1)}, bf16[1,2304,128]{2,1,0:T(8,128)(2,1)}, u32[]{:S(2)}, u32[]{:S(2)}) collective-permute-start(bf16[1,2304,128]{2,1,0:T(8,128)(2,1)} %get-tuple-element.233), channel_id=1, source_target_pairs={{0,16},{8,24},{16,0},{24,8},{1,17},{9,25},{17,1},{25,9},{2,18},{10... | collective-permute-start | bytes 1769480 | tf_op jit(solution)/shard_map/ppermute | solution.py:448
  558.8 28.2 %collective-permute-start.41 = (bf16[1,2304,128]{2,1,0:T(8,128)(2,1)}, bf16[1,2304,128]{2,1,0:T(8,128)(2,1)}, u32[]{:S(2)}, u32[]{:S(2)}) collective-permute-start(bf16[1,2304,128]{2,1,0:T(8,128)(2,1)} %get-tuple-element.234), channel_id=1, source_target_pairs={{0,8},{8,0},{16,24},{24,16},{1,9},{9,1},{17,25},{25,17},{2,10},{10... | collective-permute-start | bytes 1769480 | tf_op jit(solution)/shard_map/ppermute | solution.py:448
  592.4 30.5 %collective-permute-start.42 = (bf16[128,2048]{1,0:T(8,128)(2,1)}, bf16[128,2048]{1,0:T(8,128)(2,1)}, u32[]{:S(2)}, u32[]{:S(2)}) collective-permute-start(bf16[128,2048]{1,0:T(8,128)(2,1)} %get-tuple-element.282), channel_id=1, source_target_pairs={{0,8},{8,0},{16,24},{24,16},{1,9},{9,1},{17,25},{25,17},{2,10},{10... | collective-permute-start | bytes 1572872 | tf_op jit(solution)/shard_map/ppermute | solution.py:448
  592.8 30.0 %collective-permute-start.46 = (bf16[128,2048]{1,0:T(8,128)(2,1)}, bf16[128,2048]{1,0:T(8,128)(2,1)}, u32[]{:S(2)}, u32[]{:S(2)}) collective-permute-start(bf16[128,2048]{1,0:T(8,128)(2,1)} %get-tuple-element.283), channel_id=1, source_target_pairs={{0,16},{8,24},{16,0},{24,8},{1,17},{9,25},{17,1},{25,9},{2,18},{10... | collective-permute-start | bytes 1572872 | tf_op jit(solution)/shard_map/ppermute | solution.py:448
  (88 other events, 793.3 us)
Sparse Core Ops, SparseCore 0:
  14.2 24.9 all-gather.9
  45.4 65.0 all-gather.11
  112.1 28.8 all-gather.7
  142.5 117.5 all-gather.13
  452.9 88.8 reduce-scatter.2
  584.1 30.2 reduce-scatter.4
